TPU v7x, 32 devices: a whole 2x2x4 slice. The times are simulated.
32 devices in a mesh: parts: 2 (over y), space: 4 (over z), mem: 4 (over x, core).
Axes of the slice: x: 2, y: 2, z: 4, core: 2. Of those that a mesh axis runs over, the one named last changes fastest.
Arguments:
- prior_replicas: float32 [128, 2, 32, 2048], P(('parts', 'mem'), None, 'space'), parts along dimension 0, may hold values from -6 to 6
- wind_field: float32 [4, 2, 32, 2048], P('parts', None, 'space'), parts along dimension 0, may hold values from -0.4 to 0.4
- obs_index: int32 [16384], P(('parts', 'space')), parts along dimension 0, may hold values from 0 to 32767, as said below
- obs_count: int32 [8], P(('parts', 'space')), parts along dimension 0, may hold values from 256 to 2048, as said below
- obs_value: float32 [16384], P(('parts', 'space')), parts along dimension 0, may hold values from -6 to 6
- obs_weight: float32 [16384], P(('parts', 'space')), parts along dimension 0, may hold values from 0.05 to 0.5
Outputs:
- analysis: float32 [128, 2, 32, 2048], P(('parts', 'mem'), None, 'space'), parts along dimension 0
There are 2 independent parts, one for each index of `parts`. A program takes and returns all parts, laid end to end along the dimension named above; each array names one. Nothing has to cross between parts.
Inputs may be any that keep to these rules, and one draw needn't show every extreme that they name: `obs_index`: the slots of one strip name distinct cells of that strip, as f * 8 * 2048 + r * 2048 + c for field f, local row r and column c. `obs_count`: one entry per strip; some strip uses all 2048 slots.
All inputs are finite; a program needn't handle non-finite values.
Results may differ from a plain program's by a relative error of at most 0.0038.
Values may be sent and summed in bfloat16 or wider, within the bound.
No kernel may reach another device: no remote copies, remote signals or barrier semaphores. Data moves between devices by JAX's collectives and lax.ppermute only.
A program may use at most 128 MiB of HBM per device.

v0:
```python
import jax
import jax.numpy as jnp
from jax import lax
from jax.sharding import PartitionSpec as P

REPLICA_COUNT = 64
NS_ITERS = 5


DIFFUSION = (0.05, 0.15)


def padded(value, sides, width):
    for axis, dim in sides:
        peers, length = (lax.axis_size(axis), value.shape[dim])
        up = [(i, (i + 1) % peers) for i in range(peers - 1)]
        down = [(j, i) for i, j in up]
        last = lax.slice_in_dim(value, length - width, length, axis=dim)
        initial = lax.slice_in_dim(value, 0, width, axis=dim)
        before = lax.ppermute(last, axis, up)
        after = lax.ppermute(initial, axis, down)
        value = jnp.concatenate([before, value, after], axis=dim)
    return value


def shift_columns(field, offset):
    width = field.shape[-1]
    blank = jnp.zeros(field.shape[:-1] + (abs(offset),), field.dtype)
    if offset > 0:
        return jnp.concatenate([field[..., offset:], blank], -1)
    return jnp.concatenate([blank, field[..., : width + offset]], -1)


def advance(extended, wind_rows):
    center = extended[:, :, 2:-2]
    north_one = extended[:, :, 3:-1]
    south_one = extended[:, :, 1:-3]
    north_two = extended[:, :, 4:]
    south_two = extended[:, :, :-4]
    east_one = shift_columns(center, 1)
    west_one = shift_columns(center, -1)
    east_two = shift_columns(center, 2)
    west_two = shift_columns(center, -2)
    grad_row = (8.0 * (north_one - south_one) - (north_two - south_two)) / 12.0
    grad_col = (8.0 * (east_one - west_one) - (east_two - west_two)) / 12.0
    laplace = north_one + south_one + east_one + west_one - 4.0 * center
    diffusion = jnp.array(DIFFUSION, jnp.float32).reshape(2, 1, 1)
    return center - wind_rows[0] * grad_row - wind_rows[1] * grad_col + diffusion * laplace


def shard_terms(observed, slot_weight, obs_value):
    obs_mean = jnp.sum(observed, 0) / REPLICA_COUNT
    obs_anomaly = observed - obs_mean
    weighted = obs_anomaly * slot_weight
    gram = jnp.dot(
        weighted, obs_anomaly.T, precision=lax.Precision.HIGHEST, preferred_element_type=jnp.float32
    )
    drive = jnp.dot(
        weighted,
        obs_value - obs_mean,
        precision=lax.Precision.HIGHEST,
        preferred_element_type=jnp.float32,
    )
    return (gram, drive)


def ensemble_weights(gram, drive):
    ident = jnp.eye(REPLICA_COUNT, dtype=jnp.float32)
    system = (REPLICA_COUNT - 1.0) * ident + gram
    scale = jnp.sqrt(jnp.sum(system * system))

    def newton_turn(turn, carry):
        root, inverse_root = carry
        middle_term = 0.5 * (
            3.0 * ident
            - jnp.dot(
                inverse_root,
                root,
                precision=lax.Precision.HIGHEST,
                preferred_element_type=jnp.float32,
            )
        )
        root = jnp.dot(
            root, middle_term, precision=lax.Precision.HIGHEST, preferred_element_type=jnp.float32
        )
        inverse_root = jnp.dot(
            middle_term,
            inverse_root,
            precision=lax.Precision.HIGHEST,
            preferred_element_type=jnp.float32,
        )
        return (root, inverse_root)

    root, inverse_root = lax.fori_loop(0, NS_ITERS, newton_turn, (system / scale, ident))
    half = inverse_root / jnp.sqrt(scale)
    precision_matrix = jnp.dot(
        half, half, precision=lax.Precision.HIGHEST, preferred_element_type=jnp.float32
    )
    mean_weight = jnp.dot(
        precision_matrix, drive, precision=lax.Precision.HIGHEST, preferred_element_type=jnp.float32
    )
    spread = jnp.sqrt(REPLICA_COUNT - 1.0) * half
    return (mean_weight[:, None] + spread).astype(jnp.bfloat16)


def local(prior_replicas, wind_field, obs_index, obs_count, obs_value, obs_weight):
    member_count, field_count, row_count, col_count = prior_replicas.shape
    state = prior_replicas
    for step_index in range(2):
        extended = padded(state, (("space", 2),), 2)
        state = advance(extended, wind_field[step_index])
    capacity = obs_index.shape[0]
    raveled_vector = state.reshape(member_count, -1)
    local_obs = jnp.take(raveled_vector, obs_index, axis=1)
    slot_number = jnp.arange(capacity, dtype=jnp.int32)
    slot_weight = obs_weight * (slot_number < obs_count[0]).astype(jnp.float32)
    gathered = lax.all_gather(local_obs, "mem", axis=0, tiled=True)
    gram, drive = shard_terms(gathered, slot_weight, obs_value)
    gram, drive = lax.psum((gram, drive), "space")
    transform = ensemble_weights(gram, drive)
    transform_rows = transform.T
    block = lax.all_to_all(state, "mem", split_axis=3, concat_axis=0, tiled=True)
    replica_centroid = jnp.sum(block, 0) / REPLICA_COUNT
    replica_departure = (block - replica_centroid).astype(jnp.bfloat16)
    posterior_correction = jnp.dot(
        transform_rows,
        replica_departure.reshape(REPLICA_COUNT, -1),
        preferred_element_type=jnp.float32,
    )
    analysed = posterior_correction.reshape(block.shape) + replica_centroid
    return lax.all_to_all(analysed, "mem", split_axis=0, concat_axis=3, tiled=True)


def solution(mesh):
    in_specs = (
        P(("parts", "mem"), None, "space", None),
        P("parts", None, "space", None),
        P(("parts", "space")),
        P(("parts", "space")),
        P(("parts", "space")),
        P(("parts", "space")),
    )
    out_specs = P(("parts", "mem"), None, "space", None)
    return jax.shard_map(local, mesh=mesh, in_specs=in_specs, out_specs=out_specs, check_vma=False)
```

profile of v0, /device:TPU:0, one launch (start us, length us, event | category | flops | bytes accessed | tf_op | source)
XLA Modules:
  0.0 220.6 jit_solution(2224251359348248009)
XLA Ops:
  0.0 2.8 %fusion.44 = (f32[16,2,2,2048]{3,2,1,0:T(2,128)S(1)}, f32[16,2,2,2048]{3,2,1,0:T(2,128)S(1)}) fusion(f32[16,2,8,2048]{3,2,1,0:T(8,128)} %param.10), kind=kLoop, calls=%fused_computation.77 | loop fusion | bytes 2097152 | tf_op jit(solution)/shard_map/slice | solution.py:19
  4.0 5.7 %collective-permute-start.1 = (f32[16,2,2,2048]{3,0,2,1:T(8,128)}, f32[16,2,2,2048]{3,0,2,1:T(8,128)}, u32[]{:S(2)}, u32[]{:S(2)}) collective-permute-start(f32[16,2,2,2048]{3,0,2,1:T(8,128)} %copy.66), channel_id=1, source_target_pairs={{0,4},{4,8},{8,12},{1,5},{5,9},{9,13},{2,6},{6,10},{10,14},{3,7},{... | collective-permute-start | bytes 1572872 | tf_op jit(solution)/shard_map/ppermute | solution.py:20
  10.0 1.3 collective-permute-start
  12.9 2.5 %copy.68 = f32[16,2,8,2046]{3,0,2,1:T(8,128)} copy(f32[16,2,8,2046]{3,2,1,0:T(8,128)S(1)} %get-tuple-element.65) | data formatting | bytes 4190208
  15.4 2.6 %copy.69 = f32[16,2,8,2046]{3,0,2,1:T(8,128)} copy(f32[16,2,8,2046]{3,2,1,0:T(8,128)S(1)} %get-tuple-element.64) | data formatting | bytes 4190208
  18.0 2.5 %copy.70 = f32[16,2,8,2047]{3,0,2,1:T(8,128)} copy(f32[16,2,8,2047]{3,2,1,0:T(8,128)S(1)} %get-tuple-element.63) | data formatting | bytes 4192256
  20.5 2.6 %copy.71 = f32[16,2,8,2047]{3,0,2,1:T(8,128)} copy(f32[16,2,8,2047]{3,2,1,0:T(8,128)S(1)} %get-tuple-element.62) | data formatting | bytes 4192256
  23.8 1.2 constant_dynamic-update-slice_fusion.3
  25.1 1.2 constant_dynamic-update-slice_fusion.1
  28.0 4.0 %fusion.15 = f32[16,2,8,2048]{3,0,2,1:T(8,128)S(1)} fusion(f32[16,2,10,2048]{3,0,2,1:T(8,128)S(1)} %get-tuple-element.69, f32[16,2,10,2048]{3,0,2,1:T(8,128)S(1)} %constant_dynamic-update-slice_fusion, f32[16,2,8,2046]{3,0,2,1:T(8,128)S(1)} %copy-done.1, f32[16,2,8,2046]{3,0,2,1:T(8,128)S(1)} %copy-done.2, f32[16,2,8,2047]{3,0,2,1:T(8,128)S(1)} %copy-done.3, ...), kind=kLoop, calls=%fused_computation.25 | loop fusion | flops 9961472 | bytes 21096456 | tf_op jit(solution)/shard_map/add | solution.py:48
  32.9 1.3 collective-permute-start.2
  34.2 5.4 %collective-permute-start.3 = (f32[16,2,2,2048]{3,0,2,1:T(8,128)S(1)}, f32[16,2,2,2048]{3,0,2,1:T(8,128)S(1)}, u32[]{:S(2)}, u32[]{:S(2)}) collective-permute-start(f32[16,2,2,2048]{3,0,2,1:T(8,128)S(1)} %get-tuple-element.61), channel_id=1, source_target_pairs={{0,4},{4,8},{8,12},{1,5},{5,9},{9,13},{2,6},{6,10},{10,14},{3,7},{... | collective-permute-start | bytes 1572872 | tf_op jit(solution)/shard_map/ppermute | solution.py:20
  40.3 8.4 %collective-permute-done.2 = f32[16,2,2,2048]{3,0,2,1:T(8,128)S(1)} collective-permute-done((f32[16,2,2,2048]{3,0,2,1:T(8,128)S(1)}, f32[16,2,2,2048]{3,0,2,1:T(8,128)S(1)}, u32[]{:S(2)}, u32[]{:S(2)}) %collective-permute-start.2) | collective-permute-done | bytes 524320 | tf_op jit(solution)/shard_map/ppermute | solution.py:21
  49.9 2.5 %fusion.10 = f32[16,2,8,2048]{3,0,2,1:T(8,128)S(1)} fusion(f32[16,2,8,2048]{3,0,2,1:T(8,128)S(1)} %fusion.15, f32[16,2,2,2048]{3,0,2,1:T(8,128)S(1)} %collective-permute-done.3, f32[16,2,2,2048]{3,0,2,1:T(8,128)S(1)} %collective-permute-done.2, f32[16,2,8,2046]{3,0,2,1:T(8,128)S(1)} %get-tuple-element.59, f32[16,2,8,2046]{3,0,2,1:T(8,128)S(1)} %get-tuple-element.58, ...), kind=kLoop, calls=%fused_computation.18 | loop fusion | flops 12058624 | bytes 13756424 | tf_op jit(solution)/shard_map/add | solution.py:48
  52.5 8.5 %copy.48 = f32[16,2,8,2048]{0,3,2,1:T(8,128)} copy(f32[16,2,8,2048]{3,0,2,1:T(8,128)S(1)} %fusion.10) | data formatting | bytes 4194304 | tf_op jit(solution)/shard_map/add | solution.py:48
  61.0 11.1 %copy.51 = f32[16,2,8,2048]{0,2,1,3:T(8,128)} copy(f32[16,2,8,2048]{3,0,2,1:T(8,128)S(1)} %fusion.10) | data formatting | bytes 4194304 | tf_op jit(solution)/shard_map/add | solution.py:48
  72.1 11.2 %gather_fusion = f32[2048,16]{1,0:T(8,128)S(1)} fusion(f32[16,32768]{0,1:T(8,128)} %bitcast.70, s32[2048]{0:T(1024)S(1)} %fusion.34), kind=kCustom, calls=%fused_computation | custom fusion | bytes 270336 | tf_op jit(solution)/shard_map/jit(_take)/gather | solution.py:114
  84.0 7.2 %all_gather.3 = f32[64,2048]{1,0:T(8,128)S(1)} all-gather(f32[16,2048]{1,0:T(8,128)S(1)} %copy.49), channel_id=1, replica_groups=mesh['parts'=2,'space'=4,'mem'=4] {'mem'}, dimensions={0}, use_global_device_ids=true | all-gather | bytes 655360 | tf_op jit(solution)/shard_map/all_gather | solution.py:117
  92.3 19.9 %all-reduce.8 = (f32[64,64]{1,0:T(8,128)S(1)}, f32[64]{0:T(128)S(1)}) all-reduce(f32[64,64]{1,0:T(8,128)S(1)} %fusion.18, f32[64]{0:T(128)S(1)} %convolution_bitcast_fusion.2), channel_id=1, replica_groups=mesh['parts'=2,'space'=4,'mem'=4] {'space'}, use_global_device_ids=true, to_apply=%region_1.2 | all-reduce | flops 4160 | bytes 33280 | tf_op jit(solution)/shard_map/psum | solution.py:119
  113.7 10.1 %reshape.58 = f32[4,1,131072]{2,1,0:T(1,128)} reshape(f32[2048,2,8,16]{3,2,1,0:T(8,128)} %bitcast.68) | data formatting | bytes 4194304
  123.8 3.8 %all-to-all-start = ((f32[4,1,131072]{2,1,0:T(1,128)}), f32[4,1,131072]{2,1,0:T(1,128)S(1)}, u32[]{:S(2)}, u32[]{:S(2)}) async-start(f32[4,1,131072]{2,1,0:T(1,128)} %reshape.58), calls=%async_computation | async-start | bytes 4194304 | tf_op jit(solution)/shard_map/all_to_all | solution.py:122
  127.6 3.2 %while.13 = (s32[]{:T(128)}, f32[64,64]{0,1:T(8,128)S(1)}, f32[64,64]{1,0:T(8,128)S(1)}, s32[]{:T(128)}) while((s32[]{:T(128)}, f32[64,64]{0,1:T(8,128)S(1)}, f32[64,64]{1,0:T(8,128)S(1)}, s32[]{:T(128)}) %tuple.37), condition=%wide.region_4.5_spmd.clone, body=%wide.region_3.4_spmd.clone.sunk | while | flops 9453570 | bytes 213045 | solution.py:94
  131.2 21.9 %all-to-all-done = f32[4,1,131072]{2,1,0:T(1,128)S(1)} async-done(((f32[4,1,131072]{2,1,0:T(1,128)}), f32[4,1,131072]{2,1,0:T(1,128)S(1)}, u32[]{:S(2)}, u32[]{:S(2)}) %all-to-all-start) | async-done | bytes 2097184 | tf_op jit(solution)/shard_map/all_to_all | solution.py:122
  153.1 1.3 copy-done.5
  154.9 7.7 %reduce.1 = f32[4,131072]{1,0:T(4,128)S(1)} reduce(f32[4,1,131072]{2,1,0:T(1,128)} %copy-done.5, f32[]{:T(128)} %broadcast.101), dimensions={1}, to_apply=%all_to_all.26.reduce_sub_computation | reduce | bytes 4194308 | tf_op jit(solution)/shard_map/all_to_all | solution.py:122
  162.6 11.5 %reshape.59 = f32[2048,2,8,16]{3,2,1,0:T(8,128)} reshape(f32[4,131072]{1,0:T(4,128)S(1)} %reduce.1) | data formatting | bytes 4194304
  174.2 10.2 %copy.52 = f32[16,2,8,4,512]{4,2,1,0,3:T(8,128)S(1)} copy(f32[16,2,8,4,512]{0,2,1,4,3:T(8,128)} %bitcast.69) | data formatting | bytes 4194304 | tf_op jit(solution)/shard_map/all_to_all | solution.py:122
  184.6 1.5 all_to_all.29
  186.1 1.7 subtract_convert_fusion
  188.2 1.5 convolution_add_fusion
  190.9 28.2 %all_to_all.36 = f32[64,2,8,512]{3,2,1,0:T(8,128)S(1)} all-to-all(f32[64,2,8,512]{3,2,1,0:T(8,128)S(1)} %copy.55), channel_id=1, replica_groups=mesh['parts'=2,'space'=4,'mem'=4] {'mem'}, dimensions={0} | all-to-all | bytes 4194304 | tf_op jit(solution)/shard_map/all_to_all | solution.py:131
  219.1 1.5 copy.56
  (79 shorter events, 15.5 us)
Async XLA Ops:
  0.0 11.3 %copy-start = (f32[16,2,8,2048]{3,2,1,0:T(8,128)S(1)}, f32[16,2,8,2048]{3,2,1,0:T(8,128)}, u32[]{:S(2)}) copy-start(f32[16,2,8,2048]{3,2,1,0:T(8,128)} %param.10) | copy-start | bytes 6291460
  4.0 19.8 %collective-permute-start.1 = (f32[16,2,2,2048]{3,0,2,1:T(8,128)}, f32[16,2,2,2048]{3,0,2,1:T(8,128)}, u32[]{:S(2)}, u32[]{:S(2)}) collective-permute-start(f32[16,2,2,2048]{3,0,2,1:T(8,128)} %copy.66), channel_id=1, source_target_pairs={{0,4},{4,8},{8,12},{1,5},{5,9},{9,13},{2,6},{6,10},{10,14},{3,7},{... | collective-permute-start | bytes 1572872 | tf_op jit(solution)/shard_map/ppermute | solution.py:20
  10.0 16.3 %collective-permute-start = (f32[16,2,2,2048]{3,0,2,1:T(8,128)S(1)}, f32[16,2,2,2048]{3,0,2,1:T(8,128)S(1)}, u32[]{:S(2)}, u32[]{:S(2)}) collective-permute-start(f32[16,2,2,2048]{3,0,2,1:T(8,128)S(1)} %copy.67), channel_id=1, source_target_pairs={{4,0},{8,4},{12,8},{5,1},{9,5},{13,9},{6,2},{10,6},{14,10},{7,3},{... | collective-permute-start | bytes 1572872 | tf_op jit(solution)/shard_map/ppermute | solution.py:21
  12.1 0.8 copy-start.7
  20.5 3.2 %copy-start.8 = (f32[2048]{0:T(1024)S(1)}, f32[2048]{0:T(1024)}, u32[]{:S(2)}) copy-start(f32[2048]{0:T(1024)} %param.15) | copy-start | bytes 24580
  20.5 3.2 %copy-start.6 = (f32[2,2,8,2048]{3,2,1,0:T(8,128)S(1)}, f32[2,2,8,2048]{3,2,1,0:T(8,128)}, u32[]{:S(2)}) copy-start(f32[2,2,8,2048]{3,2,1,0:T(8,128)} %param.11) | copy-start | bytes 786436
  23.8 2.6 %copy-start.4 = (f32[16,2,8,2047]{3,0,2,1:T(8,128)S(1)}, f32[16,2,8,2047]{3,0,2,1:T(8,128)}, u32[]{:S(2)}) copy-start(f32[16,2,8,2047]{3,0,2,1:T(8,128)} %copy.71) | copy-start | bytes 6288388
  25.1 1.7 copy-start.1
  25.1 2.3 %copy-start.2 = (f32[16,2,8,2046]{3,0,2,1:T(8,128)S(1)}, f32[16,2,8,2046]{3,0,2,1:T(8,128)}, u32[]{:S(2)}) copy-start(f32[16,2,8,2046]{3,0,2,1:T(8,128)} %copy.69) | copy-start | bytes 6285316
  25.1 2.9 %copy-start.3 = (f32[16,2,8,2047]{3,0,2,1:T(8,128)S(1)}, f32[16,2,8,2047]{3,0,2,1:T(8,128)}, u32[]{:S(2)}) copy-start(f32[16,2,8,2047]{3,0,2,1:T(8,128)} %copy.70) | copy-start | bytes 6288388
  25.1 2.9 %copy-start.10 = (f32[2]{0:T(128)S(1)}, f32[2]{0:T(128)}, u32[]{:S(2)}) copy-start(f32[2]{0:T(128)} %constant.52.clone) | copy-start | bytes 28
  32.9 15.9 %collective-permute-start.2 = (f32[16,2,2,2048]{3,0,2,1:T(8,128)S(1)}, f32[16,2,2,2048]{3,0,2,1:T(8,128)S(1)}, u32[]{:S(2)}, u32[]{:S(2)}) collective-permute-start(f32[16,2,2,2048]{3,0,2,1:T(8,128)S(1)} %get-tuple-element.60), channel_id=1, source_target_pairs={{4,0},{8,4},{12,8},{5,1},{9,5},{13,9},{6,2},{10,6},{14,10},{7,3},{... | collective-permute-start | bytes 1572872 | tf_op jit(solution)/shard_map/ppermute | solution.py:21
  34.2 15.8 %collective-permute-start.3 = (f32[16,2,2,2048]{3,0,2,1:T(8,128)S(1)}, f32[16,2,2,2048]{3,0,2,1:T(8,128)S(1)}, u32[]{:S(2)}, u32[]{:S(2)}) collective-permute-start(f32[16,2,2,2048]{3,0,2,1:T(8,128)S(1)} %get-tuple-element.61), channel_id=1, source_target_pairs={{0,4},{4,8},{8,12},{1,5},{5,9},{9,13},{2,6},{6,10},{10,14},{3,7},{... | collective-permute-start | bytes 1572872 | tf_op jit(solution)/shard_map/ppermute | solution.py:20
  83.3 7.9 %copy-start.9 = (f32[2048]{0:T(1024)S(1)}, f32[2048]{0:T(1024)}, u32[]{:S(2)}) copy-start(f32[2048]{0:T(1024)} %param.14) | copy-start | bytes 24580
  123.8 29.3 %all-to-all-start = ((f32[4,1,131072]{2,1,0:T(1,128)}), f32[4,1,131072]{2,1,0:T(1,128)S(1)}, u32[]{:S(2)}, u32[]{:S(2)}) async-start(f32[4,1,131072]{2,1,0:T(1,128)} %reshape.58), calls=%async_computation | async-start | bytes 4194304 | tf_op jit(solution)/shard_map/all_to_all | solution.py:122
  153.1 1.3 copy-start.5
where the time goes:
time: 221 us
  local copies, waits for them, and re-layouts  91.4 us (41%)
  blocking collectives  55.3 us (25%)
  waiting for transfers between devices  31.5 us (14%)
  starting transfers between devices  17.5 us (8%)
  other arithmetic  17.1 us (8%)
  matrix products  5.81 us (3%)
    unnamed x35, local copies, waits for them, and re-layouts  39.1 us
    all_to_all x1, blocking collectives, local(): lax.all_to_all(analysed, 'mem', split_axis=0, concat_axis=3, tiled=True)  28.2 us
    all_to_all x1, waiting for transfers between devices, local(): lax.all_to_all(state, 'mem', split_axis=3, concat_axis=0, tiled=True)  21.9 us
    psum x1, blocking collectives, local(): gram, drive = lax.psum((gram, drive), 'space')  19.9 us
    add x2, local copies, waits for them, and re-layouts, advance(): center - wind_rows[0] * grad_row - wind_rows[1] * grad_col  19.6 us
    all_to_all x3, local copies, waits for them, and re-layouts, local(): lax.all_to_all(state, 'mem', split_axis=3, concat_axis=0, tiled=True)  12.3 us
    gather x1, local copies, waits for them, and re-layouts, local(): local_obs = jnp.take(raveled_vector, obs_index, axis=1)  11.2 us
    ppermute x2, starting transfers between devices, padded(): before = lax.ppermute(last, axis, up)  11.1 us
  transfers between devices with their start and end apart: 5, of which 3 were waited for; matrix products, arithmetic and copies ran while one was open for 8% of the time, Pallas kernels for 0%

commit v1 on v0

--- a/solution.py
+++ b/solution.py
@@ -1,6 +1,8 @@
 import jax
 import jax.numpy as jnp
 from jax import lax
+from jax.experimental import pallas as pl
+from jax.experimental.pallas import tpu as pltpu
 from jax.sharding import PartitionSpec as P
 
 REPLICA_COUNT = 64
@@ -103,7 +105,7 @@
     return (mean_weight[:, None] + spread).astype(jnp.bfloat16)
 
 
-def local(prior_replicas, wind_field, obs_index, obs_count, obs_value, obs_weight):
+def local_generic(prior_replicas, wind_field, obs_index, obs_count, obs_value, obs_weight):
     member_count, field_count, row_count, col_count = prior_replicas.shape
     state = prior_replicas
     for step_index in range(2):
@@ -131,6 +133,379 @@
     return lax.all_to_all(analysed, "mem", split_axis=0, concat_axis=3, tiled=True)
 
 
+BF = jnp.bfloat16
+F32 = jnp.float32
+PAD = 128
+
+
+def vmem():
+    return pl.BlockSpec(memory_space=pltpu.VMEM)
+
+
+def smem():
+    return pl.BlockSpec(memory_space=pltpu.SMEM)
+
+
+def params():
+    return pltpu.CompilerParams(vmem_limit_bytes=44 * 1024 * 1024)
+
+
+def pack_kernel(pos, prior, wind, turned, pay_a, pay_b):
+    for f in range(2):
+        turned[f] = jnp.swapaxes(prior[:, f], 0, 1)
+    even = (pos[0] % 2) == 0
+    start_a = jnp.where(even, 4, 0)
+    start_b = 4 - start_a
+    for f in range(2):
+        for r in range(4):
+            at = (f * 4 + r) * 16
+            pay_a[at : at + 16, :] = turned[f, start_a + r].astype(BF)
+            pay_b[at : at + 16, :] = turned[f, start_b + r].astype(BF)
+    first = jnp.concatenate([wind[0, 0, 0:2], wind[0, 1, 0:2]], 0)
+    last = jnp.concatenate([wind[0, 0, 6:8], wind[0, 1, 6:8]], 0)
+    first_high = first.astype(BF).astype(F32)
+    last_high = last.astype(BF).astype(F32)
+    first = jnp.concatenate([first_high, first - first_high], 0)
+    last = jnp.concatenate([last_high, last - last_high], 0)
+    pay_a[128:136, :] = jnp.where(even, last, first).astype(BF)
+    pay_b[128:136, :] = jnp.where(even, first, last).astype(BF)
+
+
+def maps_kernel(pos, index, count, weight, value, root_map, value_map):
+    slots = index.shape[1]
+    n = index[...]
+    used = lax.broadcasted_iota(jnp.int32, (1, slots), 1) < count[0]
+    root = jnp.where(used, jnp.sqrt(weight[...]), 0.0)
+    rooted = root * value[...]
+    block = n // 128 - pos[2] * 64
+    lane = n % 128
+    hit = lax.broadcasted_iota(jnp.int32, (64, slots), 0) == block
+    hit = jnp.where(hit, 1.0, 0.0).astype(BF)
+    lane_hit = lax.broadcasted_iota(jnp.int32, (128, slots), 0) == lane
+    pieces = []
+    for v in (root, rooted):
+        high = v.astype(BF).astype(F32)
+        for part in (high, v - high):
+            pieces.append(jnp.where(lane_hit, part, 0.0).astype(BF))
+    spread = jnp.concatenate(pieces, 0)
+    out = lax.dot_general(
+        hit, spread, (((1,), (1,)), ((), ())), preferred_element_type=F32
+    )
+    root_map[...] = out[:, 0:128] + out[:, 128:256]
+    value_map[...] = out[:, 256:384] + out[:, 384:512]
+
+
+def stencil_row(rows, wind_r, wind_c, nu):
+    south_two, south_one, center, north_one, north_two = rows
+    width = center.shape[1]
+    east_one = pltpu.roll(center, width - 1, 1)
+    west_one = pltpu.roll(center, 1, 1)
+    east_two = pltpu.roll(center, width - 2, 1)
+    west_two = pltpu.roll(center, 2, 1)
+    grad_r = 8.0 * (north_one - south_one) - (north_two - south_two)
+    grad_c = 8.0 * (east_one - west_one) - (east_two - west_two)
+    ring = (north_one + south_one) + (east_one + west_one)
+    out = (1.0 - 4.0 * nu) * center + nu * ring
+    cut = width - PAD
+    return out[:, :cut] - wind_r * grad_r[:, :cut] - wind_c * grad_c[:, :cut]
+
+
+def stencil_kernel(
+    pos, turned, recv_a, recv_b, wind, out_near, out_far, out_diag, ext, mid, wide, wide2
+):
+    cols = turned.shape[3]
+    even = (pos[0] % 2) == 0
+    start_a = jnp.where(even, 12, 0)
+    start_b = 12 - start_a
+    zeros = jnp.zeros((16, PAD), F32)
+    for f in range(2):
+        for r in range(16):
+            ext[f, r, :, cols:] = zeros
+        for r in range(12):
+            mid[f, r, :, cols:] = zeros
+        for r in range(8):
+            ext[f, r + 4, :, :cols] = turned[f, r]
+        for r in range(4):
+            at = (f * 4 + r) * 16
+            ext[f, start_a + r, :, :cols] = recv_a[at : at + 16, :].astype(F32)
+            ext[f, start_b + r, :, :cols] = recv_b[at : at + 16, :].astype(F32)
+    got_a = recv_a[128:136, :].astype(F32)
+    got_a = got_a[0:4] + got_a[4:8]
+    got_b = recv_b[128:136, :].astype(F32)
+    got_b = got_b[0:4] + got_b[4:8]
+    before = jnp.where(even, got_b, got_a)
+    after = jnp.where(even, got_a, got_b)
+    twelfth = 1.0 / 12.0
+    for c in range(2):
+        for r in range(12):
+            if r < 2:
+                row = before[2 * c + r : 2 * c + r + 1]
+            elif r < 10:
+                row = wind[0, c, r - 2 : r - 1]
+            else:
+                row = after[2 * c + r - 10 : 2 * c + r - 9]
+            wide[c, r] = jnp.broadcast_to(row * twelfth, (8, cols))
+        for r in range(8):
+            row = wind[1, c, r : r + 1]
+            wide2[c, r] = jnp.broadcast_to(row * twelfth, (8, cols))
+
+    for f in range(2):
+
+        def first_step(r, carry, f=f):
+            for g in range(2):
+                span = pl.ds(g * 8, 8)
+                rows = [ext[f, r + i, span, :] for i in range(5)]
+                mid[f, r, span, :cols] = stencil_row(
+                    rows, wide[0, r], wide[1, r], DIFFUSION[f]
+                )
+            return carry
+
+        lax.fori_loop(0, 12, first_step, 0)
+
+    @pl.when(pos[0] == 0)
+    def _():
+        mid[:, 0:2] = jnp.zeros((2, 2) + mid.shape[2:], F32)
+
+    @pl.when(pos[0] == pos[1] - 1)
+    def _():
+        mid[:, 10:12] = jnp.zeros((2, 2) + mid.shape[2:], F32)
+
+    for slot, out, place in ((2, out_far, 0), (3, out_diag, 0), (0, out_near, 0), (1, out_near, 1)):
+        quarter = jnp.bitwise_xor(pos[2], slot)
+        f = quarter // 2
+        base = (quarter % 2) * 4
+        nu = jnp.where(f == 0, DIFFUSION[0], DIFFUSION[1])
+
+        def second_step(r, carry, f=f, base=base, nu=nu, out=out, place=place):
+            row = base + r
+            both = []
+            for g in range(2):
+                span = pl.ds(g * 8, 8)
+                rows = [mid[f, row + i, span, :] for i in range(5)]
+                both.append(stencil_row(rows, wide2[0, row], wide2[1, row], nu))
+            value = jnp.concatenate(both, 0).astype(BF)
+            if place is None:
+                out[r] = value
+            else:
+                out[place * 4 + r] = value
+            return carry
+
+        lax.fori_loop(0, 4, second_step, 0)
+
+
+def gram_kernel(pos, own, mate, far, diag, root_map, value_map, out, spread):
+    tiles = own.shape[2] // 128
+    spread[4] = jnp.zeros(spread.shape[1:], BF)
+    for r in range(4):
+        for t in range(tiles):
+            cut = slice(t * 128, (t + 1) * 128)
+            at = r * tiles + t
+            into = slice(at * 128, (at + 1) * 128)
+            parts = [
+                own[r, :, cut].astype(F32),
+                mate[4 + r, :, cut].astype(F32),
+                far[r, :, cut].astype(F32),
+                diag[r, :, cut].astype(F32),
+            ]
+            total = (parts[0] + parts[1]) + (parts[2] + parts[3])
+            mean = jnp.sum(total, 0, keepdims=True) * (1.0 / REPLICA_COUNT)
+            root = root_map[at : at + 1, :]
+            gap = value_map[at : at + 1, :] - root * mean
+            for g in range(4):
+                spread[jnp.bitwise_xor(pos[2], g), :, into] = ((parts[g] - mean) * root).astype(BF)
+            high = gap.astype(BF).astype(F32)
+            pair = jnp.concatenate([high, gap - high, jnp.zeros((14, 128), F32)], 0)
+            spread[4, :, into] = pair.astype(BF)
+    cells = spread.shape[2]
+    left = spread[...].reshape(80, cells)
+    right = spread[0:4].reshape(64, cells)
+    out[...] = lax.dot_general(
+        left, right, (((1,), (1,)), ((), ())), preferred_element_type=F32
+    )
+
+
+def exact(a, b):
+    return jnp.dot(a, b, precision=lax.Precision.HIGHEST, preferred_element_type=F32)
+
+
+def weights_kernel(pos, one, two, out, keep):
+    total = one[...] + two[...]
+    gram = total[0:64]
+    drive = total[64:65] + total[65:66]
+    row = lax.broadcasted_iota(jnp.int32, (64, 64), 0)
+    col = lax.broadcasted_iota(jnp.int32, (64, 64), 1)
+    ident = jnp.where(row == col, 1.0, 0.0)
+    system = (REPLICA_COUNT - 1.0) * ident + gram
+    square = jnp.sum(jnp.sum(system * system, 1, keepdims=True), 0, keepdims=True)
+    scale = jnp.sqrt(square)
+    root = system / scale
+    inverse_root = ident
+    for turn in range(NS_ITERS):
+        if turn == 0:
+            middle = 0.5 * (3.0 * ident - root)
+            inverse_next = middle
+        else:
+            middle = 0.5 * (3.0 * ident - exact(inverse_root, root))
+            inverse_next = exact(middle, inverse_root)
+        if turn < NS_ITERS - 1:
+            root = exact(root, middle)
+        inverse_root = inverse_next
+    half = inverse_root / jnp.sqrt(scale)
+    drive8 = jnp.broadcast_to(drive, (8, 64))
+    mean_weight = exact(exact(drive8, half), half)[0:1]
+    transform_t = (mean_weight + (REPLICA_COUNT - 1.0) ** 0.5 * half).astype(BF).astype(F32)
+    total_t = jnp.sum(transform_t, 1, keepdims=True)
+    keep[...] = transform_t + (1.0 - total_t) * (1.0 / REPLICA_COUNT)
+    mine = keep[pl.ds(pl.multiple_of(pos[2] * 16, 16), 16), :]
+    swap1 = jnp.concatenate([mine[:, 16:32], mine[:, 0:16], mine[:, 48:64], mine[:, 32:48]], 1)
+    mine = jnp.where((pos[2] % 2) == 1, swap1, mine)
+    swap2 = jnp.concatenate([mine[:, 32:64], mine[:, 0:32]], 1)
+    mine = jnp.where(pos[2] >= 2, swap2, mine)
+    high = mine.astype(BF).astype(F32)
+    out[...] = jnp.concatenate([high, mine - high], 0).astype(BF)
+
+
+def final_kernel(
+    pos, weights, own_near, own_far, own_diag, mate_near, mate_far, mate_diag,
+    far, far_mate, far_near, diag, diag_mate, diag_near, out, keep
+):
+    m = weights[...]
+    for t in range(4):
+        quarter = jnp.bitwise_xor(pos[2], t)
+        f = quarter // 2
+        base = (quarter % 2) * 4
+        for r in range(4):
+            if t == 0:
+                parts = [own_near[r], mate_near[4 + r], far[r], diag[r]]
+            elif t == 1:
+                parts = [own_near[4 + r], mate_near[r], far_mate[r], diag_mate[r]]
+            elif t == 2:
+                parts = [own_far[r], mate_diag[r], far_near[r], diag_near[4 + r]]
+            else:
+                parts = [own_diag[r], mate_far[r], far_near[4 + r], diag_near[r]]
+            state = jnp.concatenate(parts, 0)
+            both = jnp.dot(m, state, preferred_element_type=F32)
+            keep[f, base + r] = both[0:16] + both[16:32]
+    for f in range(2):
+        out[:, f] = jnp.swapaxes(keep[f], 0, 1)
+
+
+def local(prior_replicas, wind_field, obs_index, obs_count, obs_value, obs_weight):
+    cols = prior_replicas.shape[3]
+    strips = lax.axis_size("space")
+    here = lax.axis_index("space")
+    group = lax.axis_index("mem")
+    pos = jnp.stack([here, jnp.int32(strips), group]).astype(jnp.int32)
+    shape = jax.ShapeDtypeStruct
+
+    turned, pay_a, pay_b = pl.pallas_call(
+        pack_kernel,
+        name="pack",
+        in_specs=[smem(), vmem(), vmem()],
+        out_specs=[vmem()] * 3,
+        out_shape=[shape((2, 8, 16, cols), F32), shape((136, cols), BF), shape((136, cols), BF)],
+        compiler_params=params(),
+    )(pos, prior_replicas, wind_field)
+
+    pairs_a = [(i, i ^ 1) for i in range(strips) if (i ^ 1) < strips]
+    pairs_b = [(i, i + 1) for i in range(1, strips - 1, 2)]
+    pairs_b = pairs_b + [(j, i) for i, j in pairs_b]
+    recv_a = lax.ppermute(pay_a, "space", pairs_a)
+    recv_b = lax.ppermute(pay_b, "space", pairs_b)
+
+    slots = obs_index.shape[0]
+    root_map, value_map = pl.pallas_call(
+        maps_kernel,
+        name="maps",
+        in_specs=[smem(), vmem(), smem(), vmem(), vmem()],
+        out_specs=[vmem()] * 2,
+        out_shape=[shape((64, 128), F32)] * 2,
+        compiler_params=params(),
+    )(
+        pos,
+        obs_index.reshape(1, slots),
+        obs_count,
+        obs_weight.reshape(1, slots),
+        obs_value.reshape(1, slots),
+    )
+
+    near, far, diag = pl.pallas_call(
+        stencil_kernel,
+        name="stencil",
+        in_specs=[smem()] + [vmem()] * 4,
+        out_specs=[vmem()] * 3,
+        out_shape=[shape((8, 16, cols), BF), shape((4, 16, cols), BF), shape((4, 16, cols), BF)],
+        scratch_shapes=[
+            pltpu.VMEM((2, 16, 16, cols + PAD), F32),
+            pltpu.VMEM((2, 12, 16, cols + PAD), F32),
+            pltpu.VMEM((2, 12, 8, cols), F32),
+            pltpu.VMEM((2, 8, 8, cols), F32),
+        ],
+        compiler_params=params(),
+    )(pos, turned, recv_a, recv_b, wind_field)
+
+    def swap(value, bits):
+        return lax.ppermute(value, "mem", [(i, i ^ bits) for i in range(4)])
+
+    got_far = swap(far, 2)
+    got_diag = swap(diag, 3)
+    mate_near = swap(near, 1)
+    got_far, got_diag, mate_near, near_late, far_late, diag_late = lax.optimization_barrier(
+        (got_far, got_diag, mate_near, near, far, diag)
+    )
+    far_near = swap(near_late, 2)
+    mate_far = swap(far_late, 1)
+    mate_diag = swap(diag_late, 1)
+    diag_mate = swap(got_far, 1)
+    far_mate = swap(got_diag, 1)
+    diag_near = swap(far_near, 1)
+
+    part = pl.pallas_call(
+        gram_kernel,
+        name="gram",
+        in_specs=[smem()] + [vmem()] * 6,
+        out_specs=vmem(),
+        out_shape=shape((80, 64), F32),
+        scratch_shapes=[pltpu.VMEM((5, 16, 4 * cols), BF)],
+        compiler_params=params(),
+    )(pos, near, mate_near, got_far, got_diag, root_map, value_map)
+
+    rounds = [("mem", 1), ("mem", 2)]
+    bit = 1
+    while bit < strips:
+        rounds.append(("space", bit))
+        bit *= 2
+    other = None
+    for axis, bits in rounds:
+        if other is not None:
+            part = part + other
+        size = lax.axis_size(axis)
+        other = lax.ppermute(part, axis, [(i, i ^ bits) for i in range(size)])
+
+    weights = pl.pallas_call(
+        weights_kernel,
+        name="weights",
+        in_specs=[smem(), vmem(), vmem()],
+        out_specs=vmem(),
+        out_shape=shape((32, 64), BF),
+        scratch_shapes=[pltpu.VMEM((64, 64), F32)],
+        compiler_params=params(),
+    )(pos, part, other)
+
+    return pl.pallas_call(
+        final_kernel,
+        name="final",
+        in_specs=[smem()] + [vmem()] * 13,
+        out_specs=vmem(),
+        out_shape=shape(prior_replicas.shape, F32),
+        scratch_shapes=[pltpu.VMEM((2, 8, 16, cols), F32)],
+        compiler_params=params(),
+    )(
+        pos, weights, near, far, diag, mate_near, mate_far, mate_diag,
+        got_far, far_mate, far_near, got_diag, diag_mate, diag_near,
+    )
+
+
 def solution(mesh):
     in_specs = (
         P(("parts", "mem"), None, "space", None),
@@ -141,4 +516,7 @@
         P(("parts", "space")),
     )
     out_specs = P(("parts", "mem"), None, "space", None)
-    return jax.shard_map(local, mesh=mesh, in_specs=in_specs, out_specs=out_specs, check_vma=False)
+    strips = mesh.shape["space"]
+    fast = mesh.shape["mem"] == 4 and strips > 1 and strips & (strips - 1) == 0
+    body = local if fast else local_generic
+    return jax.shard_map(body, mesh=mesh, in_specs=in_specs, out_specs=out_specs, check_vma=False)

time: 221 us -> 85 us (0.38)
  local copies, waits for them, and re-layouts: 91.4 us -> 2.56 us
  blocking collectives: 55.3 us -> 0 us
  Pallas kernels: 0 us -> 20.2 us
  other arithmetic: 17.1 us -> 0.1 us
  waiting for transfers between devices: 31.5 us -> 43.1 us
  matrix products: 5.81 us -> 0 us
    unnamed x35 -> x10, local copies, waits for them, and re-layouts: 39.1 us -> 2.56 us
    ppermute x4 -> x15, waiting for transfers between devices: 9.63 us -> 43.1 us  [the longest x9 24.5 us: swap(): return lax.ppermute(value, 'mem', [(i, i ^ bits) for i in range(4)])]
    all_to_all x1 -> x0, blocking collectives: 28.2 us -> none  [local(): lax.all_to_all(analysed, 'mem', split_axis=0, concat_axis=3, tiled=True)]
    all_to_all x1 -> x0, waiting for transfers between devices: 21.9 us -> none  [local(): lax.all_to_all(state, 'mem', split_axis=3, concat_axis=0, tiled=True)]
    add x3 -> x0, local copies, waits for them, and re-layouts: 20.8 us -> none  [the longest x2 19.6 us: advance(): center - wind_rows[0] * grad_row - wind_rows[1] * grad_col]
    pallas_call x0 -> x6, Pallas kernels: none -> 20.2 us  [the longest x1 10.3 us: local(): pl.pallas_call(stencil_kernel, name='stencil', in_specs=[smem()] + [vmem(...]
    psum x1 -> x0, blocking collectives: 19.9 us -> none  [local(): gram, drive = lax.psum((gram, drive), 'space')]
    all_to_all x4 -> x0, local copies, waits for them, and re-layouts: 13.8 us -> none  [the longest x3 12.3 us: local(): lax.all_to_all(state, 'mem', split_axis=3, concat_axis=0, tiled=True)]
  transfers between devices with their start and end apart: 5 -> 15, of which waited for: 3 -> 8; matrix products, arithmetic and copies ran while one was open for 8% -> 0% of each run, Pallas kernels for 0% -> 7%
where the time goes in v1:
time: 85 us; the launch traced here: 84.8 us
  waiting for transfers between devices  43.1 us (51%)
  Pallas kernels  20.2 us (24%)
  starting transfers between devices  18 us (21%)
  local copies, waits for them, and re-layouts  2.56 us (3%)
    ppermute x9, waiting for transfers between devices, swap(): return lax.ppermute(value, 'mem', [(i, i ^ bits) for i in range(4)])  24.5 us
    ppermute x1, waiting for transfers between devices, local(): recv_a = lax.ppermute(pay_a, 'space', pairs_a)  11.9 us
    pallas_call x1, Pallas kernels, local(): pl.pallas_call(stencil_kernel, name='stencil', in_specs=[smem()] + [vmem(...  10.3 us
    ppermute x4, starting transfers between devices, local(): other = lax.ppermute(part, axis, [(i, i ^ bits) for i in range(size)])  10.1 us
    ppermute x4, waiting for transfers between devices, local(): other = lax.ppermute(part, axis, [(i, i ^ bits) for i in range(size)])  6.66 us
    ppermute x9, starting transfers between devices, swap(): return lax.ppermute(value, 'mem', [(i, i ^ bits) for i in range(4)])  4.11 us
    pallas_call x1, Pallas kernels, local(): pl.pallas_call(final_kernel, name='final', in_specs=[smem()] + [vmem()] *...  3.19 us
    ppermute x1, starting transfers between devices, local(): recv_a = lax.ppermute(pay_a, 'space', pairs_a)  3.09 us
  transfers between devices with their start and end apart: 15, of which 8 were waited for; matrix products, arithmetic and copies ran while one was open for 0% of the time, Pallas kernels for 7%

profile of v1, /device:TPU:0, one launch (start us, length us, event | category | flops | bytes accessed | tf_op | source)
XLA Modules:
  0.0 84.8 jit_solution(11188827240189344969)
XLA Ops:
  0.0 0.1 pad_add_fusion.pos
  0.1 1.6 %copy-done = f32[16,2,8,2048]{3,2,1,0:T(8,128)S(1)} copy-done((f32[16,2,8,2048]{3,2,1,0:T(8,128)S(1)}, f32[16,2,8,2048]{3,2,1,0:T(8,128)}, u32[]{:S(2)}) %copy-start) | copy-done | bytes 2097176
  1.7 0.9 %copy-done.1 = f32[2,2,8,2048]{3,2,1,0:T(8,128)S(1)} copy-done((f32[2,2,8,2048]{3,2,1,0:T(8,128)S(1)}, f32[2,2,8,2048]{3,2,1,0:T(8,128)}, u32[]{:S(2)}) %copy-start.1) | copy-done | bytes 262168
  2.6 1.1 %pack.1 = (f32[2,8,16,2048]{3,2,1,0:T(8,128)S(1)}, bf16[136,2048]{1,0:T(8,128)(2,1)S(1)}, bf16[136,2048]{1,0:T(8,128)(2,1)S(1)}) custom-call(s32[3]{0:T(128)S(1)} %pad_add_fusion.pos, f32[16,2,8,2048]{3,2,1,0:T(8,128)S(1)} %copy-done, f32[2,2,8,2048]{3,2,1,0:T(8,128)S(1)} %copy-done.1), custom_call_target="tpu_custom_call" | custom-call | tf_op jit(solution)/shard_map/pack/pallas_call | solution.py:401
  3.7 0.0 copy-start.2
  3.7 0.0 copy-start.3
  3.7 0.0 copy-start.4
  3.7 3.1 %collective-permute-start = (bf16[136,2048]{1,0:T(8,128)(2,1)S(1)}, bf16[136,2048]{1,0:T(8,128)(2,1)S(1)}, u32[]{:S(2)}, u32[]{:S(2)}) collective-permute-start(bf16[136,2048]{1,0:T(8,128)(2,1)S(1)} %get-tuple-element.20), channel_id=1, source_target_pairs={{0,4},{4,0},{8,12},{12,8},{1,5},{5,1},{9,13},{13,9},{2,6},{6,2},{1... | collective-permute-start | bytes 1671176 | tf_op jit(solution)/shard_map/ppermute | solution.py:413
  6.8 0.7 collective-permute-start.1
  7.5 11.9 %collective-permute-done.recv_a = bf16[136,2048]{1,0:T(8,128)(2,1)S(1)} collective-permute-done((bf16[136,2048]{1,0:T(8,128)(2,1)S(1)}, bf16[136,2048]{1,0:T(8,128)(2,1)S(1)}, u32[]{:S(2)}, u32[]{:S(2)}) %collective-permute-start) | collective-permute-done | bytes 557088 | tf_op jit(solution)/shard_map/ppermute | solution.py:413
  19.5 10.3 %stencil.1 = (bf16[8,16,2048]{2,1,0:T(8,128)(2,1)S(1)}, bf16[4,16,2048]{2,1,0:T(8,128)(2,1)S(1)}, bf16[4,16,2048]{2,1,0:T(8,128)(2,1)S(1)}) custom-call(s32[3]{0:T(128)S(1)} %pad_add_fusion.pos, f32[2,8,16,2048]{3,2,1,0:T(8,128)S(1)} %get-tuple-element.19.turned, bf16[136,2048]{1,0:T(8,128)(2,1)S(1)} %collective-permute-done.recv_a, ...), custom_call_target="tpu_custom_call" | custom-call | tf_op jit(solution)/shard_map/stencil/pallas_call | solution.py:432
  29.8 0.1 collective-permute-start.4
  29.9 1.7 %collective-permute-start.2 = (bf16[4,16,2048]{2,1,0:T(8,128)(2,1)S(1)}, bf16[4,16,2048]{2,1,0:T(8,128)(2,1)S(1)}, u32[]{:S(2)}, u32[]{:S(2)}) collective-permute-start(bf16[4,16,2048]{2,1,0:T(8,128)(2,1)S(1)} %get-tuple-element.30.own_far), channel_id=1, source_target_pairs={{0,2},{1,3},{2,0},{3,1},{4,6},{5,7},{6,4},{7,5},{8,10},{9,11},{10,... | collective-permute-start | bytes 786440 | tf_op jit(solution)/shard_map/ppermute | solution.py:448
  31.6 0.1 collective-permute-start.3
  31.7 7.3 %collective-permute-done.2.far = bf16[4,16,2048]{2,1,0:T(8,128)(2,1)S(1)} collective-permute-done((bf16[4,16,2048]{2,1,0:T(8,128)(2,1)S(1)}, bf16[4,16,2048]{2,1,0:T(8,128)(2,1)S(1)}, u32[]{:S(2)}, u32[]{:S(2)}) %collective-permute-start.2) | collective-permute-done | bytes 262176 | tf_op jit(solution)/shard_map/ppermute | solution.py:448
  39.0 4.7 %collective-permute-done.3.diag = bf16[4,16,2048]{2,1,0:T(8,128)(2,1)S(1)} collective-permute-done((bf16[4,16,2048]{2,1,0:T(8,128)(2,1)S(1)}, bf16[4,16,2048]{2,1,0:T(8,128)(2,1)S(1)}, u32[]{:S(2)}, u32[]{:S(2)}) %collective-permute-start.3) | collective-permute-done | bytes 262176 | tf_op jit(solution)/shard_map/ppermute | solution.py:448
  43.8 1.7 %collective-permute-start.12 = (bf16[8,16,2048]{2,1,0:T(8,128)(2,1)S(1)}, bf16[8,16,2048]{2,1,0:T(8,128)(2,1)S(1)}, u32[]{:S(2)}, u32[]{:S(2)}) collective-permute-start(bf16[8,16,2048]{2,1,0:T(8,128)(2,1)S(1)} %get-tuple-element.32.own.own_near), channel_id=1, source_target_pairs={{0,2},{1,3},{2,0},{3,1},{4,6},{5,7},{6,4},{7,5},{8,10},{9,11},{10,... | collective-permute-start | bytes 1572872 | tf_op jit(solution)/shard_map/ppermute | solution.py:448
  45.4 12.4 %collective-permute-done.12.far_near = bf16[8,16,2048]{2,1,0:T(8,128)(2,1)S(1)} collective-permute-done((bf16[8,16,2048]{2,1,0:T(8,128)(2,1)S(1)}, bf16[8,16,2048]{2,1,0:T(8,128)(2,1)S(1)}, u32[]{:S(2)}, u32[]{:S(2)}) %collective-permute-start.12) | collective-permute-done | bytes 524320 | tf_op jit(solution)/shard_map/ppermute | solution.py:448
  58.5 1.3 %maps.1 = (f32[64,128]{1,0:T(8,128)S(1)}, f32[64,128]{1,0:T(8,128)S(1)}) custom-call(s32[3]{0:T(128)S(1)} %pad_add_fusion.pos, s32[1,2048]{1,0:T(1,128)S(1)} %bitcast.5, s32[1]{0:T(128)S(6)} %copy.7.count, f32[1,2048]{1,0:T(1,128)S(1)} %bitcast.6, f32[1,2048]{1,0:T(1,128)S(1)} %bitcast.7), custom_call_target="tpu_custom_call" | custom-call | tf_op jit(solution)/shard_map/maps/pallas_call | solution.py:417
  59.9 1.6 %gram.1 = f32[80,64]{1,0:T(8,128)S(1)} custom-call(s32[3]{0:T(128)S(1)} %pad_add_fusion.pos, bf16[8,16,2048]{2,1,0:T(8,128)(2,1)S(1)} %get-tuple-element.32.own.own_near, bf16[8,16,2048]{2,1,0:T(8,128)(2,1)S(1)} %collective-permute-done.4.mate.mate_near, bf16[4,16,2048]{2,1,0:T(8,128)(2,1)S(1)} %collective-permute-done.2.far, ...), custom_call_target="tpu_custom_call" | custom-call | tf_op jit(solution)/shard_map/gram/pallas_call | solution.py:463
  61.4 0.6 collective-permute-start.5
  62.0 0.9 %collective-permute-done.5 = f32[80,64]{1,0:T(8,128)S(1)} collective-permute-done((f32[80,64]{1,0:T(8,128)S(1)}, f32[80,64]{1,0:T(8,128)S(1)}, u32[]{:S(2)}, u32[]{:S(2)}) %collective-permute-start.5) | collective-permute-done | bytes 20512 | tf_op jit(solution)/shard_map/ppermute | solution.py:483
  62.9 1.7 %collective-permute-start.6 = (f32[80,64]{1,0:T(8,128)S(1)}, f32[80,64]{1,0:T(8,128)S(1)}, u32[]{:S(2)}, u32[]{:S(2)}) collective-permute-start(f32[80,64]{1,0:T(8,128)S(1)} %add.9), channel_id=1, source_target_pairs={{0,2},{1,3},{2,0},{3,1},{4,6},{5,7},{6,4},{7,5},{8,10},{9,11},{10,... | collective-permute-start | bytes 61448 | tf_op jit(solution)/shard_map/ppermute | solution.py:483
  64.5 2.3 %collective-permute-done.6 = f32[80,64]{1,0:T(8,128)S(1)} collective-permute-done((f32[80,64]{1,0:T(8,128)S(1)}, f32[80,64]{1,0:T(8,128)S(1)}, u32[]{:S(2)}, u32[]{:S(2)}) %collective-permute-start.6) | collective-permute-done | bytes 20512 | tf_op jit(solution)/shard_map/ppermute | solution.py:483
  66.9 4.7 %collective-permute-start.7 = (f32[80,64]{1,0:T(8,128)S(1)}, f32[80,64]{1,0:T(8,128)S(1)}, u32[]{:S(2)}, u32[]{:S(2)}) collective-permute-start(f32[80,64]{1,0:T(8,128)S(1)} %add.10), channel_id=1, source_target_pairs={{0,4},{4,0},{8,12},{12,8},{1,5},{5,1},{9,13},{13,9},{2,6},{6,2},{1... | collective-permute-start | bytes 61448 | tf_op jit(solution)/shard_map/ppermute | solution.py:483
  71.6 2.0 %collective-permute-done.7 = f32[80,64]{1,0:T(8,128)S(1)} collective-permute-done((f32[80,64]{1,0:T(8,128)S(1)}, f32[80,64]{1,0:T(8,128)S(1)}, u32[]{:S(2)}, u32[]{:S(2)}) %collective-permute-start.7) | collective-permute-done | bytes 20512 | tf_op jit(solution)/shard_map/ppermute | solution.py:483
  73.6 3.2 %collective-permute-start.8 = (f32[80,64]{1,0:T(8,128)S(1)}, f32[80,64]{1,0:T(8,128)S(1)}, u32[]{:S(2)}, u32[]{:S(2)}) collective-permute-start(f32[80,64]{1,0:T(8,128)S(1)} %add.11.one), channel_id=1, source_target_pairs={{0,8},{4,12},{8,0},{12,4},{1,9},{5,13},{9,1},{13,5},{2,10},{6,14},... | collective-permute-start | bytes 61448 | tf_op jit(solution)/shard_map/ppermute | solution.py:483
  76.8 0.5 collective-permute-start.9
  77.3 1.5 %collective-permute-done.8.two = f32[80,64]{1,0:T(8,128)S(1)} collective-permute-done((f32[80,64]{1,0:T(8,128)S(1)}, f32[80,64]{1,0:T(8,128)S(1)}, u32[]{:S(2)}, u32[]{:S(2)}) %collective-permute-start.8) | collective-permute-done | bytes 20512 | tf_op jit(solution)/shard_map/ppermute | solution.py:483
  78.8 2.8 %weights.1 = bf16[32,64]{1,0:T(8,128)(2,1)S(1)} custom-call(s32[3]{0:T(128)S(1)} %pad_add_fusion.pos, f32[80,64]{1,0:T(8,128)S(1)} %add.11.one, f32[80,64]{1,0:T(8,128)S(1)} %collective-permute-done.8.two), custom_call_target="tpu_custom_call" | custom-call | tf_op jit(solution)/shard_map/weights/pallas_call | solution.py:485
  81.5 0.0 collective-permute-done.9.mate_far
  81.6 3.2 %final.1 = f32[16,2,8,2048]{3,2,1,0:T(8,128)} custom-call(s32[3]{0:T(128)S(1)} %pad_add_fusion.pos, bf16[32,64]{1,0:T(8,128)(2,1)S(1)} %weights.1, bf16[8,16,2048]{2,1,0:T(8,128)(2,1)S(1)} %get-tuple-element.32.own.own_near, bf16[4,16,2048]{2,1,0:T(8,128)(2,1)S(1)} %get-tuple-element.30.own_far, bf16[4,16,2048]{2,1,0:T(8,128)(2,1)S(1)} %get-tuple-element.31.own_diag, ...), custom_call_target="tpu_custom_call" | custom-call | tf_op jit(solution)/shard_map/final/pallas_call | solution.py:495
  (18 shorter events, 0.1 us)
Async XLA Ops:
  0.1 1.6 %copy-start = (f32[16,2,8,2048]{3,2,1,0:T(8,128)S(1)}, f32[16,2,8,2048]{3,2,1,0:T(8,128)}, u32[]{:S(2)}) copy-start(f32[16,2,8,2048]{3,2,1,0:T(8,128)} %prior.1) | copy-start | bytes 6291460
  1.7 0.9 %copy-start.1 = (f32[2,2,8,2048]{3,2,1,0:T(8,128)S(1)}, f32[2,2,8,2048]{3,2,1,0:T(8,128)}, u32[]{:S(2)}) copy-start(f32[2,2,8,2048]{3,2,1,0:T(8,128)} %wind.3) | copy-start | bytes 786436
  3.7 54.8 %copy-start.2 = (s32[2048]{0:T(1024)S(1)}, s32[2048]{0:T(1024)}, u32[]{:S(2)}) copy-start(s32[2048]{0:T(1024)} %param.8) | copy-start | bytes 24580
  3.7 54.8 %copy-start.3 = (f32[2048]{0:T(1024)S(1)}, f32[2048]{0:T(1024)}, u32[]{:S(2)}) copy-start(f32[2048]{0:T(1024)} %param.11) | copy-start | bytes 24580
  3.7 54.8 %copy-start.4 = (f32[2048]{0:T(1024)S(1)}, f32[2048]{0:T(1024)}, u32[]{:S(2)}) copy-start(f32[2048]{0:T(1024)} %param.10) | copy-start | bytes 24580
  3.7 15.7 %collective-permute-start = (bf16[136,2048]{1,0:T(8,128)(2,1)S(1)}, bf16[136,2048]{1,0:T(8,128)(2,1)S(1)}, u32[]{:S(2)}, u32[]{:S(2)}) collective-permute-start(bf16[136,2048]{1,0:T(8,128)(2,1)S(1)} %get-tuple-element.20), channel_id=1, source_target_pairs={{0,4},{4,0},{8,12},{12,8},{1,5},{5,1},{9,13},{13,9},{2,6},{6,2},{1... | collective-permute-start | bytes 1671176 | tf_op jit(solution)/shard_map/ppermute | solution.py:413
  6.8 12.6 %collective-permute-start.1 = (bf16[136,2048]{1,0:T(8,128)(2,1)S(1)}, bf16[136,2048]{1,0:T(8,128)(2,1)S(1)}, u32[]{:S(2)}, u32[]{:S(2)}) collective-permute-start(bf16[136,2048]{1,0:T(8,128)(2,1)S(1)} %get-tuple-element.21), channel_id=1, source_target_pairs={{4,8},{8,4},{5,9},{9,5},{6,10},{10,6},{7,11},{11,7},{20,24},{24,20... | collective-permute-start | bytes 1671176 | tf_op jit(solution)/shard_map/ppermute | solution.py:414
  29.8 14.0 %collective-permute-start.4 = (bf16[8,16,2048]{2,1,0:T(8,128)(2,1)S(1)}, bf16[8,16,2048]{2,1,0:T(8,128)(2,1)S(1)}, u32[]{:S(2)}, u32[]{:S(2)}) collective-permute-start(bf16[8,16,2048]{2,1,0:T(8,128)(2,1)S(1)} %get-tuple-element.32.own.own_near), channel_id=1, source_target_pairs={{0,1},{1,0},{2,3},{3,2},{4,5},{5,4},{6,7},{7,6},{8,9},{9,8},{10,11... | collective-permute-start | bytes 1572872 | tf_op jit(solution)/shard_map/ppermute | solution.py:448
  29.9 9.2 %collective-permute-start.2 = (bf16[4,16,2048]{2,1,0:T(8,128)(2,1)S(1)}, bf16[4,16,2048]{2,1,0:T(8,128)(2,1)S(1)}, u32[]{:S(2)}, u32[]{:S(2)}) collective-permute-start(bf16[4,16,2048]{2,1,0:T(8,128)(2,1)S(1)} %get-tuple-element.30.own_far), channel_id=1, source_target_pairs={{0,2},{1,3},{2,0},{3,1},{4,6},{5,7},{6,4},{7,5},{8,10},{9,11},{10,... | collective-permute-start | bytes 786440 | tf_op jit(solution)/shard_map/ppermute | solution.py:448
  31.6 12.2 %collective-permute-start.3 = (bf16[4,16,2048]{2,1,0:T(8,128)(2,1)S(1)}, bf16[4,16,2048]{2,1,0:T(8,128)(2,1)S(1)}, u32[]{:S(2)}, u32[]{:S(2)}) collective-permute-start(bf16[4,16,2048]{2,1,0:T(8,128)(2,1)S(1)} %get-tuple-element.31.own_diag), channel_id=1, source_target_pairs={{0,3},{1,2},{2,1},{3,0},{4,7},{5,6},{6,5},{7,4},{8,11},{9,10},{10,... | collective-permute-start | bytes 786440 | tf_op jit(solution)/shard_map/ppermute | solution.py:448
  43.8 14.1 %collective-permute-start.12 = (bf16[8,16,2048]{2,1,0:T(8,128)(2,1)S(1)}, bf16[8,16,2048]{2,1,0:T(8,128)(2,1)S(1)}, u32[]{:S(2)}, u32[]{:S(2)}) collective-permute-start(bf16[8,16,2048]{2,1,0:T(8,128)(2,1)S(1)} %get-tuple-element.32.own.own_near), channel_id=1, source_target_pairs={{0,2},{1,3},{2,0},{3,1},{4,6},{5,7},{6,4},{7,5},{8,10},{9,11},{10,... | collective-permute-start | bytes 1572872 | tf_op jit(solution)/shard_map/ppermute | solution.py:448
  57.9 23.7 %collective-permute-start.14 = (bf16[8,16,2048]{2,1,0:T(8,128)(2,1)S(1)}, bf16[8,16,2048]{2,1,0:T(8,128)(2,1)S(1)}, u32[]{:S(2)}, u32[]{:S(2)}) collective-permute-start(bf16[8,16,2048]{2,1,0:T(8,128)(2,1)S(1)} %collective-permute-done.12.far_near), channel_id=1, source_target_pairs={{0,1},{1,0},{2,3},{3,2},{4,5},{5,4},{6,7},{7,6},{8,9},{9,8},{10,11... | collective-permute-start | bytes 1572872 | tf_op jit(solution)/shard_map/ppermute | solution.py:448
  61.4 1.4 %collective-permute-start.5 = (f32[80,64]{1,0:T(8,128)S(1)}, f32[80,64]{1,0:T(8,128)S(1)}, u32[]{:S(2)}, u32[]{:S(2)}) collective-permute-start(f32[80,64]{1,0:T(8,128)S(1)} %gram.1), channel_id=1, source_target_pairs={{0,1},{1,0},{2,3},{3,2},{4,5},{5,4},{6,7},{7,6},{8,9},{9,8},{10,11... | collective-permute-start | bytes 61448 | tf_op jit(solution)/shard_map/ppermute | solution.py:483
  62.9 4.0 %collective-permute-start.6 = (f32[80,64]{1,0:T(8,128)S(1)}, f32[80,64]{1,0:T(8,128)S(1)}, u32[]{:S(2)}, u32[]{:S(2)}) collective-permute-start(f32[80,64]{1,0:T(8,128)S(1)} %add.9), channel_id=1, source_target_pairs={{0,2},{1,3},{2,0},{3,1},{4,6},{5,7},{6,4},{7,5},{8,10},{9,11},{10,... | collective-permute-start | bytes 61448 | tf_op jit(solution)/shard_map/ppermute | solution.py:483
  66.9 6.7 %collective-permute-start.7 = (f32[80,64]{1,0:T(8,128)S(1)}, f32[80,64]{1,0:T(8,128)S(1)}, u32[]{:S(2)}, u32[]{:S(2)}) collective-permute-start(f32[80,64]{1,0:T(8,128)S(1)} %add.10), channel_id=1, source_target_pairs={{0,4},{4,0},{8,12},{12,8},{1,5},{5,1},{9,13},{13,9},{2,6},{6,2},{1... | collective-permute-start | bytes 61448 | tf_op jit(solution)/shard_map/ppermute | solution.py:483
  73.6 5.2 %collective-permute-start.8 = (f32[80,64]{1,0:T(8,128)S(1)}, f32[80,64]{1,0:T(8,128)S(1)}, u32[]{:S(2)}, u32[]{:S(2)}) collective-permute-start(f32[80,64]{1,0:T(8,128)S(1)} %add.11.one), channel_id=1, source_target_pairs={{0,8},{4,12},{8,0},{12,4},{1,9},{5,13},{9,1},{13,5},{2,10},{6,14},... | collective-permute-start | bytes 61448 | tf_op jit(solution)/shard_map/ppermute | solution.py:483
  76.8 4.8 %collective-permute-start.13 = (bf16[4,16,2048]{2,1,0:T(8,128)(2,1)S(1)}, bf16[4,16,2048]{2,1,0:T(8,128)(2,1)S(1)}, u32[]{:S(2)}, u32[]{:S(2)}) collective-permute-start(bf16[4,16,2048]{2,1,0:T(8,128)(2,1)S(1)} %collective-permute-done.2.far), channel_id=1, source_target_pairs={{0,1},{1,0},{2,3},{3,2},{4,5},{5,4},{6,7},{7,6},{8,9},{9,8},{10,11... | collective-permute-start | bytes 786440 | tf_op jit(solution)/shard_map/ppermute | solution.py:448
  76.8 4.8 %collective-permute-start.9 = (bf16[4,16,2048]{2,1,0:T(8,128)(2,1)S(1)}, bf16[4,16,2048]{2,1,0:T(8,128)(2,1)S(1)}, u32[]{:S(2)}, u32[]{:S(2)}) collective-permute-start(bf16[4,16,2048]{2,1,0:T(8,128)(2,1)S(1)} %get-tuple-element.30.own_far), channel_id=1, source_target_pairs={{0,1},{1,0},{2,3},{3,2},{4,5},{5,4},{6,7},{7,6},{8,9},{9,8},{10,11... | collective-permute-start | bytes 786440 | tf_op jit(solution)/shard_map/ppermute | solution.py:448
  77.3 4.3 %collective-permute-start.10 = (bf16[4,16,2048]{2,1,0:T(8,128)(2,1)S(1)}, bf16[4,16,2048]{2,1,0:T(8,128)(2,1)S(1)}, u32[]{:S(2)}, u32[]{:S(2)}) collective-permute-start(bf16[4,16,2048]{2,1,0:T(8,128)(2,1)S(1)} %get-tuple-element.31.own_diag), channel_id=1, source_target_pairs={{0,1},{1,0},{2,3},{3,2},{4,5},{5,4},{6,7},{7,6},{8,9},{9,8},{10,11... | collective-permute-start | bytes 786440 | tf_op jit(solution)/shard_map/ppermute | solution.py:448
  78.8 2.8 %collective-permute-start.11 = (bf16[4,16,2048]{2,1,0:T(8,128)(2,1)S(1)}, bf16[4,16,2048]{2,1,0:T(8,128)(2,1)S(1)}, u32[]{:S(2)}, u32[]{:S(2)}) collective-permute-start(bf16[4,16,2048]{2,1,0:T(8,128)(2,1)S(1)} %collective-permute-done.3.diag), channel_id=1, source_target_pairs={{0,1},{1,0},{2,3},{3,2},{4,5},{5,4},{6,7},{7,6},{8,9},{9,8},{10,11... | collective-permute-start | bytes 786440 | tf_op jit(solution)/shard_map/ppermute | solution.py:448

commit v2 on v1

--- a/solution.py
+++ b/solution.py
@@ -429,6 +429,7 @@
         obs_value.reshape(1, slots),
     )
 
+    recv_b, root_map, value_map = lax.optimization_barrier((recv_b, root_map, value_map))
     near, far, diag = pl.pallas_call(
         stencil_kernel,
         name="stencil",
@@ -454,11 +455,6 @@
         (got_far, got_diag, mate_near, near, far, diag)
     )
     far_near = swap(near_late, 2)
-    mate_far = swap(far_late, 1)
-    mate_diag = swap(diag_late, 1)
-    diag_mate = swap(got_far, 1)
-    far_mate = swap(got_diag, 1)
-    diag_near = swap(far_near, 1)
 
     part = pl.pallas_call(
         gram_kernel,
@@ -479,8 +475,14 @@
     for axis, bits in rounds:
         if other is not None:
             part = part + other
+        if (axis, bits) == ("mem", 2):
+            late = lax.optimization_barrier((far_late, diag_late, got_far, got_diag, part))
+            mate_far, mate_diag, diag_mate, far_mate = [swap(v, 1) for v in late[:4]]
         size = lax.axis_size(axis)
         other = lax.ppermute(part, axis, [(i, i ^ bits) for i in range(size)])
+
+    far_near_late, _ = lax.optimization_barrier((far_near, other))
+    diag_near = swap(far_near_late, 1)
 
     weights = pl.pallas_call(
         weights_kernel,

time: 85 us -> 78.1 us (0.919)
  waiting for transfers between devices: 43.1 us -> 39.3 us
  starting transfers between devices: 18 us -> 14.9 us
    ppermute x9, waiting for transfers between devices: 24.5 us -> 12 us  [swap(): return lax.ppermute(value, 'mem', [(i, i ^ bits) for i in range(4)])]
    ppermute x4, waiting for transfers between devices: 6.66 us -> 16.9 us  [local(): other = lax.ppermute(part, axis, [(i, i ^ bits) for i in range(size)])]
    ppermute x4, starting transfers between devices: 10.1 us -> 3.91 us  [local(): other = lax.ppermute(part, axis, [(i, i ^ bits) for i in range(size)])]
    ppermute x1, starting transfers between devices: 3.09 us -> 5.88 us  [local(): recv_a = lax.ppermute(pay_a, 'space', pairs_a)]
    ppermute x1, waiting for transfers between devices: 11.9 us -> 10.3 us  [local(): recv_a = lax.ppermute(pay_a, 'space', pairs_a)]
  transfers between devices with their start and end apart: 15 -> 15, of which waited for: 8 -> 7; matrix products, arithmetic and copies ran while one was open for 0% -> 0% of each run, Pallas kernels for 7% -> 7%
where the time goes in v2:
time: 78.1 us; the launch traced here: 77.9 us
  waiting for transfers between devices  39.3 us (50%)
  Pallas kernels  20.2 us (26%)
  starting transfers between devices  14.9 us (19%)
  local copies, waits for them, and re-layouts  2.55 us (3%)
  between operations  0.79 us (1%)
    ppermute x4, waiting for transfers between devices, local(): other = lax.ppermute(part, axis, [(i, i ^ bits) for i in range(size)])  16.9 us
    ppermute x9, waiting for transfers between devices, swap(): return lax.ppermute(value, 'mem', [(i, i ^ bits) for i in range(4)])  12 us
    ppermute x1, waiting for transfers between devices, local(): recv_a = lax.ppermute(pay_a, 'space', pairs_a)  10.3 us
    pallas_call x1, Pallas kernels, local(): pl.pallas_call(stencil_kernel, name='stencil', in_specs=[smem()] + [vmem(...  10.3 us
    ppermute x1, starting transfers between devices, local(): recv_a = lax.ppermute(pay_a, 'space', pairs_a)  5.88 us
    ppermute x9, starting transfers between devices, swap(): return lax.ppermute(value, 'mem', [(i, i ^ bits) for i in range(4)])  4.45 us
    ppermute x4, starting transfers between devices, local(): other = lax.ppermute(part, axis, [(i, i ^ bits) for i in range(size)])  3.91 us
    pallas_call x1, Pallas kernels, local(): pl.pallas_call(final_kernel, name='final', in_specs=[smem()] + [vmem()] *...  3.19 us
  transfers between devices with their start and end apart: 15, of which 7 were waited for; matrix products, arithmetic and copies ran while one was open for 0% of the time, Pallas kernels for 7%

profile of v2, /device:TPU:0, one launch (start us, length us, event | category | flops | bytes accessed | tf_op | source)
XLA Modules:
  0.0 77.9 jit_solution(4487157690715252098)
XLA Ops:
  0.0 0.1 pad_add_fusion.pos
  0.1 1.6 %copy-done = f32[16,2,8,2048]{3,2,1,0:T(8,128)S(1)} copy-done((f32[16,2,8,2048]{3,2,1,0:T(8,128)S(1)}, f32[16,2,8,2048]{3,2,1,0:T(8,128)}, u32[]{:S(2)}) %copy-start) | copy-done | bytes 2097176
  1.7 0.9 %copy-done.1 = f32[2,2,8,2048]{3,2,1,0:T(8,128)S(1)} copy-done((f32[2,2,8,2048]{3,2,1,0:T(8,128)S(1)}, f32[2,2,8,2048]{3,2,1,0:T(8,128)}, u32[]{:S(2)}) %copy-start.1) | copy-done | bytes 262168
  2.6 1.1 %pack.1 = (f32[2,8,16,2048]{3,2,1,0:T(8,128)S(1)}, bf16[136,2048]{1,0:T(8,128)(2,1)S(1)}, bf16[136,2048]{1,0:T(8,128)(2,1)S(1)}) custom-call(s32[3]{0:T(128)S(1)} %pad_add_fusion.pos, f32[16,2,8,2048]{3,2,1,0:T(8,128)S(1)} %copy-done, f32[2,2,8,2048]{3,2,1,0:T(8,128)S(1)} %copy-done.1), custom_call_target="tpu_custom_call" | custom-call | tf_op jit(solution)/shard_map/pack/pallas_call | solution.py:401
  3.7 0.7 collective-permute-start.1
  4.4 5.9 %collective-permute-start = (bf16[136,2048]{1,0:T(8,128)(2,1)S(1)}, bf16[136,2048]{1,0:T(8,128)(2,1)S(1)}, u32[]{:S(2)}, u32[]{:S(2)}) collective-permute-start(bf16[136,2048]{1,0:T(8,128)(2,1)S(1)} %get-tuple-element.28), channel_id=1, source_target_pairs={{0,4},{4,0},{8,12},{12,8},{1,5},{5,1},{9,13},{13,9},{2,6},{6,2},{1... | collective-permute-start | bytes 1671176 | tf_op jit(solution)/shard_map/ppermute | solution.py:413
  11.0 1.3 %maps.1 = (f32[64,128]{1,0:T(8,128)S(1)}, f32[64,128]{1,0:T(8,128)S(1)}) custom-call(s32[3]{0:T(128)S(1)} %pad_add_fusion.pos, s32[1,2048]{1,0:T(1,128)S(1)} %bitcast.5, s32[1]{0:T(128)S(6)} %copy.7.count, f32[1,2048]{1,0:T(1,128)S(1)} %bitcast.6, f32[1,2048]{1,0:T(1,128)S(1)} %bitcast.7), custom_call_target="tpu_custom_call" | custom-call | tf_op jit(solution)/shard_map/maps/pallas_call | solution.py:417
  12.3 10.3 %collective-permute-done.recv_a = bf16[136,2048]{1,0:T(8,128)(2,1)S(1)} collective-permute-done((bf16[136,2048]{1,0:T(8,128)(2,1)S(1)}, bf16[136,2048]{1,0:T(8,128)(2,1)S(1)}, u32[]{:S(2)}, u32[]{:S(2)}) %collective-permute-start) | collective-permute-done | bytes 557088 | tf_op jit(solution)/shard_map/ppermute | solution.py:413
  22.6 10.3 %stencil.1 = (bf16[8,16,2048]{2,1,0:T(8,128)(2,1)S(1)}, bf16[4,16,2048]{2,1,0:T(8,128)(2,1)S(1)}, bf16[4,16,2048]{2,1,0:T(8,128)(2,1)S(1)}) custom-call(s32[3]{0:T(128)S(1)} %pad_add_fusion.pos, f32[2,8,16,2048]{3,2,1,0:T(8,128)S(1)} %get-tuple-element.27.turned, bf16[136,2048]{1,0:T(8,128)(2,1)S(1)} %collective-permute-done.recv_a, ...), custom_call_target="tpu_custom_call" | custom-call | tf_op jit(solution)/shard_map/stencil/pallas_call | solution.py:433
  33.0 0.1 collective-permute-start.4
  33.0 1.6 %collective-permute-start.2 = (bf16[4,16,2048]{2,1,0:T(8,128)(2,1)S(1)}, bf16[4,16,2048]{2,1,0:T(8,128)(2,1)S(1)}, u32[]{:S(2)}, u32[]{:S(2)}) collective-permute-start(bf16[4,16,2048]{2,1,0:T(8,128)(2,1)S(1)} %get-tuple-element.43.own_far), channel_id=1, source_target_pairs={{0,2},{1,3},{2,0},{3,1},{4,6},{5,7},{6,4},{7,5},{8,10},{9,11},{10,... | collective-permute-start | bytes 786440 | tf_op jit(solution)/shard_map/ppermute | solution.py:449
  34.6 0.3 collective-permute-start.3
  34.9 7.3 %collective-permute-done.2.far = bf16[4,16,2048]{2,1,0:T(8,128)(2,1)S(1)} collective-permute-done((bf16[4,16,2048]{2,1,0:T(8,128)(2,1)S(1)}, bf16[4,16,2048]{2,1,0:T(8,128)(2,1)S(1)}, u32[]{:S(2)}, u32[]{:S(2)}) %collective-permute-start.2) | collective-permute-done | bytes 262176 | tf_op jit(solution)/shard_map/ppermute | solution.py:449
  42.2 4.7 %collective-permute-done.3.diag = bf16[4,16,2048]{2,1,0:T(8,128)(2,1)S(1)} collective-permute-done((bf16[4,16,2048]{2,1,0:T(8,128)(2,1)S(1)}, bf16[4,16,2048]{2,1,0:T(8,128)(2,1)S(1)}, u32[]{:S(2)}, u32[]{:S(2)}) %collective-permute-start.3) | collective-permute-done | bytes 262176 | tf_op jit(solution)/shard_map/ppermute | solution.py:449
  46.9 0.0 collective-permute-done.4.mate.mate_near
  46.9 1.5 %collective-permute-start.12 = (bf16[8,16,2048]{2,1,0:T(8,128)(2,1)S(1)}, bf16[8,16,2048]{2,1,0:T(8,128)(2,1)S(1)}, u32[]{:S(2)}, u32[]{:S(2)}) collective-permute-start(bf16[8,16,2048]{2,1,0:T(8,128)(2,1)S(1)} %get-tuple-element.46.own.own_near), channel_id=1, source_target_pairs={{0,2},{1,3},{2,0},{3,1},{4,6},{5,7},{6,4},{7,5},{8,10},{9,11},{10,... | collective-permute-start | bytes 1572872 | tf_op jit(solution)/shard_map/ppermute | solution.py:449
  48.4 1.5 %gram.1 = f32[80,64]{1,0:T(8,128)S(1)} custom-call(s32[3]{0:T(128)S(1)} %pad_add_fusion.pos, bf16[8,16,2048]{2,1,0:T(8,128)(2,1)S(1)} %get-tuple-element.46.own.own_near, bf16[8,16,2048]{2,1,0:T(8,128)(2,1)S(1)} %collective-permute-done.4.mate.mate_near, bf16[4,16,2048]{2,1,0:T(8,128)(2,1)S(1)} %collective-permute-done.2.far, ...), custom_call_target="tpu_custom_call" | custom-call | tf_op jit(solution)/shard_map/gram/pallas_call | solution.py:459
  50.0 0.1 collective-permute-start.5
  50.1 1.2 %collective-permute-done.5 = f32[80,64]{1,0:T(8,128)S(1)} collective-permute-done((f32[80,64]{1,0:T(8,128)S(1)}, f32[80,64]{1,0:T(8,128)S(1)}, u32[]{:S(2)}, u32[]{:S(2)}) %collective-permute-start.5) | collective-permute-done | bytes 20512 | tf_op jit(solution)/shard_map/ppermute | solution.py:482
  51.3 0.5 collective-permute-start.6
  51.8 10.1 %collective-permute-done.6 = f32[80,64]{1,0:T(8,128)S(1)} collective-permute-done((f32[80,64]{1,0:T(8,128)S(1)}, f32[80,64]{1,0:T(8,128)S(1)}, u32[]{:S(2)}, u32[]{:S(2)}) %collective-permute-start.6) | collective-permute-done | bytes 20512 | tf_op jit(solution)/shard_map/ppermute | solution.py:482
  61.9 1.7 %collective-permute-start.7 = (f32[80,64]{1,0:T(8,128)S(1)}, f32[80,64]{1,0:T(8,128)S(1)}, u32[]{:S(2)}, u32[]{:S(2)}) collective-permute-start(f32[80,64]{1,0:T(8,128)S(1)} %add.10), channel_id=1, source_target_pairs={{0,4},{4,0},{8,12},{12,8},{1,5},{5,1},{9,13},{13,9},{2,6},{6,2},{1... | collective-permute-start | bytes 61448 | tf_op jit(solution)/shard_map/ppermute | solution.py:482
  63.6 2.3 %collective-permute-done.7 = f32[80,64]{1,0:T(8,128)S(1)} collective-permute-done((f32[80,64]{1,0:T(8,128)S(1)}, f32[80,64]{1,0:T(8,128)S(1)}, u32[]{:S(2)}, u32[]{:S(2)}) %collective-permute-start.7) | collective-permute-done | bytes 20512 | tf_op jit(solution)/shard_map/ppermute | solution.py:482
  65.9 1.6 %collective-permute-start.8 = (f32[80,64]{1,0:T(8,128)S(1)}, f32[80,64]{1,0:T(8,128)S(1)}, u32[]{:S(2)}, u32[]{:S(2)}) collective-permute-start(f32[80,64]{1,0:T(8,128)S(1)} %add.11.one), channel_id=1, source_target_pairs={{0,8},{4,12},{8,0},{12,4},{1,9},{5,13},{9,1},{13,5},{2,10},{6,14},... | collective-permute-start | bytes 61448 | tf_op jit(solution)/shard_map/ppermute | solution.py:482
  67.5 3.3 %collective-permute-done.8.two = f32[80,64]{1,0:T(8,128)S(1)} collective-permute-done((f32[80,64]{1,0:T(8,128)S(1)}, f32[80,64]{1,0:T(8,128)S(1)}, u32[]{:S(2)}, u32[]{:S(2)}) %collective-permute-start.8) | collective-permute-done | bytes 20512 | tf_op jit(solution)/shard_map/ppermute | solution.py:482
  70.8 0.5 collective-permute-start.9
  71.4 0.0 collective-permute-start.10
  71.4 0.5 collective-permute-start.11
  71.9 0.0 collective-permute-start.13
  71.9 2.8 %weights.1 = bf16[32,64]{1,0:T(8,128)(2,1)S(1)} custom-call(s32[3]{0:T(128)S(1)} %pad_add_fusion.pos, f32[80,64]{1,0:T(8,128)S(1)} %add.11.one, f32[80,64]{1,0:T(8,128)S(1)} %collective-permute-done.8.two), custom_call_target="tpu_custom_call" | custom-call | tf_op jit(solution)/shard_map/weights/pallas_call | solution.py:487
  74.6 0.0 collective-permute-done.9.mate_far
  74.7 3.2 %final.1 = f32[16,2,8,2048]{3,2,1,0:T(8,128)} custom-call(s32[3]{0:T(128)S(1)} %pad_add_fusion.pos, bf16[32,64]{1,0:T(8,128)(2,1)S(1)} %weights.1, bf16[8,16,2048]{2,1,0:T(8,128)(2,1)S(1)} %get-tuple-element.46.own.own_near, bf16[4,16,2048]{2,1,0:T(8,128)(2,1)S(1)} %get-tuple-element.43.own_far, bf16[4,16,2048]{2,1,0:T(8,128)(2,1)S(1)} %get-tuple-element.44.own_diag, ...), custom_call_target="tpu_custom_call" | custom-call | tf_op jit(solution)/shard_map/final/pallas_call | solution.py:497
  (18 shorter events, 0.1 us)
Async XLA Ops:
  0.0 11.0 %copy-start.3 = (f32[2048]{0:T(1024)S(1)}, f32[2048]{0:T(1024)}, u32[]{:S(2)}) copy-start(f32[2048]{0:T(1024)} %param.11) | copy-start | bytes 24580
  0.0 11.0 %copy-start.2 = (s32[2048]{0:T(1024)S(1)}, s32[2048]{0:T(1024)}, u32[]{:S(2)}) copy-start(s32[2048]{0:T(1024)} %param.8) | copy-start | bytes 24580
  0.1 1.6 %copy-start = (f32[16,2,8,2048]{3,2,1,0:T(8,128)S(1)}, f32[16,2,8,2048]{3,2,1,0:T(8,128)}, u32[]{:S(2)}) copy-start(f32[16,2,8,2048]{3,2,1,0:T(8,128)} %prior.1) | copy-start | bytes 6291460
  1.7 0.9 %copy-start.1 = (f32[2,2,8,2048]{3,2,1,0:T(8,128)S(1)}, f32[2,2,8,2048]{3,2,1,0:T(8,128)}, u32[]{:S(2)}) copy-start(f32[2,2,8,2048]{3,2,1,0:T(8,128)} %wind.3) | copy-start | bytes 786436
  2.6 8.3 %copy-start.4 = (f32[2048]{0:T(1024)S(1)}, f32[2048]{0:T(1024)}, u32[]{:S(2)}) copy-start(f32[2048]{0:T(1024)} %param.10) | copy-start | bytes 24580
  3.7 8.6 %collective-permute-start.1 = (bf16[136,2048]{1,0:T(8,128)(2,1)S(1)}, bf16[136,2048]{1,0:T(8,128)(2,1)S(1)}, u32[]{:S(2)}, u32[]{:S(2)}) collective-permute-start(bf16[136,2048]{1,0:T(8,128)(2,1)S(1)} %get-tuple-element.29), channel_id=1, source_target_pairs={{4,8},{8,4},{5,9},{9,5},{6,10},{10,6},{7,11},{11,7},{20,24},{24,20... | collective-permute-start | bytes 1671176 | tf_op jit(solution)/shard_map/ppermute | solution.py:414
  4.4 18.2 %collective-permute-start = (bf16[136,2048]{1,0:T(8,128)(2,1)S(1)}, bf16[136,2048]{1,0:T(8,128)(2,1)S(1)}, u32[]{:S(2)}, u32[]{:S(2)}) collective-permute-start(bf16[136,2048]{1,0:T(8,128)(2,1)S(1)} %get-tuple-element.28), channel_id=1, source_target_pairs={{0,4},{4,0},{8,12},{12,8},{1,5},{5,1},{9,13},{13,9},{2,6},{6,2},{1... | collective-permute-start | bytes 1671176 | tf_op jit(solution)/shard_map/ppermute | solution.py:413
  33.0 14.0 %collective-permute-start.4 = (bf16[8,16,2048]{2,1,0:T(8,128)(2,1)S(1)}, bf16[8,16,2048]{2,1,0:T(8,128)(2,1)S(1)}, u32[]{:S(2)}, u32[]{:S(2)}) collective-permute-start(bf16[8,16,2048]{2,1,0:T(8,128)(2,1)S(1)} %get-tuple-element.46.own.own_near), channel_id=1, source_target_pairs={{0,1},{1,0},{2,3},{3,2},{4,5},{5,4},{6,7},{7,6},{8,9},{9,8},{10,11... | collective-permute-start | bytes 1572872 | tf_op jit(solution)/shard_map/ppermute | solution.py:449
  33.0 9.2 %collective-permute-start.2 = (bf16[4,16,2048]{2,1,0:T(8,128)(2,1)S(1)}, bf16[4,16,2048]{2,1,0:T(8,128)(2,1)S(1)}, u32[]{:S(2)}, u32[]{:S(2)}) collective-permute-start(bf16[4,16,2048]{2,1,0:T(8,128)(2,1)S(1)} %get-tuple-element.43.own_far), channel_id=1, source_target_pairs={{0,2},{1,3},{2,0},{3,1},{4,6},{5,7},{6,4},{7,5},{8,10},{9,11},{10,... | collective-permute-start | bytes 786440 | tf_op jit(solution)/shard_map/ppermute | solution.py:449
  34.6 12.3 %collective-permute-start.3 = (bf16[4,16,2048]{2,1,0:T(8,128)(2,1)S(1)}, bf16[4,16,2048]{2,1,0:T(8,128)(2,1)S(1)}, u32[]{:S(2)}, u32[]{:S(2)}) collective-permute-start(bf16[4,16,2048]{2,1,0:T(8,128)(2,1)S(1)} %get-tuple-element.44.own_diag), channel_id=1, source_target_pairs={{0,3},{1,2},{2,1},{3,0},{4,7},{5,6},{6,5},{7,4},{8,11},{9,10},{10,... | collective-permute-start | bytes 786440 | tf_op jit(solution)/shard_map/ppermute | solution.py:449
  46.9 23.9 %collective-permute-start.12 = (bf16[8,16,2048]{2,1,0:T(8,128)(2,1)S(1)}, bf16[8,16,2048]{2,1,0:T(8,128)(2,1)S(1)}, u32[]{:S(2)}, u32[]{:S(2)}) collective-permute-start(bf16[8,16,2048]{2,1,0:T(8,128)(2,1)S(1)} %get-tuple-element.46.own.own_near), channel_id=1, source_target_pairs={{0,2},{1,3},{2,0},{3,1},{4,6},{5,7},{6,4},{7,5},{8,10},{9,11},{10,... | collective-permute-start | bytes 1572872 | tf_op jit(solution)/shard_map/ppermute | solution.py:449
  50.0 1.3 %collective-permute-start.5 = (f32[80,64]{1,0:T(8,128)S(1)}, f32[80,64]{1,0:T(8,128)S(1)}, u32[]{:S(2)}, u32[]{:S(2)}) collective-permute-start(f32[80,64]{1,0:T(8,128)S(1)} %gram.1), channel_id=1, source_target_pairs={{0,1},{1,0},{2,3},{3,2},{4,5},{5,4},{6,7},{7,6},{8,9},{9,8},{10,11... | collective-permute-start | bytes 61448 | tf_op jit(solution)/shard_map/ppermute | solution.py:482
  51.3 10.6 %collective-permute-start.6 = (f32[80,64]{1,0:T(8,128)S(1)}, f32[80,64]{1,0:T(8,128)S(1)}, u32[]{:S(2)}, u32[]{:S(2)}) collective-permute-start(f32[80,64]{1,0:T(8,128)S(1)} %add.9), channel_id=1, source_target_pairs={{0,2},{1,3},{2,0},{3,1},{4,6},{5,7},{6,4},{7,5},{8,10},{9,11},{10,... | collective-permute-start | bytes 61448 | tf_op jit(solution)/shard_map/ppermute | solution.py:482
  61.9 4.0 %collective-permute-start.7 = (f32[80,64]{1,0:T(8,128)S(1)}, f32[80,64]{1,0:T(8,128)S(1)}, u32[]{:S(2)}, u32[]{:S(2)}) collective-permute-start(f32[80,64]{1,0:T(8,128)S(1)} %add.10), channel_id=1, source_target_pairs={{0,4},{4,0},{8,12},{12,8},{1,5},{5,1},{9,13},{13,9},{2,6},{6,2},{1... | collective-permute-start | bytes 61448 | tf_op jit(solution)/shard_map/ppermute | solution.py:482
  65.9 4.9 %collective-permute-start.8 = (f32[80,64]{1,0:T(8,128)S(1)}, f32[80,64]{1,0:T(8,128)S(1)}, u32[]{:S(2)}, u32[]{:S(2)}) collective-permute-start(f32[80,64]{1,0:T(8,128)S(1)} %add.11.one), channel_id=1, source_target_pairs={{0,8},{4,12},{8,0},{12,4},{1,9},{5,13},{9,1},{13,5},{2,10},{6,14},... | collective-permute-start | bytes 61448 | tf_op jit(solution)/shard_map/ppermute | solution.py:482
  70.8 3.9 %collective-permute-start.14 = (bf16[8,16,2048]{2,1,0:T(8,128)(2,1)S(1)}, bf16[8,16,2048]{2,1,0:T(8,128)(2,1)S(1)}, u32[]{:S(2)}, u32[]{:S(2)}) collective-permute-start(bf16[8,16,2048]{2,1,0:T(8,128)(2,1)S(1)} %collective-permute-done.12.far_near), channel_id=1, source_target_pairs={{0,1},{1,0},{2,3},{3,2},{4,5},{5,4},{6,7},{7,6},{8,9},{9,8},{10,11... | collective-permute-start | bytes 1572872 | tf_op jit(solution)/shard_map/ppermute | solution.py:449
  70.8 3.8 %collective-permute-start.9 = (bf16[4,16,2048]{2,1,0:T(8,128)(2,1)S(1)}, bf16[4,16,2048]{2,1,0:T(8,128)(2,1)S(1)}, u32[]{:S(2)}, u32[]{:S(2)}) collective-permute-start(bf16[4,16,2048]{2,1,0:T(8,128)(2,1)S(1)} %get-tuple-element.43.own_far), channel_id=1, source_target_pairs={{0,1},{1,0},{2,3},{3,2},{4,5},{5,4},{6,7},{7,6},{8,9},{9,8},{10,11... | collective-permute-start | bytes 786440 | tf_op jit(solution)/shard_map/ppermute | solution.py:449
  71.4 3.3 %collective-permute-start.10 = (bf16[4,16,2048]{2,1,0:T(8,128)(2,1)S(1)}, bf16[4,16,2048]{2,1,0:T(8,128)(2,1)S(1)}, u32[]{:S(2)}, u32[]{:S(2)}) collective-permute-start(bf16[4,16,2048]{2,1,0:T(8,128)(2,1)S(1)} %get-tuple-element.44.own_diag), channel_id=1, source_target_pairs={{0,1},{1,0},{2,3},{3,2},{4,5},{5,4},{6,7},{7,6},{8,9},{9,8},{10,11... | collective-permute-start | bytes 786440 | tf_op jit(solution)/shard_map/ppermute | solution.py:449
  71.4 3.3 %collective-permute-start.11 = (bf16[4,16,2048]{2,1,0:T(8,128)(2,1)S(1)}, bf16[4,16,2048]{2,1,0:T(8,128)(2,1)S(1)}, u32[]{:S(2)}, u32[]{:S(2)}) collective-permute-start(bf16[4,16,2048]{2,1,0:T(8,128)(2,1)S(1)} %collective-permute-done.3.diag), channel_id=1, source_target_pairs={{0,1},{1,0},{2,3},{3,2},{4,5},{5,4},{6,7},{7,6},{8,9},{9,8},{10,11... | collective-permute-start | bytes 786440 | tf_op jit(solution)/shard_map/ppermute | solution.py:449
  71.9 2.8 %collective-permute-start.13 = (bf16[4,16,2048]{2,1,0:T(8,128)(2,1)S(1)}, bf16[4,16,2048]{2,1,0:T(8,128)(2,1)S(1)}, u32[]{:S(2)}, u32[]{:S(2)}) collective-permute-start(bf16[4,16,2048]{2,1,0:T(8,128)(2,1)S(1)} %collective-permute-done.2.far), channel_id=1, source_target_pairs={{0,1},{1,0},{2,3},{3,2},{4,5},{5,4},{6,7},{7,6},{8,9},{9,8},{10,11... | collective-permute-start | bytes 786440 | tf_op jit(solution)/shard_map/ppermute | solution.py:449

commit v3 on v2

--- a/solution.py
+++ b/solution.py
@@ -1,3 +1,5 @@
+import functools
+
 import jax
 import jax.numpy as jnp
 from jax import lax
@@ -146,40 +148,56 @@
     return pl.BlockSpec(memory_space=pltpu.SMEM)
 
 
+def hbm():
+    return pl.BlockSpec(memory_space=pltpu.MemorySpace.HBM)
+
+
 def params():
     return pltpu.CompilerParams(vmem_limit_bytes=44 * 1024 * 1024)
 
 
-def pack_kernel(pos, prior, wind, turned, pay_a, pay_b):
-    for f in range(2):
-        turned[f] = jnp.swapaxes(prior[:, f], 0, 1)
+def cost(touched):
+    return pl.CostEstimate(flops=touched, bytes_accessed=touched, transcendentals=0)
+
+
+def pack_kernel(field, pos, prior, wind, turned, pay_a, pay_b, state, edge, sems):
+    load = pltpu.make_async_copy(prior.at[:, field], state, sems.at[0])
+    load.start()
+    if field == 0:
+        winds = pltpu.make_async_copy(wind.at[0], edge, sems.at[1])
+        winds.start()
     even = (pos[0] % 2) == 0
     start_a = jnp.where(even, 4, 0)
     start_b = 4 - start_a
-    for f in range(2):
-        for r in range(4):
-            at = (f * 4 + r) * 16
-            pay_a[at : at + 16, :] = turned[f, start_a + r].astype(BF)
-            pay_b[at : at + 16, :] = turned[f, start_b + r].astype(BF)
-    first = jnp.concatenate([wind[0, 0, 0:2], wind[0, 1, 0:2]], 0)
-    last = jnp.concatenate([wind[0, 0, 6:8], wind[0, 1, 6:8]], 0)
-    first_high = first.astype(BF).astype(F32)
-    last_high = last.astype(BF).astype(F32)
-    first = jnp.concatenate([first_high, first - first_high], 0)
-    last = jnp.concatenate([last_high, last - last_high], 0)
-    pay_a[128:136, :] = jnp.where(even, last, first).astype(BF)
-    pay_b[128:136, :] = jnp.where(even, first, last).astype(BF)
-
-
-def maps_kernel(pos, index, count, weight, value, root_map, value_map):
+    if field == 0:
+        winds.wait()
+        first = jnp.concatenate([edge[0, 0:2], edge[1, 0:2]], 0)
+        last = jnp.concatenate([edge[0, 6:8], edge[1, 6:8]], 0)
+        first_high = first.astype(BF).astype(F32)
+        last_high = last.astype(BF).astype(F32)
+        first = jnp.concatenate([first_high, first - first_high], 0)
+        last = jnp.concatenate([last_high, last - last_high], 0)
+        pay_a[64:72, :] = jnp.where(even, last, first).astype(BF)
+        pay_b[64:72, :] = jnp.where(even, first, last).astype(BF)
+    load.wait()
+    turned[...] = jnp.swapaxes(state[...], 0, 1)
+    for r in range(4):
+        pay_a[r * 16 : r * 16 + 16, :] = turned[start_a + r].astype(BF)
+        pay_b[r * 16 : r * 16 + 16, :] = turned[start_b + r].astype(BF)
+
+
+def maps_kernel(tiles, pos, index, count, weight, value, root_map, value_map):
     slots = index.shape[1]
     n = index[...]
     used = lax.broadcasted_iota(jnp.int32, (1, slots), 1) < count[0]
     root = jnp.where(used, jnp.sqrt(weight[...]), 0.0)
     rooted = root * value[...]
-    block = n // 128 - pos[2] * 64
+    block = n // 128
+    row = (block // tiles) % 8
+    cell = (block // (tiles * 8)) * (2 * tiles) + (row % 2) * tiles + block % tiles
+    cell = jnp.where(row // 2 == pos[2], cell, -1)
     lane = n % 128
-    hit = lax.broadcasted_iota(jnp.int32, (64, slots), 0) == block
+    hit = lax.broadcasted_iota(jnp.int32, (4 * tiles, slots), 0) == cell
     hit = jnp.where(hit, 1.0, 0.0).astype(BF)
     lane_hit = lax.broadcasted_iota(jnp.int32, (128, slots), 0) == lane
     pieces = []
@@ -211,27 +229,26 @@
 
 
 def stencil_kernel(
-    pos, turned, recv_a, recv_b, wind, out_near, out_far, out_diag, ext, mid, wide, wide2
+    nu, pos, turned, recv_a, recv_b, wind_a, wind_b, wind, out_all, out_near, out_far, out_diag,
+    ext, mid, wide, wide2
 ):
-    cols = turned.shape[3]
+    cols = turned.shape[2]
     even = (pos[0] % 2) == 0
     start_a = jnp.where(even, 12, 0)
     start_b = 12 - start_a
     zeros = jnp.zeros((16, PAD), F32)
-    for f in range(2):
-        for r in range(16):
-            ext[f, r, :, cols:] = zeros
-        for r in range(12):
-            mid[f, r, :, cols:] = zeros
-        for r in range(8):
-            ext[f, r + 4, :, :cols] = turned[f, r]
-        for r in range(4):
-            at = (f * 4 + r) * 16
-            ext[f, start_a + r, :, :cols] = recv_a[at : at + 16, :].astype(F32)
-            ext[f, start_b + r, :, :cols] = recv_b[at : at + 16, :].astype(F32)
-    got_a = recv_a[128:136, :].astype(F32)
+    for r in range(16):
+        ext[r, :, cols:] = zeros
+    for r in range(12):
+        mid[r, :, cols:] = zeros
+    for r in range(8):
+        ext[r + 4, :, :cols] = turned[r]
+    for r in range(4):
+        ext[start_a + r, :, :cols] = recv_a[r * 16 : r * 16 + 16, :].astype(F32)
+        ext[start_b + r, :, :cols] = recv_b[r * 16 : r * 16 + 16, :].astype(F32)
+    got_a = wind_a[64:72, :].astype(F32)
     got_a = got_a[0:4] + got_a[4:8]
-    got_b = recv_b[128:136, :].astype(F32)
+    got_b = wind_b[64:72, :].astype(F32)
     got_b = got_b[0:4] + got_b[4:8]
     before = jnp.where(even, got_b, got_a)
     after = jnp.where(even, got_a, got_b)
@@ -249,61 +266,52 @@
             row = wind[1, c, r : r + 1]
             wide2[c, r] = jnp.broadcast_to(row * twelfth, (8, cols))
 
-    for f in range(2):
-
-        def first_step(r, carry, f=f):
-            for g in range(2):
-                span = pl.ds(g * 8, 8)
-                rows = [ext[f, r + i, span, :] for i in range(5)]
-                mid[f, r, span, :cols] = stencil_row(
-                    rows, wide[0, r], wide[1, r], DIFFUSION[f]
-                )
-            return carry
-
-        lax.fori_loop(0, 12, first_step, 0)
+    def first_step(r, carry):
+        for g in range(2):
+            span = pl.ds(g * 8, 8)
+            rows = [ext[r + i, span, :] for i in range(5)]
+            mid[r, span, :cols] = stencil_row(rows, wide[0, r], wide[1, r], nu)
+        return carry
+
+    lax.fori_loop(0, 12, first_step, 0)
 
     @pl.when(pos[0] == 0)
     def _():
-        mid[:, 0:2] = jnp.zeros((2, 2) + mid.shape[2:], F32)
+        mid[0:2] = jnp.zeros((2,) + mid.shape[1:], F32)
 
     @pl.when(pos[0] == pos[1] - 1)
     def _():
-        mid[:, 10:12] = jnp.zeros((2, 2) + mid.shape[2:], F32)
-
-    for slot, out, place in ((2, out_far, 0), (3, out_diag, 0), (0, out_near, 0), (1, out_near, 1)):
-        quarter = jnp.bitwise_xor(pos[2], slot)
-        f = quarter // 2
-        base = (quarter % 2) * 4
-        nu = jnp.where(f == 0, DIFFUSION[0], DIFFUSION[1])
-
-        def second_step(r, carry, f=f, base=base, nu=nu, out=out, place=place):
-            row = base + r
-            both = []
-            for g in range(2):
-                span = pl.ds(g * 8, 8)
-                rows = [mid[f, row + i, span, :] for i in range(5)]
-                both.append(stencil_row(rows, wide2[0, row], wide2[1, row], nu))
-            value = jnp.concatenate(both, 0).astype(BF)
-            if place is None:
-                out[r] = value
-            else:
-                out[place * 4 + r] = value
-            return carry
-
-        lax.fori_loop(0, 4, second_step, 0)
-
-
-def gram_kernel(pos, own, mate, far, diag, root_map, value_map, out, spread):
+        mid[10:12] = jnp.zeros((2,) + mid.shape[1:], F32)
+
+    def second_step(r, carry):
+        both = []
+        for g in range(2):
+            span = pl.ds(g * 8, 8)
+            rows = [mid[r + i, span, :] for i in range(5)]
+            both.append(stencil_row(rows, wide2[0, r], wide2[1, r], nu))
+        out_all[r] = jnp.concatenate(both, 0).astype(BF)
+        return carry
+
+    lax.fori_loop(0, 8, second_step, 0)
+    for r in range(2):
+        out_far[r] = out_all[2 * jnp.bitwise_xor(pos[2], 2) + r]
+        out_diag[r] = out_all[2 * jnp.bitwise_xor(pos[2], 3) + r]
+        out_near[r] = out_all[2 * pos[2] + r]
+        out_near[2 + r] = out_all[2 * jnp.bitwise_xor(pos[2], 1) + r]
+
+
+def gram_sum(field, pos, own, mate, far, diag, root_map, value_map, spread):
     tiles = own.shape[2] // 128
     spread[4] = jnp.zeros(spread.shape[1:], BF)
-    for r in range(4):
+    for r in range(2):
+        row = 2 * pos[2] + r
         for t in range(tiles):
             cut = slice(t * 128, (t + 1) * 128)
-            at = r * tiles + t
-            into = slice(at * 128, (at + 1) * 128)
+            at = (field * 2 + r) * tiles + t
+            into = slice((r * tiles + t) * 128, (r * tiles + t + 1) * 128)
             parts = [
-                own[r, :, cut].astype(F32),
-                mate[4 + r, :, cut].astype(F32),
+                own[row, :, cut].astype(F32),
+                mate[row, :, cut].astype(F32),
                 far[r, :, cut].astype(F32),
                 diag[r, :, cut].astype(F32),
             ]
@@ -319,9 +327,23 @@
     cells = spread.shape[2]
     left = spread[...].reshape(80, cells)
     right = spread[0:4].reshape(64, cells)
-    out[...] = lax.dot_general(
+    return lax.dot_general(
         left, right, (((1,), (1,)), ((), ())), preferred_element_type=F32
     )
+
+
+def gram_first(pos, own, mate, far, diag, root_map, value_map, out, spread):
+    out[...] = gram_sum(0, pos, own, mate, far, diag, root_map, value_map, spread)
+
+
+def gram_second(
+    pos, own, mate, far, diag, root_map, value_map, part, far_zero, diag_zero, out, pass_on, spread
+):
+    out[...] = part[...] + gram_sum(1, pos, own, mate, far, diag, root_map, value_map, spread)
+    pass_on[0:2] = far_zero[...]
+    pass_on[2:4] = diag_zero[...]
+    pass_on[4:6] = far[...]
+    pass_on[6:8] = diag[...]
 
 
 def exact(a, b):
@@ -366,60 +388,83 @@
 
 
 def final_kernel(
-    pos, weights, own_near, own_far, own_diag, mate_near, mate_far, mate_diag,
-    far, far_mate, far_near, diag, diag_mate, diag_near, out, keep
+    pos, weights, own_0, own_1, mate_0, mate_1, far_0, far_1, diag_0, diag_1, passed,
+    near_0, near_1, mate_near_0, mate_near_1, out, keep, ready, sems
 ):
     m = weights[...]
-    for t in range(4):
-        quarter = jnp.bitwise_xor(pos[2], t)
-        f = quarter // 2
-        base = (quarter % 2) * 4
-        for r in range(4):
-            if t == 0:
-                parts = [own_near[r], mate_near[4 + r], far[r], diag[r]]
-            elif t == 1:
-                parts = [own_near[4 + r], mate_near[r], far_mate[r], diag_mate[r]]
-            elif t == 2:
-                parts = [own_far[r], mate_diag[r], far_near[r], diag_near[4 + r]]
-            else:
-                parts = [own_diag[r], mate_far[r], far_near[4 + r], diag_near[r]]
-            state = jnp.concatenate(parts, 0)
-            both = jnp.dot(m, state, preferred_element_type=F32)
-            keep[f, base + r] = both[0:16] + both[16:32]
+    fields = (
+        (own_0, mate_0, far_0, diag_0, near_0, mate_near_0),
+        (own_1, mate_1, far_1, diag_1, near_1, mate_near_1),
+    )
+    copies = []
     for f in range(2):
-        out[:, f] = jnp.swapaxes(keep[f], 0, 1)
+        own, mate, far, diag, near, mate_near = fields[f]
+        for t in range(4):
+            quarter = jnp.bitwise_xor(pos[2], t)
+            for r in range(2):
+                row = 2 * quarter + r
+                if t == 0:
+                    parts = [far[r], diag[r]]
+                elif t == 1:
+                    parts = [passed[4 * f + 2 + r], passed[4 * f + r]]
+                elif t == 2:
+                    parts = [near[r], mate_near[2 + r]]
+                else:
+                    parts = [near[2 + r], mate_near[r]]
+                state = jnp.concatenate([own[row], mate[row]] + parts, 0)
+                both = jnp.dot(m, state, preferred_element_type=F32)
+                keep[row] = both[0:16] + both[16:32]
+        ready[f] = jnp.swapaxes(keep[...], 0, 1)
+        copies.append(pltpu.make_async_copy(ready.at[f], out.at[:, f], sems.at[f]))
+        copies[f].start()
+    for f in range(2):
+        copies[f].wait()
 
 
 def local(prior_replicas, wind_field, obs_index, obs_count, obs_value, obs_weight):
     cols = prior_replicas.shape[3]
+    tiles = cols // 128
     strips = lax.axis_size("space")
     here = lax.axis_index("space")
     group = lax.axis_index("mem")
     pos = jnp.stack([here, jnp.int32(strips), group]).astype(jnp.int32)
     shape = jax.ShapeDtypeStruct
-
-    turned, pay_a, pay_b = pl.pallas_call(
-        pack_kernel,
-        name="pack",
-        in_specs=[smem(), vmem(), vmem()],
-        out_specs=[vmem()] * 3,
-        out_shape=[shape((2, 8, 16, cols), F32), shape((136, cols), BF), shape((136, cols), BF)],
-        compiler_params=params(),
-    )(pos, prior_replicas, wind_field)
-
-    pairs_a = [(i, i ^ 1) for i in range(strips) if (i ^ 1) < strips]
+    pairs_a = [(i, i ^ 1) for i in range(strips)]
     pairs_b = [(i, i + 1) for i in range(1, strips - 1, 2)]
     pairs_b = pairs_b + [(j, i) for i, j in pairs_b]
-    recv_a = lax.ppermute(pay_a, "space", pairs_a)
-    recv_b = lax.ppermute(pay_b, "space", pairs_b)
+
+    def swap(value, bits):
+        return lax.ppermute(value, "mem", [(i, i ^ bits) for i in range(4)])
+
+    turned = []
+    recv = []
+    for f in range(2):
+        height = 72 if f == 0 else 64
+        rows, pay_a, pay_b = pl.pallas_call(
+            functools.partial(pack_kernel, f),
+            name="pack",
+            cost_estimate=cost(40 * 16 * cols * 4),
+            in_specs=[smem(), hbm(), hbm()],
+            out_specs=[vmem()] * 3,
+            out_shape=[shape((8, 16, cols), F32)] + [shape((height, cols), BF)] * 2,
+            scratch_shapes=[
+                pltpu.VMEM((16, 8, cols), F32),
+                pltpu.VMEM((2, 8, cols), F32),
+                pltpu.SemaphoreType.DMA((2,)),
+            ],
+            compiler_params=params(),
+        )(pos, prior_replicas, wind_field)
+        turned.append(rows)
+        recv.append([lax.ppermute(pay_a, "space", pairs_a), lax.ppermute(pay_b, "space", pairs_b)])
 
     slots = obs_index.shape[0]
     root_map, value_map = pl.pallas_call(
-        maps_kernel,
+        functools.partial(maps_kernel, tiles),
         name="maps",
+        cost_estimate=cost(slots * 1024 * 4),
         in_specs=[smem(), vmem(), smem(), vmem(), vmem()],
         out_specs=[vmem()] * 2,
-        out_shape=[shape((64, 128), F32)] * 2,
+        out_shape=[shape((4 * tiles, 128), F32)] * 2,
         compiler_params=params(),
     )(
         pos,
@@ -428,46 +473,61 @@
         obs_weight.reshape(1, slots),
         obs_value.reshape(1, slots),
     )
-
-    recv_b, root_map, value_map = lax.optimization_barrier((recv_b, root_map, value_map))
-    near, far, diag = pl.pallas_call(
-        stencil_kernel,
-        name="stencil",
-        in_specs=[smem()] + [vmem()] * 4,
-        out_specs=[vmem()] * 3,
-        out_shape=[shape((8, 16, cols), BF), shape((4, 16, cols), BF), shape((4, 16, cols), BF)],
-        scratch_shapes=[
-            pltpu.VMEM((2, 16, 16, cols + PAD), F32),
-            pltpu.VMEM((2, 12, 16, cols + PAD), F32),
-            pltpu.VMEM((2, 12, 8, cols), F32),
-            pltpu.VMEM((2, 8, 8, cols), F32),
-        ],
-        compiler_params=params(),
-    )(pos, turned, recv_a, recv_b, wind_field)
-
-    def swap(value, bits):
-        return lax.ppermute(value, "mem", [(i, i ^ bits) for i in range(4)])
-
-    got_far = swap(far, 2)
-    got_diag = swap(diag, 3)
-    mate_near = swap(near, 1)
-    got_far, got_diag, mate_near, near_late, far_late, diag_late = lax.optimization_barrier(
-        (got_far, got_diag, mate_near, near, far, diag)
-    )
-    far_near = swap(near_late, 2)
-
-    part = pl.pallas_call(
-        gram_kernel,
-        name="gram",
-        in_specs=[smem()] + [vmem()] * 6,
-        out_specs=vmem(),
-        out_shape=shape((80, 64), F32),
-        scratch_shapes=[pltpu.VMEM((5, 16, 4 * cols), BF)],
-        compiler_params=params(),
-    )(pos, near, mate_near, got_far, got_diag, root_map, value_map)
-
-    rounds = [("mem", 1), ("mem", 2)]
-    bit = 1
+    recv[0][1], root_map, value_map = lax.optimization_barrier((recv[0][1], root_map, value_map))
+
+    state = []
+    got = []
+    for f in range(2):
+        every, near, far, diag = pl.pallas_call(
+            functools.partial(stencil_kernel, DIFFUSION[f]),
+            name="stencil",
+            cost_estimate=cost(180 * 16 * cols * 4),
+            in_specs=[smem()] + [vmem()] * 6,
+            out_specs=[vmem()] * 4,
+            out_shape=[
+                shape((8, 16, cols), BF),
+                shape((4, 16, cols), BF),
+                shape((2, 16, cols), BF),
+                shape((2, 16, cols), BF),
+            ],
+            scratch_shapes=[
+                pltpu.VMEM((16, 16, cols + PAD), F32),
+                pltpu.VMEM((12, 16, cols + PAD), F32),
+                pltpu.VMEM((2, 12, 8, cols), F32),
+                pltpu.VMEM((2, 8, 8, cols), F32),
+            ],
+            compiler_params=params(),
+        )(pos, turned[f], recv[f][0], recv[f][1], recv[0][0], recv[0][1], wind_field)
+        if f == 1:
+            got[0][0], got[0][1], every, far, diag = lax.optimization_barrier(
+                (got[0][0], got[0][1], every, far, diag)
+            )
+        state.append((every, near))
+        got.append([swap(far, 2), swap(diag, 3), swap(every, 1)])
+
+    def gram(kernel, f, extra, more):
+        return pl.pallas_call(
+            kernel,
+            name="gram",
+            cost_estimate=cost(24 * 64 * cols * 2),
+            in_specs=[smem()] + [vmem()] * (6 + len(extra)),
+            out_specs=[vmem()] * (1 + len(more)),
+            out_shape=[shape((80, 64), F32)] + more,
+            scratch_shapes=[pltpu.VMEM((5, 16, 2 * cols), BF)],
+            compiler_params=params(),
+        )(pos, state[f][0], got[f][2], got[f][0], got[f][1], root_map, value_map, *extra)
+
+    part = gram(gram_first, 0, [], [])[0]
+    got[1][0], got[1][1], near_0, part = lax.optimization_barrier(
+        (got[1][0], got[1][1], state[0][1], part)
+    )
+    near_0 = swap(near_0, 2)
+    part, pass_on = gram(
+        gram_second, 1, [part, got[0][0], got[0][1]], [shape((8, 16, cols), BF)]
+    )
+
+    rounds = [("mem", 1), ("space", 1), ("mem", 2)]
+    bit = 2
     while bit < strips:
         rounds.append(("space", bit))
         bit *= 2
@@ -476,17 +536,18 @@
         if other is not None:
             part = part + other
         if (axis, bits) == ("mem", 2):
-            late = lax.optimization_barrier((far_late, diag_late, got_far, got_diag, part))
-            mate_far, mate_diag, diag_mate, far_mate = [swap(v, 1) for v in late[:4]]
+            part, near_0 = lax.optimization_barrier((part, near_0))
         size = lax.axis_size(axis)
         other = lax.ppermute(part, axis, [(i, i ^ bits) for i in range(size)])
-
-    far_near_late, _ = lax.optimization_barrier((far_near, other))
-    diag_near = swap(far_near_late, 1)
+        if (axis, bits) == ("mem", 2):
+            near_1, pass_on, other = lax.optimization_barrier((state[1][1], pass_on, other))
+            near_1 = swap(near_1, 2)
+            passed = swap(pass_on, 1)
 
     weights = pl.pallas_call(
         weights_kernel,
         name="weights",
+        cost_estimate=cost(400 * 64 * 128 * 4),
         in_specs=[smem(), vmem(), vmem()],
         out_specs=vmem(),
         out_shape=shape((32, 64), BF),
@@ -494,17 +555,26 @@
         compiler_params=params(),
     )(pos, part, other)
 
+    near_0_late, _ = lax.optimization_barrier((near_0, other))
+    mate_near_0 = swap(near_0_late, 1)
+    mate_near_1 = swap(near_1, 1)
+
     return pl.pallas_call(
         final_kernel,
         name="final",
-        in_specs=[smem()] + [vmem()] * 13,
-        out_specs=vmem(),
+        cost_estimate=cost(100 * 16 * cols * 4),
+        in_specs=[smem()] + [vmem()] * 14,
+        out_specs=hbm(),
         out_shape=shape(prior_replicas.shape, F32),
-        scratch_shapes=[pltpu.VMEM((2, 8, 16, cols), F32)],
+        scratch_shapes=[
+            pltpu.VMEM((8, 16, cols), F32),
+            pltpu.VMEM((2, 16, 8, cols), F32),
+            pltpu.SemaphoreType.DMA((2,)),
+        ],
         compiler_params=params(),
     )(
-        pos, weights, near, far, diag, mate_near, mate_far, mate_diag,
-        got_far, far_mate, far_near, got_diag, diag_mate, diag_near,
+        pos, weights, state[0][0], state[1][0], got[0][2], got[1][2], got[0][0], got[1][0],
+        got[0][1], got[1][1], passed, near_0, near_1, mate_near_0, mate_near_1,
     )
 
 

time: 78.1 us -> 65.8 us (0.84)
  waiting for transfers between devices: 39.3 us -> 19.6 us
  starting transfers between devices: 14.9 us -> 20.1 us
  Pallas kernels: 20.2 us -> 22.4 us
    ppermute x4, waiting for transfers between devices: 16.9 us -> 8.44 us  [local(): other = lax.ppermute(part, axis, [(i, i ^ bits) for i in range(size)])]
    ppermute x2 -> x4, waiting for transfers between devices: 10.3 us -> 4.2 us  [the longest x2 4.2 us: local(): lax.ppermute(pay_a, 'space', pairs_a)]
    ppermute x9 -> x11, waiting for transfers between devices: 12 us -> 6.95 us  [swap(): return lax.ppermute(value, 'mem', [(i, i ^ bits) for i in range(4)])]
    ppermute x9 -> x11, starting transfers between devices: 4.45 us -> 6.96 us  [swap(): return lax.ppermute(value, 'mem', [(i, i ^ bits) for i in range(4)])]
    pallas_call x6 -> x9, Pallas kernels: 20.2 us -> 22.4 us  [the longest x2 11.2 us: local(): pl.pallas_call(functools.partial(stencil_kernel, DIFFUSION[f]), name='ste...]
    ppermute x4, starting transfers between devices: 3.91 us -> 5.84 us  [local(): other = lax.ppermute(part, axis, [(i, i ^ bits) for i in range(size)])]
    ppermute x2 -> x4, starting transfers between devices: 6.57 us -> 7.33 us  [the longest x2 5.98 us: local(): lax.ppermute(pay_a, 'space', pairs_a)]
    unnamed x10 -> x12, local copies, waits for them, and re-layouts: 2.55 us -> 2.56 us
  transfers between devices with their start and end apart: 15 -> 19, of which waited for: 7 -> 10; matrix products, arithmetic and copies ran while one was open for 0% -> 0% of each run, Pallas kernels for 7% -> 28%
where the time goes in v3:
time: 65.8 us; the launch traced here: 65.6 us
  Pallas kernels  22.4 us (34%)
  starting transfers between devices  20.1 us (31%)
  waiting for transfers between devices  19.6 us (30%)
  local copies, waits for them, and re-layouts  2.56 us (4%)
  between operations  0.81 us (1%)
    pallas_call x2, Pallas kernels, local(): pl.pallas_call(functools.partial(stencil_kernel, DIFFUSION[f]), name='ste...  11.2 us
    ppermute x4, waiting for transfers between devices, local(): other = lax.ppermute(part, axis, [(i, i ^ bits) for i in range(size)])  8.44 us
    ppermute x11, starting transfers between devices, swap(): return lax.ppermute(value, 'mem', [(i, i ^ bits) for i in range(4)])  6.96 us
    ppermute x11, waiting for transfers between devices, swap(): return lax.ppermute(value, 'mem', [(i, i ^ bits) for i in range(4)])  6.95 us
    ppermute x2, starting transfers between devices, local(): lax.ppermute(pay_a, 'space', pairs_a)  5.98 us
    ppermute x4, starting transfers between devices, local(): other = lax.ppermute(part, axis, [(i, i ^ bits) for i in range(size)])  5.84 us
    ppermute x2, waiting for transfers between devices, local(): lax.ppermute(pay_a, 'space', pairs_a)  4.2 us
    pallas_call x1, Pallas kernels, local(): pl.pallas_call(final_kernel, name='final', cost_estimate=cost(100 * 16 *...  2.82 us
  transfers between devices with their start and end apart: 19, of which 10 were waited for; matrix products, arithmetic and copies ran while one was open for 0% of the time, Pallas kernels for 28%

profile of v3, /device:TPU:0, one launch (start us, length us, event | category | flops | bytes accessed | tf_op | source)
XLA Modules:
  0.0 65.6 jit_solution(8420921585919109742)
XLA Ops:
  0.1 1.6 %copy-done = f32[16,2,8,2048]{3,2,1,0:T(8,128)S(1)} copy-done((f32[16,2,8,2048]{3,2,1,0:T(8,128)S(1)}, f32[16,2,8,2048]{3,2,1,0:T(8,128)}, u32[]{:S(2)}) %copy-start) | copy-done | bytes 2097176
  1.7 0.9 %copy-done.1 = f32[2,2,8,2048]{3,2,1,0:T(8,128)S(1)} copy-done((f32[2,2,8,2048]{3,2,1,0:T(8,128)S(1)}, f32[2,2,8,2048]{3,2,1,0:T(8,128)}, u32[]{:S(2)}) %copy-start.1) | copy-done | bytes 262168
  2.6 1.1 %pack.2 = (f32[8,16,2048]{2,1,0:T(8,128)S(1)}, bf16[72,2048]{1,0:T(8,128)(2,1)S(1)}, bf16[72,2048]{1,0:T(8,128)(2,1)S(1)}) custom-call(s32[3]{0:T(128)S(1)} %pad_add_fusion.pos, f32[16,2,8,2048]{3,2,1,0:T(8,128)S(1)} %copy-done, f32[2,2,8,2048]{3,2,1,0:T(8,128)S(1)} %copy-done.1), custom_call_target="tpu_custom_call" | custom-call | flops 5242880 | bytes 5242880 | tf_op jit(solution)/shard_map/pack/pallas_call | solution.py:443
  3.8 0.7 %collective-permute-start.1 = (bf16[72,2048]{1,0:T(8,128)(2,1)S(1)}, bf16[72,2048]{1,0:T(8,128)(2,1)S(1)}, u32[]{:S(2)}, u32[]{:S(2)}) collective-permute-start(bf16[72,2048]{1,0:T(8,128)(2,1)S(1)} %get-tuple-element.43), channel_id=1, source_target_pairs={{4,8},{8,4},{5,9},{9,5},{6,10},{10,6},{7,11},{11,7},{20,24},{24,20... | collective-permute-start | bytes 884744 | tf_op jit(solution)/shard_map/ppermute | solution.py:458
  4.4 5.9 %collective-permute-start = (bf16[72,2048]{1,0:T(8,128)(2,1)S(1)}, bf16[72,2048]{1,0:T(8,128)(2,1)S(1)}, u32[]{:S(2)}, u32[]{:S(2)}) collective-permute-start(bf16[72,2048]{1,0:T(8,128)(2,1)S(1)} %get-tuple-element.42), channel_id=1, source_target_pairs={{0,4},{4,0},{8,12},{12,8},{1,5},{5,1},{9,13},{13,9},{2,6},{6,2},{1... | collective-permute-start | bytes 884744 | tf_op jit(solution)/shard_map/ppermute | solution.py:458
  10.3 0.9 %pack.3 = (f32[8,16,2048]{2,1,0:T(8,128)S(1)}, bf16[64,2048]{1,0:T(8,128)(2,1)S(1)}, bf16[64,2048]{1,0:T(8,128)(2,1)S(1)}) custom-call(s32[3]{0:T(128)S(1)} %pad_add_fusion.pos, f32[16,2,8,2048]{3,2,1,0:T(8,128)S(1)} %copy-done, f32[2,2,8,2048]{3,2,1,0:T(8,128)S(1)} %copy-done.1), custom_call_target="tpu_custom_call" | custom-call | flops 5242880 | bytes 5242880 | tf_op jit(solution)/shard_map/pack/pallas_call | solution.py:443
  11.3 0.7 %collective-permute-start.5 = (bf16[64,2048]{1,0:T(8,128)(2,1)S(1)}, bf16[64,2048]{1,0:T(8,128)(2,1)S(1)}, u32[]{:S(2)}, u32[]{:S(2)}) collective-permute-start(bf16[64,2048]{1,0:T(8,128)(2,1)S(1)} %get-tuple-element.51), channel_id=1, source_target_pairs={{4,8},{8,4},{5,9},{9,5},{6,10},{10,6},{7,11},{11,7},{20,24},{24,20... | collective-permute-start | bytes 786440 | tf_op jit(solution)/shard_map/ppermute | solution.py:458
  12.7 1.3 %maps.1 = (f32[64,128]{1,0:T(8,128)S(1)}, f32[64,128]{1,0:T(8,128)S(1)}) custom-call(s32[3]{0:T(128)S(1)} %pad_add_fusion.pos, s32[1,2048]{1,0:T(1,128)S(1)} %bitcast.5, s32[1]{0:T(128)S(6)} %copy.7.count, f32[1,2048]{1,0:T(1,128)S(1)} %bitcast.6, f32[1,2048]{1,0:T(1,128)S(1)} %bitcast.7), custom_call_target="tpu_custom_call" | custom-call | flops 8388608 | bytes 8388608 | tf_op jit(solution)/shard_map/maps/pallas_call | solution.py:461
  14.0 4.2 %collective-permute-done.recv_a.wind_a = bf16[72,2048]{1,0:T(8,128)(2,1)S(1)} collective-permute-done((bf16[72,2048]{1,0:T(8,128)(2,1)S(1)}, bf16[72,2048]{1,0:T(8,128)(2,1)S(1)}, u32[]{:S(2)}, u32[]{:S(2)}) %collective-permute-start) | collective-permute-done | bytes 294944 | tf_op jit(solution)/shard_map/ppermute | solution.py:458
  18.2 5.6 %stencil.2 = (bf16[8,16,2048]{2,1,0:T(8,128)(2,1)S(1)}, bf16[4,16,2048]{2,1,0:T(8,128)(2,1)S(1)}, bf16[2,16,2048]{2,1,0:T(8,128)(2,1)S(1)}, bf16[2,16,2048]{2,1,0:T(8,128)(2,1)S(1)}) custom-call(s32[3]{0:T(128)S(1)} %pad_add_fusion.pos, f32[8,16,2048]{2,1,0:T(8,128)S(1)} %get-tuple-element.41.turned, ...), custom_call_target="tpu_custom_call" | custom-call | flops 23592960 | bytes 23592960 | tf_op jit(solution)/shard_map/stencil/pallas_call | solution.py:481
  23.9 1.6 %collective-permute-start.2 = (bf16[2,16,2048]{2,1,0:T(8,128)(2,1)S(1)}, bf16[2,16,2048]{2,1,0:T(8,128)(2,1)S(1)}, u32[]{:S(2)}, u32[]{:S(2)}) collective-permute-start(bf16[2,16,2048]{2,1,0:T(8,128)(2,1)S(1)} %get-tuple-element.47), channel_id=1, source_target_pairs={{0,2},{1,3},{2,0},{3,1},{4,6},{5,7},{6,4},{7,5},{8,10},{9,11},{10,... | collective-permute-start | bytes 393224 | tf_op jit(solution)/shard_map/ppermute | solution.py:437
  25.8 5.6 %stencil.3 = (bf16[8,16,2048]{2,1,0:T(8,128)(2,1)S(1)}, bf16[4,16,2048]{2,1,0:T(8,128)(2,1)S(1)}, bf16[2,16,2048]{2,1,0:T(8,128)(2,1)S(1)}, bf16[2,16,2048]{2,1,0:T(8,128)(2,1)S(1)}) custom-call(s32[3]{0:T(128)S(1)} %pad_add_fusion.pos, f32[8,16,2048]{2,1,0:T(8,128)S(1)} %get-tuple-element.49.turned, bf16[64,2048]{1,0:T(8,128)(2,1)S(1)} %collective-permute-done.4.recv_a, ...), custom_call_target="tpu_custom_call" | custom-call | flops 23592960 | bytes 23592960 | tf_op jit(solution)/shard_map/stencil/pallas_call | solution.py:481
  31.4 0.8 %collective-permute-done.3.diag.diag_zero.diag_0 = bf16[2,16,2048]{2,1,0:T(8,128)(2,1)S(1)} collective-permute-done((bf16[2,16,2048]{2,1,0:T(8,128)(2,1)S(1)}, bf16[2,16,2048]{2,1,0:T(8,128)(2,1)S(1)}, u32[]{:S(2)}, u32[]{:S(2)}) %collective-permute-start.3) | collective-permute-done | bytes 131104 | tf_op jit(solution)/shard_map/ppermute | solution.py:437
  32.5 1.5 %collective-permute-start.7 = (bf16[2,16,2048]{2,1,0:T(8,128)(2,1)S(1)}, bf16[2,16,2048]{2,1,0:T(8,128)(2,1)S(1)}, u32[]{:S(2)}, u32[]{:S(2)}) collective-permute-start(bf16[2,16,2048]{2,1,0:T(8,128)(2,1)S(1)} %get-tuple-element.56), channel_id=1, source_target_pairs={{0,2},{1,3},{2,0},{3,1},{4,6},{5,7},{6,4},{7,5},{8,10},{9,11},{10,... | collective-permute-start | bytes 393224 | tf_op jit(solution)/shard_map/ppermute | solution.py:437
  34.0 1.1 %gram.2.part = f32[80,64]{1,0:T(8,128)S(1)} custom-call(s32[3]{0:T(128)S(1)} %pad_add_fusion.pos, bf16[8,16,2048]{2,1,0:T(8,128)(2,1)S(1)} %get-tuple-element.59.own.own_0, bf16[8,16,2048]{2,1,0:T(8,128)(2,1)S(1)} %collective-permute-done.9.mate.mate_0, bf16[2,16,2048]{2,1,0:T(8,128)(2,1)S(1)} %collective-permute-done.2.far.far_zero.far_0, ...), custom_call_target="tpu_custom_call" | custom-call | flops 6291456 | bytes 6291456 | tf_op jit(solution)/shard_map/gram/pallas_call | solution.py:509
  35.2 3.6 %collective-permute-done.7.far.far_1 = bf16[2,16,2048]{2,1,0:T(8,128)(2,1)S(1)} collective-permute-done((bf16[2,16,2048]{2,1,0:T(8,128)(2,1)S(1)}, bf16[2,16,2048]{2,1,0:T(8,128)(2,1)S(1)}, u32[]{:S(2)}, u32[]{:S(2)}) %collective-permute-start.7) | collective-permute-done | bytes 131104 | tf_op jit(solution)/shard_map/ppermute | solution.py:437
  38.8 1.4 %collective-permute-done.8.diag.diag_1 = bf16[2,16,2048]{2,1,0:T(8,128)(2,1)S(1)} collective-permute-done((bf16[2,16,2048]{2,1,0:T(8,128)(2,1)S(1)}, bf16[2,16,2048]{2,1,0:T(8,128)(2,1)S(1)}, u32[]{:S(2)}, u32[]{:S(2)}) %collective-permute-start.8) | collective-permute-done | bytes 131104 | tf_op jit(solution)/shard_map/ppermute | solution.py:437
  40.2 1.5 %collective-permute-start.12 = (bf16[4,16,2048]{2,1,0:T(8,128)(2,1)S(1)}, bf16[4,16,2048]{2,1,0:T(8,128)(2,1)S(1)}, u32[]{:S(2)}, u32[]{:S(2)}) collective-permute-start(bf16[4,16,2048]{2,1,0:T(8,128)(2,1)S(1)} %get-tuple-element.68), channel_id=1, source_target_pairs={{0,2},{1,3},{2,0},{3,1},{4,6},{5,7},{6,4},{7,5},{8,10},{9,11},{10,... | collective-permute-start | bytes 786440 | tf_op jit(solution)/shard_map/ppermute | solution.py:437
  41.7 1.1 %gram.3 = (f32[80,64]{1,0:T(8,128)S(1)}, bf16[8,16,2048]{2,1,0:T(8,128)(2,1)S(1)}) custom-call(s32[3]{0:T(128)S(1)} %pad_add_fusion.pos, bf16[8,16,2048]{2,1,0:T(8,128)(2,1)S(1)} %get-tuple-element.55.own.own_1, bf16[8,16,2048]{2,1,0:T(8,128)(2,1)S(1)} %collective-permute-done.6.mate.mate_1, bf16[2,16,2048]{2,1,0:T(8,128)(2,1)S(1)} %collective-permute-done.7.far.far_1, ...), custom_call_target="tpu_custom_call" | custom-call | flops 6291456 | bytes 6291456 | tf_op jit(solution)/shard_map/gram/pallas_call | solution.py:509
  42.8 0.3 collective-permute-start.10
  43.1 1.0 %collective-permute-done.10 = f32[80,64]{1,0:T(8,128)S(1)} collective-permute-done((f32[80,64]{1,0:T(8,128)S(1)}, f32[80,64]{1,0:T(8,128)S(1)}, u32[]{:S(2)}, u32[]{:S(2)}) %collective-permute-start.10) | collective-permute-done | bytes 20512 | tf_op jit(solution)/shard_map/ppermute | solution.py:541
  44.1 2.0 %collective-permute-start.11 = (f32[80,64]{1,0:T(8,128)S(1)}, f32[80,64]{1,0:T(8,128)S(1)}, u32[]{:S(2)}, u32[]{:S(2)}) collective-permute-start(f32[80,64]{1,0:T(8,128)S(1)} %add.9), channel_id=1, source_target_pairs={{0,4},{4,0},{8,12},{12,8},{1,5},{5,1},{9,13},{13,9},{2,6},{6,2},{1... | collective-permute-start | bytes 61448 | tf_op jit(solution)/shard_map/ppermute | solution.py:541
  46.2 2.0 %collective-permute-done.11 = f32[80,64]{1,0:T(8,128)S(1)} collective-permute-done((f32[80,64]{1,0:T(8,128)S(1)}, f32[80,64]{1,0:T(8,128)S(1)}, u32[]{:S(2)}, u32[]{:S(2)}) %collective-permute-start.11) | collective-permute-done | bytes 20512 | tf_op jit(solution)/shard_map/ppermute | solution.py:541
  48.1 0.8 %collective-permute-done.12.near_0 = bf16[4,16,2048]{2,1,0:T(8,128)(2,1)S(1)} collective-permute-done((bf16[4,16,2048]{2,1,0:T(8,128)(2,1)S(1)}, bf16[4,16,2048]{2,1,0:T(8,128)(2,1)S(1)}, u32[]{:S(2)}, u32[]{:S(2)}) %collective-permute-start.12) | collective-permute-done | bytes 262176 | tf_op jit(solution)/shard_map/ppermute | solution.py:437
  48.9 1.5 %collective-permute-start.13 = (f32[80,64]{1,0:T(8,128)S(1)}, f32[80,64]{1,0:T(8,128)S(1)}, u32[]{:S(2)}, u32[]{:S(2)}) collective-permute-start(f32[80,64]{1,0:T(8,128)S(1)} %add.10), channel_id=1, source_target_pairs={{0,2},{1,3},{2,0},{3,1},{4,6},{5,7},{6,4},{7,5},{8,10},{9,11},{10,... | collective-permute-start | bytes 61448 | tf_op jit(solution)/shard_map/ppermute | solution.py:541
  50.4 2.5 %collective-permute-done.13 = f32[80,64]{1,0:T(8,128)S(1)} collective-permute-done((f32[80,64]{1,0:T(8,128)S(1)}, f32[80,64]{1,0:T(8,128)S(1)}, u32[]{:S(2)}, u32[]{:S(2)}) %collective-permute-start.13) | collective-permute-done | bytes 20512 | tf_op jit(solution)/shard_map/ppermute | solution.py:541
  52.9 1.5 %collective-permute-start.16 = (bf16[4,16,2048]{2,1,0:T(8,128)(2,1)S(1)}, bf16[4,16,2048]{2,1,0:T(8,128)(2,1)S(1)}, u32[]{:S(2)}, u32[]{:S(2)}) collective-permute-start(bf16[4,16,2048]{2,1,0:T(8,128)(2,1)S(1)} %get-tuple-element.75), channel_id=1, source_target_pairs={{0,2},{1,3},{2,0},{3,1},{4,6},{5,7},{6,4},{7,5},{8,10},{9,11},{10,... | collective-permute-start | bytes 786440 | tf_op jit(solution)/shard_map/ppermute | solution.py:437
  54.4 2.0 %collective-permute-start.14 = (f32[80,64]{1,0:T(8,128)S(1)}, f32[80,64]{1,0:T(8,128)S(1)}, u32[]{:S(2)}, u32[]{:S(2)}) collective-permute-start(f32[80,64]{1,0:T(8,128)S(1)} %add.11.one), channel_id=1, source_target_pairs={{0,8},{4,12},{8,0},{12,4},{1,9},{5,13},{9,1},{13,5},{2,10},{6,14},... | collective-permute-start | bytes 61448 | tf_op jit(solution)/shard_map/ppermute | solution.py:541
  56.4 3.0 %collective-permute-done.14.two = f32[80,64]{1,0:T(8,128)S(1)} collective-permute-done((f32[80,64]{1,0:T(8,128)S(1)}, f32[80,64]{1,0:T(8,128)S(1)}, u32[]{:S(2)}, u32[]{:S(2)}) %collective-permute-start.14) | collective-permute-done | bytes 20512 | tf_op jit(solution)/shard_map/ppermute | solution.py:541
  59.4 0.3 collective-permute-done.16.near_1
  59.9 2.8 %weights.1 = bf16[32,64]{1,0:T(8,128)(2,1)S(1)} custom-call(s32[3]{0:T(128)S(1)} %pad_add_fusion.pos, f32[80,64]{1,0:T(8,128)S(1)} %add.11.one, f32[80,64]{1,0:T(8,128)S(1)} %collective-permute-done.14.two), custom_call_target="tpu_custom_call" | custom-call | flops 13107200 | bytes 13107200 | tf_op jit(solution)/shard_map/weights/pallas_call | solution.py:547
  62.7 2.8 %final.1 = f32[16,2,8,2048]{3,2,1,0:T(8,128)} custom-call(s32[3]{0:T(128)S(1)} %pad_add_fusion.pos, bf16[32,64]{1,0:T(8,128)(2,1)S(1)} %weights.1, bf16[8,16,2048]{2,1,0:T(8,128)(2,1)S(1)} %get-tuple-element.59.own.own_0, bf16[8,16,2048]{2,1,0:T(8,128)(2,1)S(1)} %get-tuple-element.55.own.own_1, bf16[8,16,2048]{2,1,0:T(8,128)(2,1)S(1)} %collective-permute-done.9.mate.mate_0, ...), custom_call_target="tpu_custom_call" | custom-call | flops 13107200 | bytes 13107200 | tf_op jit(solution)/shard_map/final/pallas_call | solution.py:562
  (31 shorter events, 1.2 us)
Async XLA Ops:
  0.1 1.6 %copy-start = (f32[16,2,8,2048]{3,2,1,0:T(8,128)S(1)}, f32[16,2,8,2048]{3,2,1,0:T(8,128)}, u32[]{:S(2)}) copy-start(f32[16,2,8,2048]{3,2,1,0:T(8,128)} %prior.3) | copy-start | bytes 6291460
  1.7 0.9 %copy-start.1 = (f32[2,2,8,2048]{3,2,1,0:T(8,128)S(1)}, f32[2,2,8,2048]{3,2,1,0:T(8,128)}, u32[]{:S(2)}) copy-start(f32[2,2,8,2048]{3,2,1,0:T(8,128)} %wind.7) | copy-start | bytes 786436
  2.6 10.1 %copy-start.3 = (s32[2048]{0:T(1024)S(1)}, s32[2048]{0:T(1024)}, u32[]{:S(2)}) copy-start(s32[2048]{0:T(1024)} %param.8) | copy-start | bytes 24580
  2.6 10.1 %copy-start.4 = (f32[2048]{0:T(1024)S(1)}, f32[2048]{0:T(1024)}, u32[]{:S(2)}) copy-start(f32[2048]{0:T(1024)} %param.11) | copy-start | bytes 24580
  2.6 10.1 %copy-start.5 = (f32[2048]{0:T(1024)S(1)}, f32[2048]{0:T(1024)}, u32[]{:S(2)}) copy-start(f32[2048]{0:T(1024)} %param.10) | copy-start | bytes 24580
  2.6 15.6 %copy-start.2 = (f32[2,2,8,2048]{3,2,1,0:T(8,128)S(1)}, f32[2,2,8,2048]{3,2,1,0:T(8,128)}, u32[]{:S(2)}) copy-start(f32[2,2,8,2048]{3,2,1,0:T(8,128)} %wind.7) | copy-start | bytes 786436
  3.8 10.3 %collective-permute-start.1 = (bf16[72,2048]{1,0:T(8,128)(2,1)S(1)}, bf16[72,2048]{1,0:T(8,128)(2,1)S(1)}, u32[]{:S(2)}, u32[]{:S(2)}) collective-permute-start(bf16[72,2048]{1,0:T(8,128)(2,1)S(1)} %get-tuple-element.43), channel_id=1, source_target_pairs={{4,8},{8,4},{5,9},{9,5},{6,10},{10,6},{7,11},{11,7},{20,24},{24,20... | collective-permute-start | bytes 884744 | tf_op jit(solution)/shard_map/ppermute | solution.py:458
  4.4 13.8 %collective-permute-start = (bf16[72,2048]{1,0:T(8,128)(2,1)S(1)}, bf16[72,2048]{1,0:T(8,128)(2,1)S(1)}, u32[]{:S(2)}, u32[]{:S(2)}) collective-permute-start(bf16[72,2048]{1,0:T(8,128)(2,1)S(1)} %get-tuple-element.42), channel_id=1, source_target_pairs={{0,4},{4,0},{8,12},{12,8},{1,5},{5,1},{9,13},{13,9},{2,6},{6,2},{1... | collective-permute-start | bytes 884744 | tf_op jit(solution)/shard_map/ppermute | solution.py:458
  11.3 14.5 %collective-permute-start.4 = (bf16[64,2048]{1,0:T(8,128)(2,1)S(1)}, bf16[64,2048]{1,0:T(8,128)(2,1)S(1)}, u32[]{:S(2)}, u32[]{:S(2)}) collective-permute-start(bf16[64,2048]{1,0:T(8,128)(2,1)S(1)} %get-tuple-element.50), channel_id=1, source_target_pairs={{0,4},{4,0},{8,12},{12,8},{1,5},{5,1},{9,13},{13,9},{2,6},{6,2},{1... | collective-permute-start | bytes 786440 | tf_op jit(solution)/shard_map/ppermute | solution.py:458
  11.3 14.4 %collective-permute-start.5 = (bf16[64,2048]{1,0:T(8,128)(2,1)S(1)}, bf16[64,2048]{1,0:T(8,128)(2,1)S(1)}, u32[]{:S(2)}, u32[]{:S(2)}) collective-permute-start(bf16[64,2048]{1,0:T(8,128)(2,1)S(1)} %get-tuple-element.51), channel_id=1, source_target_pairs={{4,8},{8,4},{5,9},{9,5},{6,10},{10,6},{7,11},{11,7},{20,24},{24,20... | collective-permute-start | bytes 786440 | tf_op jit(solution)/shard_map/ppermute | solution.py:458
  23.8 10.2 %collective-permute-start.9 = (bf16[8,16,2048]{2,1,0:T(8,128)(2,1)S(1)}, bf16[8,16,2048]{2,1,0:T(8,128)(2,1)S(1)}, u32[]{:S(2)}, u32[]{:S(2)}) collective-permute-start(bf16[8,16,2048]{2,1,0:T(8,128)(2,1)S(1)} %get-tuple-element.59.own.own_0), channel_id=1, source_target_pairs={{0,1},{1,0},{2,3},{3,2},{4,5},{5,4},{6,7},{7,6},{8,9},{9,8},{10,11... | collective-permute-start | bytes 1572872 | tf_op jit(solution)/shard_map/ppermute | solution.py:437
  23.9 7.5 %collective-permute-start.2 = (bf16[2,16,2048]{2,1,0:T(8,128)(2,1)S(1)}, bf16[2,16,2048]{2,1,0:T(8,128)(2,1)S(1)}, u32[]{:S(2)}, u32[]{:S(2)}) collective-permute-start(bf16[2,16,2048]{2,1,0:T(8,128)(2,1)S(1)} %get-tuple-element.47), channel_id=1, source_target_pairs={{0,2},{1,3},{2,0},{3,1},{4,6},{5,7},{6,4},{7,5},{8,10},{9,11},{10,... | collective-permute-start | bytes 393224 | tf_op jit(solution)/shard_map/ppermute | solution.py:437
  25.5 6.7 %collective-permute-start.3 = (bf16[2,16,2048]{2,1,0:T(8,128)(2,1)S(1)}, bf16[2,16,2048]{2,1,0:T(8,128)(2,1)S(1)}, u32[]{:S(2)}, u32[]{:S(2)}) collective-permute-start(bf16[2,16,2048]{2,1,0:T(8,128)(2,1)S(1)} %get-tuple-element.48), channel_id=1, source_target_pairs={{0,3},{1,2},{2,1},{3,0},{4,7},{5,6},{6,5},{7,4},{8,11},{9,10},{10,... | collective-permute-start | bytes 393224 | tf_op jit(solution)/shard_map/ppermute | solution.py:437
  32.2 9.5 %collective-permute-start.6 = (bf16[8,16,2048]{2,1,0:T(8,128)(2,1)S(1)}, bf16[8,16,2048]{2,1,0:T(8,128)(2,1)S(1)}, u32[]{:S(2)}, u32[]{:S(2)}) collective-permute-start(bf16[8,16,2048]{2,1,0:T(8,128)(2,1)S(1)} %get-tuple-element.55.own.own_1), channel_id=1, source_target_pairs={{0,1},{1,0},{2,3},{3,2},{4,5},{5,4},{6,7},{7,6},{8,9},{9,8},{10,11... | collective-permute-start | bytes 1572872 | tf_op jit(solution)/shard_map/ppermute | solution.py:437
  32.5 6.3 %collective-permute-start.7 = (bf16[2,16,2048]{2,1,0:T(8,128)(2,1)S(1)}, bf16[2,16,2048]{2,1,0:T(8,128)(2,1)S(1)}, u32[]{:S(2)}, u32[]{:S(2)}) collective-permute-start(bf16[2,16,2048]{2,1,0:T(8,128)(2,1)S(1)} %get-tuple-element.56), channel_id=1, source_target_pairs={{0,2},{1,3},{2,0},{3,1},{4,6},{5,7},{6,4},{7,5},{8,10},{9,11},{10,... | collective-permute-start | bytes 393224 | tf_op jit(solution)/shard_map/ppermute | solution.py:437
  33.9 6.3 %collective-permute-start.8 = (bf16[2,16,2048]{2,1,0:T(8,128)(2,1)S(1)}, bf16[2,16,2048]{2,1,0:T(8,128)(2,1)S(1)}, u32[]{:S(2)}, u32[]{:S(2)}) collective-permute-start(bf16[2,16,2048]{2,1,0:T(8,128)(2,1)S(1)} %get-tuple-element.57), channel_id=1, source_target_pairs={{0,3},{1,2},{2,1},{3,0},{4,7},{5,6},{6,5},{7,4},{8,11},{9,10},{10,... | collective-permute-start | bytes 393224 | tf_op jit(solution)/shard_map/ppermute | solution.py:437
  40.2 8.7 %collective-permute-start.12 = (bf16[4,16,2048]{2,1,0:T(8,128)(2,1)S(1)}, bf16[4,16,2048]{2,1,0:T(8,128)(2,1)S(1)}, u32[]{:S(2)}, u32[]{:S(2)}) collective-permute-start(bf16[4,16,2048]{2,1,0:T(8,128)(2,1)S(1)} %get-tuple-element.68), channel_id=1, source_target_pairs={{0,2},{1,3},{2,0},{3,1},{4,6},{5,7},{6,4},{7,5},{8,10},{9,11},{10,... | collective-permute-start | bytes 786440 | tf_op jit(solution)/shard_map/ppermute | solution.py:437
  42.8 1.3 %collective-permute-start.10 = (f32[80,64]{1,0:T(8,128)S(1)}, f32[80,64]{1,0:T(8,128)S(1)}, u32[]{:S(2)}, u32[]{:S(2)}) collective-permute-start(f32[80,64]{1,0:T(8,128)S(1)} %get-tuple-element.67), channel_id=1, source_target_pairs={{0,1},{1,0},{2,3},{3,2},{4,5},{5,4},{6,7},{7,6},{8,9},{9,8},{10,11... | collective-permute-start | bytes 61448 | tf_op jit(solution)/shard_map/ppermute | solution.py:541
  44.1 4.0 %collective-permute-start.11 = (f32[80,64]{1,0:T(8,128)S(1)}, f32[80,64]{1,0:T(8,128)S(1)}, u32[]{:S(2)}, u32[]{:S(2)}) collective-permute-start(f32[80,64]{1,0:T(8,128)S(1)} %add.9), channel_id=1, source_target_pairs={{0,4},{4,0},{8,12},{12,8},{1,5},{5,1},{9,13},{13,9},{2,6},{6,2},{1... | collective-permute-start | bytes 61448 | tf_op jit(solution)/shard_map/ppermute | solution.py:541
  48.9 4.0 %collective-permute-start.13 = (f32[80,64]{1,0:T(8,128)S(1)}, f32[80,64]{1,0:T(8,128)S(1)}, u32[]{:S(2)}, u32[]{:S(2)}) collective-permute-start(f32[80,64]{1,0:T(8,128)S(1)} %add.10), channel_id=1, source_target_pairs={{0,2},{1,3},{2,0},{3,1},{4,6},{5,7},{6,4},{7,5},{8,10},{9,11},{10,... | collective-permute-start | bytes 61448 | tf_op jit(solution)/shard_map/ppermute | solution.py:541
  52.9 6.8 %collective-permute-start.16 = (bf16[4,16,2048]{2,1,0:T(8,128)(2,1)S(1)}, bf16[4,16,2048]{2,1,0:T(8,128)(2,1)S(1)}, u32[]{:S(2)}, u32[]{:S(2)}) collective-permute-start(bf16[4,16,2048]{2,1,0:T(8,128)(2,1)S(1)} %get-tuple-element.75), channel_id=1, source_target_pairs={{0,2},{1,3},{2,0},{3,1},{4,6},{5,7},{6,4},{7,5},{8,10},{9,11},{10,... | collective-permute-start | bytes 786440 | tf_op jit(solution)/shard_map/ppermute | solution.py:437
  54.4 8.3 %collective-permute-start.15 = (bf16[8,16,2048]{2,1,0:T(8,128)(2,1)S(1)}, bf16[8,16,2048]{2,1,0:T(8,128)(2,1)S(1)}, u32[]{:S(2)}, u32[]{:S(2)}) collective-permute-start(bf16[8,16,2048]{2,1,0:T(8,128)(2,1)S(1)} %get-tuple-element.73), channel_id=1, source_target_pairs={{0,1},{1,0},{2,3},{3,2},{4,5},{5,4},{6,7},{7,6},{8,9},{9,8},{10,11... | collective-permute-start | bytes 1572872 | tf_op jit(solution)/shard_map/ppermute | solution.py:437
  54.4 5.0 %collective-permute-start.14 = (f32[80,64]{1,0:T(8,128)S(1)}, f32[80,64]{1,0:T(8,128)S(1)}, u32[]{:S(2)}, u32[]{:S(2)}) collective-permute-start(f32[80,64]{1,0:T(8,128)S(1)} %add.11.one), channel_id=1, source_target_pairs={{0,8},{4,12},{8,0},{12,4},{1,9},{5,13},{9,1},{13,5},{2,10},{6,14},... | collective-permute-start | bytes 61448 | tf_op jit(solution)/shard_map/ppermute | solution.py:541
  59.4 3.3 %collective-permute-start.17 = (bf16[4,16,2048]{2,1,0:T(8,128)(2,1)S(1)}, bf16[4,16,2048]{2,1,0:T(8,128)(2,1)S(1)}, u32[]{:S(2)}, u32[]{:S(2)}) collective-permute-start(bf16[4,16,2048]{2,1,0:T(8,128)(2,1)S(1)} %collective-permute-done.12.near_0), channel_id=1, source_target_pairs={{0,1},{1,0},{2,3},{3,2},{4,5},{5,4},{6,7},{7,6},{8,9},{9,8},{10,11... | collective-permute-start | bytes 786440 | tf_op jit(solution)/shard_map/ppermute | solution.py:437
  59.7 3.0 %collective-permute-start.18 = (bf16[4,16,2048]{2,1,0:T(8,128)(2,1)S(1)}, bf16[4,16,2048]{2,1,0:T(8,128)(2,1)S(1)}, u32[]{:S(2)}, u32[]{:S(2)}) collective-permute-start(bf16[4,16,2048]{2,1,0:T(8,128)(2,1)S(1)} %collective-permute-done.16.near_1), channel_id=1, source_target_pairs={{0,1},{1,0},{2,3},{3,2},{4,5},{5,4},{6,7},{7,6},{8,9},{9,8},{10,11... | collective-permute-start | bytes 786440 | tf_op jit(solution)/shard_map/ppermute | solution.py:437

commit v4 on v3

--- a/solution.py
+++ b/solution.py
@@ -160,6 +160,14 @@
     return pl.CostEstimate(flops=touched, bytes_accessed=touched, transcendentals=0)
 
 
+def blank_edges(rows):
+    width = rows.shape[2]
+    for r in (0, 1, 10, 11):
+        rows[r] = jnp.zeros((16, width), F32)
+    for r in range(2, 10):
+        rows[r, :, width - PAD :] = jnp.zeros((16, PAD), F32)
+
+
 def pack_kernel(field, pos, prior, wind, turned, pay_a, pay_b, state, edge, sems):
     load = pltpu.make_async_copy(prior.at[:, field], state, sems.at[0])
     load.start()
@@ -180,10 +188,12 @@
         pay_a[64:72, :] = jnp.where(even, last, first).astype(BF)
         pay_b[64:72, :] = jnp.where(even, first, last).astype(BF)
     load.wait()
-    turned[...] = jnp.swapaxes(state[...], 0, 1)
+    cols = state.shape[2]
+    turned[2:10, :, :cols] = jnp.swapaxes(state[...], 0, 1)
     for r in range(4):
-        pay_a[r * 16 : r * 16 + 16, :] = turned[start_a + r].astype(BF)
-        pay_b[r * 16 : r * 16 + 16, :] = turned[start_b + r].astype(BF)
+        pay_a[r * 16 : r * 16 + 16, :] = turned[2 + start_a + r, :, :cols].astype(BF)
+        pay_b[r * 16 : r * 16 + 16, :] = turned[2 + start_b + r, :, :cols].astype(BF)
+    blank_edges(turned)
 
 
 def maps_kernel(tiles, pos, index, count, weight, value, root_map, value_map):
@@ -215,94 +225,143 @@
 
 def stencil_row(rows, wind_r, wind_c, nu):
     south_two, south_one, center, north_one, north_two = rows
-    width = center.shape[1]
-    east_one = pltpu.roll(center, width - 1, 1)
-    west_one = pltpu.roll(center, 1, 1)
-    east_two = pltpu.roll(center, width - 2, 1)
-    west_two = pltpu.roll(center, 2, 1)
-    grad_r = 8.0 * (north_one - south_one) - (north_two - south_two)
-    grad_c = 8.0 * (east_one - west_one) - (east_two - west_two)
-    ring = (north_one + south_one) + (east_one + west_one)
-    out = (1.0 - 4.0 * nu) * center + nu * ring
-    cut = width - PAD
-    return out[:, :cut] - wind_r * grad_r[:, :cut] - wind_c * grad_c[:, :cut]
-
-
-def stencil_kernel(
-    nu, pos, turned, recv_a, recv_b, wind_a, wind_b, wind, out_all, out_near, out_far, out_diag,
-    ext, mid, wide, wide2
+    width = [v for v in rows if v is not None][0].shape[1]
+    keep = width - PAD
+
+    def less(a, b):
+        if a is None:
+            return None if b is None else -b
+        return a if b is None else a - b
+
+    def more(a, b):
+        if a is None or b is None:
+            return b if a is None else a
+        return a + b
+
+    rows = [None if v is None else v[:, :keep] for v in rows]
+    one = less(rows[3], rows[1])
+    grad_r = less(None if one is None else 8.0 * one, less(rows[4], rows[0]))
+    ring = more(rows[3], rows[1])
+    out = -(wind_r * grad_r)
+    if center is not None:
+        east_one = pltpu.roll(center, width - 1, 1)
+        west_one = pltpu.roll(center, 1, 1)
+        east_two = pltpu.roll(center, width - 2, 1)
+        west_two = pltpu.roll(center, 2, 1)
+        grad_c = 8.0 * (east_one - west_one) - (east_two - west_two)
+        ring = more(ring, (east_one + west_one)[:, :keep])
+        out = (1.0 - 4.0 * nu) * rows[2] + out - wind_c * grad_c[:, :keep]
+    return out if ring is None else out + nu * ring
+
+
+TWELFTH = 1.0 / 12.0
+
+
+def pre_kernel(nu, turned, wind, out, mid, wide):
+    cols = out.shape[2]
+    blank_edges(mid)
+    for step in range(2):
+        for c in range(2):
+            for r in range(8):
+                wide[step, c, r] = jnp.broadcast_to(wind[step, c, r : r + 1] * TWELFTH, (8, cols))
+
+    def first_step(r, carry):
+        for g in range(2):
+            span = pl.ds(g * 8, 8)
+            rows = [turned[r + i, span, :] for i in range(5)]
+            mid[r + 2, span, :cols] = stencil_row(rows, wide[0, 0, r], wide[0, 1, r], nu)
+        return carry
+
+    lax.fori_loop(0, 8, first_step, 0)
+
+    def second_step(r, carry):
+        for g in range(2):
+            span = pl.ds(g * 8, 8)
+            rows = [mid[r + i, span, :] for i in range(5)]
+            out[r, span, :] = stencil_row(rows, wide[1, 0, r], wide[1, 1, r], nu)
+        return carry
+
+    lax.fori_loop(0, 8, second_step, 0)
+
+
+def post_kernel(
+    nu, pos, turned, begun, recv_a, recv_b, wind_a, wind_b, wind, out_all, out_near, out_far,
+    halo, delta
 ):
-    cols = turned.shape[2]
+    cols = begun.shape[2]
     even = (pos[0] % 2) == 0
-    start_a = jnp.where(even, 12, 0)
-    start_b = 12 - start_a
-    zeros = jnp.zeros((16, PAD), F32)
-    for r in range(16):
-        ext[r, :, cols:] = zeros
-    for r in range(12):
-        mid[r, :, cols:] = zeros
+    start_a = jnp.where(even, 4, 0)
+    start_b = 4 - start_a
+    blank = jnp.zeros((16, PAD), F32)
     for r in range(8):
-        ext[r + 4, :, :cols] = turned[r]
+        halo[r, :, cols:] = blank
+        delta[r, :, cols:] = blank
     for r in range(4):
-        ext[start_a + r, :, :cols] = recv_a[r * 16 : r * 16 + 16, :].astype(F32)
-        ext[start_b + r, :, :cols] = recv_b[r * 16 : r * 16 + 16, :].astype(F32)
+        halo[start_a + r, :, :cols] = recv_a[r * 16 : r * 16 + 16, :].astype(F32)
+        halo[start_b + r, :, :cols] = recv_b[r * 16 : r * 16 + 16, :].astype(F32)
     got_a = wind_a[64:72, :].astype(F32)
     got_a = got_a[0:4] + got_a[4:8]
     got_b = wind_b[64:72, :].astype(F32)
     got_b = got_b[0:4] + got_b[4:8]
-    before = jnp.where(even, got_b, got_a)
-    after = jnp.where(even, got_a, got_b)
-    twelfth = 1.0 / 12.0
-    for c in range(2):
-        for r in range(12):
-            if r < 2:
-                row = before[2 * c + r : 2 * c + r + 1]
-            elif r < 10:
-                row = wind[0, c, r - 2 : r - 1]
-            else:
-                row = after[2 * c + r - 10 : 2 * c + r - 9]
-            wide[c, r] = jnp.broadcast_to(row * twelfth, (8, cols))
-        for r in range(8):
-            row = wind[1, c, r : r + 1]
-            wide2[c, r] = jnp.broadcast_to(row * twelfth, (8, cols))
-
-    def first_step(r, carry):
-        for g in range(2):
-            span = pl.ds(g * 8, 8)
-            rows = [ext[r + i, span, :] for i in range(5)]
-            mid[r, span, :cols] = stencil_row(rows, wide[0, r], wide[1, r], nu)
-        return carry
-
-    lax.fori_loop(0, 12, first_step, 0)
-
-    @pl.when(pos[0] == 0)
-    def _():
-        mid[0:2] = jnp.zeros((2,) + mid.shape[1:], F32)
-
-    @pl.when(pos[0] == pos[1] - 1)
-    def _():
-        mid[10:12] = jnp.zeros((2,) + mid.shape[1:], F32)
-
-    def second_step(r, carry):
+    top = jnp.where(pos[0] == 0, 0.0, 1.0)
+    bottom = jnp.where(pos[0] == pos[1] - 1, 0.0, 1.0)
+    before = jnp.where(even, got_b, got_a) * TWELFTH
+    after = jnp.where(even, got_a, got_b) * TWELFTH
+
+    def broad(row):
+        return jnp.broadcast_to(row, (8, cols))
+
+    def own_wind(step, c, r):
+        return broad(wind[step, c, r : r + 1] * TWELFTH)
+
+    for g in range(2):
+        span = slice(g * 8, g * 8 + 8)
+        h = lambda i: halo[i, span, :]
+        x = lambda r: turned[2 + r, span, :]
+        for i in range(2):
+            rows = [h(0), h(1), h(2), h(3), x(0)] if i == 0 else [h(1), h(2), h(3), x(0), x(1)]
+            value = stencil_row(rows, broad(before[i : i + 1]), broad(before[2 + i : 3 + i]), nu)
+            delta[i, span, :cols] = value * top
+            rows = [x(6), x(7), h(4), h(5), h(6)] if i == 0 else [x(7), h(4), h(5), h(6), h(7)]
+            value = stencil_row(rows, broad(after[i : i + 1]), broad(after[2 + i : 3 + i]), nu)
+            delta[6 + i, span, :cols] = value * bottom
+        near = (
+            (2, 0, [h(2), h(3), None, None, None]),
+            (3, 1, [h(3), None, None, None, None]),
+            (4, 6, [None, None, None, None, h(4)]),
+            (5, 7, [None, None, None, h(4), h(5)]),
+        )
+        for at, r, rows in near:
+            delta[at, span, :cols] = stencil_row(rows, own_wind(0, 0, r), None, nu)
+
+    for r in range(8):
         both = []
         for g in range(2):
-            span = pl.ds(g * 8, 8)
-            rows = [mid[r + i, span, :] for i in range(5)]
-            both.append(stencil_row(rows, wide2[0, r], wide2[1, r], nu))
+            span = slice(g * 8, g * 8 + 8)
+            rows = []
+            for i in range(r - 2, r + 3):
+                if i <= 1 and r <= 3:
+                    rows.append(delta[i + 2, span, :])
+                elif i >= 6 and r >= 4:
+                    rows.append(delta[i - 2, span, :])
+                else:
+                    rows.append(None)
+            center = rows[2] is not None
+            value = stencil_row(
+                rows, own_wind(1, 0, r), own_wind(1, 1, r) if center else None, nu
+            )
+            both.append(begun[r, span, :] + value)
         out_all[r] = jnp.concatenate(both, 0).astype(BF)
-        return carry
-
-    lax.fori_loop(0, 8, second_step, 0)
-    for r in range(2):
-        out_far[r] = out_all[2 * jnp.bitwise_xor(pos[2], 2) + r]
-        out_diag[r] = out_all[2 * jnp.bitwise_xor(pos[2], 3) + r]
-        out_near[r] = out_all[2 * pos[2] + r]
-        out_near[2 + r] = out_all[2 * jnp.bitwise_xor(pos[2], 1) + r]
+    base = (pos[2] // 2) * 4
+    for r in range(4):
+        out_near[r] = out_all[base + r]
+        out_far[r] = out_all[4 - base + r]
 
 
 def gram_sum(field, pos, own, mate, far, diag, root_map, value_map, spread):
     tiles = own.shape[2] // 128
     spread[4] = jnp.zeros(spread.shape[1:], BF)
+    half = 2 * (pos[2] % 2)
     for r in range(2):
         row = 2 * pos[2] + r
         for t in range(tiles):
@@ -312,8 +371,8 @@
             parts = [
                 own[row, :, cut].astype(F32),
                 mate[row, :, cut].astype(F32),
-                far[r, :, cut].astype(F32),
-                diag[r, :, cut].astype(F32),
+                far[half + r, :, cut].astype(F32),
+                diag[half + r, :, cut].astype(F32),
             ]
             total = (parts[0] + parts[1]) + (parts[2] + parts[3])
             mean = jnp.sum(total, 0, keepdims=True) * (1.0 / REPLICA_COUNT)
@@ -336,14 +395,8 @@
     out[...] = gram_sum(0, pos, own, mate, far, diag, root_map, value_map, spread)
 
 
-def gram_second(
-    pos, own, mate, far, diag, root_map, value_map, part, far_zero, diag_zero, out, pass_on, spread
-):
+def gram_second(pos, own, mate, far, diag, root_map, value_map, part, out, spread):
     out[...] = part[...] + gram_sum(1, pos, own, mate, far, diag, root_map, value_map, spread)
-    pass_on[0:2] = far_zero[...]
-    pass_on[2:4] = diag_zero[...]
-    pass_on[4:6] = far[...]
-    pass_on[6:8] = diag[...]
 
 
 def exact(a, b):
@@ -388,7 +441,7 @@
 
 
 def final_kernel(
-    pos, weights, own_0, own_1, mate_0, mate_1, far_0, far_1, diag_0, diag_1, passed,
+    pos, weights, own_0, own_1, mate_0, mate_1, far_0, far_1, diag_0, diag_1,
     near_0, near_1, mate_near_0, mate_near_1, out, keep, ready, sems
 ):
     m = weights[...]
@@ -396,24 +449,16 @@
         (own_0, mate_0, far_0, diag_0, near_0, mate_near_0),
         (own_1, mate_1, far_1, diag_1, near_1, mate_near_1),
     )
+    base = (pos[2] // 2) * 4
     copies = []
     for f in range(2):
         own, mate, far, diag, near, mate_near = fields[f]
-        for t in range(4):
-            quarter = jnp.bitwise_xor(pos[2], t)
-            for r in range(2):
-                row = 2 * quarter + r
-                if t == 0:
-                    parts = [far[r], diag[r]]
-                elif t == 1:
-                    parts = [passed[4 * f + 2 + r], passed[4 * f + r]]
-                elif t == 2:
-                    parts = [near[r], mate_near[2 + r]]
-                else:
-                    parts = [near[2 + r], mate_near[r]]
-                state = jnp.concatenate([own[row], mate[row]] + parts, 0)
-                both = jnp.dot(m, state, preferred_element_type=F32)
-                keep[row] = both[0:16] + both[16:32]
+        for r in range(8):
+            row = base + r if r < 4 else 4 - base + r - 4
+            other = [far[r], diag[r]] if r < 4 else [near[r - 4], mate_near[r - 4]]
+            state = jnp.concatenate([own[row], mate[row]] + other, 0)
+            both = jnp.dot(m, state, preferred_element_type=F32)
+            keep[row] = both[0:16] + both[16:32]
         ready[f] = jnp.swapaxes(keep[...], 0, 1)
         copies.append(pltpu.make_async_copy(ready.at[f], out.at[:, f], sems.at[f]))
         copies[f].start()
@@ -436,6 +481,8 @@
     def swap(value, bits):
         return lax.ppermute(value, "mem", [(i, i ^ bits) for i in range(4)])
 
+    prior_here = pltpu.with_memory_space_constraint(prior_replicas, pltpu.MemorySpace.HBM)
+    wind_here = pltpu.with_memory_space_constraint(wind_field, pltpu.MemorySpace.HBM)
     turned = []
     recv = []
     for f in range(2):
@@ -446,14 +493,14 @@
             cost_estimate=cost(40 * 16 * cols * 4),
             in_specs=[smem(), hbm(), hbm()],
             out_specs=[vmem()] * 3,
-            out_shape=[shape((8, 16, cols), F32)] + [shape((height, cols), BF)] * 2,
+            out_shape=[shape((12, 16, cols + PAD), F32)] + [shape((height, cols), BF)] * 2,
             scratch_shapes=[
                 pltpu.VMEM((16, 8, cols), F32),
                 pltpu.VMEM((2, 8, cols), F32),
                 pltpu.SemaphoreType.DMA((2,)),
             ],
             compiler_params=params(),
-        )(pos, prior_replicas, wind_field)
+        )(pos, prior_here, wind_here)
         turned.append(rows)
         recv.append([lax.ppermute(pay_a, "space", pairs_a), lax.ppermute(pay_b, "space", pairs_b)])
 
@@ -473,76 +520,85 @@
         obs_weight.reshape(1, slots),
         obs_value.reshape(1, slots),
     )
-    recv[0][1], root_map, value_map = lax.optimization_barrier((recv[0][1], root_map, value_map))
+    begun = [
+        pl.pallas_call(
+            functools.partial(pre_kernel, DIFFUSION[f]),
+            name="pre",
+            cost_estimate=cost(150 * 16 * cols * 4),
+            in_specs=[vmem()] * 2,
+            out_specs=vmem(),
+            out_shape=shape((8, 16, cols), F32),
+            scratch_shapes=[
+                pltpu.VMEM((12, 16, cols + PAD), F32),
+                pltpu.VMEM((2, 2, 8, 8, cols), F32),
+            ],
+            compiler_params=params(),
+        )(turned[f], wind_field)
+        for f in range(2)
+    ]
 
     state = []
     got = []
     for f in range(2):
-        every, near, far, diag = pl.pallas_call(
-            functools.partial(stencil_kernel, DIFFUSION[f]),
-            name="stencil",
-            cost_estimate=cost(180 * 16 * cols * 4),
-            in_specs=[smem()] + [vmem()] * 6,
-            out_specs=[vmem()] * 4,
+        every, near, far = pl.pallas_call(
+            functools.partial(post_kernel, DIFFUSION[f]),
+            name="post",
+            cost_estimate=cost(100 * 16 * cols * 4),
+            in_specs=[smem()] + [vmem()] * 7,
+            out_specs=[vmem()] * 3,
             out_shape=[
                 shape((8, 16, cols), BF),
                 shape((4, 16, cols), BF),
-                shape((2, 16, cols), BF),
-                shape((2, 16, cols), BF),
+                shape((4, 16, cols), BF),
             ],
             scratch_shapes=[
-                pltpu.VMEM((16, 16, cols + PAD), F32),
-                pltpu.VMEM((12, 16, cols + PAD), F32),
-                pltpu.VMEM((2, 12, 8, cols), F32),
-                pltpu.VMEM((2, 8, 8, cols), F32),
+                pltpu.VMEM((8, 16, cols + PAD), F32),
+                pltpu.VMEM((8, 16, cols + PAD), F32),
             ],
             compiler_params=params(),
-        )(pos, turned[f], recv[f][0], recv[f][1], recv[0][0], recv[0][1], wind_field)
+        )(pos, turned[f], begun[f], recv[f][0], recv[f][1], recv[0][0], recv[0][1], wind_field)
         if f == 1:
-            got[0][0], got[0][1], every, far, diag = lax.optimization_barrier(
-                (got[0][0], got[0][1], every, far, diag)
-            )
+            got[0][0], every, far = lax.optimization_barrier((got[0][0], every, far))
         state.append((every, near))
-        got.append([swap(far, 2), swap(diag, 3), swap(every, 1)])
-
-    def gram(kernel, f, extra, more):
+        got.append([swap(far, 2), swap(every, 1)])
+    got[0].append(swap(got[0][0], 1))
+
+    def gram(kernel, f, extra):
         return pl.pallas_call(
             kernel,
             name="gram",
             cost_estimate=cost(24 * 64 * cols * 2),
             in_specs=[smem()] + [vmem()] * (6 + len(extra)),
-            out_specs=[vmem()] * (1 + len(more)),
-            out_shape=[shape((80, 64), F32)] + more,
+            out_specs=vmem(),
+            out_shape=shape((80, 64), F32),
             scratch_shapes=[pltpu.VMEM((5, 16, 2 * cols), BF)],
             compiler_params=params(),
-        )(pos, state[f][0], got[f][2], got[f][0], got[f][1], root_map, value_map, *extra)
-
-    part = gram(gram_first, 0, [], [])[0]
-    got[1][0], got[1][1], near_0, part = lax.optimization_barrier(
-        (got[1][0], got[1][1], state[0][1], part)
+        )(pos, state[f][0], got[f][1], got[f][0], got[f][2], root_map, value_map, *extra)
+
+    part = gram(gram_first, 0, [])
+    got[1][0], part, near_0, near_1 = lax.optimization_barrier(
+        (got[1][0], part, state[0][1], state[1][1])
     )
     near_0 = swap(near_0, 2)
-    part, pass_on = gram(
-        gram_second, 1, [part, got[0][0], got[0][1]], [shape((8, 16, cols), BF)]
-    )
-
-    rounds = [("mem", 1), ("space", 1), ("mem", 2)]
-    bit = 2
+    near_1 = swap(near_1, 2)
+    got[1].append(swap(got[1][0], 1))
+    part = gram(gram_second, 1, [part])
+
+    rounds = [("mem", 1)]
+    bit = 1
     while bit < strips:
         rounds.append(("space", bit))
         bit *= 2
+    rounds.append(("mem", 2))
     other = None
     for axis, bits in rounds:
         if other is not None:
             part = part + other
-        if (axis, bits) == ("mem", 2):
-            part, near_0 = lax.optimization_barrier((part, near_0))
         size = lax.axis_size(axis)
         other = lax.ppermute(part, axis, [(i, i ^ bits) for i in range(size)])
-        if (axis, bits) == ("mem", 2):
-            near_1, pass_on, other = lax.optimization_barrier((state[1][1], pass_on, other))
-            near_1 = swap(near_1, 2)
-            passed = swap(pass_on, 1)
+    near_0_late, near_1_late, _ = lax.optimization_barrier((near_0, near_1, other))
+    mate_near_0 = swap(near_0_late, 1)
+    mate_near_1 = swap(near_1_late, 1)
 
     weights = pl.pallas_call(
         weights_kernel,
@@ -555,15 +611,11 @@
         compiler_params=params(),
     )(pos, part, other)
 
-    near_0_late, _ = lax.optimization_barrier((near_0, other))
-    mate_near_0 = swap(near_0_late, 1)
-    mate_near_1 = swap(near_1, 1)
-
     return pl.pallas_call(
         final_kernel,
         name="final",
         cost_estimate=cost(100 * 16 * cols * 4),
-        in_specs=[smem()] + [vmem()] * 14,
+        in_specs=[smem()] + [vmem()] * 13,
         out_specs=hbm(),
         out_shape=shape(prior_replicas.shape, F32),
         scratch_shapes=[
@@ -573,8 +625,8 @@
         ],
         compiler_params=params(),
     )(
-        pos, weights, state[0][0], state[1][0], got[0][2], got[1][2], got[0][0], got[1][0],
-        got[0][1], got[1][1], passed, near_0, near_1, mate_near_0, mate_near_1,
+        pos, weights, state[0][0], state[1][0], got[0][1], got[1][1], got[0][0], got[1][0],
+        got[0][2], got[1][2], near_0, near_1, mate_near_0, mate_near_1,
     )
 
 

time: 65.8 us -> 59.5 us (0.904)
  waiting for transfers between devices: 19.6 us -> 13.6 us
  Pallas kernels: 22.4 us -> 25.4 us
  local copies, waits for them, and re-layouts: 2.56 us -> 0.02 us
  starting transfers between devices: 20.1 us -> 19.3 us
    ppermute x2, waiting for transfers between devices: 4.2 us -> 0.01 us  [local(): lax.ppermute(pay_a, 'space', pairs_a)]
    unnamed x12 -> x8, local copies, waits for them, and re-layouts: 2.56 us -> 0.02 us
    ppermute x11 -> x10, waiting for transfers between devices: 6.95 us -> 4.53 us  [swap(): return lax.ppermute(value, 'mem', [(i, i ^ bits) for i in range(4)])]
    pallas_call x2, Pallas kernels: 2.03 us -> 4.18 us  [local(): pl.pallas_call(functools.partial(pack_kernel, f), name='pack', cost_estim...]
    ppermute x2, starting transfers between devices: 5.98 us -> 7.54 us  [local(): lax.ppermute(pay_a, 'space', pairs_a)]
    ppermute x11 -> x10, starting transfers between devices: 6.96 us -> 5.4 us  [swap(): return lax.ppermute(value, 'mem', [(i, i ^ bits) for i in range(4)])]
    pallas_call x2 -> x4, Pallas kernels: 11.2 us -> 12.1 us  [the longest x2 7.73 us: local(): pl.pallas_call(functools.partial(pre_kernel, DIFFUSION[f]), name='pre', c...]
    ppermute x4, starting transfers between devices: 5.84 us -> 4.99 us  [local(): other = lax.ppermute(part, axis, [(i, i ^ bits) for i in range(size)])]
  transfers between devices with their start and end apart: 19 -> 18, of which waited for: 10 -> 6; matrix products, arithmetic and copies ran while one was open for 0% -> 0% of each run, Pallas kernels for 28% -> 35%
where the time goes in v4:
time: 59.5 us; the launch traced here: 59.3 us
  Pallas kernels  25.4 us (43%)
  starting transfers between devices  19.3 us (32%)
  waiting for transfers between devices  13.6 us (23%)
  between operations  0.87 us (1%)
    ppermute x4, waiting for transfers between devices, local(): other = lax.ppermute(part, axis, [(i, i ^ bits) for i in range(size)])  9.1 us
    pallas_call x2, Pallas kernels, local(): pl.pallas_call(functools.partial(pre_kernel, DIFFUSION[f]), name='pre', c...  7.73 us
    ppermute x2, starting transfers between devices, local(): lax.ppermute(pay_a, 'space', pairs_a)  7.54 us
    ppermute x10, starting transfers between devices, swap(): return lax.ppermute(value, 'mem', [(i, i ^ bits) for i in range(4)])  5.4 us
    ppermute x4, starting transfers between devices, local(): other = lax.ppermute(part, axis, [(i, i ^ bits) for i in range(size)])  4.99 us
    ppermute x10, waiting for transfers between devices, swap(): return lax.ppermute(value, 'mem', [(i, i ^ bits) for i in range(4)])  4.53 us
    pallas_call x2, Pallas kernels, local(): pl.pallas_call(functools.partial(post_kernel, DIFFUSION[f]), name='post',...  4.37 us
    pallas_call x2, Pallas kernels, local(): pl.pallas_call(functools.partial(pack_kernel, f), name='pack', cost_estim...  4.18 us
  transfers between devices with their start and end apart: 18, of which 6 were waited for; matrix products, arithmetic and copies ran while one was open for 0% of the time, Pallas kernels for 35%

profile of v4, /device:TPU:0, one launch (start us, length us, event | category | flops | bytes accessed | tf_op | source)
XLA Modules:
  0.0 59.3 jit_solution(9213843891198306671)
XLA Ops:
  0.0 0.1 pad_add_fusion.pos
  0.1 2.1 %pack.2 = (f32[12,16,2176]{2,1,0:T(8,128)S(1)}, bf16[72,2048]{1,0:T(8,128)(2,1)S(1)}, bf16[72,2048]{1,0:T(8,128)(2,1)S(1)}) custom-call(s32[3]{0:T(128)S(1)} %pad_add_fusion.pos, f32[16,2,8,2048]{3,2,1,0:T(8,128)} %prior.3, f32[2,2,8,2048]{3,2,1,0:T(8,128)} %wind.11), custom_call_target="tpu_custom_call" | custom-call | flops 5242880 | bytes 5242880 | tf_op jit(solution)/shard_map/pack/pallas_call | solution.py:490
  2.2 3.1 %collective-permute-start = (bf16[72,2048]{1,0:T(8,128)(2,1)S(1)}, bf16[72,2048]{1,0:T(8,128)(2,1)S(1)}, u32[]{:S(2)}, u32[]{:S(2)}) collective-permute-start(bf16[72,2048]{1,0:T(8,128)(2,1)S(1)} %get-tuple-element.29), channel_id=1, source_target_pairs={{0,4},{4,0},{8,12},{12,8},{1,5},{5,1},{9,13},{13,9},{2,6},{6,2},{1... | collective-permute-start | bytes 884744 | tf_op jit(solution)/shard_map/ppermute | solution.py:505
  5.3 0.7 %collective-permute-start.1 = (bf16[72,2048]{1,0:T(8,128)(2,1)S(1)}, bf16[72,2048]{1,0:T(8,128)(2,1)S(1)}, u32[]{:S(2)}, u32[]{:S(2)}) collective-permute-start(bf16[72,2048]{1,0:T(8,128)(2,1)S(1)} %get-tuple-element.30), channel_id=1, source_target_pairs={{4,8},{8,4},{5,9},{9,5},{6,10},{10,6},{7,11},{11,7},{20,24},{24,20... | collective-permute-start | bytes 884744 | tf_op jit(solution)/shard_map/ppermute | solution.py:505
  6.0 2.1 %pack.3 = (f32[12,16,2176]{2,1,0:T(8,128)S(1)}, bf16[64,2048]{1,0:T(8,128)(2,1)S(1)}, bf16[64,2048]{1,0:T(8,128)(2,1)S(1)}) custom-call(s32[3]{0:T(128)S(1)} %pad_add_fusion.pos, f32[16,2,8,2048]{3,2,1,0:T(8,128)} %prior.3, f32[2,2,8,2048]{3,2,1,0:T(8,128)} %wind.11), custom_call_target="tpu_custom_call" | custom-call | flops 5242880 | bytes 5242880 | tf_op jit(solution)/shard_map/pack/pallas_call | solution.py:490
  8.0 4.4 %collective-permute-start.3 = (bf16[64,2048]{1,0:T(8,128)(2,1)S(1)}, bf16[64,2048]{1,0:T(8,128)(2,1)S(1)}, u32[]{:S(2)}, u32[]{:S(2)}) collective-permute-start(bf16[64,2048]{1,0:T(8,128)(2,1)S(1)} %get-tuple-element.33), channel_id=1, source_target_pairs={{0,4},{4,0},{8,12},{12,8},{1,5},{5,1},{9,13},{13,9},{2,6},{6,2},{1... | collective-permute-start | bytes 786440 | tf_op jit(solution)/shard_map/ppermute | solution.py:505
  12.5 0.7 %collective-permute-start.4 = (bf16[64,2048]{1,0:T(8,128)(2,1)S(1)}, bf16[64,2048]{1,0:T(8,128)(2,1)S(1)}, u32[]{:S(2)}, u32[]{:S(2)}) collective-permute-start(bf16[64,2048]{1,0:T(8,128)(2,1)S(1)} %get-tuple-element.34), channel_id=1, source_target_pairs={{4,8},{8,4},{5,9},{9,5},{6,10},{10,6},{7,11},{11,7},{20,24},{24,20... | collective-permute-start | bytes 786440 | tf_op jit(solution)/shard_map/ppermute | solution.py:505
  13.2 3.9 %pre.2.begun = f32[8,16,2048]{2,1,0:T(8,128)S(1)} custom-call(f32[12,16,2176]{2,1,0:T(8,128)S(1)} %get-tuple-element.28.turned, f32[2,2,8,2048]{3,2,1,0:T(8,128)S(1)} %copy-done), custom_call_target="tpu_custom_call" | custom-call | flops 19660800 | bytes 19660800 | tf_op jit(solution)/shard_map/pre/pallas_call | solution.py:524
  17.1 2.2 %post.2 = (bf16[8,16,2048]{2,1,0:T(8,128)(2,1)S(1)}, bf16[4,16,2048]{2,1,0:T(8,128)(2,1)S(1)}, bf16[4,16,2048]{2,1,0:T(8,128)(2,1)S(1)}) custom-call(s32[3]{0:T(128)S(1)} %pad_add_fusion.pos, f32[12,16,2176]{2,1,0:T(8,128)S(1)} %get-tuple-element.28.turned, f32[8,16,2048]{2,1,0:T(8,128)S(1)} %pre.2.begun, ...), custom_call_target="tpu_custom_call" | custom-call | flops 13107200 | bytes 13107200 | tf_op jit(solution)/shard_map/post/pallas_call | solution.py:543
  19.3 1.6 %collective-permute-start.2 = (bf16[4,16,2048]{2,1,0:T(8,128)(2,1)S(1)}, bf16[4,16,2048]{2,1,0:T(8,128)(2,1)S(1)}, u32[]{:S(2)}, u32[]{:S(2)}) collective-permute-start(bf16[4,16,2048]{2,1,0:T(8,128)(2,1)S(1)} %get-tuple-element.31), channel_id=1, source_target_pairs={{0,2},{1,3},{2,0},{3,1},{4,6},{5,7},{6,4},{7,5},{8,10},{9,11},{10,... | collective-permute-start | bytes 786440 | tf_op jit(solution)/shard_map/ppermute | solution.py:482
  20.8 3.9 %pre.3.begun = f32[8,16,2048]{2,1,0:T(8,128)S(1)} custom-call(f32[12,16,2176]{2,1,0:T(8,128)S(1)} %get-tuple-element.32.turned, f32[2,2,8,2048]{3,2,1,0:T(8,128)S(1)} %copy-done), custom_call_target="tpu_custom_call" | custom-call | flops 19660800 | bytes 19660800 | tf_op jit(solution)/shard_map/pre/pallas_call | solution.py:524
  24.7 2.2 %post.3 = (bf16[8,16,2048]{2,1,0:T(8,128)(2,1)S(1)}, bf16[4,16,2048]{2,1,0:T(8,128)(2,1)S(1)}, bf16[4,16,2048]{2,1,0:T(8,128)(2,1)S(1)}) custom-call(s32[3]{0:T(128)S(1)} %pad_add_fusion.pos, f32[12,16,2176]{2,1,0:T(8,128)S(1)} %get-tuple-element.32.turned, f32[8,16,2048]{2,1,0:T(8,128)S(1)} %pre.3.begun, ...), custom_call_target="tpu_custom_call" | custom-call | flops 13107200 | bytes 13107200 | tf_op jit(solution)/shard_map/post/pallas_call | solution.py:543
  26.9 0.6 collective-permute-start.8
  27.5 0.5 collective-permute-start.6
  28.1 0.2 collective-permute-start.5
  28.9 1.3 %maps.1 = (f32[64,128]{1,0:T(8,128)S(1)}, f32[64,128]{1,0:T(8,128)S(1)}) custom-call(s32[3]{0:T(128)S(1)} %pad_add_fusion.pos, s32[1,2048]{1,0:T(1,128)S(1)} %bitcast.5, s32[1]{0:T(128)S(6)} %copy.7.count, f32[1,2048]{1,0:T(1,128)S(1)} %bitcast.6, f32[1,2048]{1,0:T(1,128)S(1)} %bitcast.7), custom_call_target="tpu_custom_call" | custom-call | flops 8388608 | bytes 8388608 | tf_op jit(solution)/shard_map/maps/pallas_call | solution.py:508
  30.3 1.1 %gram.2.part = f32[80,64]{1,0:T(8,128)S(1)} custom-call(s32[3]{0:T(128)S(1)} %pad_add_fusion.pos, bf16[8,16,2048]{2,1,0:T(8,128)(2,1)S(1)} %get-tuple-element.39.own.own_0, bf16[8,16,2048]{2,1,0:T(8,128)(2,1)S(1)} %collective-permute-done.7.mate.mate_0, bf16[4,16,2048]{2,1,0:T(8,128)(2,1)S(1)} %collective-permute-done.2.far.far_0, ...), custom_call_target="tpu_custom_call" | custom-call | flops 6291456 | bytes 6291456 | tf_op jit(solution)/shard_map/gram/pallas_call | solution.py:567
  31.4 4.4 %collective-permute-done.6.far.far_1 = bf16[4,16,2048]{2,1,0:T(8,128)(2,1)S(1)} collective-permute-done((bf16[4,16,2048]{2,1,0:T(8,128)(2,1)S(1)}, bf16[4,16,2048]{2,1,0:T(8,128)(2,1)S(1)}, u32[]{:S(2)}, u32[]{:S(2)}) %collective-permute-start.6) | collective-permute-done | bytes 262176 | tf_op jit(solution)/shard_map/ppermute | solution.py:482
  35.8 0.9 %collective-permute-start.14 = (bf16[4,16,2048]{2,1,0:T(8,128)(2,1)S(1)}, bf16[4,16,2048]{2,1,0:T(8,128)(2,1)S(1)}, u32[]{:S(2)}, u32[]{:S(2)}) collective-permute-start(bf16[4,16,2048]{2,1,0:T(8,128)(2,1)S(1)} %get-tuple-element.47), channel_id=1, source_target_pairs={{0,2},{1,3},{2,0},{3,1},{4,6},{5,7},{6,4},{7,5},{8,10},{9,11},{10,... | collective-permute-start | bytes 786440 | tf_op jit(solution)/shard_map/ppermute | solution.py:482
  36.7 1.1 %collective-permute-start.15 = (bf16[4,16,2048]{2,1,0:T(8,128)(2,1)S(1)}, bf16[4,16,2048]{2,1,0:T(8,128)(2,1)S(1)}, u32[]{:S(2)}, u32[]{:S(2)}) collective-permute-start(bf16[4,16,2048]{2,1,0:T(8,128)(2,1)S(1)} %get-tuple-element.48), channel_id=1, source_target_pairs={{0,2},{1,3},{2,0},{3,1},{4,6},{5,7},{6,4},{7,5},{8,10},{9,11},{10,... | collective-permute-start | bytes 786440 | tf_op jit(solution)/shard_map/ppermute | solution.py:482
  37.8 1.1 %gram.3 = f32[80,64]{1,0:T(8,128)S(1)} custom-call(s32[3]{0:T(128)S(1)} %pad_add_fusion.pos, bf16[8,16,2048]{2,1,0:T(8,128)(2,1)S(1)} %get-tuple-element.37.own.own_1, bf16[8,16,2048]{2,1,0:T(8,128)(2,1)S(1)} %collective-permute-done.5.mate.mate_1, bf16[4,16,2048]{2,1,0:T(8,128)(2,1)S(1)} %collective-permute-done.6.far.far_1, ...), custom_call_target="tpu_custom_call" | custom-call | flops 6291456 | bytes 6291456 | tf_op jit(solution)/shard_map/gram/pallas_call | solution.py:567
  39.1 1.2 %collective-permute-done.10 = f32[80,64]{1,0:T(8,128)S(1)} collective-permute-done((f32[80,64]{1,0:T(8,128)S(1)}, f32[80,64]{1,0:T(8,128)S(1)}, u32[]{:S(2)}, u32[]{:S(2)}) %collective-permute-start.10) | collective-permute-done | bytes 20512 | tf_op jit(solution)/shard_map/ppermute | solution.py:598
  40.3 1.3 %collective-permute-start.11 = (f32[80,64]{1,0:T(8,128)S(1)}, f32[80,64]{1,0:T(8,128)S(1)}, u32[]{:S(2)}, u32[]{:S(2)}) collective-permute-start(f32[80,64]{1,0:T(8,128)S(1)} %add.9), channel_id=1, source_target_pairs={{0,4},{4,0},{8,12},{12,8},{1,5},{5,1},{9,13},{13,9},{2,6},{6,2},{1... | collective-permute-start | bytes 61448 | tf_op jit(solution)/shard_map/ppermute | solution.py:598
  41.5 2.7 %collective-permute-done.11 = f32[80,64]{1,0:T(8,128)S(1)} collective-permute-done((f32[80,64]{1,0:T(8,128)S(1)}, f32[80,64]{1,0:T(8,128)S(1)}, u32[]{:S(2)}, u32[]{:S(2)}) %collective-permute-start.11) | collective-permute-done | bytes 20512 | tf_op jit(solution)/shard_map/ppermute | solution.py:598
  44.3 2.7 %collective-permute-start.12 = (f32[80,64]{1,0:T(8,128)S(1)}, f32[80,64]{1,0:T(8,128)S(1)}, u32[]{:S(2)}, u32[]{:S(2)}) collective-permute-start(f32[80,64]{1,0:T(8,128)S(1)} %add.10), channel_id=1, source_target_pairs={{0,8},{4,12},{8,0},{12,4},{1,9},{5,13},{9,1},{13,5},{2,10},{6,14},... | collective-permute-start | bytes 61448 | tf_op jit(solution)/shard_map/ppermute | solution.py:598
  47.0 2.2 %collective-permute-done.12 = f32[80,64]{1,0:T(8,128)S(1)} collective-permute-done((f32[80,64]{1,0:T(8,128)S(1)}, f32[80,64]{1,0:T(8,128)S(1)}, u32[]{:S(2)}, u32[]{:S(2)}) %collective-permute-start.12) | collective-permute-done | bytes 20512 | tf_op jit(solution)/shard_map/ppermute | solution.py:598
  49.2 0.9 %collective-permute-start.13 = (f32[80,64]{1,0:T(8,128)S(1)}, f32[80,64]{1,0:T(8,128)S(1)}, u32[]{:S(2)}, u32[]{:S(2)}) collective-permute-start(f32[80,64]{1,0:T(8,128)S(1)} %add.11.one), channel_id=1, source_target_pairs={{0,2},{1,3},{2,0},{3,1},{4,6},{5,7},{6,4},{7,5},{8,10},{9,11},{10,... | collective-permute-start | bytes 61448 | tf_op jit(solution)/shard_map/ppermute | solution.py:598
  50.1 0.1 collective-permute-done.15.near_1
  50.2 3.0 %collective-permute-done.13.two = f32[80,64]{1,0:T(8,128)S(1)} collective-permute-done((f32[80,64]{1,0:T(8,128)S(1)}, f32[80,64]{1,0:T(8,128)S(1)}, u32[]{:S(2)}, u32[]{:S(2)}) %collective-permute-start.13) | collective-permute-done | bytes 20512 | tf_op jit(solution)/shard_map/ppermute | solution.py:598
  53.2 0.5 collective-permute-start.17
  53.7 2.8 %weights.1 = bf16[32,64]{1,0:T(8,128)(2,1)S(1)} custom-call(s32[3]{0:T(128)S(1)} %pad_add_fusion.pos, f32[80,64]{1,0:T(8,128)S(1)} %add.11.one, f32[80,64]{1,0:T(8,128)S(1)} %collective-permute-done.13.two), custom_call_target="tpu_custom_call" | custom-call | flops 13107200 | bytes 13107200 | tf_op jit(solution)/shard_map/weights/pallas_call | solution.py:603
  56.5 2.8 %final.1 = f32[16,2,8,2048]{3,2,1,0:T(8,128)} custom-call(s32[3]{0:T(128)S(1)} %pad_add_fusion.pos, bf16[32,64]{1,0:T(8,128)(2,1)S(1)} %weights.1, bf16[8,16,2048]{2,1,0:T(8,128)(2,1)S(1)} %get-tuple-element.39.own.own_0, bf16[8,16,2048]{2,1,0:T(8,128)(2,1)S(1)} %get-tuple-element.37.own.own_1, bf16[8,16,2048]{2,1,0:T(8,128)(2,1)S(1)} %collective-permute-done.7.mate.mate_0, ...), custom_call_target="tpu_custom_call" | custom-call | flops 13107200 | bytes 13107200 | tf_op jit(solution)/shard_map/final/pallas_call | solution.py:614
  (27 shorter events, 0.2 us)
Async XLA Ops:
  0.1 13.1 %copy-start = (f32[2,2,8,2048]{3,2,1,0:T(8,128)S(1)}, f32[2,2,8,2048]{3,2,1,0:T(8,128)}, u32[]{:S(2)}) copy-start(f32[2,2,8,2048]{3,2,1,0:T(8,128)} %wind.11) | copy-start | bytes 786436
  2.2 14.9 %collective-permute-start = (bf16[72,2048]{1,0:T(8,128)(2,1)S(1)}, bf16[72,2048]{1,0:T(8,128)(2,1)S(1)}, u32[]{:S(2)}, u32[]{:S(2)}) collective-permute-start(bf16[72,2048]{1,0:T(8,128)(2,1)S(1)} %get-tuple-element.29), channel_id=1, source_target_pairs={{0,4},{4,0},{8,12},{12,8},{1,5},{5,1},{9,13},{13,9},{2,6},{6,2},{1... | collective-permute-start | bytes 884744 | tf_op jit(solution)/shard_map/ppermute | solution.py:505
  5.3 11.8 %collective-permute-start.1 = (bf16[72,2048]{1,0:T(8,128)(2,1)S(1)}, bf16[72,2048]{1,0:T(8,128)(2,1)S(1)}, u32[]{:S(2)}, u32[]{:S(2)}) collective-permute-start(bf16[72,2048]{1,0:T(8,128)(2,1)S(1)} %get-tuple-element.30), channel_id=1, source_target_pairs={{4,8},{8,4},{5,9},{9,5},{6,10},{10,6},{7,11},{11,7},{20,24},{24,20... | collective-permute-start | bytes 884744 | tf_op jit(solution)/shard_map/ppermute | solution.py:505
  8.0 16.7 %collective-permute-start.3 = (bf16[64,2048]{1,0:T(8,128)(2,1)S(1)}, bf16[64,2048]{1,0:T(8,128)(2,1)S(1)}, u32[]{:S(2)}, u32[]{:S(2)}) collective-permute-start(bf16[64,2048]{1,0:T(8,128)(2,1)S(1)} %get-tuple-element.33), channel_id=1, source_target_pairs={{0,4},{4,0},{8,12},{12,8},{1,5},{5,1},{9,13},{13,9},{2,6},{6,2},{1... | collective-permute-start | bytes 786440 | tf_op jit(solution)/shard_map/ppermute | solution.py:505
  12.5 12.3 %collective-permute-start.4 = (bf16[64,2048]{1,0:T(8,128)(2,1)S(1)}, bf16[64,2048]{1,0:T(8,128)(2,1)S(1)}, u32[]{:S(2)}, u32[]{:S(2)}) collective-permute-start(bf16[64,2048]{1,0:T(8,128)(2,1)S(1)} %get-tuple-element.34), channel_id=1, source_target_pairs={{4,8},{8,4},{5,9},{9,5},{6,10},{10,6},{7,11},{11,7},{20,24},{24,20... | collective-permute-start | bytes 786440 | tf_op jit(solution)/shard_map/ppermute | solution.py:505
  19.3 7.7 %collective-permute-start.2 = (bf16[4,16,2048]{2,1,0:T(8,128)(2,1)S(1)}, bf16[4,16,2048]{2,1,0:T(8,128)(2,1)S(1)}, u32[]{:S(2)}, u32[]{:S(2)}) collective-permute-start(bf16[4,16,2048]{2,1,0:T(8,128)(2,1)S(1)} %get-tuple-element.31), channel_id=1, source_target_pairs={{0,2},{1,3},{2,0},{3,1},{4,6},{5,7},{6,4},{7,5},{8,10},{9,11},{10,... | collective-permute-start | bytes 786440 | tf_op jit(solution)/shard_map/ppermute | solution.py:482
  20.8 9.4 %collective-permute-start.7 = (bf16[8,16,2048]{2,1,0:T(8,128)(2,1)S(1)}, bf16[8,16,2048]{2,1,0:T(8,128)(2,1)S(1)}, u32[]{:S(2)}, u32[]{:S(2)}) collective-permute-start(bf16[8,16,2048]{2,1,0:T(8,128)(2,1)S(1)} %get-tuple-element.39.own.own_0), channel_id=1, source_target_pairs={{0,1},{1,0},{2,3},{3,2},{4,5},{5,4},{6,7},{7,6},{8,9},{9,8},{10,11... | collective-permute-start | bytes 1572872 | tf_op jit(solution)/shard_map/ppermute | solution.py:482
  24.7 4.2 %copy-start.1 = (s32[2048]{0:T(1024)S(1)}, s32[2048]{0:T(1024)}, u32[]{:S(2)}) copy-start(s32[2048]{0:T(1024)} %param.8) | copy-start | bytes 24580
  24.7 4.2 %copy-start.2 = (f32[2048]{0:T(1024)S(1)}, f32[2048]{0:T(1024)}, u32[]{:S(2)}) copy-start(f32[2048]{0:T(1024)} %param.11) | copy-start | bytes 24580
  24.7 4.2 %copy-start.3 = (f32[2048]{0:T(1024)S(1)}, f32[2048]{0:T(1024)}, u32[]{:S(2)}) copy-start(f32[2048]{0:T(1024)} %param.10) | copy-start | bytes 24580
  26.9 3.3 %collective-permute-start.8 = (bf16[4,16,2048]{2,1,0:T(8,128)(2,1)S(1)}, bf16[4,16,2048]{2,1,0:T(8,128)(2,1)S(1)}, u32[]{:S(2)}, u32[]{:S(2)}) collective-permute-start(bf16[4,16,2048]{2,1,0:T(8,128)(2,1)S(1)} %collective-permute-done.2.far.far_0), channel_id=1, source_target_pairs={{0,1},{1,0},{2,3},{3,2},{4,5},{5,4},{6,7},{7,6},{8,9},{9,8},{10,11... | collective-permute-start | bytes 786440 | tf_op jit(solution)/shard_map/ppermute | solution.py:482
  27.5 8.3 %collective-permute-start.6 = (bf16[4,16,2048]{2,1,0:T(8,128)(2,1)S(1)}, bf16[4,16,2048]{2,1,0:T(8,128)(2,1)S(1)}, u32[]{:S(2)}, u32[]{:S(2)}) collective-permute-start(bf16[4,16,2048]{2,1,0:T(8,128)(2,1)S(1)} %get-tuple-element.38), channel_id=1, source_target_pairs={{0,2},{1,3},{2,0},{3,1},{4,6},{5,7},{6,4},{7,5},{8,10},{9,11},{10,... | collective-permute-start | bytes 786440 | tf_op jit(solution)/shard_map/ppermute | solution.py:482
  28.1 9.8 %collective-permute-start.5 = (bf16[8,16,2048]{2,1,0:T(8,128)(2,1)S(1)}, bf16[8,16,2048]{2,1,0:T(8,128)(2,1)S(1)}, u32[]{:S(2)}, u32[]{:S(2)}) collective-permute-start(bf16[8,16,2048]{2,1,0:T(8,128)(2,1)S(1)} %get-tuple-element.37.own.own_1), channel_id=1, source_target_pairs={{0,1},{1,0},{2,3},{3,2},{4,5},{5,4},{6,7},{7,6},{8,9},{9,8},{10,11... | collective-permute-start | bytes 1572872 | tf_op jit(solution)/shard_map/ppermute | solution.py:482
  35.8 2.0 %collective-permute-start.9 = (bf16[4,16,2048]{2,1,0:T(8,128)(2,1)S(1)}, bf16[4,16,2048]{2,1,0:T(8,128)(2,1)S(1)}, u32[]{:S(2)}, u32[]{:S(2)}) collective-permute-start(bf16[4,16,2048]{2,1,0:T(8,128)(2,1)S(1)} %collective-permute-done.6.far.far_1), channel_id=1, source_target_pairs={{0,1},{1,0},{2,3},{3,2},{4,5},{5,4},{6,7},{7,6},{8,9},{9,8},{10,11... | collective-permute-start | bytes 786440 | tf_op jit(solution)/shard_map/ppermute | solution.py:482
  35.8 14.3 %collective-permute-start.14 = (bf16[4,16,2048]{2,1,0:T(8,128)(2,1)S(1)}, bf16[4,16,2048]{2,1,0:T(8,128)(2,1)S(1)}, u32[]{:S(2)}, u32[]{:S(2)}) collective-permute-start(bf16[4,16,2048]{2,1,0:T(8,128)(2,1)S(1)} %get-tuple-element.47), channel_id=1, source_target_pairs={{0,2},{1,3},{2,0},{3,1},{4,6},{5,7},{6,4},{7,5},{8,10},{9,11},{10,... | collective-permute-start | bytes 786440 | tf_op jit(solution)/shard_map/ppermute | solution.py:482
  36.7 13.5 %collective-permute-start.15 = (bf16[4,16,2048]{2,1,0:T(8,128)(2,1)S(1)}, bf16[4,16,2048]{2,1,0:T(8,128)(2,1)S(1)}, u32[]{:S(2)}, u32[]{:S(2)}) collective-permute-start(bf16[4,16,2048]{2,1,0:T(8,128)(2,1)S(1)} %get-tuple-element.48), channel_id=1, source_target_pairs={{0,2},{1,3},{2,0},{3,1},{4,6},{5,7},{6,4},{7,5},{8,10},{9,11},{10,... | collective-permute-start | bytes 786440 | tf_op jit(solution)/shard_map/ppermute | solution.py:482
  39.0 1.3 %collective-permute-start.10 = (f32[80,64]{1,0:T(8,128)S(1)}, f32[80,64]{1,0:T(8,128)S(1)}, u32[]{:S(2)}, u32[]{:S(2)}) collective-permute-start(f32[80,64]{1,0:T(8,128)S(1)} %gram.3), channel_id=1, source_target_pairs={{0,1},{1,0},{2,3},{3,2},{4,5},{5,4},{6,7},{7,6},{8,9},{9,8},{10,11... | collective-permute-start | bytes 61448 | tf_op jit(solution)/shard_map/ppermute | solution.py:598
  40.3 4.0 %collective-permute-start.11 = (f32[80,64]{1,0:T(8,128)S(1)}, f32[80,64]{1,0:T(8,128)S(1)}, u32[]{:S(2)}, u32[]{:S(2)}) collective-permute-start(f32[80,64]{1,0:T(8,128)S(1)} %add.9), channel_id=1, source_target_pairs={{0,4},{4,0},{8,12},{12,8},{1,5},{5,1},{9,13},{13,9},{2,6},{6,2},{1... | collective-permute-start | bytes 61448 | tf_op jit(solution)/shard_map/ppermute | solution.py:598
  44.3 4.9 %collective-permute-start.12 = (f32[80,64]{1,0:T(8,128)S(1)}, f32[80,64]{1,0:T(8,128)S(1)}, u32[]{:S(2)}, u32[]{:S(2)}) collective-permute-start(f32[80,64]{1,0:T(8,128)S(1)} %add.10), channel_id=1, source_target_pairs={{0,8},{4,12},{8,0},{12,4},{1,9},{5,13},{9,1},{13,5},{2,10},{6,14},... | collective-permute-start | bytes 61448 | tf_op jit(solution)/shard_map/ppermute | solution.py:598
  49.2 4.0 %collective-permute-start.13 = (f32[80,64]{1,0:T(8,128)S(1)}, f32[80,64]{1,0:T(8,128)S(1)}, u32[]{:S(2)}, u32[]{:S(2)}) collective-permute-start(f32[80,64]{1,0:T(8,128)S(1)} %add.11.one), channel_id=1, source_target_pairs={{0,2},{1,3},{2,0},{3,1},{4,6},{5,7},{6,4},{7,5},{8,10},{9,11},{10,... | collective-permute-start | bytes 61448 | tf_op jit(solution)/shard_map/ppermute | solution.py:598
  53.2 3.3 %collective-permute-start.16 = (bf16[4,16,2048]{2,1,0:T(8,128)(2,1)S(1)}, bf16[4,16,2048]{2,1,0:T(8,128)(2,1)S(1)}, u32[]{:S(2)}, u32[]{:S(2)}) collective-permute-start(bf16[4,16,2048]{2,1,0:T(8,128)(2,1)S(1)} %collective-permute-done.14.near_0), channel_id=1, source_target_pairs={{0,1},{1,0},{2,3},{3,2},{4,5},{5,4},{6,7},{7,6},{8,9},{9,8},{10,11... | collective-permute-start | bytes 786440 | tf_op jit(solution)/shard_map/ppermute | solution.py:482
  53.2 3.3 %collective-permute-start.17 = (bf16[4,16,2048]{2,1,0:T(8,128)(2,1)S(1)}, bf16[4,16,2048]{2,1,0:T(8,128)(2,1)S(1)}, u32[]{:S(2)}, u32[]{:S(2)}) collective-permute-start(bf16[4,16,2048]{2,1,0:T(8,128)(2,1)S(1)} %collective-permute-done.15.near_1), channel_id=1, source_target_pairs={{0,1},{1,0},{2,3},{3,2},{4,5},{5,4},{6,7},{7,6},{8,9},{9,8},{10,11... | collective-permute-start | bytes 786440 | tf_op jit(solution)/shard_map/ppermute | solution.py:482

commit v5 on v4

--- a/solution.py
+++ b/solution.py
@@ -284,10 +284,8 @@
     lax.fori_loop(0, 8, second_step, 0)
 
 
-def post_kernel(
-    nu, pos, turned, begun, recv_a, recv_b, wind_a, wind_b, wind, out_all, out_near, out_far,
-    halo, delta
-):
+def post_kernel(nu, pos, turned, begun, recv_a, recv_b, wind_a, wind_b, wind, *refs):
+    out_all, out_near, out_far, halo, delta = refs[-5:]
     cols = begun.shape[2]
     even = (pos[0] % 2) == 0
     start_a = jnp.where(even, 4, 0)
@@ -353,8 +351,10 @@
             both.append(begun[r, span, :] + value)
         out_all[r] = jnp.concatenate(both, 0).astype(BF)
     base = (pos[2] // 2) * 4
+    if len(refs) == 6:
+        out_near[0:4] = refs[0][...]
     for r in range(4):
-        out_near[r] = out_all[base + r]
+        out_near[out_near.shape[0] - 4 + r] = out_all[base + r]
         out_far[r] = out_all[4 - base + r]
 
 
@@ -442,20 +442,17 @@
 
 def final_kernel(
     pos, weights, own_0, own_1, mate_0, mate_1, far_0, far_1, diag_0, diag_1,
-    near_0, near_1, mate_near_0, mate_near_1, out, keep, ready, sems
+    near, mate_near, out, keep, ready, sems
 ):
     m = weights[...]
-    fields = (
-        (own_0, mate_0, far_0, diag_0, near_0, mate_near_0),
-        (own_1, mate_1, far_1, diag_1, near_1, mate_near_1),
-    )
+    fields = ((own_0, mate_0, far_0, diag_0), (own_1, mate_1, far_1, diag_1))
     base = (pos[2] // 2) * 4
     copies = []
     for f in range(2):
-        own, mate, far, diag, near, mate_near = fields[f]
+        own, mate, far, diag = fields[f]
         for r in range(8):
             row = base + r if r < 4 else 4 - base + r - 4
-            other = [far[r], diag[r]] if r < 4 else [near[r - 4], mate_near[r - 4]]
+            other = [far[r], diag[r]] if r < 4 else [near[4 * f + r - 4], mate_near[4 * f + r - 4]]
             state = jnp.concatenate([own[row], mate[row]] + other, 0)
             both = jnp.dot(m, state, preferred_element_type=F32)
             keep[row] = both[0:16] + both[16:32]
@@ -483,9 +480,8 @@
 
     prior_here = pltpu.with_memory_space_constraint(prior_replicas, pltpu.MemorySpace.HBM)
     wind_here = pltpu.with_memory_space_constraint(wind_field, pltpu.MemorySpace.HBM)
-    turned = []
-    recv = []
-    for f in range(2):
+
+    def pack(f, when, prior, wind):
         height = 72 if f == 0 else 64
         rows, pay_a, pay_b = pl.pallas_call(
             functools.partial(pack_kernel, f),
@@ -500,28 +496,11 @@
                 pltpu.SemaphoreType.DMA((2,)),
             ],
             compiler_params=params(),
-        )(pos, prior_here, wind_here)
-        turned.append(rows)
-        recv.append([lax.ppermute(pay_a, "space", pairs_a), lax.ppermute(pay_b, "space", pairs_b)])
-
-    slots = obs_index.shape[0]
-    root_map, value_map = pl.pallas_call(
-        functools.partial(maps_kernel, tiles),
-        name="maps",
-        cost_estimate=cost(slots * 1024 * 4),
-        in_specs=[smem(), vmem(), smem(), vmem(), vmem()],
-        out_specs=[vmem()] * 2,
-        out_shape=[shape((4 * tiles, 128), F32)] * 2,
-        compiler_params=params(),
-    )(
-        pos,
-        obs_index.reshape(1, slots),
-        obs_count,
-        obs_weight.reshape(1, slots),
-        obs_value.reshape(1, slots),
-    )
-    begun = [
-        pl.pallas_call(
+        )(when, prior, wind)
+        return rows, lax.ppermute(pay_a, "space", pairs_a), lax.ppermute(pay_b, "space", pairs_b)
+
+    def pre(f, rows):
+        return pl.pallas_call(
             functools.partial(pre_kernel, DIFFUSION[f]),
             name="pre",
             cost_estimate=cost(150 * 16 * cols * 4),
@@ -533,10 +512,36 @@
                 pltpu.VMEM((2, 2, 8, 8, cols), F32),
             ],
             compiler_params=params(),
-        )(turned[f], wind_field)
-        for f in range(2)
-    ]
-
+        )(rows, wind_field)
+
+    packed = [pack(0, pos, prior_here, wind_here)]
+    begun = [pre(0, packed[0][0])]
+    later, begun[0] = lax.optimization_barrier((pos, begun[0]))
+    packed.append(pack(1, later, prior_here, wind_here))
+    begun.append(pre(1, packed[1][0]))
+    turned = [v[0] for v in packed]
+    recv = [[v[1], v[2]] for v in packed]
+
+    slots = obs_index.shape[0]
+
+    def maps(when):
+        return pl.pallas_call(
+            functools.partial(maps_kernel, tiles),
+            name="maps",
+            cost_estimate=cost(slots * 1024 * 4),
+            in_specs=[smem(), vmem(), smem(), vmem(), vmem()],
+            out_specs=[vmem()] * 2,
+            out_shape=[shape((4 * tiles, 128), F32)] * 2,
+            compiler_params=params(),
+        )(
+            when,
+            obs_index.reshape(1, slots),
+            obs_count,
+            obs_weight.reshape(1, slots),
+            obs_value.reshape(1, slots),
+        )
+
+    root_map, value_map = maps(pos)
     state = []
     got = []
     for f in range(2):
@@ -544,11 +549,11 @@
             functools.partial(post_kernel, DIFFUSION[f]),
             name="post",
             cost_estimate=cost(100 * 16 * cols * 4),
-            in_specs=[smem()] + [vmem()] * 7,
+            in_specs=[smem()] + [vmem()] * (7 + f),
             out_specs=[vmem()] * 3,
             out_shape=[
                 shape((8, 16, cols), BF),
-                shape((4, 16, cols), BF),
+                shape((4 + 4 * f, 16, cols), BF),
                 shape((4, 16, cols), BF),
             ],
             scratch_shapes=[
@@ -556,7 +561,10 @@
                 pltpu.VMEM((8, 16, cols + PAD), F32),
             ],
             compiler_params=params(),
-        )(pos, turned[f], begun[f], recv[f][0], recv[f][1], recv[0][0], recv[0][1], wind_field)
+        )(
+            pos, turned[f], begun[f], recv[f][0], recv[f][1], recv[0][0], recv[0][1], wind_field,
+            *[v[1] for v in state]
+        )
         if f == 1:
             got[0][0], every, far = lax.optimization_barrier((got[0][0], every, far))
         state.append((every, near))
@@ -576,11 +584,9 @@
         )(pos, state[f][0], got[f][1], got[f][0], got[f][2], root_map, value_map, *extra)
 
     part = gram(gram_first, 0, [])
-    got[1][0], part, near_0, near_1 = lax.optimization_barrier(
-        (got[1][0], part, state[0][1], state[1][1])
-    )
-    near_0 = swap(near_0, 2)
-    near_1 = swap(near_1, 2)
+    part, near = lax.optimization_barrier((part, state[1][1]))
+    near = swap(near, 2)
+    got[1][0], _ = lax.optimization_barrier((got[1][0], part))
     got[1].append(swap(got[1][0], 1))
     part = gram(gram_second, 1, [part])
 
@@ -596,9 +602,8 @@
             part = part + other
         size = lax.axis_size(axis)
         other = lax.ppermute(part, axis, [(i, i ^ bits) for i in range(size)])
-    near_0_late, near_1_late, _ = lax.optimization_barrier((near_0, near_1, other))
-    mate_near_0 = swap(near_0_late, 1)
-    mate_near_1 = swap(near_1_late, 1)
+    near_late, _ = lax.optimization_barrier((near, other))
+    mate_near = swap(near_late, 1)
 
     weights = pl.pallas_call(
         weights_kernel,
@@ -615,7 +620,7 @@
         final_kernel,
         name="final",
         cost_estimate=cost(100 * 16 * cols * 4),
-        in_specs=[smem()] + [vmem()] * 13,
+        in_specs=[smem()] + [vmem()] * 11,
         out_specs=hbm(),
         out_shape=shape(prior_replicas.shape, F32),
         scratch_shapes=[
@@ -626,7 +631,7 @@
         compiler_params=params(),
     )(
         pos, weights, state[0][0], state[1][0], got[0][1], got[1][1], got[0][0], got[1][0],
-        got[0][2], got[1][2], near_0, near_1, mate_near_0, mate_near_1,
+        got[0][2], got[1][2], near, mate_near,
     )
 
 

time: 59.5 us -> 59.5 us (level)
  starting transfers between devices: 19.3 us -> 17.8 us
  waiting for transfers between devices: 13.6 us -> 15 us
    ppermute x10 -> x8, starting transfers between devices: 5.4 us -> 4.23 us  [swap(): return lax.ppermute(value, 'mem', [(i, i ^ bits) for i in range(4)])]
    ppermute x10 -> x8, waiting for transfers between devices: 4.53 us -> 5.48 us  [swap(): return lax.ppermute(value, 'mem', [(i, i ^ bits) for i in range(4)])]
  transfers between devices with their start and end apart: 18 -> 16, of which waited for: 6 -> 6; matrix products, arithmetic and copies ran while one was open for 0% -> 0% of each run, Pallas kernels for 35% -> 35%
where the time goes in v5:
time: 59.5 us; the launch traced here: 59.2 us
  Pallas kernels  25.4 us (43%)
  starting transfers between devices  17.8 us (30%)
  waiting for transfers between devices  15 us (25%)
  between operations  0.87 us (1%)
    ppermute x4, waiting for transfers between devices, local(): other = lax.ppermute(part, axis, [(i, i ^ bits) for i in range(size)])  9.52 us
    pallas_call x2, Pallas kernels, pre(): pl.pallas_call(functools.partial(pre_kernel, DIFFUSION[f]), name='pre', c...  7.73 us
    ppermute x2, starting transfers between devices, pack(): lax.ppermute(pay_a, 'space', pairs_a)  7.54 us
    ppermute x8, waiting for transfers between devices, swap(): return lax.ppermute(value, 'mem', [(i, i ^ bits) for i in range(4)])  5.48 us
    ppermute x4, starting transfers between devices, local(): other = lax.ppermute(part, axis, [(i, i ^ bits) for i in range(size)])  4.67 us
    pallas_call x2, Pallas kernels, local(): pl.pallas_call(functools.partial(post_kernel, DIFFUSION[f]), name='post',...  4.38 us
    ppermute x8, starting transfers between devices, swap(): return lax.ppermute(value, 'mem', [(i, i ^ bits) for i in range(4)])  4.23 us
    pallas_call x2, Pallas kernels, pack(): pl.pallas_call(functools.partial(pack_kernel, f), name='pack', cost_estim...  4.18 us
  transfers between devices with their start and end apart: 16, of which 6 were waited for; matrix products, arithmetic and copies ran while one was open for 0% of the time, Pallas kernels for 35%

profile of v5, /device:TPU:0, one launch (start us, length us, event | category | flops | bytes accessed | tf_op | source)
XLA Modules:
  0.0 59.2 jit_solution(3360523422527756580)
XLA Ops:
  0.0 0.1 pad_add_fusion.pos
  0.1 2.1 %pack.2 = (f32[12,16,2176]{2,1,0:T(8,128)S(1)}, bf16[72,2048]{1,0:T(8,128)(2,1)S(1)}, bf16[72,2048]{1,0:T(8,128)(2,1)S(1)}) custom-call(s32[3]{0:T(128)S(1)} %pad_add_fusion.pos, f32[16,2,8,2048]{3,2,1,0:T(8,128)} %prior.3, f32[2,2,8,2048]{3,2,1,0:T(8,128)} %wind.11), custom_call_target="tpu_custom_call" | custom-call | flops 5242880 | bytes 5242880 | tf_op jit(solution)/shard_map/pack/pallas_call | solution.py:486
  2.2 3.1 %collective-permute-start = (bf16[72,2048]{1,0:T(8,128)(2,1)S(1)}, bf16[72,2048]{1,0:T(8,128)(2,1)S(1)}, u32[]{:S(2)}, u32[]{:S(2)}) collective-permute-start(bf16[72,2048]{1,0:T(8,128)(2,1)S(1)} %get-tuple-element.30), channel_id=1, source_target_pairs={{0,4},{4,0},{8,12},{12,8},{1,5},{5,1},{9,13},{13,9},{2,6},{6,2},{1... | collective-permute-start | bytes 884744 | tf_op jit(solution)/shard_map/ppermute | solution.py:500
  5.3 0.7 %collective-permute-start.1 = (bf16[72,2048]{1,0:T(8,128)(2,1)S(1)}, bf16[72,2048]{1,0:T(8,128)(2,1)S(1)}, u32[]{:S(2)}, u32[]{:S(2)}) collective-permute-start(bf16[72,2048]{1,0:T(8,128)(2,1)S(1)} %get-tuple-element.31), channel_id=1, source_target_pairs={{4,8},{8,4},{5,9},{9,5},{6,10},{10,6},{7,11},{11,7},{20,24},{24,20... | collective-permute-start | bytes 884744 | tf_op jit(solution)/shard_map/ppermute | solution.py:500
  6.0 3.9 %pre.2.begun = f32[8,16,2048]{2,1,0:T(8,128)S(1)} custom-call(f32[12,16,2176]{2,1,0:T(8,128)S(1)} %get-tuple-element.28.turned, f32[2,2,8,2048]{3,2,1,0:T(8,128)S(1)} %copy-done), custom_call_target="tpu_custom_call" | custom-call | flops 19660800 | bytes 19660800 | tf_op jit(solution)/shard_map/pre/pallas_call | solution.py:503
  9.9 2.1 %pack.3 = (f32[12,16,2176]{2,1,0:T(8,128)S(1)}, bf16[64,2048]{1,0:T(8,128)(2,1)S(1)}, bf16[64,2048]{1,0:T(8,128)(2,1)S(1)}) custom-call(s32[3]{0:T(128)S(1)} %pad_add_fusion.pos, f32[16,2,8,2048]{3,2,1,0:T(8,128)} %prior.3, f32[2,2,8,2048]{3,2,1,0:T(8,128)} %wind.11), custom_call_target="tpu_custom_call" | custom-call | flops 5242880 | bytes 5242880 | tf_op jit(solution)/shard_map/pack/pallas_call | solution.py:486
  11.9 4.4 %collective-permute-start.3 = (bf16[64,2048]{1,0:T(8,128)(2,1)S(1)}, bf16[64,2048]{1,0:T(8,128)(2,1)S(1)}, u32[]{:S(2)}, u32[]{:S(2)}) collective-permute-start(bf16[64,2048]{1,0:T(8,128)(2,1)S(1)} %get-tuple-element.35), channel_id=1, source_target_pairs={{0,4},{4,0},{8,12},{12,8},{1,5},{5,1},{9,13},{13,9},{2,6},{6,2},{1... | collective-permute-start | bytes 786440 | tf_op jit(solution)/shard_map/ppermute | solution.py:500
  16.4 0.7 %collective-permute-start.4 = (bf16[64,2048]{1,0:T(8,128)(2,1)S(1)}, bf16[64,2048]{1,0:T(8,128)(2,1)S(1)}, u32[]{:S(2)}, u32[]{:S(2)}) collective-permute-start(bf16[64,2048]{1,0:T(8,128)(2,1)S(1)} %get-tuple-element.36), channel_id=1, source_target_pairs={{4,8},{8,4},{5,9},{9,5},{6,10},{10,6},{7,11},{11,7},{20,24},{24,20... | collective-permute-start | bytes 786440 | tf_op jit(solution)/shard_map/ppermute | solution.py:500
  17.1 2.2 %post.2 = (bf16[8,16,2048]{2,1,0:T(8,128)(2,1)S(1)}, bf16[4,16,2048]{2,1,0:T(8,128)(2,1)S(1)}, bf16[4,16,2048]{2,1,0:T(8,128)(2,1)S(1)}) custom-call(s32[3]{0:T(128)S(1)} %pad_add_fusion.pos, f32[12,16,2176]{2,1,0:T(8,128)S(1)} %get-tuple-element.28.turned, f32[8,16,2048]{2,1,0:T(8,128)S(1)} %pre.2.begun, ...), custom_call_target="tpu_custom_call" | custom-call | flops 13107200 | bytes 13107200 | tf_op jit(solution)/shard_map/post/pallas_call | solution.py:548
  19.3 1.6 %collective-permute-start.2 = (bf16[4,16,2048]{2,1,0:T(8,128)(2,1)S(1)}, bf16[4,16,2048]{2,1,0:T(8,128)(2,1)S(1)}, u32[]{:S(2)}, u32[]{:S(2)}) collective-permute-start(bf16[4,16,2048]{2,1,0:T(8,128)(2,1)S(1)} %get-tuple-element.32), channel_id=1, source_target_pairs={{0,2},{1,3},{2,0},{3,1},{4,6},{5,7},{6,4},{7,5},{8,10},{9,11},{10,... | collective-permute-start | bytes 786440 | tf_op jit(solution)/shard_map/ppermute | solution.py:479
  20.8 3.9 %pre.3.begun = f32[8,16,2048]{2,1,0:T(8,128)S(1)} custom-call(f32[12,16,2176]{2,1,0:T(8,128)S(1)} %get-tuple-element.34.turned, f32[2,2,8,2048]{3,2,1,0:T(8,128)S(1)} %copy-done.1), custom_call_target="tpu_custom_call" | custom-call | flops 19660800 | bytes 19660800 | tf_op jit(solution)/shard_map/pre/pallas_call | solution.py:503
  24.8 2.2 %post.3 = (bf16[8,16,2048]{2,1,0:T(8,128)(2,1)S(1)}, bf16[8,16,2048]{2,1,0:T(8,128)(2,1)S(1)}, bf16[4,16,2048]{2,1,0:T(8,128)(2,1)S(1)}) custom-call(s32[3]{0:T(128)S(1)} %pad_add_fusion.pos, f32[12,16,2176]{2,1,0:T(8,128)S(1)} %get-tuple-element.34.turned, f32[8,16,2048]{2,1,0:T(8,128)S(1)} %pre.3.begun, ...), custom_call_target="tpu_custom_call" | custom-call | flops 13107200 | bytes 13107200 | tf_op jit(solution)/shard_map/post/pallas_call | solution.py:548
  27.0 0.6 collective-permute-start.8
  27.6 0.5 collective-permute-start.6
  28.1 0.2 collective-permute-start.5
  29.0 1.3 %maps.1 = (f32[64,128]{1,0:T(8,128)S(1)}, f32[64,128]{1,0:T(8,128)S(1)}) custom-call(s32[3]{0:T(128)S(1)} %pad_add_fusion.pos, s32[1,2048]{1,0:T(1,128)S(1)} %bitcast.5, s32[1]{0:T(128)S(6)} %copy.7.count, f32[1,2048]{1,0:T(1,128)S(1)} %bitcast.6, f32[1,2048]{1,0:T(1,128)S(1)} %bitcast.7), custom_call_target="tpu_custom_call" | custom-call | flops 8388608 | bytes 8388608 | tf_op jit(solution)/shard_map/maps/pallas_call | solution.py:528
  30.3 1.1 %gram.2.part = f32[80,64]{1,0:T(8,128)S(1)} custom-call(s32[3]{0:T(128)S(1)} %pad_add_fusion.pos, bf16[8,16,2048]{2,1,0:T(8,128)(2,1)S(1)} %get-tuple-element.42.own.own_0, bf16[8,16,2048]{2,1,0:T(8,128)(2,1)S(1)} %collective-permute-done.7.mate.mate_0, bf16[4,16,2048]{2,1,0:T(8,128)(2,1)S(1)} %collective-permute-done.2.far.far_0, ...), custom_call_target="tpu_custom_call" | custom-call | flops 6291456 | bytes 6291456 | tf_op jit(solution)/shard_map/gram/pallas_call | solution.py:575
  31.4 1.4 %collective-permute-start.14 = (bf16[8,16,2048]{2,1,0:T(8,128)(2,1)S(1)}, bf16[8,16,2048]{2,1,0:T(8,128)(2,1)S(1)}, u32[]{:S(2)}, u32[]{:S(2)}) collective-permute-start(bf16[8,16,2048]{2,1,0:T(8,128)(2,1)S(1)} %get-tuple-element.49), channel_id=1, source_target_pairs={{0,2},{1,3},{2,0},{3,1},{4,6},{5,7},{6,4},{7,5},{8,10},{9,11},{10,... | collective-permute-start | bytes 1572872 | tf_op jit(solution)/shard_map/ppermute | solution.py:479
  32.8 3.9 %collective-permute-done.6.far.far_1 = bf16[4,16,2048]{2,1,0:T(8,128)(2,1)S(1)} collective-permute-done((bf16[4,16,2048]{2,1,0:T(8,128)(2,1)S(1)}, bf16[4,16,2048]{2,1,0:T(8,128)(2,1)S(1)}, u32[]{:S(2)}, u32[]{:S(2)}) %collective-permute-start.6) | collective-permute-done | bytes 262176 | tf_op jit(solution)/shard_map/ppermute | solution.py:479
  36.7 1.5 %collective-permute-done.9.diag.diag_1 = bf16[4,16,2048]{2,1,0:T(8,128)(2,1)S(1)} collective-permute-done((bf16[4,16,2048]{2,1,0:T(8,128)(2,1)S(1)}, bf16[4,16,2048]{2,1,0:T(8,128)(2,1)S(1)}, u32[]{:S(2)}, u32[]{:S(2)}) %collective-permute-start.9) | collective-permute-done | bytes 262176 | tf_op jit(solution)/shard_map/ppermute | solution.py:479
  38.3 1.1 %gram.3 = f32[80,64]{1,0:T(8,128)S(1)} custom-call(s32[3]{0:T(128)S(1)} %pad_add_fusion.pos, bf16[8,16,2048]{2,1,0:T(8,128)(2,1)S(1)} %get-tuple-element.40.own.own_1, bf16[8,16,2048]{2,1,0:T(8,128)(2,1)S(1)} %collective-permute-done.5.mate.mate_1, bf16[4,16,2048]{2,1,0:T(8,128)(2,1)S(1)} %collective-permute-done.6.far.far_1, ...), custom_call_target="tpu_custom_call" | custom-call | flops 6291456 | bytes 6291456 | tf_op jit(solution)/shard_map/gram/pallas_call | solution.py:575
  39.4 0.2 collective-permute-start.10
  39.6 1.1 %collective-permute-done.10 = f32[80,64]{1,0:T(8,128)S(1)} collective-permute-done((f32[80,64]{1,0:T(8,128)S(1)}, f32[80,64]{1,0:T(8,128)S(1)}, u32[]{:S(2)}, u32[]{:S(2)}) %collective-permute-start.10) | collective-permute-done | bytes 20512 | tf_op jit(solution)/shard_map/ppermute | solution.py:604
  40.7 1.3 %collective-permute-start.11 = (f32[80,64]{1,0:T(8,128)S(1)}, f32[80,64]{1,0:T(8,128)S(1)}, u32[]{:S(2)}, u32[]{:S(2)}) collective-permute-start(f32[80,64]{1,0:T(8,128)S(1)} %add.9), channel_id=1, source_target_pairs={{0,4},{4,0},{8,12},{12,8},{1,5},{5,1},{9,13},{13,9},{2,6},{6,2},{1... | collective-permute-start | bytes 61448 | tf_op jit(solution)/shard_map/ppermute | solution.py:604
  41.9 2.7 %collective-permute-done.11 = f32[80,64]{1,0:T(8,128)S(1)} collective-permute-done((f32[80,64]{1,0:T(8,128)S(1)}, f32[80,64]{1,0:T(8,128)S(1)}, u32[]{:S(2)}, u32[]{:S(2)}) %collective-permute-start.11) | collective-permute-done | bytes 20512 | tf_op jit(solution)/shard_map/ppermute | solution.py:604
  44.7 2.7 %collective-permute-start.12 = (f32[80,64]{1,0:T(8,128)S(1)}, f32[80,64]{1,0:T(8,128)S(1)}, u32[]{:S(2)}, u32[]{:S(2)}) collective-permute-start(f32[80,64]{1,0:T(8,128)S(1)} %add.10), channel_id=1, source_target_pairs={{0,8},{4,12},{8,0},{12,4},{1,9},{5,13},{9,1},{13,5},{2,10},{6,14},... | collective-permute-start | bytes 61448 | tf_op jit(solution)/shard_map/ppermute | solution.py:604
  47.4 2.2 %collective-permute-done.12 = f32[80,64]{1,0:T(8,128)S(1)} collective-permute-done((f32[80,64]{1,0:T(8,128)S(1)}, f32[80,64]{1,0:T(8,128)S(1)}, u32[]{:S(2)}, u32[]{:S(2)}) %collective-permute-start.12) | collective-permute-done | bytes 20512 | tf_op jit(solution)/shard_map/ppermute | solution.py:604
  49.6 0.5 collective-permute-start.13
  50.1 3.5 %collective-permute-done.13.two = f32[80,64]{1,0:T(8,128)S(1)} collective-permute-done((f32[80,64]{1,0:T(8,128)S(1)}, f32[80,64]{1,0:T(8,128)S(1)}, u32[]{:S(2)}, u32[]{:S(2)}) %collective-permute-start.13) | collective-permute-done | bytes 20512 | tf_op jit(solution)/shard_map/ppermute | solution.py:604
  53.6 2.8 %weights.1 = bf16[32,64]{1,0:T(8,128)(2,1)S(1)} custom-call(s32[3]{0:T(128)S(1)} %pad_add_fusion.pos, f32[80,64]{1,0:T(8,128)S(1)} %add.11.one, f32[80,64]{1,0:T(8,128)S(1)} %collective-permute-done.13.two), custom_call_target="tpu_custom_call" | custom-call | flops 13107200 | bytes 13107200 | tf_op jit(solution)/shard_map/weights/pallas_call | solution.py:608
  56.4 0.0 collective-permute-done.15.mate_near
  56.4 2.8 %final.1 = f32[16,2,8,2048]{3,2,1,0:T(8,128)} custom-call(s32[3]{0:T(128)S(1)} %pad_add_fusion.pos, bf16[32,64]{1,0:T(8,128)(2,1)S(1)} %weights.1, bf16[8,16,2048]{2,1,0:T(8,128)(2,1)S(1)} %get-tuple-element.42.own.own_0, bf16[8,16,2048]{2,1,0:T(8,128)(2,1)S(1)} %get-tuple-element.40.own.own_1, bf16[8,16,2048]{2,1,0:T(8,128)(2,1)S(1)} %collective-permute-done.7.mate.mate_0, ...), custom_call_target="tpu_custom_call" | custom-call | flops 13107200 | bytes 13107200 | tf_op jit(solution)/shard_map/final/pallas_call | solution.py:619
  (25 shorter events, 0.1 us)
Async XLA Ops:
  0.0 6.0 %copy-start = (f32[2,2,8,2048]{3,2,1,0:T(8,128)S(1)}, f32[2,2,8,2048]{3,2,1,0:T(8,128)}, u32[]{:S(2)}) copy-start(f32[2,2,8,2048]{3,2,1,0:T(8,128)} %wind.11) | copy-start | bytes 786436
  2.2 14.9 %collective-permute-start = (bf16[72,2048]{1,0:T(8,128)(2,1)S(1)}, bf16[72,2048]{1,0:T(8,128)(2,1)S(1)}, u32[]{:S(2)}, u32[]{:S(2)}) collective-permute-start(bf16[72,2048]{1,0:T(8,128)(2,1)S(1)} %get-tuple-element.30), channel_id=1, source_target_pairs={{0,4},{4,0},{8,12},{12,8},{1,5},{5,1},{9,13},{13,9},{2,6},{6,2},{1... | collective-permute-start | bytes 884744 | tf_op jit(solution)/shard_map/ppermute | solution.py:500
  5.3 11.8 %collective-permute-start.1 = (bf16[72,2048]{1,0:T(8,128)(2,1)S(1)}, bf16[72,2048]{1,0:T(8,128)(2,1)S(1)}, u32[]{:S(2)}, u32[]{:S(2)}) collective-permute-start(bf16[72,2048]{1,0:T(8,128)(2,1)S(1)} %get-tuple-element.31), channel_id=1, source_target_pairs={{4,8},{8,4},{5,9},{9,5},{6,10},{10,6},{7,11},{11,7},{20,24},{24,20... | collective-permute-start | bytes 884744 | tf_op jit(solution)/shard_map/ppermute | solution.py:500
  6.0 11.1 %copy-start.1 = (f32[2,2,8,2048]{3,2,1,0:T(8,128)S(1)}, f32[2,2,8,2048]{3,2,1,0:T(8,128)}, u32[]{:S(2)}) copy-start(f32[2,2,8,2048]{3,2,1,0:T(8,128)} %wind.11) | copy-start | bytes 786436
  11.9 12.8 %collective-permute-start.3 = (bf16[64,2048]{1,0:T(8,128)(2,1)S(1)}, bf16[64,2048]{1,0:T(8,128)(2,1)S(1)}, u32[]{:S(2)}, u32[]{:S(2)}) collective-permute-start(bf16[64,2048]{1,0:T(8,128)(2,1)S(1)} %get-tuple-element.35), channel_id=1, source_target_pairs={{0,4},{4,0},{8,12},{12,8},{1,5},{5,1},{9,13},{13,9},{2,6},{6,2},{1... | collective-permute-start | bytes 786440 | tf_op jit(solution)/shard_map/ppermute | solution.py:500
  16.4 8.3 %collective-permute-start.4 = (bf16[64,2048]{1,0:T(8,128)(2,1)S(1)}, bf16[64,2048]{1,0:T(8,128)(2,1)S(1)}, u32[]{:S(2)}, u32[]{:S(2)}) collective-permute-start(bf16[64,2048]{1,0:T(8,128)(2,1)S(1)} %get-tuple-element.36), channel_id=1, source_target_pairs={{4,8},{8,4},{5,9},{9,5},{6,10},{10,6},{7,11},{11,7},{20,24},{24,20... | collective-permute-start | bytes 786440 | tf_op jit(solution)/shard_map/ppermute | solution.py:500
  19.3 7.7 %collective-permute-start.2 = (bf16[4,16,2048]{2,1,0:T(8,128)(2,1)S(1)}, bf16[4,16,2048]{2,1,0:T(8,128)(2,1)S(1)}, u32[]{:S(2)}, u32[]{:S(2)}) collective-permute-start(bf16[4,16,2048]{2,1,0:T(8,128)(2,1)S(1)} %get-tuple-element.32), channel_id=1, source_target_pairs={{0,2},{1,3},{2,0},{3,1},{4,6},{5,7},{6,4},{7,5},{8,10},{9,11},{10,... | collective-permute-start | bytes 786440 | tf_op jit(solution)/shard_map/ppermute | solution.py:479
  20.8 9.4 %collective-permute-start.7 = (bf16[8,16,2048]{2,1,0:T(8,128)(2,1)S(1)}, bf16[8,16,2048]{2,1,0:T(8,128)(2,1)S(1)}, u32[]{:S(2)}, u32[]{:S(2)}) collective-permute-start(bf16[8,16,2048]{2,1,0:T(8,128)(2,1)S(1)} %get-tuple-element.42.own.own_0), channel_id=1, source_target_pairs={{0,1},{1,0},{2,3},{3,2},{4,5},{5,4},{6,7},{7,6},{8,9},{9,8},{10,11... | collective-permute-start | bytes 1572872 | tf_op jit(solution)/shard_map/ppermute | solution.py:479
  24.7 4.2 %copy-start.2 = (s32[2048]{0:T(1024)S(1)}, s32[2048]{0:T(1024)}, u32[]{:S(2)}) copy-start(s32[2048]{0:T(1024)} %param.8) | copy-start | bytes 24580
  24.7 4.2 %copy-start.3 = (f32[2048]{0:T(1024)S(1)}, f32[2048]{0:T(1024)}, u32[]{:S(2)}) copy-start(f32[2048]{0:T(1024)} %param.11) | copy-start | bytes 24580
  24.8 4.2 %copy-start.4 = (f32[2048]{0:T(1024)S(1)}, f32[2048]{0:T(1024)}, u32[]{:S(2)}) copy-start(f32[2048]{0:T(1024)} %param.10) | copy-start | bytes 24580
  27.0 3.3 %collective-permute-start.8 = (bf16[4,16,2048]{2,1,0:T(8,128)(2,1)S(1)}, bf16[4,16,2048]{2,1,0:T(8,128)(2,1)S(1)}, u32[]{:S(2)}, u32[]{:S(2)}) collective-permute-start(bf16[4,16,2048]{2,1,0:T(8,128)(2,1)S(1)} %collective-permute-done.2.far.far_0), channel_id=1, source_target_pairs={{0,1},{1,0},{2,3},{3,2},{4,5},{5,4},{6,7},{7,6},{8,9},{9,8},{10,11... | collective-permute-start | bytes 786440 | tf_op jit(solution)/shard_map/ppermute | solution.py:479
  27.6 9.2 %collective-permute-start.6 = (bf16[4,16,2048]{2,1,0:T(8,128)(2,1)S(1)}, bf16[4,16,2048]{2,1,0:T(8,128)(2,1)S(1)}, u32[]{:S(2)}, u32[]{:S(2)}) collective-permute-start(bf16[4,16,2048]{2,1,0:T(8,128)(2,1)S(1)} %get-tuple-element.41), channel_id=1, source_target_pairs={{0,2},{1,3},{2,0},{3,1},{4,6},{5,7},{6,4},{7,5},{8,10},{9,11},{10,... | collective-permute-start | bytes 786440 | tf_op jit(solution)/shard_map/ppermute | solution.py:479
  28.1 10.2 %collective-permute-start.5 = (bf16[8,16,2048]{2,1,0:T(8,128)(2,1)S(1)}, bf16[8,16,2048]{2,1,0:T(8,128)(2,1)S(1)}, u32[]{:S(2)}, u32[]{:S(2)}) collective-permute-start(bf16[8,16,2048]{2,1,0:T(8,128)(2,1)S(1)} %get-tuple-element.40.own.own_1), channel_id=1, source_target_pairs={{0,1},{1,0},{2,3},{3,2},{4,5},{5,4},{6,7},{7,6},{8,9},{9,8},{10,11... | collective-permute-start | bytes 1572872 | tf_op jit(solution)/shard_map/ppermute | solution.py:479
  31.4 22.2 %collective-permute-start.14 = (bf16[8,16,2048]{2,1,0:T(8,128)(2,1)S(1)}, bf16[8,16,2048]{2,1,0:T(8,128)(2,1)S(1)}, u32[]{:S(2)}, u32[]{:S(2)}) collective-permute-start(bf16[8,16,2048]{2,1,0:T(8,128)(2,1)S(1)} %get-tuple-element.49), channel_id=1, source_target_pairs={{0,2},{1,3},{2,0},{3,1},{4,6},{5,7},{6,4},{7,5},{8,10},{9,11},{10,... | collective-permute-start | bytes 1572872 | tf_op jit(solution)/shard_map/ppermute | solution.py:479
  36.7 1.5 %collective-permute-start.9 = (bf16[4,16,2048]{2,1,0:T(8,128)(2,1)S(1)}, bf16[4,16,2048]{2,1,0:T(8,128)(2,1)S(1)}, u32[]{:S(2)}, u32[]{:S(2)}) collective-permute-start(bf16[4,16,2048]{2,1,0:T(8,128)(2,1)S(1)} %collective-permute-done.6.far.far_1), channel_id=1, source_target_pairs={{0,1},{1,0},{2,3},{3,2},{4,5},{5,4},{6,7},{7,6},{8,9},{9,8},{10,11... | collective-permute-start | bytes 786440 | tf_op jit(solution)/shard_map/ppermute | solution.py:479
  39.4 1.3 %collective-permute-start.10 = (f32[80,64]{1,0:T(8,128)S(1)}, f32[80,64]{1,0:T(8,128)S(1)}, u32[]{:S(2)}, u32[]{:S(2)}) collective-permute-start(f32[80,64]{1,0:T(8,128)S(1)} %gram.3), channel_id=1, source_target_pairs={{0,1},{1,0},{2,3},{3,2},{4,5},{5,4},{6,7},{7,6},{8,9},{9,8},{10,11... | collective-permute-start | bytes 61448 | tf_op jit(solution)/shard_map/ppermute | solution.py:604
  40.7 4.0 %collective-permute-start.11 = (f32[80,64]{1,0:T(8,128)S(1)}, f32[80,64]{1,0:T(8,128)S(1)}, u32[]{:S(2)}, u32[]{:S(2)}) collective-permute-start(f32[80,64]{1,0:T(8,128)S(1)} %add.9), channel_id=1, source_target_pairs={{0,4},{4,0},{8,12},{12,8},{1,5},{5,1},{9,13},{13,9},{2,6},{6,2},{1... | collective-permute-start | bytes 61448 | tf_op jit(solution)/shard_map/ppermute | solution.py:604
  44.7 4.9 %collective-permute-start.12 = (f32[80,64]{1,0:T(8,128)S(1)}, f32[80,64]{1,0:T(8,128)S(1)}, u32[]{:S(2)}, u32[]{:S(2)}) collective-permute-start(f32[80,64]{1,0:T(8,128)S(1)} %add.10), channel_id=1, source_target_pairs={{0,8},{4,12},{8,0},{12,4},{1,9},{5,13},{9,1},{13,5},{2,10},{6,14},... | collective-permute-start | bytes 61448 | tf_op jit(solution)/shard_map/ppermute | solution.py:604
  49.6 4.0 %collective-permute-start.13 = (f32[80,64]{1,0:T(8,128)S(1)}, f32[80,64]{1,0:T(8,128)S(1)}, u32[]{:S(2)}, u32[]{:S(2)}) collective-permute-start(f32[80,64]{1,0:T(8,128)S(1)} %add.11.one), channel_id=1, source_target_pairs={{0,2},{1,3},{2,0},{3,1},{4,6},{5,7},{6,4},{7,5},{8,10},{9,11},{10,... | collective-permute-start | bytes 61448 | tf_op jit(solution)/shard_map/ppermute | solution.py:604
  53.6 2.8 %collective-permute-start.15 = (bf16[8,16,2048]{2,1,0:T(8,128)(2,1)S(1)}, bf16[8,16,2048]{2,1,0:T(8,128)(2,1)S(1)}, u32[]{:S(2)}, u32[]{:S(2)}) collective-permute-start(bf16[8,16,2048]{2,1,0:T(8,128)(2,1)S(1)} %collective-permute-done.14.near), channel_id=1, source_target_pairs={{0,1},{1,0},{2,3},{3,2},{4,5},{5,4},{6,7},{7,6},{8,9},{9,8},{10,11... | collective-permute-start | bytes 1572872 | tf_op jit(solution)/shard_map/ppermute | solution.py:479

commit v6 on v5

--- a/solution.py
+++ b/solution.py
@@ -168,59 +168,73 @@
         rows[r, :, width - PAD :] = jnp.zeros((16, PAD), F32)
 
 
-def pack_kernel(field, pos, prior, wind, turned, pay_a, pay_b, state, edge, sems):
-    load = pltpu.make_async_copy(prior.at[:, field], state, sems.at[0])
-    load.start()
-    if field == 0:
-        winds = pltpu.make_async_copy(wind.at[0], edge, sems.at[1])
-        winds.start()
+def pack_kernel(
+    pos, prior, wind, turned_0, turned_1, pay_a, pay_b, state, edge, sems
+):
+    winds = pltpu.make_async_copy(wind.at[0], edge, sems.at[2])
+    loads = [pltpu.make_async_copy(prior.at[:, f], state.at[f], sems.at[f]) for f in range(2)]
+    loads[0].start()
+    winds.start()
+    loads[1].start()
     even = (pos[0] % 2) == 0
     start_a = jnp.where(even, 4, 0)
     start_b = 4 - start_a
-    if field == 0:
-        winds.wait()
-        first = jnp.concatenate([edge[0, 0:2], edge[1, 0:2]], 0)
-        last = jnp.concatenate([edge[0, 6:8], edge[1, 6:8]], 0)
-        first_high = first.astype(BF).astype(F32)
-        last_high = last.astype(BF).astype(F32)
-        first = jnp.concatenate([first_high, first - first_high], 0)
-        last = jnp.concatenate([last_high, last - last_high], 0)
-        pay_a[64:72, :] = jnp.where(even, last, first).astype(BF)
-        pay_b[64:72, :] = jnp.where(even, first, last).astype(BF)
-    load.wait()
-    cols = state.shape[2]
-    turned[2:10, :, :cols] = jnp.swapaxes(state[...], 0, 1)
-    for r in range(4):
-        pay_a[r * 16 : r * 16 + 16, :] = turned[2 + start_a + r, :, :cols].astype(BF)
-        pay_b[r * 16 : r * 16 + 16, :] = turned[2 + start_b + r, :, :cols].astype(BF)
-    blank_edges(turned)
-
-
-def maps_kernel(tiles, pos, index, count, weight, value, root_map, value_map):
+    cols = state.shape[3]
+    for f in range(2):
+        turned = (turned_0, turned_1)[f]
+        blank_edges(turned)
+        loads[f].wait()
+        turned[2:10, :, :cols] = jnp.swapaxes(state[f], 0, 1)
+        for r in range(4):
+            at = (f * 4 + r) * 16
+            pay_a[at : at + 16, :] = turned[2 + start_a + r, :, :cols].astype(BF)
+            pay_b[at : at + 16, :] = turned[2 + start_b + r, :, :cols].astype(BF)
+    winds.wait()
+    first = jnp.concatenate([edge[0, 0:2], edge[1, 0:2]], 0)
+    last = jnp.concatenate([edge[0, 6:8], edge[1, 6:8]], 0)
+    first_high = first.astype(BF).astype(F32)
+    last_high = last.astype(BF).astype(F32)
+    first = jnp.concatenate([first_high, first - first_high], 0)
+    last = jnp.concatenate([last_high, last - last_high], 0)
+    pay_a[128:136, :] = jnp.where(even, last, first).astype(BF)
+    pay_b[128:136, :] = jnp.where(even, first, last).astype(BF)
+
+
+def slots_kernel(index, count, weight, value, place, chunk, root_out, rooted_out):
     slots = index.shape[1]
+    width = place.shape[0]
     n = index[...]
     used = lax.broadcasted_iota(jnp.int32, (1, slots), 1) < count[0]
     root = jnp.where(used, jnp.sqrt(weight[...]), 0.0)
-    rooted = root * value[...]
-    block = n // 128
-    row = (block // tiles) % 8
-    cell = (block // (tiles * 8)) * (2 * tiles) + (row % 2) * tiles + block % tiles
-    cell = jnp.where(row // 2 == pos[2], cell, -1)
-    lane = n % 128
-    hit = lax.broadcasted_iota(jnp.int32, (4 * tiles, slots), 0) == cell
-    hit = jnp.where(hit, 1.0, 0.0).astype(BF)
-    lane_hit = lax.broadcasted_iota(jnp.int32, (128, slots), 0) == lane
-    pieces = []
-    for v in (root, rooted):
-        high = v.astype(BF).astype(F32)
-        for part in (high, v - high):
-            pieces.append(jnp.where(lane_hit, part, 0.0).astype(BF))
-    spread = jnp.concatenate(pieces, 0)
-    out = lax.dot_general(
-        hit, spread, (((1,), (1,)), ((), ())), preferred_element_type=F32
-    )
-    root_map[...] = out[:, 0:128] + out[:, 128:256]
-    value_map[...] = out[:, 256:384] + out[:, 384:512]
+    root_out[...] = root
+    rooted_out[...] = root * value[...]
+    chunk[...] = jnp.broadcast_to(n // width, (16, slots))
+    column = n % width
+    step = 64
+    for r in range(0, width, step):
+        hit = lax.broadcasted_iota(jnp.int32, (step, slots), 0) == column - r
+        place[r : r + step, :] = jnp.where(hit, 1.0, 0.0).astype(BF)
+
+
+def pick_kernel(place, chunk, one, more, out, tall):
+    width, slots = place.shape
+    parts = one.shape[2] // width
+    at = 0
+    for ref in (one, more):
+        for r in range(ref.shape[0]):
+            for p in range(parts):
+                tall[at * 16 : at * 16 + 16, :] = ref[r, :, p * width : (p + 1) * width]
+                at += 1
+    count = at
+    step = 256
+    for o in range(0, slots, step):
+        cut = slice(o, o + step)
+        seen = jnp.dot(tall[...], place[:, cut], preferred_element_type=F32)
+        number = chunk[:, cut]
+        total = jnp.zeros((16, step), F32)
+        for at in range(count):
+            total = total + jnp.where(number == at, seen[at * 16 : at * 16 + 16], 0.0)
+        out[:, cut] = total.astype(BF)
 
 
 def stencil_row(rows, wind_r, wind_c, nu):
@@ -284,8 +298,10 @@
     lax.fori_loop(0, 8, second_step, 0)
 
 
-def post_kernel(nu, pos, turned, begun, recv_a, recv_b, wind_a, wind_b, wind, *refs):
-    out_all, out_near, out_far, halo, delta = refs[-5:]
+def post_kernel(field, pos, turned, begun, recv_a, recv_b, wind, *refs):
+    outs = refs[-4:-2] if field == 0 else refs[-3:-2]
+    halo, delta = refs[-2:]
+    nu = DIFFUSION[field]
     cols = begun.shape[2]
     even = (pos[0] % 2) == 0
     start_a = jnp.where(even, 4, 0)
@@ -295,11 +311,12 @@
         halo[r, :, cols:] = blank
         delta[r, :, cols:] = blank
     for r in range(4):
-        halo[start_a + r, :, :cols] = recv_a[r * 16 : r * 16 + 16, :].astype(F32)
-        halo[start_b + r, :, :cols] = recv_b[r * 16 : r * 16 + 16, :].astype(F32)
-    got_a = wind_a[64:72, :].astype(F32)
+        at = (field * 4 + r) * 16
+        halo[start_a + r, :, :cols] = recv_a[at : at + 16, :].astype(F32)
+        halo[start_b + r, :, :cols] = recv_b[at : at + 16, :].astype(F32)
+    got_a = recv_a[128:136, :].astype(F32)
     got_a = got_a[0:4] + got_a[4:8]
-    got_b = wind_b[64:72, :].astype(F32)
+    got_b = recv_b[128:136, :].astype(F32)
     got_b = got_b[0:4] + got_b[4:8]
     top = jnp.where(pos[0] == 0, 0.0, 1.0)
     bottom = jnp.where(pos[0] == pos[1] - 1, 0.0, 1.0)
@@ -349,54 +366,32 @@
                 rows, own_wind(1, 0, r), own_wind(1, 1, r) if center else None, nu
             )
             both.append(begun[r, span, :] + value)
-        out_all[r] = jnp.concatenate(both, 0).astype(BF)
-    base = (pos[2] // 2) * 4
-    if len(refs) == 6:
-        out_near[0:4] = refs[0][...]
-    for r in range(4):
-        out_near[out_near.shape[0] - 4 + r] = out_all[base + r]
-        out_far[r] = out_all[4 - base + r]
-
-
-def gram_sum(field, pos, own, mate, far, diag, root_map, value_map, spread):
-    tiles = own.shape[2] // 128
-    spread[4] = jnp.zeros(spread.shape[1:], BF)
-    half = 2 * (pos[2] % 2)
-    for r in range(2):
-        row = 2 * pos[2] + r
-        for t in range(tiles):
-            cut = slice(t * 128, (t + 1) * 128)
-            at = (field * 2 + r) * tiles + t
-            into = slice((r * tiles + t) * 128, (r * tiles + t + 1) * 128)
-            parts = [
-                own[row, :, cut].astype(F32),
-                mate[row, :, cut].astype(F32),
-                far[half + r, :, cut].astype(F32),
-                diag[half + r, :, cut].astype(F32),
-            ]
-            total = (parts[0] + parts[1]) + (parts[2] + parts[3])
-            mean = jnp.sum(total, 0, keepdims=True) * (1.0 / REPLICA_COUNT)
-            root = root_map[at : at + 1, :]
-            gap = value_map[at : at + 1, :] - root * mean
-            for g in range(4):
-                spread[jnp.bitwise_xor(pos[2], g), :, into] = ((parts[g] - mean) * root).astype(BF)
-            high = gap.astype(BF).astype(F32)
-            pair = jnp.concatenate([high, gap - high, jnp.zeros((14, 128), F32)], 0)
-            spread[4, :, into] = pair.astype(BF)
-    cells = spread.shape[2]
-    left = spread[...].reshape(80, cells)
-    right = spread[0:4].reshape(64, cells)
-    return lax.dot_general(
+        whole = jnp.concatenate(both, 0).astype(BF)
+        if field == 0:
+            outs[r // 4][r % 4] = whole
+        else:
+            outs[0][4 + r] = whole
+    if field == 1:
+        outs[0][0:4] = refs[0][...]
+
+
+def gram_kernel(pos, own, mate, far, diag, root, rooted, out, spread):
+    parts = [v[...].astype(F32) for v in (own, mate, far, diag)]
+    total = (parts[0] + parts[1]) + (parts[2] + parts[3])
+    mean = jnp.sum(total, 0, keepdims=True) * (1.0 / REPLICA_COUNT)
+    weight = root[...]
+    gap = rooted[...] - weight * mean
+    for g in range(4):
+        spread[jnp.bitwise_xor(pos[2], g)] = ((parts[g] - mean) * weight).astype(BF)
+    high = gap.astype(BF).astype(F32)
+    slots = root.shape[1]
+    pair = jnp.concatenate([high, gap - high, jnp.zeros((14, slots), F32)], 0)
+    spread[4] = pair.astype(BF)
+    left = spread[...].reshape(80, slots)
+    right = spread[0:4].reshape(64, slots)
+    out[...] = lax.dot_general(
         left, right, (((1,), (1,)), ((), ())), preferred_element_type=F32
     )
-
-
-def gram_first(pos, own, mate, far, diag, root_map, value_map, out, spread):
-    out[...] = gram_sum(0, pos, own, mate, far, diag, root_map, value_map, spread)
-
-
-def gram_second(pos, own, mate, far, diag, root_map, value_map, part, out, spread):
-    out[...] = part[...] + gram_sum(1, pos, own, mate, far, diag, root_map, value_map, spread)
 
 
 def exact(a, b):
@@ -441,21 +436,18 @@
 
 
 def final_kernel(
-    pos, weights, own_0, own_1, mate_0, mate_1, far_0, far_1, diag_0, diag_1,
-    near, mate_near, out, keep, ready, sems
+    weights, own, mate, far, diag, own_more, mate_more, far_more, diag_more, out, keep, ready, sems
 ):
     m = weights[...]
-    fields = ((own_0, mate_0, far_0, diag_0), (own_1, mate_1, far_1, diag_1))
-    base = (pos[2] // 2) * 4
     copies = []
     for f in range(2):
-        own, mate, far, diag = fields[f]
         for r in range(8):
-            row = base + r if r < 4 else 4 - base + r - 4
-            other = [far[r], diag[r]] if r < 4 else [near[4 * f + r - 4], mate_near[4 * f + r - 4]]
-            state = jnp.concatenate([own[row], mate[row]] + other, 0)
+            first = f == 0 and r < 4
+            refs = (own, mate, far, diag) if first else (own_more, mate_more, far_more, diag_more)
+            at = r if first else f * 8 + r - 4
+            state = jnp.concatenate([v[at] for v in refs], 0)
             both = jnp.dot(m, state, preferred_element_type=F32)
-            keep[row] = both[0:16] + both[16:32]
+            keep[r] = both[0:16] + both[16:32]
         ready[f] = jnp.swapaxes(keep[...], 0, 1)
         copies.append(pltpu.make_async_copy(ready.at[f], out.at[:, f], sems.at[f]))
         copies[f].start()
@@ -465,7 +457,6 @@
 
 def local(prior_replicas, wind_field, obs_index, obs_count, obs_value, obs_weight):
     cols = prior_replicas.shape[3]
-    tiles = cols // 128
     strips = lax.axis_size("space")
     here = lax.axis_index("space")
     group = lax.axis_index("mem")
@@ -481,23 +472,24 @@
     prior_here = pltpu.with_memory_space_constraint(prior_replicas, pltpu.MemorySpace.HBM)
     wind_here = pltpu.with_memory_space_constraint(wind_field, pltpu.MemorySpace.HBM)
 
-    def pack(f, when, prior, wind):
-        height = 72 if f == 0 else 64
-        rows, pay_a, pay_b = pl.pallas_call(
-            functools.partial(pack_kernel, f),
-            name="pack",
-            cost_estimate=cost(40 * 16 * cols * 4),
-            in_specs=[smem(), hbm(), hbm()],
-            out_specs=[vmem()] * 3,
-            out_shape=[shape((12, 16, cols + PAD), F32)] + [shape((height, cols), BF)] * 2,
-            scratch_shapes=[
-                pltpu.VMEM((16, 8, cols), F32),
-                pltpu.VMEM((2, 8, cols), F32),
-                pltpu.SemaphoreType.DMA((2,)),
-            ],
-            compiler_params=params(),
-        )(when, prior, wind)
-        return rows, lax.ppermute(pay_a, "space", pairs_a), lax.ppermute(pay_b, "space", pairs_b)
+    packed = pl.pallas_call(
+        pack_kernel,
+        name="pack",
+        cost_estimate=cost(80 * 16 * cols * 4),
+        in_specs=[smem(), hbm(), hbm()],
+        out_specs=[vmem()] * 4,
+        out_shape=[shape((12, 16, cols + PAD), F32)] * 2
+        + [shape((136, cols), BF)] * 2,
+        scratch_shapes=[
+            pltpu.VMEM((2, 16, 8, cols), F32),
+            pltpu.VMEM((2, 8, cols), F32),
+            pltpu.SemaphoreType.DMA((3,)),
+        ],
+        compiler_params=params(),
+    )(pos, prior_here, wind_here)
+    turned = packed[0:2]
+    recv_a = lax.ppermute(packed[2], "space", pairs_a)
+    recv_b = lax.ppermute(packed[3], "space", pairs_b)
 
     def pre(f, rows):
         return pl.pallas_call(
@@ -514,96 +506,92 @@
             compiler_params=params(),
         )(rows, wind_field)
 
-    packed = [pack(0, pos, prior_here, wind_here)]
-    begun = [pre(0, packed[0][0])]
-    later, begun[0] = lax.optimization_barrier((pos, begun[0]))
-    packed.append(pack(1, later, prior_here, wind_here))
-    begun.append(pre(1, packed[1][0]))
-    turned = [v[0] for v in packed]
-    recv = [[v[1], v[2]] for v in packed]
+    begun = [pre(f, turned[f]) for f in range(2)]
 
     slots = obs_index.shape[0]
-
-    def maps(when):
+    width = 512
+    place, chunk, root, rooted = pl.pallas_call(
+        slots_kernel,
+        name="slots",
+        cost_estimate=cost(width * slots * 2),
+        in_specs=[vmem(), smem(), vmem(), vmem()],
+        out_specs=[vmem()] * 4,
+        out_shape=[
+            shape((width, slots), BF),
+            shape((16, slots), jnp.int32),
+            shape((1, slots), F32),
+            shape((1, slots), F32),
+        ],
+        compiler_params=params(),
+    )(
+        obs_index.reshape(1, slots),
+        obs_count,
+        obs_weight.reshape(1, slots),
+        obs_value.reshape(1, slots),
+    )
+    recv_a, begun[0], begun[1], place = lax.optimization_barrier(
+        (recv_a, begun[0], begun[1], place)
+    )
+
+    def post(f, extra):
+        heights = (4, 4) if f == 0 else (12,)
         return pl.pallas_call(
-            functools.partial(maps_kernel, tiles),
-            name="maps",
-            cost_estimate=cost(slots * 1024 * 4),
-            in_specs=[smem(), vmem(), smem(), vmem(), vmem()],
-            out_specs=[vmem()] * 2,
-            out_shape=[shape((4 * tiles, 128), F32)] * 2,
-            compiler_params=params(),
-        )(
-            when,
-            obs_index.reshape(1, slots),
-            obs_count,
-            obs_weight.reshape(1, slots),
-            obs_value.reshape(1, slots),
-        )
-
-    root_map, value_map = maps(pos)
-    state = []
-    got = []
-    for f in range(2):
-        every, near, far = pl.pallas_call(
-            functools.partial(post_kernel, DIFFUSION[f]),
+            functools.partial(post_kernel, f),
             name="post",
-            cost_estimate=cost(100 * 16 * cols * 4),
-            in_specs=[smem()] + [vmem()] * (7 + f),
-            out_specs=[vmem()] * 3,
-            out_shape=[
-                shape((8, 16, cols), BF),
-                shape((4 + 4 * f, 16, cols), BF),
-                shape((4, 16, cols), BF),
-            ],
+            cost_estimate=cost(8),
+            in_specs=[smem()] + [vmem()] * (5 + f),
+            out_specs=[vmem()] * len(heights),
+            out_shape=[shape((v, 16, cols), BF) for v in heights],
             scratch_shapes=[
                 pltpu.VMEM((8, 16, cols + PAD), F32),
                 pltpu.VMEM((8, 16, cols + PAD), F32),
             ],
             compiler_params=params(),
-        )(
-            pos, turned[f], begun[f], recv[f][0], recv[f][1], recv[0][0], recv[0][1], wind_field,
-            *[v[1] for v in state]
-        )
-        if f == 1:
-            got[0][0], every, far = lax.optimization_barrier((got[0][0], every, far))
-        state.append((every, near))
-        got.append([swap(far, 2), swap(every, 1)])
-    got[0].append(swap(got[0][0], 1))
-
-    def gram(kernel, f, extra):
-        return pl.pallas_call(
-            kernel,
-            name="gram",
-            cost_estimate=cost(24 * 64 * cols * 2),
-            in_specs=[smem()] + [vmem()] * (6 + len(extra)),
-            out_specs=vmem(),
-            out_shape=shape((80, 64), F32),
-            scratch_shapes=[pltpu.VMEM((5, 16, 2 * cols), BF)],
-            compiler_params=params(),
-        )(pos, state[f][0], got[f][1], got[f][0], got[f][2], root_map, value_map, *extra)
-
-    part = gram(gram_first, 0, [])
-    part, near = lax.optimization_barrier((part, state[1][1]))
-    near = swap(near, 2)
-    got[1][0], _ = lax.optimization_barrier((got[1][0], part))
-    got[1].append(swap(got[1][0], 1))
-    part = gram(gram_second, 1, [part])
-
-    rounds = [("mem", 1)]
-    bit = 1
-    while bit < strips:
-        rounds.append(("space", bit))
-        bit *= 2
-    rounds.append(("mem", 2))
+        )(pos, turned[f], begun[f], recv_a, recv_b, wind_field, *extra)
+
+    one, two = post(0, [])
+    far_one = swap(one, 2)
+    more = post(1, [two])[0]
+    seen = pl.pallas_call(
+        pick_kernel,
+        name="pick",
+        cost_estimate=cost(8),
+        in_specs=[vmem()] * 4,
+        out_specs=vmem(),
+        out_shape=shape((16, slots), BF),
+        scratch_shapes=[pltpu.VMEM((16 * 16 * cols // width, width), BF)],
+        compiler_params=params(),
+    )(place, chunk, one, more)
+
+    seen_far = swap(seen, 2)
+    seen_mate = swap(seen, 1)
+    seen_far, far_one, late = lax.optimization_barrier((seen_far, far_one, more))
+    far_more = swap(late, 2)
+    seen_diag = swap(seen_far, 1)
+
+    part = pl.pallas_call(
+        gram_kernel,
+        name="gram",
+        cost_estimate=cost(24 * 64 * slots),
+        in_specs=[smem()] + [vmem()] * 6,
+        out_specs=vmem(),
+        out_shape=shape((80, 64), F32),
+        scratch_shapes=[pltpu.VMEM((5, 16, slots), BF)],
+        compiler_params=params(),
+    )(pos, seen, seen_mate, seen_far, seen_diag, root, rooted)
+
+    bits = 1
     other = None
-    for axis, bits in rounds:
+    while bits < strips:
         if other is not None:
             part = part + other
-        size = lax.axis_size(axis)
-        other = lax.ppermute(part, axis, [(i, i ^ bits) for i in range(size)])
-    near_late, _ = lax.optimization_barrier((near, other))
-    mate_near = swap(near_late, 1)
+        other = lax.ppermute(part, "space", [(i, i ^ bits) for i in range(strips)])
+        bits *= 2
+
+    late = lax.optimization_barrier((one, more, far_one, part))
+    mate_one, mate_more, diag_one = [swap(v, 1) for v in late[:3]]
+    late, _ = lax.optimization_barrier((far_more, other))
+    diag_more = swap(late, 1)
 
     weights = pl.pallas_call(
         weights_kernel,
@@ -620,7 +608,7 @@
         final_kernel,
         name="final",
         cost_estimate=cost(100 * 16 * cols * 4),
-        in_specs=[smem()] + [vmem()] * 11,
+        in_specs=[vmem()] * 9,
         out_specs=hbm(),
         out_shape=shape(prior_replicas.shape, F32),
         scratch_shapes=[
@@ -630,8 +618,7 @@
         ],
         compiler_params=params(),
     )(
-        pos, weights, state[0][0], state[1][0], got[0][1], got[1][1], got[0][0], got[1][0],
-        got[0][2], got[1][2], near, mate_near,
+        weights, one, mate_one, far_one, diag_one, more, mate_more, far_more, diag_more
     )
 
 

time: 59.5 us -> 56.1 us (0.943)
  the two profiles are of different devices: /device:TPU:0 before, /device:TPU:11 now
where the time goes in v6:
time: 56.1 us; the launch traced here: 56 us
  Pallas kernels  23.2 us (41%)
  waiting for transfers between devices  16.3 us (29%)
  starting transfers between devices  15.5 us (28%)
  between operations  0.81 us (1%)
    ppermute x9, starting transfers between devices, swap(): return lax.ppermute(value, 'mem', [(i, i ^ bits) for i in range(4)])  9.29 us
    ppermute x9, waiting for transfers between devices, swap(): return lax.ppermute(value, 'mem', [(i, i ^ bits) for i in range(4)])  8.81 us
    pallas_call x2, Pallas kernels, pre(): pl.pallas_call(functools.partial(pre_kernel, DIFFUSION[f]), name='pre', c...  7.74 us
    ppermute x2, waiting for transfers between devices, local(): other = lax.ppermute(part, 'space', [(i, i ^ bits) for i in range(strips)])  4.34 us
    ppermute x1, starting transfers between devices, local(): recv_b = lax.ppermute(packed[3], 'space', pairs_b)  4.32 us
    pallas_call x2, Pallas kernels, post(): pl.pallas_call(functools.partial(post_kernel, f), name='post', cost_estim...  4.3 us
    ppermute x1, waiting for transfers between devices, local(): recv_b = lax.ppermute(packed[3], 'space', pairs_b)  3.02 us
    pallas_call x1, Pallas kernels, local(): pl.pallas_call(weights_kernel, name='weights', cost_estimate=cost(400 * 6...  2.77 us
  transfers between devices with their start and end apart: 13, of which 8 were waited for; matrix products, arithmetic and copies ran while one was open for 0% of the time, Pallas kernels for 29%

profile of v6, /device:TPU:11, one launch (start us, length us, event | category | flops | bytes accessed | tf_op | source)
XLA Modules:
  0.0 56.0 jit_solution(5053464415865506114)
XLA Ops:
  0.0 0.1 pad_add_fusion.pos
  0.1 2.5 %pack.1 = (f32[12,16,2176]{2,1,0:T(8,128)S(1)}, f32[12,16,2176]{2,1,0:T(8,128)S(1)}, bf16[136,2048]{1,0:T(8,128)(2,1)S(1)}, bf16[136,2048]{1,0:T(8,128)(2,1)S(1)}) custom-call(s32[3]{0:T(128)S(1)} %pad_add_fusion.pos, f32[16,2,8,2048]{3,2,1,0:T(8,128)} %prior.1, f32[2,2,8,2048]{3,2,1,0:T(8,128)} %wind.9), custom_call_target="tpu_custom_call" | custom-call | flops 10485760 | bytes 10485760 | tf_op jit(solution)/shard_map/pack/pallas_call | solution.py:475
  2.6 0.2 collective-permute-start
  2.8 4.3 %collective-permute-start.1 = (bf16[136,2048]{1,0:T(8,128)(2,1)S(1)}, bf16[136,2048]{1,0:T(8,128)(2,1)S(1)}, u32[]{:S(2)}, u32[]{:S(2)}) collective-permute-start(bf16[136,2048]{1,0:T(8,128)(2,1)S(1)} %get-tuple-element.34), channel_id=1, source_target_pairs={{4,8},{8,4},{5,9},{9,5},{6,10},{10,6},{7,11},{11,7},{20,24},{24,20... | collective-permute-start | bytes 1671176 | tf_op jit(solution)/shard_map/ppermute | solution.py:492
  7.8 0.4 slots.1
  8.2 3.9 %pre.2.begun = f32[8,16,2048]{2,1,0:T(8,128)S(1)} custom-call(f32[12,16,2176]{2,1,0:T(8,128)S(1)} %get-tuple-element.27.turned, f32[2,2,8,2048]{3,2,1,0:T(8,128)S(1)} %copy-done), custom_call_target="tpu_custom_call" | custom-call | flops 19660800 | bytes 19660800 | tf_op jit(solution)/shard_map/pre/pallas_call | solution.py:495
  12.1 3.9 %pre.3.begun = f32[8,16,2048]{2,1,0:T(8,128)S(1)} custom-call(f32[12,16,2176]{2,1,0:T(8,128)S(1)} %get-tuple-element.28.turned, f32[2,2,8,2048]{3,2,1,0:T(8,128)S(1)} %copy-done), custom_call_target="tpu_custom_call" | custom-call | flops 19660800 | bytes 19660800 | tf_op jit(solution)/shard_map/pre/pallas_call | solution.py:495
  16.0 0.2 collective-permute-done.recv_a
  16.1 3.0 %collective-permute-done.1.recv_b = bf16[136,2048]{1,0:T(8,128)(2,1)S(1)} collective-permute-done((bf16[136,2048]{1,0:T(8,128)(2,1)S(1)}, bf16[136,2048]{1,0:T(8,128)(2,1)S(1)}, u32[]{:S(2)}, u32[]{:S(2)}) %collective-permute-start.1) | collective-permute-done | bytes 557088 | tf_op jit(solution)/shard_map/ppermute | solution.py:492
  19.2 2.1 %post.2 = (bf16[4,16,2048]{2,1,0:T(8,128)(2,1)S(1)}, bf16[4,16,2048]{2,1,0:T(8,128)(2,1)S(1)}) custom-call(s32[3]{0:T(128)S(1)} %pad_add_fusion.pos, f32[12,16,2176]{2,1,0:T(8,128)S(1)} %get-tuple-element.27.turned, f32[8,16,2048]{2,1,0:T(8,128)S(1)} %pre.2.begun, bf16[136,2048]{1,0:T(8,128)(2,1)S(1)} %collective-permute-done.recv_a, ...), custom_call_target="tpu_custom_call" | custom-call | flops 8 | bytes 8 | tf_op jit(solution)/shard_map/post/pallas_call | solution.py:538
  21.3 0.3 collective-permute-start.4
  21.6 2.2 %post.3.more.own_more = bf16[12,16,2048]{2,1,0:T(8,128)(2,1)S(1)} custom-call(s32[3]{0:T(128)S(1)} %pad_add_fusion.pos, f32[12,16,2176]{2,1,0:T(8,128)S(1)} %get-tuple-element.28.turned, f32[8,16,2048]{2,1,0:T(8,128)S(1)} %pre.3.begun, bf16[136,2048]{1,0:T(8,128)(2,1)S(1)} %collective-permute-done.recv_a, ...), custom_call_target="tpu_custom_call" | custom-call | flops 8 | bytes 8 | tf_op jit(solution)/shard_map/post/pallas_call | solution.py:538
  23.8 2.4 %pick.1.own = bf16[16,2048]{1,0:T(8,128)(2,1)S(1)} custom-call(bf16[512,2048]{1,0:T(8,128)(2,1)S(1)} %get-tuple-element.30.place, s32[16,2048]{1,0:T(8,128)S(1)} %get-tuple-element.31.chunk, bf16[4,16,2048]{2,1,0:T(8,128)(2,1)S(1)} %get-tuple-element.42.one.own, bf16[12,16,2048]{2,1,0:T(8,128)(2,1)S(1)} %post.3.more.own_more), custom_call_target="tpu_custom_call" | custom-call | flops 8 | bytes 8 | tf_op jit(solution)/shard_map/pick/pallas_call | solution.py:555
  26.2 1.3 %collective-permute-start.3 = (bf16[16,2048]{1,0:T(8,128)(2,1)S(1)}, bf16[16,2048]{1,0:T(8,128)(2,1)S(1)}, u32[]{:S(2)}, u32[]{:S(2)}) collective-permute-start(bf16[16,2048]{1,0:T(8,128)(2,1)S(1)} %pick.1.own), channel_id=1, source_target_pairs={{0,2},{1,3},{2,0},{3,1},{4,6},{5,7},{6,4},{7,5},{8,10},{9,11},{10,... | collective-permute-start | bytes 196616 | tf_op jit(solution)/shard_map/ppermute | solution.py:470
  27.4 3.0 %collective-permute-done.3.far = bf16[16,2048]{1,0:T(8,128)(2,1)S(1)} collective-permute-done((bf16[16,2048]{1,0:T(8,128)(2,1)S(1)}, bf16[16,2048]{1,0:T(8,128)(2,1)S(1)}, u32[]{:S(2)}, u32[]{:S(2)}) %collective-permute-start.3) | collective-permute-done | bytes 65568 | tf_op jit(solution)/shard_map/ppermute | solution.py:470
  30.4 0.2 collective-permute-start.11
  30.6 3.3 %collective-permute-start.2 = (bf16[16,2048]{1,0:T(8,128)(2,1)S(1)}, bf16[16,2048]{1,0:T(8,128)(2,1)S(1)}, u32[]{:S(2)}, u32[]{:S(2)}) collective-permute-start(bf16[16,2048]{1,0:T(8,128)(2,1)S(1)} %pick.1.own), channel_id=1, source_target_pairs={{0,1},{1,0},{2,3},{3,2},{4,5},{5,4},{6,7},{7,6},{8,9},{9,8},{10,11... | collective-permute-start | bytes 196616 | tf_op jit(solution)/shard_map/ppermute | solution.py:470
  33.8 0.9 %collective-permute-done.2.mate = bf16[16,2048]{1,0:T(8,128)(2,1)S(1)} collective-permute-done((bf16[16,2048]{1,0:T(8,128)(2,1)S(1)}, bf16[16,2048]{1,0:T(8,128)(2,1)S(1)}, u32[]{:S(2)}, u32[]{:S(2)}) %collective-permute-start.2) | collective-permute-done | bytes 65568 | tf_op jit(solution)/shard_map/ppermute | solution.py:470
  34.7 0.4 collective-permute-done.5.diag
  35.1 0.9 %gram.1 = f32[80,64]{1,0:T(8,128)S(1)} custom-call(s32[3]{0:T(128)S(1)} %pad_add_fusion.pos, bf16[16,2048]{1,0:T(8,128)(2,1)S(1)} %pick.1.own, bf16[16,2048]{1,0:T(8,128)(2,1)S(1)} %collective-permute-done.2.mate, bf16[16,2048]{1,0:T(8,128)(2,1)S(1)} %collective-permute-done.3.far, bf16[16,2048]{1,0:T(8,128)(2,1)S(1)} %collective-permute-done.5.diag, ...), custom_call_target="tpu_custom_call" | custom-call | flops 3145728 | bytes 3145728 | tf_op jit(solution)/shard_map/gram/pallas_call | solution.py:572
  36.0 0.1 collective-permute-start.6
  36.1 3.1 %collective-permute-done.6 = f32[80,64]{1,0:T(8,128)S(1)} collective-permute-done((f32[80,64]{1,0:T(8,128)S(1)}, f32[80,64]{1,0:T(8,128)S(1)}, u32[]{:S(2)}, u32[]{:S(2)}) %collective-permute-start.6) | collective-permute-done | bytes 20512 | tf_op jit(solution)/shard_map/ppermute | solution.py:588
  39.2 1.6 %collective-permute-start.7 = (f32[80,64]{1,0:T(8,128)S(1)}, f32[80,64]{1,0:T(8,128)S(1)}, u32[]{:S(2)}, u32[]{:S(2)}) collective-permute-start(f32[80,64]{1,0:T(8,128)S(1)} %add.3.one), channel_id=1, source_target_pairs={{0,8},{4,12},{8,0},{12,4},{1,9},{5,13},{9,1},{13,5},{2,10},{6,14},... | collective-permute-start | bytes 61448 | tf_op jit(solution)/shard_map/ppermute | solution.py:588
  40.8 0.9 %collective-permute-start.10 = (bf16[12,16,2048]{2,1,0:T(8,128)(2,1)S(1)}, bf16[12,16,2048]{2,1,0:T(8,128)(2,1)S(1)}, u32[]{:S(2)}, u32[]{:S(2)}) collective-permute-start(bf16[12,16,2048]{2,1,0:T(8,128)(2,1)S(1)} %post.3.more.own_more), channel_id=1, source_target_pairs={{0,1},{1,0},{2,3},{3,2},{4,5},{5,4},{6,7},{7,6},{8,9},{9,8},{10,11... | collective-permute-start | bytes 2359304 | tf_op jit(solution)/shard_map/ppermute | solution.py:470
  41.7 1.2 %collective-permute-done.7.two = f32[80,64]{1,0:T(8,128)S(1)} collective-permute-done((f32[80,64]{1,0:T(8,128)S(1)}, f32[80,64]{1,0:T(8,128)S(1)}, u32[]{:S(2)}, u32[]{:S(2)}) %collective-permute-start.7) | collective-permute-done | bytes 20512 | tf_op jit(solution)/shard_map/ppermute | solution.py:588
  43.0 4.6 %collective-permute-done.11.far_more = bf16[12,16,2048]{2,1,0:T(8,128)(2,1)S(1)} collective-permute-done((bf16[12,16,2048]{2,1,0:T(8,128)(2,1)S(1)}, bf16[12,16,2048]{2,1,0:T(8,128)(2,1)S(1)}, u32[]{:S(2)}, u32[]{:S(2)}) %collective-permute-start.11) | collective-permute-done | bytes 786464 | tf_op jit(solution)/shard_map/ppermute | solution.py:470
  47.5 2.8 %collective-permute-start.12 = (bf16[12,16,2048]{2,1,0:T(8,128)(2,1)S(1)}, bf16[12,16,2048]{2,1,0:T(8,128)(2,1)S(1)}, u32[]{:S(2)}, u32[]{:S(2)}) collective-permute-start(bf16[12,16,2048]{2,1,0:T(8,128)(2,1)S(1)} %collective-permute-done.11.far_more), channel_id=1, source_target_pairs={{0,1},{1,0},{2,3},{3,2},{4,5},{5,4},{6,7},{7,6},{8,9},{9,8},{10,11... | collective-permute-start | bytes 2359304 | tf_op jit(solution)/shard_map/ppermute | solution.py:470
  50.4 0.0 collective-permute-start.8
  50.4 0.5 collective-permute-start.9
  50.9 2.8 %weights.1 = bf16[32,64]{1,0:T(8,128)(2,1)S(1)} custom-call(s32[3]{0:T(128)S(1)} %pad_add_fusion.pos, f32[80,64]{1,0:T(8,128)S(1)} %add.3.one, f32[80,64]{1,0:T(8,128)S(1)} %collective-permute-done.7.two), custom_call_target="tpu_custom_call" | custom-call | flops 13107200 | bytes 13107200 | tf_op jit(solution)/shard_map/weights/pallas_call | solution.py:596
  53.6 0.0 collective-permute-done.8.mate
  53.7 2.3 %final.1 = f32[16,2,8,2048]{3,2,1,0:T(8,128)} custom-call(bf16[32,64]{1,0:T(8,128)(2,1)S(1)} %weights.1, bf16[4,16,2048]{2,1,0:T(8,128)(2,1)S(1)} %get-tuple-element.42.one.own, bf16[4,16,2048]{2,1,0:T(8,128)(2,1)S(1)} %collective-permute-done.8.mate, bf16[4,16,2048]{2,1,0:T(8,128)(2,1)S(1)} %collective-permute-done.4.far, ...), custom_call_target="tpu_custom_call" | custom-call | flops 13107200 | bytes 13107200 | tf_op jit(solution)/shard_map/final/pallas_call | solution.py:607
  (14 shorter events, 0.0 us)
Async XLA Ops:
  0.0 8.2 %copy-start = (f32[2,2,8,2048]{3,2,1,0:T(8,128)S(1)}, f32[2,2,8,2048]{3,2,1,0:T(8,128)}, u32[]{:S(2)}) copy-start(f32[2,2,8,2048]{3,2,1,0:T(8,128)} %wind.9) | copy-start | bytes 786436
  0.0 7.8 %copy-start.2 = (f32[2048]{0:T(1024)S(1)}, f32[2048]{0:T(1024)}, u32[]{:S(2)}) copy-start(f32[2048]{0:T(1024)} %param.11) | copy-start | bytes 24580
  0.0 7.8 %copy-start.3 = (f32[2048]{0:T(1024)S(1)}, f32[2048]{0:T(1024)}, u32[]{:S(2)}) copy-start(f32[2048]{0:T(1024)} %param.10) | copy-start | bytes 24580
  0.0 7.8 %copy-start.1 = (s32[2048]{0:T(1024)S(1)}, s32[2048]{0:T(1024)}, u32[]{:S(2)}) copy-start(s32[2048]{0:T(1024)} %param.8) | copy-start | bytes 24580
  2.6 13.6 %collective-permute-start = (bf16[136,2048]{1,0:T(8,128)(2,1)S(1)}, bf16[136,2048]{1,0:T(8,128)(2,1)S(1)}, u32[]{:S(2)}, u32[]{:S(2)}) collective-permute-start(bf16[136,2048]{1,0:T(8,128)(2,1)S(1)} %get-tuple-element.26), channel_id=1, source_target_pairs={{0,4},{4,0},{8,12},{12,8},{1,5},{5,1},{9,13},{13,9},{2,6},{6,2},{1... | collective-permute-start | bytes 1671176 | tf_op jit(solution)/shard_map/ppermute | solution.py:491
  2.8 16.3 %collective-permute-start.1 = (bf16[136,2048]{1,0:T(8,128)(2,1)S(1)}, bf16[136,2048]{1,0:T(8,128)(2,1)S(1)}, u32[]{:S(2)}, u32[]{:S(2)}) collective-permute-start(bf16[136,2048]{1,0:T(8,128)(2,1)S(1)} %get-tuple-element.34), channel_id=1, source_target_pairs={{4,8},{8,4},{5,9},{9,5},{6,10},{10,6},{7,11},{11,7},{20,24},{24,20... | collective-permute-start | bytes 1671176 | tf_op jit(solution)/shard_map/ppermute | solution.py:492
  21.3 9.1 %collective-permute-start.4 = (bf16[4,16,2048]{2,1,0:T(8,128)(2,1)S(1)}, bf16[4,16,2048]{2,1,0:T(8,128)(2,1)S(1)}, u32[]{:S(2)}, u32[]{:S(2)}) collective-permute-start(bf16[4,16,2048]{2,1,0:T(8,128)(2,1)S(1)} %get-tuple-element.42.one.own), channel_id=1, source_target_pairs={{0,2},{1,3},{2,0},{3,1},{4,6},{5,7},{6,4},{7,5},{8,10},{9,11},{10,... | collective-permute-start | bytes 786440 | tf_op jit(solution)/shard_map/ppermute | solution.py:470
  26.2 4.2 %collective-permute-start.3 = (bf16[16,2048]{1,0:T(8,128)(2,1)S(1)}, bf16[16,2048]{1,0:T(8,128)(2,1)S(1)}, u32[]{:S(2)}, u32[]{:S(2)}) collective-permute-start(bf16[16,2048]{1,0:T(8,128)(2,1)S(1)} %pick.1.own), channel_id=1, source_target_pairs={{0,2},{1,3},{2,0},{3,1},{4,6},{5,7},{6,4},{7,5},{8,10},{9,11},{10,... | collective-permute-start | bytes 196616 | tf_op jit(solution)/shard_map/ppermute | solution.py:470
  30.4 17.1 %collective-permute-start.11 = (bf16[12,16,2048]{2,1,0:T(8,128)(2,1)S(1)}, bf16[12,16,2048]{2,1,0:T(8,128)(2,1)S(1)}, u32[]{:S(2)}, u32[]{:S(2)}) collective-permute-start(bf16[12,16,2048]{2,1,0:T(8,128)(2,1)S(1)} %post.3.more.own_more), channel_id=1, source_target_pairs={{0,2},{1,3},{2,0},{3,1},{4,6},{5,7},{6,4},{7,5},{8,10},{9,11},{10,... | collective-permute-start | bytes 2359304 | tf_op jit(solution)/shard_map/ppermute | solution.py:470
  30.6 4.2 %collective-permute-start.2 = (bf16[16,2048]{1,0:T(8,128)(2,1)S(1)}, bf16[16,2048]{1,0:T(8,128)(2,1)S(1)}, u32[]{:S(2)}, u32[]{:S(2)}) collective-permute-start(bf16[16,2048]{1,0:T(8,128)(2,1)S(1)} %pick.1.own), channel_id=1, source_target_pairs={{0,1},{1,0},{2,3},{3,2},{4,5},{5,4},{6,7},{7,6},{8,9},{9,8},{10,11... | collective-permute-start | bytes 196616 | tf_op jit(solution)/shard_map/ppermute | solution.py:470
  33.8 1.3 %collective-permute-start.5 = (bf16[16,2048]{1,0:T(8,128)(2,1)S(1)}, bf16[16,2048]{1,0:T(8,128)(2,1)S(1)}, u32[]{:S(2)}, u32[]{:S(2)}) collective-permute-start(bf16[16,2048]{1,0:T(8,128)(2,1)S(1)} %collective-permute-done.3.far), channel_id=1, source_target_pairs={{0,1},{1,0},{2,3},{3,2},{4,5},{5,4},{6,7},{7,6},{8,9},{9,8},{10,11... | collective-permute-start | bytes 196616 | tf_op jit(solution)/shard_map/ppermute | solution.py:470
  36.0 3.2 %collective-permute-start.6 = (f32[80,64]{1,0:T(8,128)S(1)}, f32[80,64]{1,0:T(8,128)S(1)}, u32[]{:S(2)}, u32[]{:S(2)}) collective-permute-start(f32[80,64]{1,0:T(8,128)S(1)} %gram.1), channel_id=1, source_target_pairs={{0,4},{4,0},{8,12},{12,8},{1,5},{5,1},{9,13},{13,9},{2,6},{6,2},{1... | collective-permute-start | bytes 61448 | tf_op jit(solution)/shard_map/ppermute | solution.py:588
  39.2 3.8 %collective-permute-start.7 = (f32[80,64]{1,0:T(8,128)S(1)}, f32[80,64]{1,0:T(8,128)S(1)}, u32[]{:S(2)}, u32[]{:S(2)}) collective-permute-start(f32[80,64]{1,0:T(8,128)S(1)} %add.3.one), channel_id=1, source_target_pairs={{0,8},{4,12},{8,0},{12,4},{1,9},{5,13},{9,1},{13,5},{2,10},{6,14},... | collective-permute-start | bytes 61448 | tf_op jit(solution)/shard_map/ppermute | solution.py:588
  40.8 12.9 %collective-permute-start.10 = (bf16[12,16,2048]{2,1,0:T(8,128)(2,1)S(1)}, bf16[12,16,2048]{2,1,0:T(8,128)(2,1)S(1)}, u32[]{:S(2)}, u32[]{:S(2)}) collective-permute-start(bf16[12,16,2048]{2,1,0:T(8,128)(2,1)S(1)} %post.3.more.own_more), channel_id=1, source_target_pairs={{0,1},{1,0},{2,3},{3,2},{4,5},{5,4},{6,7},{7,6},{8,9},{9,8},{10,11... | collective-permute-start | bytes 2359304 | tf_op jit(solution)/shard_map/ppermute | solution.py:470
  47.5 6.2 %collective-permute-start.12 = (bf16[12,16,2048]{2,1,0:T(8,128)(2,1)S(1)}, bf16[12,16,2048]{2,1,0:T(8,128)(2,1)S(1)}, u32[]{:S(2)}, u32[]{:S(2)}) collective-permute-start(bf16[12,16,2048]{2,1,0:T(8,128)(2,1)S(1)} %collective-permute-done.11.far_more), channel_id=1, source_target_pairs={{0,1},{1,0},{2,3},{3,2},{4,5},{5,4},{6,7},{7,6},{8,9},{9,8},{10,11... | collective-permute-start | bytes 2359304 | tf_op jit(solution)/shard_map/ppermute | solution.py:470
  50.4 3.3 %collective-permute-start.8 = (bf16[4,16,2048]{2,1,0:T(8,128)(2,1)S(1)}, bf16[4,16,2048]{2,1,0:T(8,128)(2,1)S(1)}, u32[]{:S(2)}, u32[]{:S(2)}) collective-permute-start(bf16[4,16,2048]{2,1,0:T(8,128)(2,1)S(1)} %get-tuple-element.42.one.own), channel_id=1, source_target_pairs={{0,1},{1,0},{2,3},{3,2},{4,5},{5,4},{6,7},{7,6},{8,9},{9,8},{10,11... | collective-permute-start | bytes 786440 | tf_op jit(solution)/shard_map/ppermute | solution.py:470
  50.4 3.3 %collective-permute-start.9 = (bf16[4,16,2048]{2,1,0:T(8,128)(2,1)S(1)}, bf16[4,16,2048]{2,1,0:T(8,128)(2,1)S(1)}, u32[]{:S(2)}, u32[]{:S(2)}) collective-permute-start(bf16[4,16,2048]{2,1,0:T(8,128)(2,1)S(1)} %collective-permute-done.4.far), channel_id=1, source_target_pairs={{0,1},{1,0},{2,3},{3,2},{4,5},{5,4},{6,7},{7,6},{8,9},{9,8},{10,11... | collective-permute-start | bytes 786440 | tf_op jit(solution)/shard_map/ppermute | solution.py:470

commit v7 on v6

--- a/solution.py
+++ b/solution.py
@@ -395,7 +395,15 @@
 
 
 def exact(a, b):
-    return jnp.dot(a, b, precision=lax.Precision.HIGHEST, preferred_element_type=F32)
+    a_high = a.astype(BF)
+    b_high = b.astype(BF)
+    a_low = (a - a_high.astype(F32)).astype(BF)
+    b_low = (b - b_high.astype(F32)).astype(BF)
+
+    def product(x, y):
+        return jnp.dot(x, y, preferred_element_type=F32)
+
+    return product(a_high, b_high) + (product(a_high, b_low) + product(a_low, b_high))
 
 
 def weights_kernel(pos, one, two, out, keep):
@@ -580,16 +588,17 @@
         compiler_params=params(),
     )(pos, seen, seen_mate, seen_far, seen_diag, root, rooted)
 
+    mate_more = swap(more, 1)
+    mate_one = swap(one, 1)
+    diag_one = swap(far_one, 1)
     bits = 1
     other = None
     while bits < strips:
         if other is not None:
             part = part + other
+            part, mate_one, diag_one = lax.optimization_barrier((part, mate_one, diag_one))
         other = lax.ppermute(part, "space", [(i, i ^ bits) for i in range(strips)])
         bits *= 2
-
-    late = lax.optimization_barrier((one, more, far_one, part))
-    mate_one, mate_more, diag_one = [swap(v, 1) for v in late[:3]]
     late, _ = lax.optimization_barrier((far_more, other))
     diag_more = swap(late, 1)
 

time: 56.1 us -> 55.3 us (0.986)
  waiting for transfers between devices: 16.3 us -> 15.7 us
    ppermute x9, waiting for transfers between devices: 8.81 us -> 8.22 us  [swap(): return lax.ppermute(value, 'mem', [(i, i ^ bits) for i in range(4)])]
where the time goes in v7:
time: 55.3 us; the launch traced here: 55.1 us
  Pallas kernels  22.9 us (41%)
  starting transfers between devices  15.7 us (28%)
  waiting for transfers between devices  15.7 us (28%)
  between operations  0.81 us (1%)
    ppermute x9, starting transfers between devices, swap(): return lax.ppermute(value, 'mem', [(i, i ^ bits) for i in range(4)])  9.53 us
    ppermute x9, waiting for transfers between devices, swap(): return lax.ppermute(value, 'mem', [(i, i ^ bits) for i in range(4)])  8.22 us
    pallas_call x2, Pallas kernels, pre(): pl.pallas_call(functools.partial(pre_kernel, DIFFUSION[f]), name='pre', c...  7.74 us
    ppermute x1, starting transfers between devices, local(): recv_b = lax.ppermute(packed[3], 'space', pairs_b)  4.32 us
    pallas_call x2, Pallas kernels, post(): pl.pallas_call(functools.partial(post_kernel, f), name='post', cost_estim...  4.3 us
    ppermute x2, waiting for transfers between devices, local(): other = lax.ppermute(part, 'space', [(i, i ^ bits) for i in range(strips)])  4.26 us
    ppermute x1, waiting for transfers between devices, local(): recv_b = lax.ppermute(packed[3], 'space', pairs_b)  3.02 us
    pallas_call x1, Pallas kernels, local(): pl.pallas_call(weights_kernel, name='weights', cost_estimate=cost(400 * 6...  2.48 us
  transfers between devices with their start and end apart: 13, of which 8 were waited for; matrix products, arithmetic and copies ran while one was open for 0% of the time, Pallas kernels for 29%

profile of v7, /device:TPU:11, one launch (start us, length us, event | category | flops | bytes accessed | tf_op | source)
XLA Modules:
  0.0 55.1 jit_solution(8389991708040008350)
XLA Ops:
  0.0 0.1 pad_add_fusion.pos
  0.1 2.5 %pack.1 = (f32[12,16,2176]{2,1,0:T(8,128)S(1)}, f32[12,16,2176]{2,1,0:T(8,128)S(1)}, bf16[136,2048]{1,0:T(8,128)(2,1)S(1)}, bf16[136,2048]{1,0:T(8,128)(2,1)S(1)}) custom-call(s32[3]{0:T(128)S(1)} %pad_add_fusion.pos, f32[16,2,8,2048]{3,2,1,0:T(8,128)} %prior.1, f32[2,2,8,2048]{3,2,1,0:T(8,128)} %wind.9), custom_call_target="tpu_custom_call" | custom-call | flops 10485760 | bytes 10485760 | tf_op jit(solution)/shard_map/pack/pallas_call | solution.py:483
  2.6 0.2 collective-permute-start
  2.8 4.3 %collective-permute-start.1 = (bf16[136,2048]{1,0:T(8,128)(2,1)S(1)}, bf16[136,2048]{1,0:T(8,128)(2,1)S(1)}, u32[]{:S(2)}, u32[]{:S(2)}) collective-permute-start(bf16[136,2048]{1,0:T(8,128)(2,1)S(1)} %get-tuple-element.34), channel_id=1, source_target_pairs={{4,8},{8,4},{5,9},{9,5},{6,10},{10,6},{7,11},{11,7},{20,24},{24,20... | collective-permute-start | bytes 1671176 | tf_op jit(solution)/shard_map/ppermute | solution.py:500
  7.8 0.4 slots.1
  8.2 3.9 %pre.2.begun = f32[8,16,2048]{2,1,0:T(8,128)S(1)} custom-call(f32[12,16,2176]{2,1,0:T(8,128)S(1)} %get-tuple-element.27.turned, f32[2,2,8,2048]{3,2,1,0:T(8,128)S(1)} %copy-done), custom_call_target="tpu_custom_call" | custom-call | flops 19660800 | bytes 19660800 | tf_op jit(solution)/shard_map/pre/pallas_call | solution.py:503
  12.1 3.9 %pre.3.begun = f32[8,16,2048]{2,1,0:T(8,128)S(1)} custom-call(f32[12,16,2176]{2,1,0:T(8,128)S(1)} %get-tuple-element.28.turned, f32[2,2,8,2048]{3,2,1,0:T(8,128)S(1)} %copy-done), custom_call_target="tpu_custom_call" | custom-call | flops 19660800 | bytes 19660800 | tf_op jit(solution)/shard_map/pre/pallas_call | solution.py:503
  16.0 0.2 collective-permute-done.recv_a
  16.1 3.0 %collective-permute-done.1.recv_b = bf16[136,2048]{1,0:T(8,128)(2,1)S(1)} collective-permute-done((bf16[136,2048]{1,0:T(8,128)(2,1)S(1)}, bf16[136,2048]{1,0:T(8,128)(2,1)S(1)}, u32[]{:S(2)}, u32[]{:S(2)}) %collective-permute-start.1) | collective-permute-done | bytes 557088 | tf_op jit(solution)/shard_map/ppermute | solution.py:500
  19.2 2.1 %post.2 = (bf16[4,16,2048]{2,1,0:T(8,128)(2,1)S(1)}, bf16[4,16,2048]{2,1,0:T(8,128)(2,1)S(1)}) custom-call(s32[3]{0:T(128)S(1)} %pad_add_fusion.pos, f32[12,16,2176]{2,1,0:T(8,128)S(1)} %get-tuple-element.27.turned, f32[8,16,2048]{2,1,0:T(8,128)S(1)} %pre.2.begun, bf16[136,2048]{1,0:T(8,128)(2,1)S(1)} %collective-permute-done.recv_a, ...), custom_call_target="tpu_custom_call" | custom-call | flops 8 | bytes 8 | tf_op jit(solution)/shard_map/post/pallas_call | solution.py:546
  21.3 0.3 collective-permute-start.4
  21.6 2.2 %post.3.more.own_more = bf16[12,16,2048]{2,1,0:T(8,128)(2,1)S(1)} custom-call(s32[3]{0:T(128)S(1)} %pad_add_fusion.pos, f32[12,16,2176]{2,1,0:T(8,128)S(1)} %get-tuple-element.28.turned, f32[8,16,2048]{2,1,0:T(8,128)S(1)} %pre.3.begun, bf16[136,2048]{1,0:T(8,128)(2,1)S(1)} %collective-permute-done.recv_a, ...), custom_call_target="tpu_custom_call" | custom-call | flops 8 | bytes 8 | tf_op jit(solution)/shard_map/post/pallas_call | solution.py:546
  23.8 2.4 %pick.1.own = bf16[16,2048]{1,0:T(8,128)(2,1)S(1)} custom-call(bf16[512,2048]{1,0:T(8,128)(2,1)S(1)} %get-tuple-element.30.place, s32[16,2048]{1,0:T(8,128)S(1)} %get-tuple-element.31.chunk, bf16[4,16,2048]{2,1,0:T(8,128)(2,1)S(1)} %get-tuple-element.35.one.own, bf16[12,16,2048]{2,1,0:T(8,128)(2,1)S(1)} %post.3.more.own_more), custom_call_target="tpu_custom_call" | custom-call | flops 8 | bytes 8 | tf_op jit(solution)/shard_map/pick/pallas_call | solution.py:563
  26.2 1.3 %collective-permute-start.3 = (bf16[16,2048]{1,0:T(8,128)(2,1)S(1)}, bf16[16,2048]{1,0:T(8,128)(2,1)S(1)}, u32[]{:S(2)}, u32[]{:S(2)}) collective-permute-start(bf16[16,2048]{1,0:T(8,128)(2,1)S(1)} %pick.1.own), channel_id=1, source_target_pairs={{0,2},{1,3},{2,0},{3,1},{4,6},{5,7},{6,4},{7,5},{8,10},{9,11},{10,... | collective-permute-start | bytes 196616 | tf_op jit(solution)/shard_map/ppermute | solution.py:478
  27.4 3.0 %collective-permute-done.3.far = bf16[16,2048]{1,0:T(8,128)(2,1)S(1)} collective-permute-done((bf16[16,2048]{1,0:T(8,128)(2,1)S(1)}, bf16[16,2048]{1,0:T(8,128)(2,1)S(1)}, u32[]{:S(2)}, u32[]{:S(2)}) %collective-permute-start.3) | collective-permute-done | bytes 65568 | tf_op jit(solution)/shard_map/ppermute | solution.py:478
  30.4 0.0 collective-permute-done.4.far
  30.4 0.2 collective-permute-start.11
  30.6 3.3 %collective-permute-start.7 = (bf16[4,16,2048]{2,1,0:T(8,128)(2,1)S(1)}, bf16[4,16,2048]{2,1,0:T(8,128)(2,1)S(1)}, u32[]{:S(2)}, u32[]{:S(2)}) collective-permute-start(bf16[4,16,2048]{2,1,0:T(8,128)(2,1)S(1)} %get-tuple-element.35.one.own), channel_id=1, source_target_pairs={{0,1},{1,0},{2,3},{3,2},{4,5},{5,4},{6,7},{7,6},{8,9},{9,8},{10,11... | collective-permute-start | bytes 786440 | tf_op jit(solution)/shard_map/ppermute | solution.py:478
  33.8 0.5 collective-permute-start.2
  34.3 1.1 %collective-permute-done.2.mate = bf16[16,2048]{1,0:T(8,128)(2,1)S(1)} collective-permute-done((bf16[16,2048]{1,0:T(8,128)(2,1)S(1)}, bf16[16,2048]{1,0:T(8,128)(2,1)S(1)}, u32[]{:S(2)}, u32[]{:S(2)}) %collective-permute-start.2) | collective-permute-done | bytes 65568 | tf_op jit(solution)/shard_map/ppermute | solution.py:478
  35.4 0.1 collective-permute-done.5.diag
  35.6 0.9 %gram.1 = f32[80,64]{1,0:T(8,128)S(1)} custom-call(s32[3]{0:T(128)S(1)} %pad_add_fusion.pos, bf16[16,2048]{1,0:T(8,128)(2,1)S(1)} %pick.1.own, bf16[16,2048]{1,0:T(8,128)(2,1)S(1)} %collective-permute-done.2.mate, bf16[16,2048]{1,0:T(8,128)(2,1)S(1)} %collective-permute-done.3.far, bf16[16,2048]{1,0:T(8,128)(2,1)S(1)} %collective-permute-done.5.diag, ...), custom_call_target="tpu_custom_call" | custom-call | flops 3145728 | bytes 3145728 | tf_op jit(solution)/shard_map/gram/pallas_call | solution.py:580
  36.5 0.1 collective-permute-start.6
  36.6 3.1 %collective-permute-done.6 = f32[80,64]{1,0:T(8,128)S(1)} collective-permute-done((f32[80,64]{1,0:T(8,128)S(1)}, f32[80,64]{1,0:T(8,128)S(1)}, u32[]{:S(2)}, u32[]{:S(2)}) %collective-permute-start.6) | collective-permute-done | bytes 20512 | tf_op jit(solution)/shard_map/ppermute | solution.py:600
  39.7 1.5 %collective-permute-start.9 = (f32[80,64]{1,0:T(8,128)S(1)}, f32[80,64]{1,0:T(8,128)S(1)}, u32[]{:S(2)}, u32[]{:S(2)}) collective-permute-start(f32[80,64]{1,0:T(8,128)S(1)} %add.3.one), channel_id=1, source_target_pairs={{0,8},{4,12},{8,0},{12,4},{1,9},{5,13},{9,1},{13,5},{2,10},{6,14},... | collective-permute-start | bytes 61448 | tf_op jit(solution)/shard_map/ppermute | solution.py:600
  41.2 1.2 %collective-permute-start.10 = (bf16[12,16,2048]{2,1,0:T(8,128)(2,1)S(1)}, bf16[12,16,2048]{2,1,0:T(8,128)(2,1)S(1)}, u32[]{:S(2)}, u32[]{:S(2)}) collective-permute-start(bf16[12,16,2048]{2,1,0:T(8,128)(2,1)S(1)} %post.3.more.own_more), channel_id=1, source_target_pairs={{0,1},{1,0},{2,3},{3,2},{4,5},{5,4},{6,7},{7,6},{8,9},{9,8},{10,11... | collective-permute-start | bytes 2359304 | tf_op jit(solution)/shard_map/ppermute | solution.py:478
  42.4 1.1 %collective-permute-done.9.two = f32[80,64]{1,0:T(8,128)S(1)} collective-permute-done((f32[80,64]{1,0:T(8,128)S(1)}, f32[80,64]{1,0:T(8,128)S(1)}, u32[]{:S(2)}, u32[]{:S(2)}) %collective-permute-start.9) | collective-permute-done | bytes 20512 | tf_op jit(solution)/shard_map/ppermute | solution.py:600
  43.5 4.0 %collective-permute-done.11.far_more = bf16[12,16,2048]{2,1,0:T(8,128)(2,1)S(1)} collective-permute-done((bf16[12,16,2048]{2,1,0:T(8,128)(2,1)S(1)}, bf16[12,16,2048]{2,1,0:T(8,128)(2,1)S(1)}, u32[]{:S(2)}, u32[]{:S(2)}) %collective-permute-start.11) | collective-permute-done | bytes 786464 | tf_op jit(solution)/shard_map/ppermute | solution.py:478
  47.5 2.8 %collective-permute-start.12 = (bf16[12,16,2048]{2,1,0:T(8,128)(2,1)S(1)}, bf16[12,16,2048]{2,1,0:T(8,128)(2,1)S(1)}, u32[]{:S(2)}, u32[]{:S(2)}) collective-permute-start(bf16[12,16,2048]{2,1,0:T(8,128)(2,1)S(1)} %collective-permute-done.11.far_more), channel_id=1, source_target_pairs={{0,1},{1,0},{2,3},{3,2},{4,5},{5,4},{6,7},{7,6},{8,9},{9,8},{10,11... | collective-permute-start | bytes 2359304 | tf_op jit(solution)/shard_map/ppermute | solution.py:478
  50.4 2.5 %weights.1 = bf16[32,64]{1,0:T(8,128)(2,1)S(1)} custom-call(s32[3]{0:T(128)S(1)} %pad_add_fusion.pos, f32[80,64]{1,0:T(8,128)S(1)} %add.3.one, f32[80,64]{1,0:T(8,128)S(1)} %collective-permute-done.9.two), custom_call_target="tpu_custom_call" | custom-call | flops 13107200 | bytes 13107200 | tf_op jit(solution)/shard_map/weights/pallas_call | solution.py:605
  52.8 0.0 collective-permute-done.10.mate_more
  52.9 2.3 %final.1 = f32[16,2,8,2048]{3,2,1,0:T(8,128)} custom-call(bf16[32,64]{1,0:T(8,128)(2,1)S(1)} %weights.1, bf16[4,16,2048]{2,1,0:T(8,128)(2,1)S(1)} %get-tuple-element.35.one.own, bf16[4,16,2048]{2,1,0:T(8,128)(2,1)S(1)} %collective-permute-done.7.mate, bf16[4,16,2048]{2,1,0:T(8,128)(2,1)S(1)} %collective-permute-done.4.far, ...), custom_call_target="tpu_custom_call" | custom-call | flops 13107200 | bytes 13107200 | tf_op jit(solution)/shard_map/final/pallas_call | solution.py:616
  (14 shorter events, 0.0 us)
Async XLA Ops:
  0.0 8.2 %copy-start = (f32[2,2,8,2048]{3,2,1,0:T(8,128)S(1)}, f32[2,2,8,2048]{3,2,1,0:T(8,128)}, u32[]{:S(2)}) copy-start(f32[2,2,8,2048]{3,2,1,0:T(8,128)} %wind.9) | copy-start | bytes 786436
  0.0 7.8 %copy-start.2 = (f32[2048]{0:T(1024)S(1)}, f32[2048]{0:T(1024)}, u32[]{:S(2)}) copy-start(f32[2048]{0:T(1024)} %param.11) | copy-start | bytes 24580
  0.0 7.8 %copy-start.3 = (f32[2048]{0:T(1024)S(1)}, f32[2048]{0:T(1024)}, u32[]{:S(2)}) copy-start(f32[2048]{0:T(1024)} %param.10) | copy-start | bytes 24580
  0.0 7.8 %copy-start.1 = (s32[2048]{0:T(1024)S(1)}, s32[2048]{0:T(1024)}, u32[]{:S(2)}) copy-start(s32[2048]{0:T(1024)} %param.8) | copy-start | bytes 24580
  2.6 13.6 %collective-permute-start = (bf16[136,2048]{1,0:T(8,128)(2,1)S(1)}, bf16[136,2048]{1,0:T(8,128)(2,1)S(1)}, u32[]{:S(2)}, u32[]{:S(2)}) collective-permute-start(bf16[136,2048]{1,0:T(8,128)(2,1)S(1)} %get-tuple-element.26), channel_id=1, source_target_pairs={{0,4},{4,0},{8,12},{12,8},{1,5},{5,1},{9,13},{13,9},{2,6},{6,2},{1... | collective-permute-start | bytes 1671176 | tf_op jit(solution)/shard_map/ppermute | solution.py:499
  2.8 16.3 %collective-permute-start.1 = (bf16[136,2048]{1,0:T(8,128)(2,1)S(1)}, bf16[136,2048]{1,0:T(8,128)(2,1)S(1)}, u32[]{:S(2)}, u32[]{:S(2)}) collective-permute-start(bf16[136,2048]{1,0:T(8,128)(2,1)S(1)} %get-tuple-element.34), channel_id=1, source_target_pairs={{4,8},{8,4},{5,9},{9,5},{6,10},{10,6},{7,11},{11,7},{20,24},{24,20... | collective-permute-start | bytes 1671176 | tf_op jit(solution)/shard_map/ppermute | solution.py:500
  21.3 9.1 %collective-permute-start.4 = (bf16[4,16,2048]{2,1,0:T(8,128)(2,1)S(1)}, bf16[4,16,2048]{2,1,0:T(8,128)(2,1)S(1)}, u32[]{:S(2)}, u32[]{:S(2)}) collective-permute-start(bf16[4,16,2048]{2,1,0:T(8,128)(2,1)S(1)} %get-tuple-element.35.one.own), channel_id=1, source_target_pairs={{0,2},{1,3},{2,0},{3,1},{4,6},{5,7},{6,4},{7,5},{8,10},{9,11},{10,... | collective-permute-start | bytes 786440 | tf_op jit(solution)/shard_map/ppermute | solution.py:478
  26.2 4.2 %collective-permute-start.3 = (bf16[16,2048]{1,0:T(8,128)(2,1)S(1)}, bf16[16,2048]{1,0:T(8,128)(2,1)S(1)}, u32[]{:S(2)}, u32[]{:S(2)}) collective-permute-start(bf16[16,2048]{1,0:T(8,128)(2,1)S(1)} %pick.1.own), channel_id=1, source_target_pairs={{0,2},{1,3},{2,0},{3,1},{4,6},{5,7},{6,4},{7,5},{8,10},{9,11},{10,... | collective-permute-start | bytes 196616 | tf_op jit(solution)/shard_map/ppermute | solution.py:478
  30.4 17.1 %collective-permute-start.11 = (bf16[12,16,2048]{2,1,0:T(8,128)(2,1)S(1)}, bf16[12,16,2048]{2,1,0:T(8,128)(2,1)S(1)}, u32[]{:S(2)}, u32[]{:S(2)}) collective-permute-start(bf16[12,16,2048]{2,1,0:T(8,128)(2,1)S(1)} %post.3.more.own_more), channel_id=1, source_target_pairs={{0,2},{1,3},{2,0},{3,1},{4,6},{5,7},{6,4},{7,5},{8,10},{9,11},{10,... | collective-permute-start | bytes 2359304 | tf_op jit(solution)/shard_map/ppermute | solution.py:478
  30.6 9.2 %collective-permute-start.7 = (bf16[4,16,2048]{2,1,0:T(8,128)(2,1)S(1)}, bf16[4,16,2048]{2,1,0:T(8,128)(2,1)S(1)}, u32[]{:S(2)}, u32[]{:S(2)}) collective-permute-start(bf16[4,16,2048]{2,1,0:T(8,128)(2,1)S(1)} %get-tuple-element.35.one.own), channel_id=1, source_target_pairs={{0,1},{1,0},{2,3},{3,2},{4,5},{5,4},{6,7},{7,6},{8,9},{9,8},{10,11... | collective-permute-start | bytes 786440 | tf_op jit(solution)/shard_map/ppermute | solution.py:478
  33.8 5.9 %collective-permute-start.8 = (bf16[4,16,2048]{2,1,0:T(8,128)(2,1)S(1)}, bf16[4,16,2048]{2,1,0:T(8,128)(2,1)S(1)}, u32[]{:S(2)}, u32[]{:S(2)}) collective-permute-start(bf16[4,16,2048]{2,1,0:T(8,128)(2,1)S(1)} %collective-permute-done.4.far), channel_id=1, source_target_pairs={{0,1},{1,0},{2,3},{3,2},{4,5},{5,4},{6,7},{7,6},{8,9},{9,8},{10,11... | collective-permute-start | bytes 786440 | tf_op jit(solution)/shard_map/ppermute | solution.py:478
  33.8 1.6 %collective-permute-start.2 = (bf16[16,2048]{1,0:T(8,128)(2,1)S(1)}, bf16[16,2048]{1,0:T(8,128)(2,1)S(1)}, u32[]{:S(2)}, u32[]{:S(2)}) collective-permute-start(bf16[16,2048]{1,0:T(8,128)(2,1)S(1)} %pick.1.own), channel_id=1, source_target_pairs={{0,1},{1,0},{2,3},{3,2},{4,5},{5,4},{6,7},{7,6},{8,9},{9,8},{10,11... | collective-permute-start | bytes 196616 | tf_op jit(solution)/shard_map/ppermute | solution.py:478
  34.3 1.3 %collective-permute-start.5 = (bf16[16,2048]{1,0:T(8,128)(2,1)S(1)}, bf16[16,2048]{1,0:T(8,128)(2,1)S(1)}, u32[]{:S(2)}, u32[]{:S(2)}) collective-permute-start(bf16[16,2048]{1,0:T(8,128)(2,1)S(1)} %collective-permute-done.3.far), channel_id=1, source_target_pairs={{0,1},{1,0},{2,3},{3,2},{4,5},{5,4},{6,7},{7,6},{8,9},{9,8},{10,11... | collective-permute-start | bytes 196616 | tf_op jit(solution)/shard_map/ppermute | solution.py:478
  36.5 3.2 %collective-permute-start.6 = (f32[80,64]{1,0:T(8,128)S(1)}, f32[80,64]{1,0:T(8,128)S(1)}, u32[]{:S(2)}, u32[]{:S(2)}) collective-permute-start(f32[80,64]{1,0:T(8,128)S(1)} %gram.1), channel_id=1, source_target_pairs={{0,4},{4,0},{8,12},{12,8},{1,5},{5,1},{9,13},{13,9},{2,6},{6,2},{1... | collective-permute-start | bytes 61448 | tf_op jit(solution)/shard_map/ppermute | solution.py:600
  39.7 3.8 %collective-permute-start.9 = (f32[80,64]{1,0:T(8,128)S(1)}, f32[80,64]{1,0:T(8,128)S(1)}, u32[]{:S(2)}, u32[]{:S(2)}) collective-permute-start(f32[80,64]{1,0:T(8,128)S(1)} %add.3.one), channel_id=1, source_target_pairs={{0,8},{4,12},{8,0},{12,4},{1,9},{5,13},{9,1},{13,5},{2,10},{6,14},... | collective-permute-start | bytes 61448 | tf_op jit(solution)/shard_map/ppermute | solution.py:600
  41.2 11.6 %collective-permute-start.10 = (bf16[12,16,2048]{2,1,0:T(8,128)(2,1)S(1)}, bf16[12,16,2048]{2,1,0:T(8,128)(2,1)S(1)}, u32[]{:S(2)}, u32[]{:S(2)}) collective-permute-start(bf16[12,16,2048]{2,1,0:T(8,128)(2,1)S(1)} %post.3.more.own_more), channel_id=1, source_target_pairs={{0,1},{1,0},{2,3},{3,2},{4,5},{5,4},{6,7},{7,6},{8,9},{9,8},{10,11... | collective-permute-start | bytes 2359304 | tf_op jit(solution)/shard_map/ppermute | solution.py:478
  47.5 5.4 %collective-permute-start.12 = (bf16[12,16,2048]{2,1,0:T(8,128)(2,1)S(1)}, bf16[12,16,2048]{2,1,0:T(8,128)(2,1)S(1)}, u32[]{:S(2)}, u32[]{:S(2)}) collective-permute-start(bf16[12,16,2048]{2,1,0:T(8,128)(2,1)S(1)} %collective-permute-done.11.far_more), channel_id=1, source_target_pairs={{0,1},{1,0},{2,3},{3,2},{4,5},{5,4},{6,7},{7,6},{8,9},{9,8},{10,11... | collective-permute-start | bytes 2359304 | tf_op jit(solution)/shard_map/ppermute | solution.py:478

commit v8 on v7

--- a/solution.py
+++ b/solution.py
@@ -171,20 +171,28 @@
 def pack_kernel(
     pos, prior, wind, turned_0, turned_1, pay_a, pay_b, state, edge, sems
 ):
-    winds = pltpu.make_async_copy(wind.at[0], edge, sems.at[2])
-    loads = [pltpu.make_async_copy(prior.at[:, f], state.at[f], sems.at[f]) for f in range(2)]
-    loads[0].start()
+    winds = pltpu.make_async_copy(wind.at[0], edge, sems.at[4])
+    loads = {}
+    for f in range(2):
+        for g in range(2):
+            span = slice(8 * g, 8 * g + 8)
+            loads[f, g] = pltpu.make_async_copy(
+                prior.at[span, f], state.at[f, span], sems.at[2 * f + g]
+            )
+            loads[f, g].start()
     winds.start()
-    loads[1].start()
     even = (pos[0] % 2) == 0
     start_a = jnp.where(even, 4, 0)
     start_b = 4 - start_a
     cols = state.shape[3]
+    blank_edges(turned_0)
+    blank_edges(turned_1)
     for f in range(2):
         turned = (turned_0, turned_1)[f]
-        blank_edges(turned)
-        loads[f].wait()
-        turned[2:10, :, :cols] = jnp.swapaxes(state[f], 0, 1)
+        for g in range(2):
+            span = slice(8 * g, 8 * g + 8)
+            loads[f, g].wait()
+            turned[2:10, span, :cols] = jnp.swapaxes(state[f, span], 0, 1)
         for r in range(4):
             at = (f * 4 + r) * 16
             pay_a[at : at + 16, :] = turned[2 + start_a + r, :, :cols].astype(BF)
@@ -440,27 +448,45 @@
     swap2 = jnp.concatenate([mine[:, 32:64], mine[:, 0:32]], 1)
     mine = jnp.where(pos[2] >= 2, swap2, mine)
     high = mine.astype(BF).astype(F32)
-    out[...] = jnp.concatenate([high, mine - high], 0).astype(BF)
+    pair = jnp.concatenate([high, mine - high], 0)
+    blank = jnp.zeros((32, 64), F32)
+    for r in range(4):
+        line = [pair if k == r else blank for k in range(4)]
+        out[r * 32 : r * 32 + 32, :] = jnp.concatenate(line, 1).astype(BF)
 
 
 def final_kernel(
     weights, own, mate, far, diag, own_more, mate_more, far_more, diag_more, out, keep, ready, sems
 ):
-    m = weights[...]
     copies = []
+    cols = own.shape[2]
+    step = 512
+    half = cols // 2
     for f in range(2):
-        for r in range(8):
-            first = f == 0 and r < 4
-            refs = (own, mate, far, diag) if first else (own_more, mate_more, far_more, diag_more)
-            at = r if first else f * 8 + r - 4
-            state = jnp.concatenate([v[at] for v in refs], 0)
-            both = jnp.dot(m, state, preferred_element_type=F32)
-            keep[r] = both[0:16] + both[16:32]
-        ready[f] = jnp.swapaxes(keep[...], 0, 1)
-        copies.append(pltpu.make_async_copy(ready.at[f], out.at[:, f], sems.at[f]))
-        copies[f].start()
-    for f in range(2):
-        copies[f].wait()
+        for part in range(2):
+            span = slice(part * half, part * half + half)
+            for base in (0, 4):
+                first = f == 0 and base == 0
+                refs = (own, mate, far, diag) if first else (own_more, mate_more, far_more, diag_more)
+                at = 0 if first else f * 8 + base - 4
+                for c in range(part * half, part * half + half, step):
+                    cut = slice(c, c + step)
+                    parts = [v[at + r, :, cut] for r in range(4) for v in refs]
+                    both = jnp.dot(
+                        weights[...], jnp.concatenate(parts, 0), preferred_element_type=F32
+                    )
+                    for r in range(4):
+                        high = both[r * 32 : r * 32 + 16]
+                        keep[base + r, :, cut] = high + both[r * 32 + 16 : r * 32 + 32]
+            ready[f, :, :, span] = jnp.swapaxes(keep[:, :, span], 0, 1)
+            copies.append(
+                pltpu.make_async_copy(
+                    ready.at[f, :, :, span], out.at[:, f, :, span], sems.at[2 * f + part]
+                )
+            )
+            copies[-1].start()
+    for copy in copies:
+        copy.wait()
 
 
 def local(prior_replicas, wind_field, obs_index, obs_count, obs_value, obs_weight):
@@ -491,7 +517,7 @@
         scratch_shapes=[
             pltpu.VMEM((2, 16, 8, cols), F32),
             pltpu.VMEM((2, 8, cols), F32),
-            pltpu.SemaphoreType.DMA((3,)),
+            pltpu.SemaphoreType.DMA((5,)),
         ],
         compiler_params=params(),
     )(pos, prior_here, wind_here)
@@ -608,7 +634,7 @@
         cost_estimate=cost(400 * 64 * 128 * 4),
         in_specs=[smem(), vmem(), vmem()],
         out_specs=vmem(),
-        out_shape=shape((32, 64), BF),
+        out_shape=shape((128, 256), BF),
         scratch_shapes=[pltpu.VMEM((64, 64), F32)],
         compiler_params=params(),
     )(pos, part, other)
@@ -623,7 +649,7 @@
         scratch_shapes=[
             pltpu.VMEM((8, 16, cols), F32),
             pltpu.VMEM((2, 16, 8, cols), F32),
-            pltpu.SemaphoreType.DMA((2,)),
+            pltpu.SemaphoreType.DMA((4,)),
         ],
         compiler_params=params(),
     )(

time: 55.3 us -> 54.9 us (level)
  no operation moved by 1% of the time
where the time goes in v8:
time: 54.9 us; the launch traced here: 54.7 us
  Pallas kernels  22.5 us (41%)
  starting transfers between devices  15.7 us (29%)
  waiting for transfers between devices  15.6 us (28%)
  between operations  0.81 us (1%)
    ppermute x9, starting transfers between devices, swap(): return lax.ppermute(value, 'mem', [(i, i ^ bits) for i in range(4)])  9.54 us
    ppermute x9, waiting for transfers between devices, swap(): return lax.ppermute(value, 'mem', [(i, i ^ bits) for i in range(4)])  8.21 us
    pallas_call x2, Pallas kernels, pre(): pl.pallas_call(functools.partial(pre_kernel, DIFFUSION[f]), name='pre', c...  7.74 us
    ppermute x1, starting transfers between devices, local(): recv_b = lax.ppermute(packed[3], 'space', pairs_b)  4.32 us
    pallas_call x2, Pallas kernels, post(): pl.pallas_call(functools.partial(post_kernel, f), name='post', cost_estim...  4.29 us
    ppermute x2, waiting for transfers between devices, local(): other = lax.ppermute(part, 'space', [(i, i ^ bits) for i in range(strips)])  4.26 us
    ppermute x1, waiting for transfers between devices, local(): recv_b = lax.ppermute(packed[3], 'space', pairs_b)  3.02 us
    pallas_call x1, Pallas kernels, local(): pl.pallas_call(weights_kernel, name='weights', cost_estimate=cost(400 * 6...  2.57 us
  transfers between devices with their start and end apart: 13, of which 8 were waited for; matrix products, arithmetic and copies ran while one was open for 0% of the time, Pallas kernels for 29%

profile of v8, /device:TPU:11, one launch (start us, length us, event | category | flops | bytes accessed | tf_op | source)
XLA Modules:
  0.0 54.7 jit_solution(3997744763036741889)
XLA Ops:
  0.0 0.1 pad_add_fusion.pos
  0.1 2.4 %pack.1 = (f32[12,16,2176]{2,1,0:T(8,128)S(1)}, f32[12,16,2176]{2,1,0:T(8,128)S(1)}, bf16[136,2048]{1,0:T(8,128)(2,1)S(1)}, bf16[136,2048]{1,0:T(8,128)(2,1)S(1)}) custom-call(s32[3]{0:T(128)S(1)} %pad_add_fusion.pos, f32[16,2,8,2048]{3,2,1,0:T(8,128)} %prior.1, f32[2,2,8,2048]{3,2,1,0:T(8,128)} %wind.9), custom_call_target="tpu_custom_call" | custom-call | flops 10485760 | bytes 10485760 | tf_op jit(solution)/shard_map/pack/pallas_call | solution.py:509
  2.5 0.2 collective-permute-start
  2.7 4.3 %collective-permute-start.1 = (bf16[136,2048]{1,0:T(8,128)(2,1)S(1)}, bf16[136,2048]{1,0:T(8,128)(2,1)S(1)}, u32[]{:S(2)}, u32[]{:S(2)}) collective-permute-start(bf16[136,2048]{1,0:T(8,128)(2,1)S(1)} %get-tuple-element.34), channel_id=1, source_target_pairs={{4,8},{8,4},{5,9},{9,5},{6,10},{10,6},{7,11},{11,7},{20,24},{24,20... | collective-permute-start | bytes 1671176 | tf_op jit(solution)/shard_map/ppermute | solution.py:526
  7.7 0.4 slots.1
  8.1 3.9 %pre.2.begun = f32[8,16,2048]{2,1,0:T(8,128)S(1)} custom-call(f32[12,16,2176]{2,1,0:T(8,128)S(1)} %get-tuple-element.27.turned, f32[2,2,8,2048]{3,2,1,0:T(8,128)S(1)} %copy-done), custom_call_target="tpu_custom_call" | custom-call | flops 19660800 | bytes 19660800 | tf_op jit(solution)/shard_map/pre/pallas_call | solution.py:529
  12.0 3.9 %pre.3.begun = f32[8,16,2048]{2,1,0:T(8,128)S(1)} custom-call(f32[12,16,2176]{2,1,0:T(8,128)S(1)} %get-tuple-element.28.turned, f32[2,2,8,2048]{3,2,1,0:T(8,128)S(1)} %copy-done), custom_call_target="tpu_custom_call" | custom-call | flops 19660800 | bytes 19660800 | tf_op jit(solution)/shard_map/pre/pallas_call | solution.py:529
  15.9 0.2 collective-permute-done.recv_a
  16.0 3.0 %collective-permute-done.1.recv_b = bf16[136,2048]{1,0:T(8,128)(2,1)S(1)} collective-permute-done((bf16[136,2048]{1,0:T(8,128)(2,1)S(1)}, bf16[136,2048]{1,0:T(8,128)(2,1)S(1)}, u32[]{:S(2)}, u32[]{:S(2)}) %collective-permute-start.1) | collective-permute-done | bytes 557088 | tf_op jit(solution)/shard_map/ppermute | solution.py:526
  19.1 2.1 %post.2 = (bf16[4,16,2048]{2,1,0:T(8,128)(2,1)S(1)}, bf16[4,16,2048]{2,1,0:T(8,128)(2,1)S(1)}) custom-call(s32[3]{0:T(128)S(1)} %pad_add_fusion.pos, f32[12,16,2176]{2,1,0:T(8,128)S(1)} %get-tuple-element.27.turned, f32[8,16,2048]{2,1,0:T(8,128)S(1)} %pre.2.begun, bf16[136,2048]{1,0:T(8,128)(2,1)S(1)} %collective-permute-done.recv_a, ...), custom_call_target="tpu_custom_call" | custom-call | flops 8 | bytes 8 | tf_op jit(solution)/shard_map/post/pallas_call | solution.py:572
  21.2 0.3 collective-permute-start.4
  21.5 2.2 %post.3.more.own_more = bf16[12,16,2048]{2,1,0:T(8,128)(2,1)S(1)} custom-call(s32[3]{0:T(128)S(1)} %pad_add_fusion.pos, f32[12,16,2176]{2,1,0:T(8,128)S(1)} %get-tuple-element.28.turned, f32[8,16,2048]{2,1,0:T(8,128)S(1)} %pre.3.begun, bf16[136,2048]{1,0:T(8,128)(2,1)S(1)} %collective-permute-done.recv_a, ...), custom_call_target="tpu_custom_call" | custom-call | flops 8 | bytes 8 | tf_op jit(solution)/shard_map/post/pallas_call | solution.py:572
  23.7 2.4 %pick.1.own = bf16[16,2048]{1,0:T(8,128)(2,1)S(1)} custom-call(bf16[512,2048]{1,0:T(8,128)(2,1)S(1)} %get-tuple-element.30.place, s32[16,2048]{1,0:T(8,128)S(1)} %get-tuple-element.31.chunk, bf16[4,16,2048]{2,1,0:T(8,128)(2,1)S(1)} %get-tuple-element.35.one.own, bf16[12,16,2048]{2,1,0:T(8,128)(2,1)S(1)} %post.3.more.own_more), custom_call_target="tpu_custom_call" | custom-call | flops 8 | bytes 8 | tf_op jit(solution)/shard_map/pick/pallas_call | solution.py:589
  26.1 1.3 %collective-permute-start.3 = (bf16[16,2048]{1,0:T(8,128)(2,1)S(1)}, bf16[16,2048]{1,0:T(8,128)(2,1)S(1)}, u32[]{:S(2)}, u32[]{:S(2)}) collective-permute-start(bf16[16,2048]{1,0:T(8,128)(2,1)S(1)} %pick.1.own), channel_id=1, source_target_pairs={{0,2},{1,3},{2,0},{3,1},{4,6},{5,7},{6,4},{7,5},{8,10},{9,11},{10,... | collective-permute-start | bytes 196616 | tf_op jit(solution)/shard_map/ppermute | solution.py:504
  27.3 3.0 %collective-permute-done.3.far = bf16[16,2048]{1,0:T(8,128)(2,1)S(1)} collective-permute-done((bf16[16,2048]{1,0:T(8,128)(2,1)S(1)}, bf16[16,2048]{1,0:T(8,128)(2,1)S(1)}, u32[]{:S(2)}, u32[]{:S(2)}) %collective-permute-start.3) | collective-permute-done | bytes 65568 | tf_op jit(solution)/shard_map/ppermute | solution.py:504
  30.3 0.2 collective-permute-start.11
  30.5 3.3 %collective-permute-start.7 = (bf16[4,16,2048]{2,1,0:T(8,128)(2,1)S(1)}, bf16[4,16,2048]{2,1,0:T(8,128)(2,1)S(1)}, u32[]{:S(2)}, u32[]{:S(2)}) collective-permute-start(bf16[4,16,2048]{2,1,0:T(8,128)(2,1)S(1)} %get-tuple-element.35.one.own), channel_id=1, source_target_pairs={{0,1},{1,0},{2,3},{3,2},{4,5},{5,4},{6,7},{7,6},{8,9},{9,8},{10,11... | collective-permute-start | bytes 786440 | tf_op jit(solution)/shard_map/ppermute | solution.py:504
  33.7 0.0 collective-permute-start.8
  33.7 0.5 collective-permute-start.2
  34.2 1.1 %collective-permute-done.2.mate = bf16[16,2048]{1,0:T(8,128)(2,1)S(1)} collective-permute-done((bf16[16,2048]{1,0:T(8,128)(2,1)S(1)}, bf16[16,2048]{1,0:T(8,128)(2,1)S(1)}, u32[]{:S(2)}, u32[]{:S(2)}) %collective-permute-start.2) | collective-permute-done | bytes 65568 | tf_op jit(solution)/shard_map/ppermute | solution.py:504
  35.3 0.1 collective-permute-done.5.diag
  35.5 0.9 %gram.1 = f32[80,64]{1,0:T(8,128)S(1)} custom-call(s32[3]{0:T(128)S(1)} %pad_add_fusion.pos, bf16[16,2048]{1,0:T(8,128)(2,1)S(1)} %pick.1.own, bf16[16,2048]{1,0:T(8,128)(2,1)S(1)} %collective-permute-done.2.mate, bf16[16,2048]{1,0:T(8,128)(2,1)S(1)} %collective-permute-done.3.far, bf16[16,2048]{1,0:T(8,128)(2,1)S(1)} %collective-permute-done.5.diag, ...), custom_call_target="tpu_custom_call" | custom-call | flops 3145728 | bytes 3145728 | tf_op jit(solution)/shard_map/gram/pallas_call | solution.py:606
  36.4 0.1 collective-permute-start.6
  36.5 3.1 %collective-permute-done.6 = f32[80,64]{1,0:T(8,128)S(1)} collective-permute-done((f32[80,64]{1,0:T(8,128)S(1)}, f32[80,64]{1,0:T(8,128)S(1)}, u32[]{:S(2)}, u32[]{:S(2)}) %collective-permute-start.6) | collective-permute-done | bytes 20512 | tf_op jit(solution)/shard_map/ppermute | solution.py:626
  39.6 1.5 %collective-permute-start.9 = (f32[80,64]{1,0:T(8,128)S(1)}, f32[80,64]{1,0:T(8,128)S(1)}, u32[]{:S(2)}, u32[]{:S(2)}) collective-permute-start(f32[80,64]{1,0:T(8,128)S(1)} %add.3.one), channel_id=1, source_target_pairs={{0,8},{4,12},{8,0},{12,4},{1,9},{5,13},{9,1},{13,5},{2,10},{6,14},... | collective-permute-start | bytes 61448 | tf_op jit(solution)/shard_map/ppermute | solution.py:626
  41.1 1.2 %collective-permute-start.10 = (bf16[12,16,2048]{2,1,0:T(8,128)(2,1)S(1)}, bf16[12,16,2048]{2,1,0:T(8,128)(2,1)S(1)}, u32[]{:S(2)}, u32[]{:S(2)}) collective-permute-start(bf16[12,16,2048]{2,1,0:T(8,128)(2,1)S(1)} %post.3.more.own_more), channel_id=1, source_target_pairs={{0,1},{1,0},{2,3},{3,2},{4,5},{5,4},{6,7},{7,6},{8,9},{9,8},{10,11... | collective-permute-start | bytes 2359304 | tf_op jit(solution)/shard_map/ppermute | solution.py:504
  42.3 1.1 %collective-permute-done.9.two = f32[80,64]{1,0:T(8,128)S(1)} collective-permute-done((f32[80,64]{1,0:T(8,128)S(1)}, f32[80,64]{1,0:T(8,128)S(1)}, u32[]{:S(2)}, u32[]{:S(2)}) %collective-permute-start.9) | collective-permute-done | bytes 20512 | tf_op jit(solution)/shard_map/ppermute | solution.py:626
  43.4 4.0 %collective-permute-done.11.far_more = bf16[12,16,2048]{2,1,0:T(8,128)(2,1)S(1)} collective-permute-done((bf16[12,16,2048]{2,1,0:T(8,128)(2,1)S(1)}, bf16[12,16,2048]{2,1,0:T(8,128)(2,1)S(1)}, u32[]{:S(2)}, u32[]{:S(2)}) %collective-permute-start.11) | collective-permute-done | bytes 786464 | tf_op jit(solution)/shard_map/ppermute | solution.py:504
  47.4 2.8 %collective-permute-start.12 = (bf16[12,16,2048]{2,1,0:T(8,128)(2,1)S(1)}, bf16[12,16,2048]{2,1,0:T(8,128)(2,1)S(1)}, u32[]{:S(2)}, u32[]{:S(2)}) collective-permute-start(bf16[12,16,2048]{2,1,0:T(8,128)(2,1)S(1)} %collective-permute-done.11.far_more), channel_id=1, source_target_pairs={{0,1},{1,0},{2,3},{3,2},{4,5},{5,4},{6,7},{7,6},{8,9},{9,8},{10,11... | collective-permute-start | bytes 2359304 | tf_op jit(solution)/shard_map/ppermute | solution.py:504
  50.3 2.6 %weights.1 = bf16[128,256]{1,0:T(8,128)(2,1)S(1)} custom-call(s32[3]{0:T(128)S(1)} %pad_add_fusion.pos, f32[80,64]{1,0:T(8,128)S(1)} %add.3.one, f32[80,64]{1,0:T(8,128)S(1)} %collective-permute-done.9.two), custom_call_target="tpu_custom_call" | custom-call | flops 13107200 | bytes 13107200 | tf_op jit(solution)/shard_map/weights/pallas_call | solution.py:631
  52.8 0.0 collective-permute-done.10.mate_more
  52.8 1.9 %final.1 = f32[16,2,8,2048]{3,2,1,0:T(8,128)} custom-call(bf16[128,256]{1,0:T(8,128)(2,1)S(1)} %weights.1, bf16[4,16,2048]{2,1,0:T(8,128)(2,1)S(1)} %get-tuple-element.35.one.own, bf16[4,16,2048]{2,1,0:T(8,128)(2,1)S(1)} %collective-permute-done.7.mate, bf16[4,16,2048]{2,1,0:T(8,128)(2,1)S(1)} %collective-permute-done.4.far, ...), custom_call_target="tpu_custom_call" | custom-call | flops 13107200 | bytes 13107200 | tf_op jit(solution)/shard_map/final/pallas_call | solution.py:642
  (14 shorter events, 0.0 us)
Async XLA Ops:
  0.0 8.1 %copy-start = (f32[2,2,8,2048]{3,2,1,0:T(8,128)S(1)}, f32[2,2,8,2048]{3,2,1,0:T(8,128)}, u32[]{:S(2)}) copy-start(f32[2,2,8,2048]{3,2,1,0:T(8,128)} %wind.9) | copy-start | bytes 786436
  0.0 7.7 %copy-start.2 = (f32[2048]{0:T(1024)S(1)}, f32[2048]{0:T(1024)}, u32[]{:S(2)}) copy-start(f32[2048]{0:T(1024)} %param.11) | copy-start | bytes 24580
  0.0 7.7 %copy-start.3 = (f32[2048]{0:T(1024)S(1)}, f32[2048]{0:T(1024)}, u32[]{:S(2)}) copy-start(f32[2048]{0:T(1024)} %param.10) | copy-start | bytes 24580
  0.0 7.7 %copy-start.1 = (s32[2048]{0:T(1024)S(1)}, s32[2048]{0:T(1024)}, u32[]{:S(2)}) copy-start(s32[2048]{0:T(1024)} %param.8) | copy-start | bytes 24580
  2.5 13.6 %collective-permute-start = (bf16[136,2048]{1,0:T(8,128)(2,1)S(1)}, bf16[136,2048]{1,0:T(8,128)(2,1)S(1)}, u32[]{:S(2)}, u32[]{:S(2)}) collective-permute-start(bf16[136,2048]{1,0:T(8,128)(2,1)S(1)} %get-tuple-element.26), channel_id=1, source_target_pairs={{0,4},{4,0},{8,12},{12,8},{1,5},{5,1},{9,13},{13,9},{2,6},{6,2},{1... | collective-permute-start | bytes 1671176 | tf_op jit(solution)/shard_map/ppermute | solution.py:525
  2.7 16.3 %collective-permute-start.1 = (bf16[136,2048]{1,0:T(8,128)(2,1)S(1)}, bf16[136,2048]{1,0:T(8,128)(2,1)S(1)}, u32[]{:S(2)}, u32[]{:S(2)}) collective-permute-start(bf16[136,2048]{1,0:T(8,128)(2,1)S(1)} %get-tuple-element.34), channel_id=1, source_target_pairs={{4,8},{8,4},{5,9},{9,5},{6,10},{10,6},{7,11},{11,7},{20,24},{24,20... | collective-permute-start | bytes 1671176 | tf_op jit(solution)/shard_map/ppermute | solution.py:526
  21.2 9.1 %collective-permute-start.4 = (bf16[4,16,2048]{2,1,0:T(8,128)(2,1)S(1)}, bf16[4,16,2048]{2,1,0:T(8,128)(2,1)S(1)}, u32[]{:S(2)}, u32[]{:S(2)}) collective-permute-start(bf16[4,16,2048]{2,1,0:T(8,128)(2,1)S(1)} %get-tuple-element.35.one.own), channel_id=1, source_target_pairs={{0,2},{1,3},{2,0},{3,1},{4,6},{5,7},{6,4},{7,5},{8,10},{9,11},{10,... | collective-permute-start | bytes 786440 | tf_op jit(solution)/shard_map/ppermute | solution.py:504
  26.1 4.2 %collective-permute-start.3 = (bf16[16,2048]{1,0:T(8,128)(2,1)S(1)}, bf16[16,2048]{1,0:T(8,128)(2,1)S(1)}, u32[]{:S(2)}, u32[]{:S(2)}) collective-permute-start(bf16[16,2048]{1,0:T(8,128)(2,1)S(1)} %pick.1.own), channel_id=1, source_target_pairs={{0,2},{1,3},{2,0},{3,1},{4,6},{5,7},{6,4},{7,5},{8,10},{9,11},{10,... | collective-permute-start | bytes 196616 | tf_op jit(solution)/shard_map/ppermute | solution.py:504
  30.3 17.1 %collective-permute-start.11 = (bf16[12,16,2048]{2,1,0:T(8,128)(2,1)S(1)}, bf16[12,16,2048]{2,1,0:T(8,128)(2,1)S(1)}, u32[]{:S(2)}, u32[]{:S(2)}) collective-permute-start(bf16[12,16,2048]{2,1,0:T(8,128)(2,1)S(1)} %post.3.more.own_more), channel_id=1, source_target_pairs={{0,2},{1,3},{2,0},{3,1},{4,6},{5,7},{6,4},{7,5},{8,10},{9,11},{10,... | collective-permute-start | bytes 2359304 | tf_op jit(solution)/shard_map/ppermute | solution.py:504
  30.5 9.2 %collective-permute-start.7 = (bf16[4,16,2048]{2,1,0:T(8,128)(2,1)S(1)}, bf16[4,16,2048]{2,1,0:T(8,128)(2,1)S(1)}, u32[]{:S(2)}, u32[]{:S(2)}) collective-permute-start(bf16[4,16,2048]{2,1,0:T(8,128)(2,1)S(1)} %get-tuple-element.35.one.own), channel_id=1, source_target_pairs={{0,1},{1,0},{2,3},{3,2},{4,5},{5,4},{6,7},{7,6},{8,9},{9,8},{10,11... | collective-permute-start | bytes 786440 | tf_op jit(solution)/shard_map/ppermute | solution.py:504
  33.7 5.9 %collective-permute-start.8 = (bf16[4,16,2048]{2,1,0:T(8,128)(2,1)S(1)}, bf16[4,16,2048]{2,1,0:T(8,128)(2,1)S(1)}, u32[]{:S(2)}, u32[]{:S(2)}) collective-permute-start(bf16[4,16,2048]{2,1,0:T(8,128)(2,1)S(1)} %collective-permute-done.4.far), channel_id=1, source_target_pairs={{0,1},{1,0},{2,3},{3,2},{4,5},{5,4},{6,7},{7,6},{8,9},{9,8},{10,11... | collective-permute-start | bytes 786440 | tf_op jit(solution)/shard_map/ppermute | solution.py:504
  33.7 1.6 %collective-permute-start.2 = (bf16[16,2048]{1,0:T(8,128)(2,1)S(1)}, bf16[16,2048]{1,0:T(8,128)(2,1)S(1)}, u32[]{:S(2)}, u32[]{:S(2)}) collective-permute-start(bf16[16,2048]{1,0:T(8,128)(2,1)S(1)} %pick.1.own), channel_id=1, source_target_pairs={{0,1},{1,0},{2,3},{3,2},{4,5},{5,4},{6,7},{7,6},{8,9},{9,8},{10,11... | collective-permute-start | bytes 196616 | tf_op jit(solution)/shard_map/ppermute | solution.py:504
  34.2 1.3 %collective-permute-start.5 = (bf16[16,2048]{1,0:T(8,128)(2,1)S(1)}, bf16[16,2048]{1,0:T(8,128)(2,1)S(1)}, u32[]{:S(2)}, u32[]{:S(2)}) collective-permute-start(bf16[16,2048]{1,0:T(8,128)(2,1)S(1)} %collective-permute-done.3.far), channel_id=1, source_target_pairs={{0,1},{1,0},{2,3},{3,2},{4,5},{5,4},{6,7},{7,6},{8,9},{9,8},{10,11... | collective-permute-start | bytes 196616 | tf_op jit(solution)/shard_map/ppermute | solution.py:504
  36.4 3.2 %collective-permute-start.6 = (f32[80,64]{1,0:T(8,128)S(1)}, f32[80,64]{1,0:T(8,128)S(1)}, u32[]{:S(2)}, u32[]{:S(2)}) collective-permute-start(f32[80,64]{1,0:T(8,128)S(1)} %gram.1), channel_id=1, source_target_pairs={{0,4},{4,0},{8,12},{12,8},{1,5},{5,1},{9,13},{13,9},{2,6},{6,2},{1... | collective-permute-start | bytes 61448 | tf_op jit(solution)/shard_map/ppermute | solution.py:626
  39.6 3.8 %collective-permute-start.9 = (f32[80,64]{1,0:T(8,128)S(1)}, f32[80,64]{1,0:T(8,128)S(1)}, u32[]{:S(2)}, u32[]{:S(2)}) collective-permute-start(f32[80,64]{1,0:T(8,128)S(1)} %add.3.one), channel_id=1, source_target_pairs={{0,8},{4,12},{8,0},{12,4},{1,9},{5,13},{9,1},{13,5},{2,10},{6,14},... | collective-permute-start | bytes 61448 | tf_op jit(solution)/shard_map/ppermute | solution.py:626
  41.1 11.7 %collective-permute-start.10 = (bf16[12,16,2048]{2,1,0:T(8,128)(2,1)S(1)}, bf16[12,16,2048]{2,1,0:T(8,128)(2,1)S(1)}, u32[]{:S(2)}, u32[]{:S(2)}) collective-permute-start(bf16[12,16,2048]{2,1,0:T(8,128)(2,1)S(1)} %post.3.more.own_more), channel_id=1, source_target_pairs={{0,1},{1,0},{2,3},{3,2},{4,5},{5,4},{6,7},{7,6},{8,9},{9,8},{10,11... | collective-permute-start | bytes 2359304 | tf_op jit(solution)/shard_map/ppermute | solution.py:504
  47.4 5.4 %collective-permute-start.12 = (bf16[12,16,2048]{2,1,0:T(8,128)(2,1)S(1)}, bf16[12,16,2048]{2,1,0:T(8,128)(2,1)S(1)}, u32[]{:S(2)}, u32[]{:S(2)}) collective-permute-start(bf16[12,16,2048]{2,1,0:T(8,128)(2,1)S(1)} %collective-permute-done.11.far_more), channel_id=1, source_target_pairs={{0,1},{1,0},{2,3},{3,2},{4,5},{5,4},{6,7},{7,6},{8,9},{9,8},{10,11... | collective-permute-start | bytes 2359304 | tf_op jit(solution)/shard_map/ppermute | solution.py:504

commit v9 on v8

--- a/solution.py
+++ b/solution.py
@@ -208,7 +208,7 @@
     pay_b[128:136, :] = jnp.where(even, first, last).astype(BF)
 
 
-def slots_kernel(index, count, weight, value, place, chunk, root_out, rooted_out):
+def slots_kernel(parts, pos, index, count, weight, value, place, chunk, root_out, rooted_out):
     slots = index.shape[1]
     width = place.shape[0]
     n = index[...]
@@ -216,7 +216,12 @@
     root = jnp.where(used, jnp.sqrt(weight[...]), 0.0)
     root_out[...] = root
     rooted_out[...] = root * value[...]
-    chunk[...] = jnp.broadcast_to(n // width, (16, slots))
+    cell = n // width
+    row = (cell // parts) % 8
+    first = jnp.where((pos[0] % 2) == 0, 1, 0)
+    phase = jnp.where(row // 4 == first, 0, 1)
+    stand = (phase * 2 + cell // (8 * parts)) * 4 + row % 4
+    chunk[...] = jnp.broadcast_to(stand * parts + cell % parts, (16, slots))
     column = n % width
     step = 64
     for r in range(0, width, step):
@@ -306,30 +311,28 @@
     lax.fori_loop(0, 8, second_step, 0)
 
 
-def post_kernel(field, pos, turned, begun, recv_a, recv_b, wind, *refs):
-    outs = refs[-4:-2] if field == 0 else refs[-3:-2]
-    halo, delta = refs[-2:]
+def post_kernel(field, phase, pos, turned, begun, recv, wind, *refs):
+    out, halo, delta = refs[-3:]
+    ahead = refs[0] if len(refs) == 4 else None
     nu = DIFFUSION[field]
     cols = begun.shape[2]
     even = (pos[0] % 2) == 0
-    start_a = jnp.where(even, 4, 0)
-    start_b = 4 - start_a
     blank = jnp.zeros((16, PAD), F32)
-    for r in range(8):
+    start = 0
+    if ahead is not None:
+        start = ahead.shape[0]
+        out[0:start] = ahead[...]
+    for r in range(4):
+        at = (field * 4 + r) * 16
+        halo[r, :, :cols] = recv[at : at + 16, :].astype(F32)
         halo[r, :, cols:] = blank
         delta[r, :, cols:] = blank
-    for r in range(4):
-        at = (field * 4 + r) * 16
-        halo[start_a + r, :, :cols] = recv_a[at : at + 16, :].astype(F32)
-        halo[start_b + r, :, :cols] = recv_b[at : at + 16, :].astype(F32)
-    got_a = recv_a[128:136, :].astype(F32)
-    got_a = got_a[0:4] + got_a[4:8]
-    got_b = recv_b[128:136, :].astype(F32)
-    got_b = got_b[0:4] + got_b[4:8]
-    top = jnp.where(pos[0] == 0, 0.0, 1.0)
-    bottom = jnp.where(pos[0] == pos[1] - 1, 0.0, 1.0)
-    before = jnp.where(even, got_b, got_a) * TWELFTH
-    after = jnp.where(even, got_a, got_b) * TWELFTH
+    outer = recv[128:136, :].astype(F32)
+    outer = (outer[0:4] + outer[4:8]) * TWELFTH
+    scale = (
+        jnp.where(pos[0] == 0, 0.0, 1.0),
+        jnp.where(pos[0] == pos[1] - 1, 0.0, 1.0),
+    )
 
     def broad(row):
         return jnp.broadcast_to(row, (8, cols))
@@ -337,50 +340,48 @@
     def own_wind(step, c, r):
         return broad(wind[step, c, r : r + 1] * TWELFTH)
 
-    for g in range(2):
-        span = slice(g * 8, g * 8 + 8)
-        h = lambda i: halo[i, span, :]
-        x = lambda r: turned[2 + r, span, :]
-        for i in range(2):
-            rows = [h(0), h(1), h(2), h(3), x(0)] if i == 0 else [h(1), h(2), h(3), x(0), x(1)]
-            value = stencil_row(rows, broad(before[i : i + 1]), broad(before[2 + i : 3 + i]), nu)
-            delta[i, span, :cols] = value * top
-            rows = [x(6), x(7), h(4), h(5), h(6)] if i == 0 else [x(7), h(4), h(5), h(6), h(7)]
-            value = stencil_row(rows, broad(after[i : i + 1]), broad(after[2 + i : 3 + i]), nu)
-            delta[6 + i, span, :cols] = value * bottom
-        near = (
-            (2, 0, [h(2), h(3), None, None, None]),
-            (3, 1, [h(3), None, None, None, None]),
-            (4, 6, [None, None, None, None, h(4)]),
-            (5, 7, [None, None, None, h(4), h(5)]),
-        )
-        for at, r, rows in near:
-            delta[at, span, :cols] = stencil_row(rows, own_wind(0, 0, r), None, nu)
-
-    for r in range(8):
-        both = []
+    def work(side):
         for g in range(2):
             span = slice(g * 8, g * 8 + 8)
-            rows = []
-            for i in range(r - 2, r + 3):
-                if i <= 1 and r <= 3:
-                    rows.append(delta[i + 2, span, :])
-                elif i >= 6 and r >= 4:
-                    rows.append(delta[i - 2, span, :])
-                else:
-                    rows.append(None)
-            center = rows[2] is not None
-            value = stencil_row(
-                rows, own_wind(1, 0, r), own_wind(1, 1, r) if center else None, nu
-            )
-            both.append(begun[r, span, :] + value)
-        whole = jnp.concatenate(both, 0).astype(BF)
-        if field == 0:
-            outs[r // 4][r % 4] = whole
-        else:
-            outs[0][4 + r] = whole
-    if field == 1:
-        outs[0][0:4] = refs[0][...]
+            h = lambda i: halo[i, span, :]
+            x = lambda r: turned[2 + r, span, :]
+            if side == 0:
+                line = [h(0), h(1), h(2), h(3), x(0), x(1)]
+                inner = (
+                    (2, 0, [h(2), h(3), None, None, None]),
+                    (3, 1, [h(3), None, None, None, None]),
+                )
+            else:
+                line = [x(6), x(7), h(0), h(1), h(2), h(3)]
+                inner = (
+                    (0, 6, [None, None, None, None, h(0)]),
+                    (1, 7, [None, None, None, h(0), h(1)]),
+                )
+            for i in range(2):
+                value = stencil_row(
+                    line[i : i + 5], broad(outer[i : i + 1]), broad(outer[2 + i : 3 + i]), nu
+                )
+                delta[2 * side + i, span, :cols] = value * scale[side]
+            for at, r, near in inner:
+                delta[at, span, :cols] = stencil_row(near, own_wind(0, 0, r), None, nu)
+        low = 6 if side else -2
+        for k in range(4):
+            r = 4 * side + k
+            both = []
+            for g in range(2):
+                span = slice(g * 8, g * 8 + 8)
+                near = []
+                for i in range(r - 2, r + 3):
+                    near.append(delta[i - low, span, :] if low <= i < low + 4 else None)
+                center = near[2] is not None
+                value = stencil_row(
+                    near, own_wind(1, 0, r), own_wind(1, 1, r) if center else None, nu
+                )
+                both.append(begun[r, span, :] + value)
+            out[start + k] = jnp.concatenate(both, 0).astype(BF)
+
+    pl.when(even)(lambda: work(1 - phase))
+    pl.when(jnp.logical_not(even))(lambda: work(phase))
 
 
 def gram_kernel(pos, own, mate, far, diag, root, rooted, out, spread):
@@ -456,36 +457,46 @@
 
 
 def final_kernel(
-    weights, own, mate, far, diag, own_more, mate_more, far_more, diag_more, out, keep, ready, sems
+    pos, weights, own, mate, far, diag, own_more, mate_more, far_more, diag_more, out, keep, ready, sems
 ):
-    copies = []
     cols = own.shape[2]
     step = 512
     half = cols // 2
+    copies = {}
     for f in range(2):
         for part in range(2):
             span = slice(part * half, part * half + half)
-            for base in (0, 4):
-                first = f == 0 and base == 0
-                refs = (own, mate, far, diag) if first else (own_more, mate_more, far_more, diag_more)
-                at = 0 if first else f * 8 + base - 4
-                for c in range(part * half, part * half + half, step):
-                    cut = slice(c, c + step)
-                    parts = [v[at + r, :, cut] for r in range(4) for v in refs]
-                    both = jnp.dot(
-                        weights[...], jnp.concatenate(parts, 0), preferred_element_type=F32
-                    )
-                    for r in range(4):
-                        high = both[r * 32 : r * 32 + 16]
-                        keep[base + r, :, cut] = high + both[r * 32 + 16 : r * 32 + 32]
-            ready[f, :, :, span] = jnp.swapaxes(keep[:, :, span], 0, 1)
-            copies.append(
-                pltpu.make_async_copy(
-                    ready.at[f, :, :, span], out.at[:, f, :, span], sems.at[2 * f + part]
-                )
+            copies[f, part] = pltpu.make_async_copy(
+                ready.at[f, :, :, span], out.at[:, f, :, span], sems.at[2 * f + part]
             )
-            copies[-1].start()
-    for copy in copies:
+
+    def work(early):
+        for f in range(2):
+            for part in range(2):
+                span = slice(part * half, part * half + half)
+                for turn in range(2):
+                    first = f == 0 and turn == 0
+                    refs = (own, mate, far, diag)
+                    if not first:
+                        refs = (own_more, mate_more, far_more, diag_more)
+                    at = 4 + 4 * f if turn else 0
+                    base = 4 - early if turn else early
+                    for c in range(part * half, part * half + half, step):
+                        cut = slice(c, c + step)
+                        parts = [v[at + r, :, cut] for r in range(4) for v in refs]
+                        both = jnp.dot(
+                            weights[...], jnp.concatenate(parts, 0), preferred_element_type=F32
+                        )
+                        for r in range(4):
+                            high = both[r * 32 : r * 32 + 16]
+                            keep[base + r, :, cut] = high + both[r * 32 + 16 : r * 32 + 32]
+                ready[f, :, :, span] = jnp.swapaxes(keep[:, :, span], 0, 1)
+                copies[f, part].start()
+
+    even = (pos[0] % 2) == 0
+    pl.when(even)(lambda: work(4))
+    pl.when(jnp.logical_not(even))(lambda: work(0))
+    for copy in copies.values():
         copy.wait()
 
 
@@ -545,10 +556,10 @@
     slots = obs_index.shape[0]
     width = 512
     place, chunk, root, rooted = pl.pallas_call(
-        slots_kernel,
+        functools.partial(slots_kernel, cols // width),
         name="slots",
         cost_estimate=cost(width * slots * 2),
-        in_specs=[vmem(), smem(), vmem(), vmem()],
+        in_specs=[smem(), vmem(), smem(), vmem(), vmem()],
         out_specs=[vmem()] * 4,
         out_shape=[
             shape((width, slots), BF),
@@ -558,6 +569,7 @@
         ],
         compiler_params=params(),
     )(
+        pos,
         obs_index.reshape(1, slots),
         obs_count,
         obs_weight.reshape(1, slots),
@@ -567,25 +579,28 @@
         (recv_a, begun[0], begun[1], place)
     )
 
-    def post(f, extra):
-        heights = (4, 4) if f == 0 else (12,)
+    def post(f, phase, recv, extra):
+        height = 4 + sum(v.shape[0] for v in extra)
         return pl.pallas_call(
-            functools.partial(post_kernel, f),
+            functools.partial(post_kernel, f, phase),
             name="post",
             cost_estimate=cost(8),
-            in_specs=[smem()] + [vmem()] * (5 + f),
-            out_specs=[vmem()] * len(heights),
-            out_shape=[shape((v, 16, cols), BF) for v in heights],
+            in_specs=[smem()] + [vmem()] * (4 + len(extra)),
+            out_specs=vmem(),
+            out_shape=shape((height, 16, cols), BF),
             scratch_shapes=[
-                pltpu.VMEM((8, 16, cols + PAD), F32),
-                pltpu.VMEM((8, 16, cols + PAD), F32),
+                pltpu.VMEM((4, 16, cols + PAD), F32),
+                pltpu.VMEM((4, 16, cols + PAD), F32),
             ],
             compiler_params=params(),
-        )(pos, turned[f], begun[f], recv_a, recv_b, wind_field, *extra)
-
-    one, two = post(0, [])
+        )(pos, turned[f], begun[f], recv, wind_field, *extra)
+
+    one = post(0, 0, recv_a, [])
     far_one = swap(one, 2)
-    more = post(1, [two])[0]
+    more = post(1, 0, recv_a, [])
+    recv_b, more = lax.optimization_barrier((recv_b, more))
+    more = post(0, 1, recv_b, [more])
+    more = post(1, 1, recv_b, [more])
     seen = pl.pallas_call(
         pick_kernel,
         name="pick",
@@ -643,7 +658,7 @@
         final_kernel,
         name="final",
         cost_estimate=cost(100 * 16 * cols * 4),
-        in_specs=[vmem()] * 9,
+        in_specs=[smem()] + [vmem()] * 9,
         out_specs=hbm(),
         out_shape=shape(prior_replicas.shape, F32),
         scratch_shapes=[
@@ -653,7 +668,7 @@
         ],
         compiler_params=params(),
     )(
-        weights, one, mate_one, far_one, diag_one, more, mate_more, far_more, diag_more
+        pos, weights, one, mate_one, far_one, diag_one, more, mate_more, far_more, diag_more
     )
 
 

time: 54.9 us -> 54.2 us (0.987)
  the two profiles are of different devices: /device:TPU:11 before, /device:TPU:0 now
where the time goes in v9:
time: 54.2 us; the launch traced here: 54 us
  Pallas kernels  24.6 us (45%)
  waiting for transfers between devices  16.4 us (30%)
  starting transfers between devices  12.1 us (22%)
  between operations  0.81 us (1%)
    ppermute x9, waiting for transfers between devices, swap(): return lax.ppermute(value, 'mem', [(i, i ^ bits) for i in range(4)])  9.47 us
    pallas_call x2, Pallas kernels, pre(): pl.pallas_call(functools.partial(pre_kernel, DIFFUSION[f]), name='pre', c...  7.74 us
    pallas_call x4, Pallas kernels, post(): pl.pallas_call(functools.partial(post_kernel, f, phase), name='post', cos...  5.36 us
    ppermute x2, starting transfers between devices, local(): other = lax.ppermute(part, 'space', [(i, i ^ bits) for i in range(strips)])  4.72 us
    ppermute x2, waiting for transfers between devices, local(): other = lax.ppermute(part, 'space', [(i, i ^ bits) for i in range(strips)])  4.36 us
    ppermute x9, starting transfers between devices, swap(): return lax.ppermute(value, 'mem', [(i, i ^ bits) for i in range(4)])  3.55 us
    ppermute x1, starting transfers between devices, local(): recv_a = lax.ppermute(packed[2], 'space', pairs_a)  3.11 us
    pallas_call x1, Pallas kernels, local(): pl.pallas_call(weights_kernel, name='weights', cost_estimate=cost(400 * 6...  2.57 us
  transfers between devices with their start and end apart: 13, of which 7 were waited for; matrix products, arithmetic and copies ran while one was open for 0% of the time, Pallas kernels for 37%

profile of v9, /device:TPU:0, one launch (start us, length us, event | category | flops | bytes accessed | tf_op | source)
XLA Modules:
  0.0 54.0 jit_solution(15120226364024119640)
XLA Ops:
  0.0 0.1 pad_add_fusion.pos
  0.1 2.4 %pack.1 = (f32[12,16,2176]{2,1,0:T(8,128)S(1)}, f32[12,16,2176]{2,1,0:T(8,128)S(1)}, bf16[136,2048]{1,0:T(8,128)(2,1)S(1)}, bf16[136,2048]{1,0:T(8,128)(2,1)S(1)}) custom-call(s32[3]{0:T(128)S(1)} %pad_add_fusion.pos, f32[16,2,8,2048]{3,2,1,0:T(8,128)} %prior.1, f32[2,2,8,2048]{3,2,1,0:T(8,128)} %wind.13), custom_call_target="tpu_custom_call" | custom-call | flops 10485760 | bytes 10485760 | tf_op jit(solution)/shard_map/pack/pallas_call | solution.py:520
  2.5 3.1 %collective-permute-start = (bf16[136,2048]{1,0:T(8,128)(2,1)S(1)}, bf16[136,2048]{1,0:T(8,128)(2,1)S(1)}, u32[]{:S(2)}, u32[]{:S(2)}) collective-permute-start(bf16[136,2048]{1,0:T(8,128)(2,1)S(1)} %get-tuple-element.26), channel_id=1, source_target_pairs={{0,4},{4,0},{8,12},{12,8},{1,5},{5,1},{9,13},{13,9},{2,6},{6,2},{1... | collective-permute-start | bytes 1671176 | tf_op jit(solution)/shard_map/ppermute | solution.py:536
  5.6 0.7 %collective-permute-start.1 = (bf16[136,2048]{1,0:T(8,128)(2,1)S(1)}, bf16[136,2048]{1,0:T(8,128)(2,1)S(1)}, u32[]{:S(2)}, u32[]{:S(2)}) collective-permute-start(bf16[136,2048]{1,0:T(8,128)(2,1)S(1)} %get-tuple-element.35), channel_id=1, source_target_pairs={{4,8},{8,4},{5,9},{9,5},{6,10},{10,6},{7,11},{11,7},{20,24},{24,20... | collective-permute-start | bytes 1671176 | tf_op jit(solution)/shard_map/ppermute | solution.py:537
  6.9 1.0 %slots.1 = (bf16[512,2048]{1,0:T(8,128)(2,1)S(1)}, s32[16,2048]{1,0:T(8,128)S(1)}, f32[1,2048]{1,0:T(1,128)S(1)}, f32[1,2048]{1,0:T(1,128)S(1)}) custom-call(s32[3]{0:T(128)S(1)} %pad_add_fusion.pos, s32[1,2048]{1,0:T(1,128)S(1)} %bitcast.5, s32[1]{0:T(128)S(6)} %copy.7.count, f32[1,2048]{1,0:T(1,128)S(1)} %bitcast.6, f32[1,2048]{1,0:T(1,128)S(1)} %bitcast.7), custom_call_target="tpu_custom_call" | custom-call | flops 2097152 | bytes 2097152 | tf_op jit(solution)/shard_map/slots/pallas_call | solution.py:558
  7.9 3.9 %pre.2.begun = f32[8,16,2048]{2,1,0:T(8,128)S(1)} custom-call(f32[12,16,2176]{2,1,0:T(8,128)S(1)} %get-tuple-element.27.turned, f32[2,2,8,2048]{3,2,1,0:T(8,128)S(1)} %copy-done), custom_call_target="tpu_custom_call" | custom-call | flops 19660800 | bytes 19660800 | tf_op jit(solution)/shard_map/pre/pallas_call | solution.py:540
  11.8 3.9 %pre.3.begun = f32[8,16,2048]{2,1,0:T(8,128)S(1)} custom-call(f32[12,16,2176]{2,1,0:T(8,128)S(1)} %get-tuple-element.28.turned, f32[2,2,8,2048]{3,2,1,0:T(8,128)S(1)} %copy-done), custom_call_target="tpu_custom_call" | custom-call | flops 19660800 | bytes 19660800 | tf_op jit(solution)/shard_map/pre/pallas_call | solution.py:540
  15.7 2.5 %collective-permute-done.recv = bf16[136,2048]{1,0:T(8,128)(2,1)S(1)} collective-permute-done((bf16[136,2048]{1,0:T(8,128)(2,1)S(1)}, bf16[136,2048]{1,0:T(8,128)(2,1)S(1)}, u32[]{:S(2)}, u32[]{:S(2)}) %collective-permute-start) | collective-permute-done | bytes 557088 | tf_op jit(solution)/shard_map/ppermute | solution.py:536
  18.2 1.3 %post.4.one.own = bf16[4,16,2048]{2,1,0:T(8,128)(2,1)S(1)} custom-call(s32[3]{0:T(128)S(1)} %pad_add_fusion.pos, f32[12,16,2176]{2,1,0:T(8,128)S(1)} %get-tuple-element.27.turned, f32[8,16,2048]{2,1,0:T(8,128)S(1)} %pre.2.begun, bf16[136,2048]{1,0:T(8,128)(2,1)S(1)} %collective-permute-done.recv, f32[2,2,8,2048]{3,2,1,0:T(8,128)S(1)} %copy-done), custom_call_target="tpu_custom_call" | custom-call | flops 8 | bytes 8 | tf_op jit(solution)/shard_map/post/pallas_call | solution.py:584
  19.5 1.7 %collective-permute-start.4 = (bf16[4,16,2048]{2,1,0:T(8,128)(2,1)S(1)}, bf16[4,16,2048]{2,1,0:T(8,128)(2,1)S(1)}, u32[]{:S(2)}, u32[]{:S(2)}) collective-permute-start(bf16[4,16,2048]{2,1,0:T(8,128)(2,1)S(1)} %post.4.one.own), channel_id=1, source_target_pairs={{0,2},{1,3},{2,0},{3,1},{4,6},{5,7},{6,4},{7,5},{8,10},{9,11},{10,... | collective-permute-start | bytes 786440 | tf_op jit(solution)/shard_map/ppermute | solution.py:515
  21.2 1.3 %post.5.refs_0_ = bf16[4,16,2048]{2,1,0:T(8,128)(2,1)S(1)} custom-call(s32[3]{0:T(128)S(1)} %pad_add_fusion.pos, f32[12,16,2176]{2,1,0:T(8,128)S(1)} %get-tuple-element.28.turned, f32[8,16,2048]{2,1,0:T(8,128)S(1)} %pre.3.begun, bf16[136,2048]{1,0:T(8,128)(2,1)S(1)} %collective-permute-done.recv, f32[2,2,8,2048]{3,2,1,0:T(8,128)S(1)} %copy-done), custom_call_target="tpu_custom_call" | custom-call | flops 8 | bytes 8 | tf_op jit(solution)/shard_map/post/pallas_call | solution.py:584
  22.6 1.4 %post.6.refs_0_ = bf16[8,16,2048]{2,1,0:T(8,128)(2,1)S(1)} custom-call(s32[3]{0:T(128)S(1)} %pad_add_fusion.pos, f32[12,16,2176]{2,1,0:T(8,128)S(1)} %get-tuple-element.27.turned, f32[8,16,2048]{2,1,0:T(8,128)S(1)} %pre.2.begun, bf16[136,2048]{1,0:T(8,128)(2,1)S(1)} %collective-permute-done.1.recv, f32[2,2,8,2048]{3,2,1,0:T(8,128)S(1)} %copy-done, ...), custom_call_target="tpu_custom_call" | custom-call | flops 8 | bytes 8 | tf_op jit(solution)/shard_map/post/pallas_call | solution.py:584
  23.9 1.4 %post.7.more.own_more = bf16[12,16,2048]{2,1,0:T(8,128)(2,1)S(1)} custom-call(s32[3]{0:T(128)S(1)} %pad_add_fusion.pos, f32[12,16,2176]{2,1,0:T(8,128)S(1)} %get-tuple-element.28.turned, f32[8,16,2048]{2,1,0:T(8,128)S(1)} %pre.3.begun, bf16[136,2048]{1,0:T(8,128)(2,1)S(1)} %collective-permute-done.1.recv, f32[2,2,8,2048]{3,2,1,0:T(8,128)S(1)} %copy-done, ...), custom_call_target="tpu_custom_call" | custom-call | flops 8 | bytes 8 | tf_op jit(solution)/shard_map/post/pallas_call | solution.py:584
  25.3 2.4 %pick.1.own = bf16[16,2048]{1,0:T(8,128)(2,1)S(1)} custom-call(bf16[512,2048]{1,0:T(8,128)(2,1)S(1)} %get-tuple-element.30.place, s32[16,2048]{1,0:T(8,128)S(1)} %get-tuple-element.31.chunk, bf16[4,16,2048]{2,1,0:T(8,128)(2,1)S(1)} %post.4.one.own, bf16[12,16,2048]{2,1,0:T(8,128)(2,1)S(1)} %post.7.more.own_more), custom_call_target="tpu_custom_call" | custom-call | flops 8 | bytes 8 | tf_op jit(solution)/shard_map/pick/pallas_call | solution.py:604
  27.7 0.4 collective-permute-start.3
  28.1 3.9 %collective-permute-done.3.far = bf16[16,2048]{1,0:T(8,128)(2,1)S(1)} collective-permute-done((bf16[16,2048]{1,0:T(8,128)(2,1)S(1)}, bf16[16,2048]{1,0:T(8,128)(2,1)S(1)}, u32[]{:S(2)}, u32[]{:S(2)}) %collective-permute-start.3) | collective-permute-done | bytes 65568 | tf_op jit(solution)/shard_map/ppermute | solution.py:515
  32.0 0.4 collective-permute-start.11
  32.4 0.0 collective-permute-start.7
  32.4 0.5 collective-permute-start.8
  32.9 0.5 collective-permute-start.5
  33.4 1.0 %collective-permute-done.2.mate = bf16[16,2048]{1,0:T(8,128)(2,1)S(1)} collective-permute-done((bf16[16,2048]{1,0:T(8,128)(2,1)S(1)}, bf16[16,2048]{1,0:T(8,128)(2,1)S(1)}, u32[]{:S(2)}, u32[]{:S(2)}) %collective-permute-start.2) | collective-permute-done | bytes 65568 | tf_op jit(solution)/shard_map/ppermute | solution.py:515
  34.4 0.1 collective-permute-done.5.diag
  34.5 0.9 %gram.1 = f32[80,64]{1,0:T(8,128)S(1)} custom-call(s32[3]{0:T(128)S(1)} %pad_add_fusion.pos, bf16[16,2048]{1,0:T(8,128)(2,1)S(1)} %pick.1.own, bf16[16,2048]{1,0:T(8,128)(2,1)S(1)} %collective-permute-done.2.mate, bf16[16,2048]{1,0:T(8,128)(2,1)S(1)} %collective-permute-done.3.far, bf16[16,2048]{1,0:T(8,128)(2,1)S(1)} %collective-permute-done.5.diag, ...), custom_call_target="tpu_custom_call" | custom-call | flops 3145728 | bytes 3145728 | tf_op jit(solution)/shard_map/gram/pallas_call | solution.py:621
  35.4 1.9 %collective-permute-start.6 = (f32[80,64]{1,0:T(8,128)S(1)}, f32[80,64]{1,0:T(8,128)S(1)}, u32[]{:S(2)}, u32[]{:S(2)}) collective-permute-start(f32[80,64]{1,0:T(8,128)S(1)} %gram.1), channel_id=1, source_target_pairs={{0,4},{4,0},{8,12},{12,8},{1,5},{5,1},{9,13},{13,9},{2,6},{6,2},{1... | collective-permute-start | bytes 61448 | tf_op jit(solution)/shard_map/ppermute | solution.py:641
  37.3 2.2 %collective-permute-done.6 = f32[80,64]{1,0:T(8,128)S(1)} collective-permute-done((f32[80,64]{1,0:T(8,128)S(1)}, f32[80,64]{1,0:T(8,128)S(1)}, u32[]{:S(2)}, u32[]{:S(2)}) %collective-permute-start.6) | collective-permute-done | bytes 20512 | tf_op jit(solution)/shard_map/ppermute | solution.py:641
  39.5 0.0 collective-permute-done.7.mate
  39.5 2.8 %collective-permute-start.9 = (f32[80,64]{1,0:T(8,128)S(1)}, f32[80,64]{1,0:T(8,128)S(1)}, u32[]{:S(2)}, u32[]{:S(2)}) collective-permute-start(f32[80,64]{1,0:T(8,128)S(1)} %add.3.one), channel_id=1, source_target_pairs={{0,8},{4,12},{8,0},{12,4},{1,9},{5,13},{9,1},{13,5},{2,10},{6,14},... | collective-permute-start | bytes 61448 | tf_op jit(solution)/shard_map/ppermute | solution.py:641
  42.3 2.2 %collective-permute-done.9.two = f32[80,64]{1,0:T(8,128)S(1)} collective-permute-done((f32[80,64]{1,0:T(8,128)S(1)}, f32[80,64]{1,0:T(8,128)S(1)}, u32[]{:S(2)}, u32[]{:S(2)}) %collective-permute-start.9) | collective-permute-done | bytes 20512 | tf_op jit(solution)/shard_map/ppermute | solution.py:641
  44.5 4.5 %collective-permute-done.11.far_more = bf16[12,16,2048]{2,1,0:T(8,128)(2,1)S(1)} collective-permute-done((bf16[12,16,2048]{2,1,0:T(8,128)(2,1)S(1)}, bf16[12,16,2048]{2,1,0:T(8,128)(2,1)S(1)}, u32[]{:S(2)}, u32[]{:S(2)}) %collective-permute-start.11) | collective-permute-done | bytes 786464 | tf_op jit(solution)/shard_map/ppermute | solution.py:515
  49.0 2.6 %weights.1 = bf16[128,256]{1,0:T(8,128)(2,1)S(1)} custom-call(s32[3]{0:T(128)S(1)} %pad_add_fusion.pos, f32[80,64]{1,0:T(8,128)S(1)} %add.3.one, f32[80,64]{1,0:T(8,128)S(1)} %collective-permute-done.9.two), custom_call_target="tpu_custom_call" | custom-call | flops 13107200 | bytes 13107200 | tf_op jit(solution)/shard_map/weights/pallas_call | solution.py:646
  51.6 0.0 collective-permute-done.10.mate_more
  51.6 2.4 %final.1 = f32[16,2,8,2048]{3,2,1,0:T(8,128)} custom-call(s32[3]{0:T(128)S(1)} %pad_add_fusion.pos, bf16[128,256]{1,0:T(8,128)(2,1)S(1)} %weights.1, bf16[4,16,2048]{2,1,0:T(8,128)(2,1)S(1)} %post.4.one.own, bf16[4,16,2048]{2,1,0:T(8,128)(2,1)S(1)} %collective-permute-done.7.mate, bf16[4,16,2048]{2,1,0:T(8,128)(2,1)S(1)} %collective-permute-done.4.far, ...), custom_call_target="tpu_custom_call" | custom-call | flops 13107200 | bytes 13107200 | tf_op jit(solution)/shard_map/final/pallas_call | solution.py:657
  (16 shorter events, 0.0 us)
Async XLA Ops:
  0.0 7.9 %copy-start = (f32[2,2,8,2048]{3,2,1,0:T(8,128)S(1)}, f32[2,2,8,2048]{3,2,1,0:T(8,128)}, u32[]{:S(2)}) copy-start(f32[2,2,8,2048]{3,2,1,0:T(8,128)} %wind.13) | copy-start | bytes 786436
  0.0 6.9 %copy-start.2 = (f32[2048]{0:T(1024)S(1)}, f32[2048]{0:T(1024)}, u32[]{:S(2)}) copy-start(f32[2048]{0:T(1024)} %param.11) | copy-start | bytes 24580
  0.0 6.9 %copy-start.3 = (f32[2048]{0:T(1024)S(1)}, f32[2048]{0:T(1024)}, u32[]{:S(2)}) copy-start(f32[2048]{0:T(1024)} %param.10) | copy-start | bytes 24580
  0.0 6.9 %copy-start.1 = (s32[2048]{0:T(1024)S(1)}, s32[2048]{0:T(1024)}, u32[]{:S(2)}) copy-start(s32[2048]{0:T(1024)} %param.8) | copy-start | bytes 24580
  2.5 15.7 %collective-permute-start = (bf16[136,2048]{1,0:T(8,128)(2,1)S(1)}, bf16[136,2048]{1,0:T(8,128)(2,1)S(1)}, u32[]{:S(2)}, u32[]{:S(2)}) collective-permute-start(bf16[136,2048]{1,0:T(8,128)(2,1)S(1)} %get-tuple-element.26), channel_id=1, source_target_pairs={{0,4},{4,0},{8,12},{12,8},{1,5},{5,1},{9,13},{13,9},{2,6},{6,2},{1... | collective-permute-start | bytes 1671176 | tf_op jit(solution)/shard_map/ppermute | solution.py:536
  5.6 17.0 %collective-permute-start.1 = (bf16[136,2048]{1,0:T(8,128)(2,1)S(1)}, bf16[136,2048]{1,0:T(8,128)(2,1)S(1)}, u32[]{:S(2)}, u32[]{:S(2)}) collective-permute-start(bf16[136,2048]{1,0:T(8,128)(2,1)S(1)} %get-tuple-element.35), channel_id=1, source_target_pairs={{4,8},{8,4},{5,9},{9,5},{6,10},{10,6},{7,11},{11,7},{20,24},{24,20... | collective-permute-start | bytes 1671176 | tf_op jit(solution)/shard_map/ppermute | solution.py:537
  19.5 12.5 %collective-permute-start.4 = (bf16[4,16,2048]{2,1,0:T(8,128)(2,1)S(1)}, bf16[4,16,2048]{2,1,0:T(8,128)(2,1)S(1)}, u32[]{:S(2)}, u32[]{:S(2)}) collective-permute-start(bf16[4,16,2048]{2,1,0:T(8,128)(2,1)S(1)} %post.4.one.own), channel_id=1, source_target_pairs={{0,2},{1,3},{2,0},{3,1},{4,6},{5,7},{6,4},{7,5},{8,10},{9,11},{10,... | collective-permute-start | bytes 786440 | tf_op jit(solution)/shard_map/ppermute | solution.py:515
  27.7 4.3 %collective-permute-start.3 = (bf16[16,2048]{1,0:T(8,128)(2,1)S(1)}, bf16[16,2048]{1,0:T(8,128)(2,1)S(1)}, u32[]{:S(2)}, u32[]{:S(2)}) collective-permute-start(bf16[16,2048]{1,0:T(8,128)(2,1)S(1)} %pick.1.own), channel_id=1, source_target_pairs={{0,2},{1,3},{2,0},{3,1},{4,6},{5,7},{6,4},{7,5},{8,10},{9,11},{10,... | collective-permute-start | bytes 196616 | tf_op jit(solution)/shard_map/ppermute | solution.py:515
  32.0 17.0 %collective-permute-start.11 = (bf16[12,16,2048]{2,1,0:T(8,128)(2,1)S(1)}, bf16[12,16,2048]{2,1,0:T(8,128)(2,1)S(1)}, u32[]{:S(2)}, u32[]{:S(2)}) collective-permute-start(bf16[12,16,2048]{2,1,0:T(8,128)(2,1)S(1)} %post.7.more.own_more), channel_id=1, source_target_pairs={{0,2},{1,3},{2,0},{3,1},{4,6},{5,7},{6,4},{7,5},{8,10},{9,11},{10,... | collective-permute-start | bytes 2359304 | tf_op jit(solution)/shard_map/ppermute | solution.py:515
  32.4 7.1 %collective-permute-start.7 = (bf16[4,16,2048]{2,1,0:T(8,128)(2,1)S(1)}, bf16[4,16,2048]{2,1,0:T(8,128)(2,1)S(1)}, u32[]{:S(2)}, u32[]{:S(2)}) collective-permute-start(bf16[4,16,2048]{2,1,0:T(8,128)(2,1)S(1)} %post.4.one.own), channel_id=1, source_target_pairs={{0,1},{1,0},{2,3},{3,2},{4,5},{5,4},{6,7},{7,6},{8,9},{9,8},{10,11... | collective-permute-start | bytes 786440 | tf_op jit(solution)/shard_map/ppermute | solution.py:515
  32.4 7.1 %collective-permute-start.8 = (bf16[4,16,2048]{2,1,0:T(8,128)(2,1)S(1)}, bf16[4,16,2048]{2,1,0:T(8,128)(2,1)S(1)}, u32[]{:S(2)}, u32[]{:S(2)}) collective-permute-start(bf16[4,16,2048]{2,1,0:T(8,128)(2,1)S(1)} %collective-permute-done.4.far), channel_id=1, source_target_pairs={{0,1},{1,0},{2,3},{3,2},{4,5},{5,4},{6,7},{7,6},{8,9},{9,8},{10,11... | collective-permute-start | bytes 786440 | tf_op jit(solution)/shard_map/ppermute | solution.py:515
  32.9 1.5 %collective-permute-start.2 = (bf16[16,2048]{1,0:T(8,128)(2,1)S(1)}, bf16[16,2048]{1,0:T(8,128)(2,1)S(1)}, u32[]{:S(2)}, u32[]{:S(2)}) collective-permute-start(bf16[16,2048]{1,0:T(8,128)(2,1)S(1)} %pick.1.own), channel_id=1, source_target_pairs={{0,1},{1,0},{2,3},{3,2},{4,5},{5,4},{6,7},{7,6},{8,9},{9,8},{10,11... | collective-permute-start | bytes 196616 | tf_op jit(solution)/shard_map/ppermute | solution.py:515
  32.9 1.6 %collective-permute-start.5 = (bf16[16,2048]{1,0:T(8,128)(2,1)S(1)}, bf16[16,2048]{1,0:T(8,128)(2,1)S(1)}, u32[]{:S(2)}, u32[]{:S(2)}) collective-permute-start(bf16[16,2048]{1,0:T(8,128)(2,1)S(1)} %collective-permute-done.3.far), channel_id=1, source_target_pairs={{0,1},{1,0},{2,3},{3,2},{4,5},{5,4},{6,7},{7,6},{8,9},{9,8},{10,11... | collective-permute-start | bytes 196616 | tf_op jit(solution)/shard_map/ppermute | solution.py:515
  35.4 4.1 %collective-permute-start.6 = (f32[80,64]{1,0:T(8,128)S(1)}, f32[80,64]{1,0:T(8,128)S(1)}, u32[]{:S(2)}, u32[]{:S(2)}) collective-permute-start(f32[80,64]{1,0:T(8,128)S(1)} %gram.1), channel_id=1, source_target_pairs={{0,4},{4,0},{8,12},{12,8},{1,5},{5,1},{9,13},{13,9},{2,6},{6,2},{1... | collective-permute-start | bytes 61448 | tf_op jit(solution)/shard_map/ppermute | solution.py:641
  39.5 5.0 %collective-permute-start.9 = (f32[80,64]{1,0:T(8,128)S(1)}, f32[80,64]{1,0:T(8,128)S(1)}, u32[]{:S(2)}, u32[]{:S(2)}) collective-permute-start(f32[80,64]{1,0:T(8,128)S(1)} %add.3.one), channel_id=1, source_target_pairs={{0,8},{4,12},{8,0},{12,4},{1,9},{5,13},{9,1},{13,5},{2,10},{6,14},... | collective-permute-start | bytes 61448 | tf_op jit(solution)/shard_map/ppermute | solution.py:641
  42.3 9.3 %collective-permute-start.10 = (bf16[12,16,2048]{2,1,0:T(8,128)(2,1)S(1)}, bf16[12,16,2048]{2,1,0:T(8,128)(2,1)S(1)}, u32[]{:S(2)}, u32[]{:S(2)}) collective-permute-start(bf16[12,16,2048]{2,1,0:T(8,128)(2,1)S(1)} %post.7.more.own_more), channel_id=1, source_target_pairs={{0,1},{1,0},{2,3},{3,2},{4,5},{5,4},{6,7},{7,6},{8,9},{9,8},{10,11... | collective-permute-start | bytes 2359304 | tf_op jit(solution)/shard_map/ppermute | solution.py:515
  49.0 2.6 %collective-permute-start.12 = (bf16[12,16,2048]{2,1,0:T(8,128)(2,1)S(1)}, bf16[12,16,2048]{2,1,0:T(8,128)(2,1)S(1)}, u32[]{:S(2)}, u32[]{:S(2)}) collective-permute-start(bf16[12,16,2048]{2,1,0:T(8,128)(2,1)S(1)} %collective-permute-done.11.far_more), channel_id=1, source_target_pairs={{0,1},{1,0},{2,3},{3,2},{4,5},{5,4},{6,7},{7,6},{8,9},{9,8},{10,11... | collective-permute-start | bytes 2359304 | tf_op jit(solution)/shard_map/ppermute | solution.py:515

commit v10 on v9

--- a/solution.py
+++ b/solution.py
@@ -640,9 +640,6 @@
             part, mate_one, diag_one = lax.optimization_barrier((part, mate_one, diag_one))
         other = lax.ppermute(part, "space", [(i, i ^ bits) for i in range(strips)])
         bits *= 2
-    late, _ = lax.optimization_barrier((far_more, other))
-    diag_more = swap(late, 1)
-
     weights = pl.pallas_call(
         weights_kernel,
         name="weights",
@@ -653,6 +650,9 @@
         scratch_shapes=[pltpu.VMEM((64, 64), F32)],
         compiler_params=params(),
     )(pos, part, other)
+
+    late, weights = lax.optimization_barrier((far_more, weights))
+    diag_more = swap(late, 1)
 
     return pl.pallas_call(
         final_kernel,

time: 54.2 us -> 53.8 us (level)
  transfers between devices with their start and end apart: 13 -> 13, of which waited for: 7 -> 8; matrix products, arithmetic and copies ran while one was open for 0% -> 0% of each run, Pallas kernels for 37% -> 37%
where the time goes in v10:
time: 53.8 us; the launch traced here: 53.7 us
  Pallas kernels  24.6 us (46%)
  waiting for transfers between devices  16.1 us (30%)
  starting transfers between devices  12.1 us (22%)
  between operations  0.8 us (1%)
    ppermute x9, waiting for transfers between devices, swap(): return lax.ppermute(value, 'mem', [(i, i ^ bits) for i in range(4)])  9.18 us
    pallas_call x2, Pallas kernels, pre(): pl.pallas_call(functools.partial(pre_kernel, DIFFUSION[f]), name='pre', c...  7.74 us
    pallas_call x4, Pallas kernels, post(): pl.pallas_call(functools.partial(post_kernel, f, phase), name='post', cos...  5.36 us
    ppermute x2, starting transfers between devices, local(): other = lax.ppermute(part, 'space', [(i, i ^ bits) for i in range(strips)])  4.72 us
    ppermute x2, waiting for transfers between devices, local(): other = lax.ppermute(part, 'space', [(i, i ^ bits) for i in range(strips)])  4.36 us
    ppermute x9, starting transfers between devices, swap(): return lax.ppermute(value, 'mem', [(i, i ^ bits) for i in range(4)])  3.55 us
    ppermute x1, starting transfers between devices, local(): recv_a = lax.ppermute(packed[2], 'space', pairs_a)  3.11 us
    pallas_call x1, Pallas kernels, local(): pl.pallas_call(weights_kernel, name='weights', cost_estimate=cost(400 * 6...  2.56 us
  transfers between devices with their start and end apart: 13, of which 8 were waited for; matrix products, arithmetic and copies ran while one was open for 0% of the time, Pallas kernels for 37%

profile of v10, /device:TPU:0, one launch (start us, length us, event | category | flops | bytes accessed | tf_op | source)
XLA Modules:
  0.0 53.7 jit_solution(1847188488936440192)
XLA Ops:
  0.0 0.1 pad_add_fusion.pos
  0.1 2.4 %pack.1 = (f32[12,16,2176]{2,1,0:T(8,128)S(1)}, f32[12,16,2176]{2,1,0:T(8,128)S(1)}, bf16[136,2048]{1,0:T(8,128)(2,1)S(1)}, bf16[136,2048]{1,0:T(8,128)(2,1)S(1)}) custom-call(s32[3]{0:T(128)S(1)} %pad_add_fusion.pos, f32[16,2,8,2048]{3,2,1,0:T(8,128)} %prior.1, f32[2,2,8,2048]{3,2,1,0:T(8,128)} %wind.13), custom_call_target="tpu_custom_call" | custom-call | flops 10485760 | bytes 10485760 | tf_op jit(solution)/shard_map/pack/pallas_call | solution.py:520
  2.5 3.1 %collective-permute-start = (bf16[136,2048]{1,0:T(8,128)(2,1)S(1)}, bf16[136,2048]{1,0:T(8,128)(2,1)S(1)}, u32[]{:S(2)}, u32[]{:S(2)}) collective-permute-start(bf16[136,2048]{1,0:T(8,128)(2,1)S(1)} %get-tuple-element.27), channel_id=1, source_target_pairs={{0,4},{4,0},{8,12},{12,8},{1,5},{5,1},{9,13},{13,9},{2,6},{6,2},{1... | collective-permute-start | bytes 1671176 | tf_op jit(solution)/shard_map/ppermute | solution.py:536
  5.6 0.7 %collective-permute-start.1 = (bf16[136,2048]{1,0:T(8,128)(2,1)S(1)}, bf16[136,2048]{1,0:T(8,128)(2,1)S(1)}, u32[]{:S(2)}, u32[]{:S(2)}) collective-permute-start(bf16[136,2048]{1,0:T(8,128)(2,1)S(1)} %get-tuple-element.36), channel_id=1, source_target_pairs={{4,8},{8,4},{5,9},{9,5},{6,10},{10,6},{7,11},{11,7},{20,24},{24,20... | collective-permute-start | bytes 1671176 | tf_op jit(solution)/shard_map/ppermute | solution.py:537
  6.9 1.0 %slots.1 = (bf16[512,2048]{1,0:T(8,128)(2,1)S(1)}, s32[16,2048]{1,0:T(8,128)S(1)}, f32[1,2048]{1,0:T(1,128)S(1)}, f32[1,2048]{1,0:T(1,128)S(1)}) custom-call(s32[3]{0:T(128)S(1)} %pad_add_fusion.pos, s32[1,2048]{1,0:T(1,128)S(1)} %bitcast.5, s32[1]{0:T(128)S(6)} %copy.7.count, f32[1,2048]{1,0:T(1,128)S(1)} %bitcast.6, f32[1,2048]{1,0:T(1,128)S(1)} %bitcast.7), custom_call_target="tpu_custom_call" | custom-call | flops 2097152 | bytes 2097152 | tf_op jit(solution)/shard_map/slots/pallas_call | solution.py:558
  7.9 3.9 %pre.2.begun = f32[8,16,2048]{2,1,0:T(8,128)S(1)} custom-call(f32[12,16,2176]{2,1,0:T(8,128)S(1)} %get-tuple-element.28.turned, f32[2,2,8,2048]{3,2,1,0:T(8,128)S(1)} %copy-done), custom_call_target="tpu_custom_call" | custom-call | flops 19660800 | bytes 19660800 | tf_op jit(solution)/shard_map/pre/pallas_call | solution.py:540
  11.8 3.9 %pre.3.begun = f32[8,16,2048]{2,1,0:T(8,128)S(1)} custom-call(f32[12,16,2176]{2,1,0:T(8,128)S(1)} %get-tuple-element.29.turned, f32[2,2,8,2048]{3,2,1,0:T(8,128)S(1)} %copy-done), custom_call_target="tpu_custom_call" | custom-call | flops 19660800 | bytes 19660800 | tf_op jit(solution)/shard_map/pre/pallas_call | solution.py:540
  15.7 2.5 %collective-permute-done.recv = bf16[136,2048]{1,0:T(8,128)(2,1)S(1)} collective-permute-done((bf16[136,2048]{1,0:T(8,128)(2,1)S(1)}, bf16[136,2048]{1,0:T(8,128)(2,1)S(1)}, u32[]{:S(2)}, u32[]{:S(2)}) %collective-permute-start) | collective-permute-done | bytes 557088 | tf_op jit(solution)/shard_map/ppermute | solution.py:536
  18.2 1.3 %post.4.one.own = bf16[4,16,2048]{2,1,0:T(8,128)(2,1)S(1)} custom-call(s32[3]{0:T(128)S(1)} %pad_add_fusion.pos, f32[12,16,2176]{2,1,0:T(8,128)S(1)} %get-tuple-element.28.turned, f32[8,16,2048]{2,1,0:T(8,128)S(1)} %pre.2.begun, bf16[136,2048]{1,0:T(8,128)(2,1)S(1)} %collective-permute-done.recv, f32[2,2,8,2048]{3,2,1,0:T(8,128)S(1)} %copy-done), custom_call_target="tpu_custom_call" | custom-call | flops 8 | bytes 8 | tf_op jit(solution)/shard_map/post/pallas_call | solution.py:584
  19.5 1.7 %collective-permute-start.3 = (bf16[4,16,2048]{2,1,0:T(8,128)(2,1)S(1)}, bf16[4,16,2048]{2,1,0:T(8,128)(2,1)S(1)}, u32[]{:S(2)}, u32[]{:S(2)}) collective-permute-start(bf16[4,16,2048]{2,1,0:T(8,128)(2,1)S(1)} %post.4.one.own), channel_id=1, source_target_pairs={{0,2},{1,3},{2,0},{3,1},{4,6},{5,7},{6,4},{7,5},{8,10},{9,11},{10,... | collective-permute-start | bytes 786440 | tf_op jit(solution)/shard_map/ppermute | solution.py:515
  21.2 1.3 %post.5.refs_0_ = bf16[4,16,2048]{2,1,0:T(8,128)(2,1)S(1)} custom-call(s32[3]{0:T(128)S(1)} %pad_add_fusion.pos, f32[12,16,2176]{2,1,0:T(8,128)S(1)} %get-tuple-element.29.turned, f32[8,16,2048]{2,1,0:T(8,128)S(1)} %pre.3.begun, bf16[136,2048]{1,0:T(8,128)(2,1)S(1)} %collective-permute-done.recv, f32[2,2,8,2048]{3,2,1,0:T(8,128)S(1)} %copy-done), custom_call_target="tpu_custom_call" | custom-call | flops 8 | bytes 8 | tf_op jit(solution)/shard_map/post/pallas_call | solution.py:584
  22.6 0.0 collective-permute-done.1.recv
  22.6 1.4 %post.6.refs_0_ = bf16[8,16,2048]{2,1,0:T(8,128)(2,1)S(1)} custom-call(s32[3]{0:T(128)S(1)} %pad_add_fusion.pos, f32[12,16,2176]{2,1,0:T(8,128)S(1)} %get-tuple-element.28.turned, f32[8,16,2048]{2,1,0:T(8,128)S(1)} %pre.2.begun, bf16[136,2048]{1,0:T(8,128)(2,1)S(1)} %collective-permute-done.1.recv, f32[2,2,8,2048]{3,2,1,0:T(8,128)S(1)} %copy-done, ...), custom_call_target="tpu_custom_call" | custom-call | flops 8 | bytes 8 | tf_op jit(solution)/shard_map/post/pallas_call | solution.py:584
  23.9 1.4 %post.7.more.own_more = bf16[12,16,2048]{2,1,0:T(8,128)(2,1)S(1)} custom-call(s32[3]{0:T(128)S(1)} %pad_add_fusion.pos, f32[12,16,2176]{2,1,0:T(8,128)S(1)} %get-tuple-element.29.turned, f32[8,16,2048]{2,1,0:T(8,128)S(1)} %pre.3.begun, bf16[136,2048]{1,0:T(8,128)(2,1)S(1)} %collective-permute-done.1.recv, f32[2,2,8,2048]{3,2,1,0:T(8,128)S(1)} %copy-done, ...), custom_call_target="tpu_custom_call" | custom-call | flops 8 | bytes 8 | tf_op jit(solution)/shard_map/post/pallas_call | solution.py:584
  25.3 2.4 %pick.1.own = bf16[16,2048]{1,0:T(8,128)(2,1)S(1)} custom-call(bf16[512,2048]{1,0:T(8,128)(2,1)S(1)} %get-tuple-element.31.place, s32[16,2048]{1,0:T(8,128)S(1)} %get-tuple-element.32.chunk, bf16[4,16,2048]{2,1,0:T(8,128)(2,1)S(1)} %post.4.one.own, bf16[12,16,2048]{2,1,0:T(8,128)(2,1)S(1)} %post.7.more.own_more), custom_call_target="tpu_custom_call" | custom-call | flops 8 | bytes 8 | tf_op jit(solution)/shard_map/pick/pallas_call | solution.py:604
  27.7 0.4 collective-permute-start.2
  28.1 3.9 %collective-permute-done.2.far = bf16[16,2048]{1,0:T(8,128)(2,1)S(1)} collective-permute-done((bf16[16,2048]{1,0:T(8,128)(2,1)S(1)}, bf16[16,2048]{1,0:T(8,128)(2,1)S(1)}, u32[]{:S(2)}, u32[]{:S(2)}) %collective-permute-start.2) | collective-permute-done | bytes 65568 | tf_op jit(solution)/shard_map/ppermute | solution.py:515
  32.0 0.0 collective-permute-done.3.far
  32.0 0.4 collective-permute-start.4
  32.4 0.5 collective-permute-start.9
  32.9 0.5 collective-permute-start.6
  33.4 1.0 %collective-permute-done.5.mate = bf16[16,2048]{1,0:T(8,128)(2,1)S(1)} collective-permute-done((bf16[16,2048]{1,0:T(8,128)(2,1)S(1)}, bf16[16,2048]{1,0:T(8,128)(2,1)S(1)}, u32[]{:S(2)}, u32[]{:S(2)}) %collective-permute-start.5) | collective-permute-done | bytes 65568 | tf_op jit(solution)/shard_map/ppermute | solution.py:515
  34.4 0.1 collective-permute-done.6.diag
  34.5 0.9 %gram.1 = f32[80,64]{1,0:T(8,128)S(1)} custom-call(s32[3]{0:T(128)S(1)} %pad_add_fusion.pos, bf16[16,2048]{1,0:T(8,128)(2,1)S(1)} %pick.1.own, bf16[16,2048]{1,0:T(8,128)(2,1)S(1)} %collective-permute-done.5.mate, bf16[16,2048]{1,0:T(8,128)(2,1)S(1)} %collective-permute-done.2.far, bf16[16,2048]{1,0:T(8,128)(2,1)S(1)} %collective-permute-done.6.diag, ...), custom_call_target="tpu_custom_call" | custom-call | flops 3145728 | bytes 3145728 | tf_op jit(solution)/shard_map/gram/pallas_call | solution.py:621
  35.4 1.9 %collective-permute-start.7 = (f32[80,64]{1,0:T(8,128)S(1)}, f32[80,64]{1,0:T(8,128)S(1)}, u32[]{:S(2)}, u32[]{:S(2)}) collective-permute-start(f32[80,64]{1,0:T(8,128)S(1)} %gram.1), channel_id=1, source_target_pairs={{0,4},{4,0},{8,12},{12,8},{1,5},{5,1},{9,13},{13,9},{2,6},{6,2},{1... | collective-permute-start | bytes 61448 | tf_op jit(solution)/shard_map/ppermute | solution.py:641
  37.3 2.2 %collective-permute-done.7 = f32[80,64]{1,0:T(8,128)S(1)} collective-permute-done((f32[80,64]{1,0:T(8,128)S(1)}, f32[80,64]{1,0:T(8,128)S(1)}, u32[]{:S(2)}, u32[]{:S(2)}) %collective-permute-start.7) | collective-permute-done | bytes 20512 | tf_op jit(solution)/shard_map/ppermute | solution.py:641
  39.5 2.8 %collective-permute-start.10 = (f32[80,64]{1,0:T(8,128)S(1)}, f32[80,64]{1,0:T(8,128)S(1)}, u32[]{:S(2)}, u32[]{:S(2)}) collective-permute-start(f32[80,64]{1,0:T(8,128)S(1)} %add.3.one), channel_id=1, source_target_pairs={{0,8},{4,12},{8,0},{12,4},{1,9},{5,13},{9,1},{13,5},{2,10},{6,14},... | collective-permute-start | bytes 61448 | tf_op jit(solution)/shard_map/ppermute | solution.py:641
  42.3 2.2 %collective-permute-done.10.two = f32[80,64]{1,0:T(8,128)S(1)} collective-permute-done((f32[80,64]{1,0:T(8,128)S(1)}, f32[80,64]{1,0:T(8,128)S(1)}, u32[]{:S(2)}, u32[]{:S(2)}) %collective-permute-start.10) | collective-permute-done | bytes 20512 | tf_op jit(solution)/shard_map/ppermute | solution.py:641
  44.5 2.6 %weights.1 = bf16[128,256]{1,0:T(8,128)(2,1)S(1)} custom-call(s32[3]{0:T(128)S(1)} %pad_add_fusion.pos, f32[80,64]{1,0:T(8,128)S(1)} %add.3.one, f32[80,64]{1,0:T(8,128)S(1)} %collective-permute-done.10.two), custom_call_target="tpu_custom_call" | custom-call | flops 13107200 | bytes 13107200 | tf_op jit(solution)/shard_map/weights/pallas_call | solution.py:643
  47.1 1.9 %collective-permute-done.4.far_more = bf16[12,16,2048]{2,1,0:T(8,128)(2,1)S(1)} collective-permute-done((bf16[12,16,2048]{2,1,0:T(8,128)(2,1)S(1)}, bf16[12,16,2048]{2,1,0:T(8,128)(2,1)S(1)}, u32[]{:S(2)}, u32[]{:S(2)}) %collective-permute-start.4) | collective-permute-done | bytes 786464 | tf_op jit(solution)/shard_map/ppermute | solution.py:515
  49.0 2.3 %collective-permute-done.12.diag_more = bf16[12,16,2048]{2,1,0:T(8,128)(2,1)S(1)} collective-permute-done((bf16[12,16,2048]{2,1,0:T(8,128)(2,1)S(1)}, bf16[12,16,2048]{2,1,0:T(8,128)(2,1)S(1)}, u32[]{:S(2)}, u32[]{:S(2)}) %collective-permute-start.12) | collective-permute-done | bytes 786464 | tf_op jit(solution)/shard_map/ppermute | solution.py:515
  51.3 2.4 %final.1 = f32[16,2,8,2048]{3,2,1,0:T(8,128)} custom-call(s32[3]{0:T(128)S(1)} %pad_add_fusion.pos, bf16[128,256]{1,0:T(8,128)(2,1)S(1)} %weights.1, bf16[4,16,2048]{2,1,0:T(8,128)(2,1)S(1)} %post.4.one.own, bf16[4,16,2048]{2,1,0:T(8,128)(2,1)S(1)} %collective-permute-done.8.mate, bf16[4,16,2048]{2,1,0:T(8,128)(2,1)S(1)} %collective-permute-done.3.far, ...), custom_call_target="tpu_custom_call" | custom-call | flops 13107200 | bytes 13107200 | tf_op jit(solution)/shard_map/final/pallas_call | solution.py:657
  (16 shorter events, 0.0 us)
Async XLA Ops:
  0.0 7.9 %copy-start = (f32[2,2,8,2048]{3,2,1,0:T(8,128)S(1)}, f32[2,2,8,2048]{3,2,1,0:T(8,128)}, u32[]{:S(2)}) copy-start(f32[2,2,8,2048]{3,2,1,0:T(8,128)} %wind.13) | copy-start | bytes 786436
  0.0 6.9 %copy-start.2 = (f32[2048]{0:T(1024)S(1)}, f32[2048]{0:T(1024)}, u32[]{:S(2)}) copy-start(f32[2048]{0:T(1024)} %param.11) | copy-start | bytes 24580
  0.0 6.9 %copy-start.3 = (f32[2048]{0:T(1024)S(1)}, f32[2048]{0:T(1024)}, u32[]{:S(2)}) copy-start(f32[2048]{0:T(1024)} %param.10) | copy-start | bytes 24580
  0.0 6.9 %copy-start.1 = (s32[2048]{0:T(1024)S(1)}, s32[2048]{0:T(1024)}, u32[]{:S(2)}) copy-start(s32[2048]{0:T(1024)} %param.8) | copy-start | bytes 24580
  2.5 15.7 %collective-permute-start = (bf16[136,2048]{1,0:T(8,128)(2,1)S(1)}, bf16[136,2048]{1,0:T(8,128)(2,1)S(1)}, u32[]{:S(2)}, u32[]{:S(2)}) collective-permute-start(bf16[136,2048]{1,0:T(8,128)(2,1)S(1)} %get-tuple-element.27), channel_id=1, source_target_pairs={{0,4},{4,0},{8,12},{12,8},{1,5},{5,1},{9,13},{13,9},{2,6},{6,2},{1... | collective-permute-start | bytes 1671176 | tf_op jit(solution)/shard_map/ppermute | solution.py:536
  5.6 17.0 %collective-permute-start.1 = (bf16[136,2048]{1,0:T(8,128)(2,1)S(1)}, bf16[136,2048]{1,0:T(8,128)(2,1)S(1)}, u32[]{:S(2)}, u32[]{:S(2)}) collective-permute-start(bf16[136,2048]{1,0:T(8,128)(2,1)S(1)} %get-tuple-element.36), channel_id=1, source_target_pairs={{4,8},{8,4},{5,9},{9,5},{6,10},{10,6},{7,11},{11,7},{20,24},{24,20... | collective-permute-start | bytes 1671176 | tf_op jit(solution)/shard_map/ppermute | solution.py:537
  19.5 12.5 %collective-permute-start.3 = (bf16[4,16,2048]{2,1,0:T(8,128)(2,1)S(1)}, bf16[4,16,2048]{2,1,0:T(8,128)(2,1)S(1)}, u32[]{:S(2)}, u32[]{:S(2)}) collective-permute-start(bf16[4,16,2048]{2,1,0:T(8,128)(2,1)S(1)} %post.4.one.own), channel_id=1, source_target_pairs={{0,2},{1,3},{2,0},{3,1},{4,6},{5,7},{6,4},{7,5},{8,10},{9,11},{10,... | collective-permute-start | bytes 786440 | tf_op jit(solution)/shard_map/ppermute | solution.py:515
  27.7 4.3 %collective-permute-start.2 = (bf16[16,2048]{1,0:T(8,128)(2,1)S(1)}, bf16[16,2048]{1,0:T(8,128)(2,1)S(1)}, u32[]{:S(2)}, u32[]{:S(2)}) collective-permute-start(bf16[16,2048]{1,0:T(8,128)(2,1)S(1)} %pick.1.own), channel_id=1, source_target_pairs={{0,2},{1,3},{2,0},{3,1},{4,6},{5,7},{6,4},{7,5},{8,10},{9,11},{10,... | collective-permute-start | bytes 196616 | tf_op jit(solution)/shard_map/ppermute | solution.py:515
  32.0 17.0 %collective-permute-start.4 = (bf16[12,16,2048]{2,1,0:T(8,128)(2,1)S(1)}, bf16[12,16,2048]{2,1,0:T(8,128)(2,1)S(1)}, u32[]{:S(2)}, u32[]{:S(2)}) collective-permute-start(bf16[12,16,2048]{2,1,0:T(8,128)(2,1)S(1)} %post.7.more.own_more), channel_id=1, source_target_pairs={{0,2},{1,3},{2,0},{3,1},{4,6},{5,7},{6,4},{7,5},{8,10},{9,11},{10,... | collective-permute-start | bytes 2359304 | tf_op jit(solution)/shard_map/ppermute | solution.py:515
  32.4 7.1 %collective-permute-start.8 = (bf16[4,16,2048]{2,1,0:T(8,128)(2,1)S(1)}, bf16[4,16,2048]{2,1,0:T(8,128)(2,1)S(1)}, u32[]{:S(2)}, u32[]{:S(2)}) collective-permute-start(bf16[4,16,2048]{2,1,0:T(8,128)(2,1)S(1)} %post.4.one.own), channel_id=1, source_target_pairs={{0,1},{1,0},{2,3},{3,2},{4,5},{5,4},{6,7},{7,6},{8,9},{9,8},{10,11... | collective-permute-start | bytes 786440 | tf_op jit(solution)/shard_map/ppermute | solution.py:515
  32.4 7.1 %collective-permute-start.9 = (bf16[4,16,2048]{2,1,0:T(8,128)(2,1)S(1)}, bf16[4,16,2048]{2,1,0:T(8,128)(2,1)S(1)}, u32[]{:S(2)}, u32[]{:S(2)}) collective-permute-start(bf16[4,16,2048]{2,1,0:T(8,128)(2,1)S(1)} %collective-permute-done.3.far), channel_id=1, source_target_pairs={{0,1},{1,0},{2,3},{3,2},{4,5},{5,4},{6,7},{7,6},{8,9},{9,8},{10,11... | collective-permute-start | bytes 786440 | tf_op jit(solution)/shard_map/ppermute | solution.py:515
  32.9 1.5 %collective-permute-start.5 = (bf16[16,2048]{1,0:T(8,128)(2,1)S(1)}, bf16[16,2048]{1,0:T(8,128)(2,1)S(1)}, u32[]{:S(2)}, u32[]{:S(2)}) collective-permute-start(bf16[16,2048]{1,0:T(8,128)(2,1)S(1)} %pick.1.own), channel_id=1, source_target_pairs={{0,1},{1,0},{2,3},{3,2},{4,5},{5,4},{6,7},{7,6},{8,9},{9,8},{10,11... | collective-permute-start | bytes 196616 | tf_op jit(solution)/shard_map/ppermute | solution.py:515
  32.9 1.6 %collective-permute-start.6 = (bf16[16,2048]{1,0:T(8,128)(2,1)S(1)}, bf16[16,2048]{1,0:T(8,128)(2,1)S(1)}, u32[]{:S(2)}, u32[]{:S(2)}) collective-permute-start(bf16[16,2048]{1,0:T(8,128)(2,1)S(1)} %collective-permute-done.2.far), channel_id=1, source_target_pairs={{0,1},{1,0},{2,3},{3,2},{4,5},{5,4},{6,7},{7,6},{8,9},{9,8},{10,11... | collective-permute-start | bytes 196616 | tf_op jit(solution)/shard_map/ppermute | solution.py:515
  35.4 4.1 %collective-permute-start.7 = (f32[80,64]{1,0:T(8,128)S(1)}, f32[80,64]{1,0:T(8,128)S(1)}, u32[]{:S(2)}, u32[]{:S(2)}) collective-permute-start(f32[80,64]{1,0:T(8,128)S(1)} %gram.1), channel_id=1, source_target_pairs={{0,4},{4,0},{8,12},{12,8},{1,5},{5,1},{9,13},{13,9},{2,6},{6,2},{1... | collective-permute-start | bytes 61448 | tf_op jit(solution)/shard_map/ppermute | solution.py:641
  39.5 5.0 %collective-permute-start.10 = (f32[80,64]{1,0:T(8,128)S(1)}, f32[80,64]{1,0:T(8,128)S(1)}, u32[]{:S(2)}, u32[]{:S(2)}) collective-permute-start(f32[80,64]{1,0:T(8,128)S(1)} %add.3.one), channel_id=1, source_target_pairs={{0,8},{4,12},{8,0},{12,4},{1,9},{5,13},{9,1},{13,5},{2,10},{6,14},... | collective-permute-start | bytes 61448 | tf_op jit(solution)/shard_map/ppermute | solution.py:641
  42.3 6.7 %collective-permute-start.11 = (bf16[12,16,2048]{2,1,0:T(8,128)(2,1)S(1)}, bf16[12,16,2048]{2,1,0:T(8,128)(2,1)S(1)}, u32[]{:S(2)}, u32[]{:S(2)}) collective-permute-start(bf16[12,16,2048]{2,1,0:T(8,128)(2,1)S(1)} %post.7.more.own_more), channel_id=1, source_target_pairs={{0,1},{1,0},{2,3},{3,2},{4,5},{5,4},{6,7},{7,6},{8,9},{9,8},{10,11... | collective-permute-start | bytes 2359304 | tf_op jit(solution)/shard_map/ppermute | solution.py:515
  49.0 2.3 %collective-permute-start.12 = (bf16[12,16,2048]{2,1,0:T(8,128)(2,1)S(1)}, bf16[12,16,2048]{2,1,0:T(8,128)(2,1)S(1)}, u32[]{:S(2)}, u32[]{:S(2)}) collective-permute-start(bf16[12,16,2048]{2,1,0:T(8,128)(2,1)S(1)} %collective-permute-done.4.far_more), channel_id=1, source_target_pairs={{0,1},{1,0},{2,3},{3,2},{4,5},{5,4},{6,7},{7,6},{8,9},{9,8},{10,11... | collective-permute-start | bytes 2359304 | tf_op jit(solution)/shard_map/ppermute | solution.py:515
